TPU v7x, 32 devices: a whole 2x2x4 slice. The times are simulated.
32 devices in a mesh: groups: 2 (over y), blk: 8 (over z, x), head: 2 (over core).
Axes of the slice: x: 2, y: 2, z: 4, core: 2. Of those that a mesh axis runs over, the one named last changes fastest.
Arguments:
- tokens: float32 [3072, 1024], P(('groups', 'blk'), 'head'), parts along dimension 0, may hold values from -20 to 20
- norm_gain: float32 [1024], replicated, may hold values from 0.1 to 1.9
- qkv_weight: bfloat16 [3, 1024, 1024], P(None, None, 'head'), may hold values from -20 to 20
- out_weight: bfloat16 [1024, 1024], P('head'), may hold values from -0.1875 to 0.1875
- lateral_weight: bfloat16 [2, 1024, 256], replicated, may hold values from -0.1875 to 0.1875
- conv_weight: bfloat16 [2, 3, 3, 256, 256], replicated, may hold values from -0.125 to 0.125
- level_gains: float32 [2, 2, 256], replicated, may hold values from 0.1 to 1.9
Outputs:
- fine_map: bfloat16 [32, 96, 256], P(('groups', 'blk'), 'head'), parts along dimension 0
- coarse_map: bfloat16 [16, 48, 256], P(('groups', 'blk'), 'head'), parts along dimension 0
There are 2 independent parts, one for each index of `groups`. A program takes and returns all parts, laid end to end along the dimension named above; an argument that names none is the same for every part. Nothing has to cross between parts.
All inputs are finite; a program needn't handle non-finite values.
Results may differ from a plain program's by a relative error of at most 0.014.
The roundings to bfloat16 on the way count: a program that leaves them out, or rounds other values in their place, can miss the bound.
Values may be sent and summed in bfloat16 or wider, within the bound.
No kernel may reach another device: no remote copies, remote signals or barrier semaphores. Data moves between devices by JAX's collectives and lax.ppermute only.
A program may use at most 128 MiB of HBM per device.

v0:
```python
import math

import jax
import jax.numpy as jnp
from jax import lax
from jax.sharding import PartitionSpec as P

HEAD_DIM = 64
ROWS_DEV = 2
GW = 96


def padded_2(cells, sides, width):
    for axis, dim in sides:
        count = lax.axis_size(axis)
        ends = count - 1
        head = lax.slice_in_dim(cells, 0, width, axis=dim)
        tail = lax.slice_in_dim(cells, cells.shape[dim] - width, cells.shape[dim], axis=dim)
        cells = jnp.concatenate(
            [
                lax.ppermute(tail, axis, [(i, (i + 1) % count) for i in range(ends)]),
                cells,
                lax.ppermute(head, axis, [((i + 1) % count, i) for i in range(ends)]),
            ],
            axis=dim,
        )
    return cells


def layer_norm(values_in, gain_row):
    mean_row = jnp.mean(values_in, axis=-1, keepdims=True)
    centred = values_in - mean_row
    spread = jnp.mean(centred * centred, axis=-1, keepdims=True)
    return centred * lax.rsqrt(spread + 1e-06) * gain_row


def conv_taps(padded, kernel, row_count, col_count):
    total_out = jnp.zeros((row_count, col_count, kernel.shape[-1]), jnp.float32)
    for tap_row in range(3):
        for tap_col in range(3):
            window = padded[tap_row : tap_row + row_count, tap_col : tap_col + col_count]
            total_out = total_out + jnp.einsum(
                "rcd,de->rce", window, kernel[tap_row, tap_col], preferred_element_type=jnp.float32
            )
    return total_out


def lateral_norm(tile_in, lateral, gains):
    mixed = jnp.einsum("rcd,de->rce", tile_in, lateral, preferred_element_type=jnp.float32)
    return layer_norm(mixed, gains[0]).astype(jnp.bfloat16)


def make_attend(query_heads):
    tok_rows = query_heads.shape[0]
    heads_here = query_heads.shape[1]
    width_here = heads_here * HEAD_DIM
    score_scale = HEAD_DIM ** (-0.5)

    def attend_block(running_state, block_pair):
        running, totals, weighted = running_state
        key_block, value_block = block_pair
        key_count = key_block.shape[0]
        scores = (
            jnp.einsum(
                "qhd,khd->hqk",
                query_heads,
                key_block.reshape(key_count, heads_here, HEAD_DIM),
                preferred_element_type=jnp.float32,
            )
            * score_scale
        )
        newmax = jnp.maximum(running, jnp.max(scores, axis=-1))
        weights = jnp.exp(scores - newmax[:, :, None])
        factor = jnp.exp(running - newmax)
        totals = totals * factor + jnp.sum(weights, axis=-1)
        mixed_values = jnp.einsum(
            "hqk,khd->qhd",
            weights.astype(jnp.bfloat16),
            value_block.reshape(key_count, heads_here, HEAD_DIM),
            preferred_element_type=jnp.float32,
        )
        weighted = (
            weighted.reshape(tok_rows, heads_here, HEAD_DIM) * factor.T[:, :, None] + mixed_values
        )
        return ((newmax, totals, weighted.reshape(tok_rows, width_here)), None)

    def attend_piece(running_state, piece, start):
        key_piece, value_piece = piece
        key_count = key_piece.shape[0]
        block_rows = math.gcd(key_count, 1536)
        block_pairs = (
            key_piece.reshape(key_count // block_rows, block_rows, width_here),
            value_piece.reshape(key_count // block_rows, block_rows, width_here),
        )
        running_state, unused = lax.scan(attend_block, running_state, block_pairs)
        return running_state

    initial = (
        jnp.full((heads_here, tok_rows), -jnp.inf, jnp.float32),
        jnp.zeros((heads_here, tok_rows), jnp.float32),
        jnp.zeros((tok_rows, width_here), jnp.float32),
    )
    return (attend_piece, initial)


def finish_state(final_state):
    running, totals, weighted = final_state
    heads_here = totals.shape[0]
    tok_rows = totals.shape[1]
    return (
        (weighted.reshape(tok_rows, heads_here, HEAD_DIM) / totals.T[:, :, None])
        .reshape(tok_rows, heads_here * HEAD_DIM)
        .astype(jnp.bfloat16)
    )


def body(tokens, norm_gain, qkv_weight, out_weight, lateral_weight, conv_weight, level_gains):
    gathered = lax.all_gather(tokens, "head", axis=1, tiled=True)
    normed = layer_norm(gathered, norm_gain).astype(jnp.bfloat16)
    queries = jnp.dot(normed, qkv_weight[0], preferred_element_type=jnp.float32).astype(
        jnp.bfloat16
    )
    key_rows = jnp.dot(normed, qkv_weight[1], preferred_element_type=jnp.float32).astype(
        jnp.bfloat16
    )
    value_rows = jnp.dot(normed, qkv_weight[2], preferred_element_type=jnp.float32).astype(
        jnp.bfloat16
    )
    tok_rows = queries.shape[0]
    width_dev = queries.shape[1]
    heads_dev = width_dev // HEAD_DIM
    blk_count = lax.axis_size("blk")
    slices = blk_count // heads_dev
    slice_rows = tok_rows // slices
    query_send = jnp.transpose(
        queries.reshape(slices, slice_rows, heads_dev, HEAD_DIM), (2, 0, 1, 3)
    ).reshape(blk_count, slice_rows * HEAD_DIM)
    pair_heads = jnp.concatenate(
        (
            key_rows.reshape(tok_rows, heads_dev, HEAD_DIM),
            value_rows.reshape(tok_rows, heads_dev, HEAD_DIM),
        ),
        axis=2,
    )
    pair_heads = jnp.transpose(pair_heads, (1, 0, 2))
    pair_send = jnp.broadcast_to(
        pair_heads[:, None], (heads_dev, slices, tok_rows, 2 * HEAD_DIM)
    ).reshape(blk_count, tok_rows, 2 * HEAD_DIM)
    query_moved, pair_moved = (
        lax.all_to_all(query_send, "blk", split_axis=0, concat_axis=0, tiled=True),
        lax.all_to_all(pair_send, "blk", split_axis=0, concat_axis=0, tiled=True),
    )
    query_count = blk_count * slice_rows
    pair_whole = pair_moved.reshape(blk_count * tok_rows, 2 * HEAD_DIM)
    attend_piece, initial = make_attend(query_moved.reshape(query_count, 1, HEAD_DIM))
    one_head = finish_state(
        attend_piece(initial, (pair_whole[:, :HEAD_DIM], pair_whole[:, HEAD_DIM:]), 0)
    )
    returned = lax.all_to_all(
        one_head.reshape(blk_count, slice_rows * HEAD_DIM),
        "blk",
        split_axis=0,
        concat_axis=0,
        tiled=True,
    )
    attended = jnp.transpose(
        returned.reshape(heads_dev, slices, slice_rows, HEAD_DIM), (1, 2, 0, 3)
    ).reshape(tok_rows, width_dev)
    col_width = GW // lax.axis_size("head")
    partial_value = jnp.dot(attended, out_weight, preferred_element_type=jnp.float32).reshape(
        ROWS_DEV, GW, -1
    )
    branch = lax.psum_scatter(
        partial_value.astype(jnp.bfloat16), "head", scatter_dimension=1, tiled=True
    ).astype(jnp.float32)
    residual = lax.dynamic_slice_in_dim(
        gathered.reshape(ROWS_DEV, GW, -1), lax.axis_index("head") * col_width, col_width, 1
    )
    block_out = (residual + branch).astype(jnp.bfloat16)
    fine_in = lateral_norm(block_out, lateral_weight[0], level_gains[0])
    fine_pad = padded_2(fine_in, (("blk", 0), ("head", 1)), 1)
    fine_level = layer_norm(
        conv_taps(fine_pad, conv_weight[0], ROWS_DEV, col_width), level_gains[0, 1]
    ).astype(jnp.bfloat16)
    pooled = jnp.max(block_out.reshape(ROWS_DEV // 2, 2, col_width // 2, 2, -1), axis=(1, 3))
    coarse_in = lateral_norm(pooled, lateral_weight[1], level_gains[1])
    coarse_pad = padded_2(coarse_in, (("blk", 0), ("head", 1)), 1)
    coarse_level = layer_norm(
        conv_taps(coarse_pad, conv_weight[1], ROWS_DEV // 2, col_width // 2), level_gains[1, 1]
    ).astype(jnp.bfloat16)
    return (fine_level, coarse_level)


def solution(mesh):
    in_specs = (
        P(("groups", "blk"), "head"),
        P(),
        P(None, None, "head"),
        P("head", None),
        P(),
        P(),
        P(),
    )
    out_specs = (P(("groups", "blk"), "head", None), P(("groups", "blk"), "head", None))
    return jax.shard_map(body, mesh=mesh, in_specs=in_specs, out_specs=out_specs, check_vma=False)
```

profile of v0, /device:TPU:9, one launch (start us, length us, event | category | flops | bytes accessed | tf_op | source)
XLA Modules:
  0.0 112.7 jit_solution(10356113668897213138)
XLA Ops:
  7.2 3.0 %all_gather.3 = f32[192,1024]{1,0:T(8,128)S(1)} all-gather(f32[192,512]{1,0:T(8,128)} %param.7), channel_id=1, replica_groups=mesh['groups'=2,'blk'=8,'head'=2] {'head'}, dimensions={1}, use_global_device_ids=true | all-gather | bytes 1179648 | tf_op jit(solution)/shard_map/all_gather | solution.py:118
  10.3 0.2 multiply_reduce_fusion
  10.6 0.2 multiply_convert_fusion
  10.8 1.6 %convolution_convert_fusion.3 = bf16[192,512]{1,0:T(8,128)(2,1)S(1)} fusion(bf16[192,1024]{1,0:T(8,128)(2,1)S(1)} %multiply_convert_fusion, bf16[3,1024,512]{2,1,0:T(8,128)(2,1)} %param.9), kind=kOutput, calls=%fused_computation.16 | convolution fusion | flops 201424896 | bytes 1638400 | tf_op jit(solution)/shard_map/dot_general | solution.py:120
  12.5 0.2 copy.38
  12.7 0.2 all_to_all.17
  13.0 0.5 broadcast.179
  13.5 1.8 %reduce.17 = bf16[8,12288]{1,0:T(8,128)(2,1)S(1)} reduce(bf16[8,1,12288]{2,1,0:T(2,128)(2,1)S(1)} %all_to_all.17, bf16[]{:T(256)} %broadcast.179), dimensions={1}, to_apply=%all_to_all.17.reduce_sub_computation | reduce | bytes 393218 | tf_op jit(solution)/shard_map/all_to_all | solution.py:150
  15.3 0.8 reshape.309
  16.1 5.7 %all-to-all-start = ((bf16[8,2,6144]{2,1,0:T(2,128)(2,1)}), bf16[8,2,6144]{2,1,0:T(2,128)(2,1)S(1)}, u32[]{:S(2)}, u32[]{:S(2)}) async-start(bf16[8,2,6144]{2,1,0:T(2,128)(2,1)} %reshape.309), calls=%async_computation | async-start | bytes 393216 | tf_op jit(solution)/shard_map/all_to_all | solution.py:150
  21.8 1.6 %convolution_convert_fusion.2 = bf16[192,512]{1,0:T(8,128)(2,1)S(1)} fusion(bf16[192,1024]{1,0:T(8,128)(2,1)S(1)} %multiply_convert_fusion, bf16[3,1024,512]{2,1,0:T(8,128)(2,1)} %param.9), kind=kOutput, calls=%fused_computation.15 | convolution fusion | flops 201424896 | bytes 1638400 | tf_op jit(solution)/shard_map/dot_general | solution.py:123
  23.5 1.6 %convolution_convert_fusion.1 = bf16[192,512]{1,0:T(8,128)(2,1)S(1)} fusion(bf16[192,1024]{1,0:T(8,128)(2,1)S(1)} %multiply_convert_fusion, bf16[3,1024,512]{2,1,0:T(8,128)(2,1)} %param.9), kind=kOutput, calls=%fused_computation.14 | convolution fusion | flops 201424896 | bytes 1638400 | tf_op jit(solution)/shard_map/dot_general | solution.py:126
  25.3 0.9 copy.42
  26.3 1.1 all-to-all-done
  27.3 5.3 %all-to-all-start.1 = ((bf16[8,192,128]{2,1,0:T(8,128)(2,1)}), bf16[8,192,128]{2,1,0:T(8,128)(2,1)S(1)}, u32[]{:S(2)}, u32[]{:S(2)}) async-start(bf16[8,192,128]{2,1,0:T(8,128)(2,1)} %copy.42), calls=%async_computation.1 | async-start | bytes 786432 | tf_op jit(solution)/shard_map/all_to_all | solution.py:151
  32.6 0.2 reshape.310
  32.8 1.2 %reduce.15 = bf16[8,12288]{1,0:T(8,128)(2,1)S(1)} reduce(bf16[8,1,12288]{2,1,0:T(2,128)(2,1)S(1)} %reshape.310, bf16[]{:T(256)} %constant.51), dimensions={1}, to_apply=%all_to_all.14.reduce_sub_computation | reduce | bytes 393218 | tf_op jit(solution)/shard_map/all_to_all | solution.py:150
  34.0 0.4 reshape.279
  34.4 6.4 %all-to-all-done.1 = bf16[8,192,128]{2,1,0:T(8,128)(2,1)S(1)} async-done(((bf16[8,192,128]{2,1,0:T(8,128)(2,1)}), bf16[8,192,128]{2,1,0:T(8,128)(2,1)S(1)}, u32[]{:S(2)}, u32[]{:S(2)}) %all-to-all-start.1) | async-done | bytes 393248 | tf_op jit(solution)/shard_map/all_to_all | solution.py:151
  40.7 1.4 %fusion.119 = (f32[1536]{0:T(1024)S(1)}, f32[1536,1536]{0,1:T(8,128)S(1)}) fusion(bf16[1536,64]{1,0:T(8,128)(2,1)S(1)} %reshape.279, bf16[1536,128]{1,0:T(8,128)(2,1)S(1)} %bitcast.176), kind=kOutput, calls=%fused_computation.177 | convolution fusion | flops 306706944 | bytes 10033152 | tf_op jit(solution)/shard_map/while/body/eval_jaxpr/qhd,khd->hqk/dot_general | solution.py:64
  42.2 1.3 %fusion = f32[1536]{0:T(1024)S(1)} fusion(f32[1536,1536]{0,1:T(8,128)S(1)} %get-tuple-element.42, f32[1536]{0:T(1024)S(1)} %get-tuple-element.41), kind=kLoop, calls=%fused_computation.2 | loop fusion | flops 4717056 | bytes 9449472 | tf_op jit(solution)/shard_map/while/body/eval_jaxpr/reduce_sum | solution.py:75
  43.5 1.6 %fusion.17 = bf16[1536,1,64]{0,2,1:T(8,128)(2,1)S(1)} fusion(f32[1536,1536]{0,1:T(8,128)S(1)} %get-tuple-element.42, f32[1536]{0:T(1024)S(1)} %get-tuple-element.41, bf16[1536,128]{1,0:T(8,128)(2,1)S(1)} %bitcast.177, f32[1536]{0:T(1024)S(1)} %get-tuple-element.36, f32[1536]{0:T(1024)S(1)} %get-tuple-element.35), kind=kOutput, calls=%fused_computation.10 | convolution fusion | flops 307003392 | bytes 10045440 | tf_op jit(solution)/shard_map/while/body/eval_jaxpr/hqk,khd->qhd/dot_general | solution.py:76
  45.1 0.2 copy.43
  45.3 0.2 convert_element_type.78
  45.6 1.8 %reduce.18 = bf16[8,12288]{1,0:T(8,128)(2,1)S(1)} reduce(bf16[8,1,12288]{2,1,0:T(2,128)(2,1)S(1)} %convert_element_type.78, bf16[]{:T(256)} %broadcast.179), dimensions={1}, to_apply=%convert_element_type.78.reduce_sub_computation | reduce | bytes 393218 | tf_op jit(solution)/shard_map/convert_element_type | solution.py:113
  47.5 11.7 %all_to_all.21 = bf16[8,2,6144]{2,1,0:T(2,128)(2,1)S(1)} all-to-all(bf16[8,2,6144]{2,1,0:T(2,128)(2,1)S(1)} %reshape.311), channel_id=1, replica_groups=mesh['groups'=2,'blk'=8,'head'=2] {'blk'}, dimensions={0} | all-to-all | bytes 393216 | tf_op jit(solution)/shard_map/all_to_all | solution.py:159
  59.3 0.2 reshape.312
  59.4 1.2 %reduce.16 = bf16[8,12288]{1,0:T(8,128)(2,1)S(1)} reduce(bf16[8,1,12288]{2,1,0:T(2,128)(2,1)S(1)} %reshape.312, bf16[]{:T(256)} %constant.51), dimensions={1}, to_apply=%all_to_all.16.reduce_sub_computation | reduce | bytes 393218 | tf_op jit(solution)/shard_map/all_to_all | solution.py:159
  60.6 0.4 reshape.283
  61.0 0.3 copy.48
  61.3 0.3 reshape.303
  61.5 1.2 %convolution_convert_fusion = bf16[2,96,1024]{2,1,0:T(8,128)(2,1)} fusion(bf16[2,96,512]{2,1,0:T(8,128)(2,1)S(1)} %reshape.303, bf16[512,1024]{1,0:T(8,128)(2,1)S(1)} %copy-done), kind=kOutput, calls=%fused_computation.11 | convolution fusion | flops 201523200 | bytes 1638400 | tf_op jit(solution)/shard_map/dot_general | solution.py:170
  62.7 2.8 %slice_bitcast_fusion = (bf16[3,3,256,256]{3,2,1,0:T(8,128)(2,1)}, bf16[3,3,256,256]{3,2,1,0:T(8,128)(2,1)S(1)}) fusion(bf16[2,3,3,256,256]{4,3,2,1,0:T(8,128)(2,1)} %param.12), kind=kLoop, calls=%fused_computation.12 | loop fusion | bytes 4718592 | tf_op jit(solution)/shard_map/squeeze | solution.py:189
  65.6 7.5 %reduce-scatter.2.cloned.1.call-done = bf16[2,48,1024]{2,1,0:T(8,128)(2,1)} async-done(((bf16[2,96,1024]{2,1,0:T(8,128)(2,1)}), bf16[2,48,1024]{2,1,0:T(8,128)(2,1)}) %reduce-scatter.2.cloned.1.call-update) | async-done | bytes 196624 | tf_op jit(solution)/shard_map/reduce_scatter | solution.py:173
  73.0 1.0 fusion.116
  74.1 0.2 reduce_max.29
  74.4 1.4 %fusion.122 = (f32[24]{0:T(128)S(1)}, f32[24,256]{1,0:T(8,128)S(1)}) fusion(bf16[24,1024]{1,0:T(8,128)(2,1)S(1)} %reduce_max.29, bf16[2,1024,256]{2,1,0:T(8,128)(2,1)} %param.11), kind=kOutput, calls=%fused_computation.180 | convolution fusion | flops 12589032 | bytes 598112 | tf_op jit(solution)/shard_map/rcd,de->rce/dot_general | solution.py:49
  75.8 0.2 multiply_reduce_fusion.4
  76.1 3.1 %collective-permute-start.4 = (bf16[1,24,256]{2,1,0:T(8,128)(2,1)S(1)}, bf16[1,24,256]{2,1,0:T(8,128)(2,1)S(1)}, u32[]{:S(2)}, u32[]{:S(2)}) collective-permute-start(bf16[1,24,256]{2,1,0:T(8,128)(2,1)S(1)} %fusion.115), channel_id=1, source_target_pairs={{0,2},{2,4},{4,6},{6,8},{8,10},{10,12},{12,14},{1,3},{3,5},{5,7},{... | collective-permute-start | bytes 36872 | tf_op jit(solution)/shard_map/ppermute | solution.py:21
  79.2 3.1 %collective-permute-start.5 = (bf16[1,24,256]{2,1,0:T(8,128)(2,1)S(1)}, bf16[1,24,256]{2,1,0:T(8,128)(2,1)S(1)}, u32[]{:S(2)}, u32[]{:S(2)}) collective-permute-start(bf16[1,24,256]{2,1,0:T(8,128)(2,1)S(1)} %fusion.115), channel_id=1, source_target_pairs={{2,0},{4,2},{6,4},{8,6},{10,8},{12,10},{14,12},{3,1},{5,3},{7,5},{... | collective-permute-start | bytes 36872 | tf_op jit(solution)/shard_map/ppermute | solution.py:23
  82.3 1.3 %fusion.120 = (f32[2,48]{1,0:T(2,128)S(1)}, f32[2,48,256]{2,1,0:T(8,128)S(1)}) fusion(bf16[2,48,1024]{2,1,0:T(8,128)(2,1)S(1)} %get-tuple-element.17, bf16[2,1024,256]{2,1,0:T(8,128)(2,1)} %param.11), kind=kOutput, calls=%fused_computation.178 | convolution fusion | flops 50356128 | bytes 819584 | tf_op jit(solution)/shard_map/rcd,de->rce/dot_general | solution.py:49
  83.6 0.2 multiply_reduce_fusion.2
  83.9 2.2 %collective-permute-start = (bf16[1,48,256]{2,1,0:T(8,128)(2,1)S(1)}, bf16[1,48,256]{2,1,0:T(8,128)(2,1)S(1)}, u32[]{:S(2)}, u32[]{:S(2)}) collective-permute-start(bf16[1,48,256]{2,1,0:T(8,128)(2,1)S(1)} %get-tuple-element.31), channel_id=1, source_target_pairs={{0,2},{2,4},{4,6},{6,8},{8,10},{10,12},{12,14},{1,3},{3,5},{5,7},{... | collective-permute-start | bytes 73736 | tf_op jit(solution)/shard_map/ppermute | solution.py:21
  86.1 4.0 %collective-permute-start.1 = (bf16[1,48,256]{2,1,0:T(8,128)(2,1)S(1)}, bf16[1,48,256]{2,1,0:T(8,128)(2,1)S(1)}, u32[]{:S(2)}, u32[]{:S(2)}) collective-permute-start(bf16[1,48,256]{2,1,0:T(8,128)(2,1)S(1)} %get-tuple-element.32), channel_id=1, source_target_pairs={{2,0},{4,2},{6,4},{8,6},{10,8},{12,10},{14,12},{3,1},{5,3},{7,5},{... | collective-permute-start | bytes 73736 | tf_op jit(solution)/shard_map/ppermute | solution.py:23
  90.3 0.2 fusion.50
  90.5 3.2 %collective-permute-start.7 = (bf16[3,1,256]{2,1,0:T(2,128)(2,1)S(1)}, bf16[3,1,256]{2,1,0:T(2,128)(2,1)S(1)}, u32[]{:S(2)}, u32[]{:S(2)}) collective-permute-start(bf16[3,1,256]{2,1,0:T(2,128)(2,1)S(1)} %get-tuple-element.34), channel_id=1, source_target_pairs={{1,0},{3,2},{5,4},{7,6},{9,8},{11,10},{13,12},{15,14},{17,16},{19,... | collective-permute-start | bytes 4616 | tf_op jit(solution)/shard_map/ppermute | solution.py:23
  93.7 1.3 %collective-permute-start.6 = (bf16[3,1,256]{2,1,0:T(2,128)(2,1)S(1)}, bf16[3,1,256]{2,1,0:T(2,128)(2,1)S(1)}, u32[]{:S(2)}, u32[]{:S(2)}) collective-permute-start(bf16[3,1,256]{2,1,0:T(2,128)(2,1)S(1)} %get-tuple-element.33), channel_id=1, source_target_pairs={{0,1},{2,3},{4,5},{6,7},{8,9},{10,11},{12,13},{14,15},{16,17},{18,... | collective-permute-start | bytes 4616 | tf_op jit(solution)/shard_map/ppermute | solution.py:21
  95.3 1.5 %collective-permute-done.6 = bf16[3,1,256]{2,1,0:T(2,128)(2,1)S(1)} collective-permute-done((bf16[3,1,256]{2,1,0:T(2,128)(2,1)S(1)}, bf16[3,1,256]{2,1,0:T(2,128)(2,1)S(1)}, u32[]{:S(2)}, u32[]{:S(2)}) %collective-permute-start.6) | collective-permute-done | bytes 1568 | tf_op jit(solution)/shard_map/ppermute | solution.py:21
  97.1 0.2 fusion.52
  97.4 0.2 fusion.31
  97.5 0.3 fusion.123
  97.8 0.2 multiply_reduce_fusion.3
  98.0 0.7 fusion.73
  98.7 1.3 %collective-permute-start.2 = (bf16[4,1,256]{2,1,0:T(2,128)(2,1)S(1)}, bf16[4,1,256]{2,1,0:T(2,128)(2,1)S(1)}, u32[]{:S(2)}, u32[]{:S(2)}) collective-permute-start(bf16[4,1,256]{2,1,0:T(2,128)(2,1)S(1)} %get-tuple-element.29), channel_id=1, source_target_pairs={{0,1},{2,3},{4,5},{6,7},{8,9},{10,11},{12,13},{14,15},{16,17},{18,... | collective-permute-start | bytes 6152 | tf_op jit(solution)/shard_map/ppermute | solution.py:21
  100.0 3.0 %collective-permute-start.3 = (bf16[4,1,256]{2,1,0:T(2,128)(2,1)S(1)}, bf16[4,1,256]{2,1,0:T(2,128)(2,1)S(1)}, u32[]{:S(2)}, u32[]{:S(2)}) collective-permute-start(bf16[4,1,256]{2,1,0:T(2,128)(2,1)S(1)} %get-tuple-element.30), channel_id=1, source_target_pairs={{1,0},{3,2},{5,4},{7,6},{9,8},{11,10},{13,12},{15,14},{17,16},{19,... | collective-permute-start | bytes 6152 | tf_op jit(solution)/shard_map/ppermute | solution.py:23
  103.2 0.2 fusion.55
  103.4 0.5 collective-permute-done.3
  104.1 0.2 fusion.56
  104.2 0.2 fusion.59
  104.4 0.2 fusion.54
  104.5 0.2 fusion.22
  104.7 0.2 fusion.121
  105.0 0.2 multiply_reduce_fusion.1
  105.1 0.7 multiply_convert_fusion.1
  (49 shorter events, 2.4 us)
Async XLA Ops:
  7.2 54.4 %copy-start = (bf16[512,1024]{1,0:T(8,128)(2,1)S(1)}, bf16[512,1024]{1,0:T(8,128)(2,1)}, u32[]{:S(2)}) copy-start(bf16[512,1024]{1,0:T(8,128)(2,1)} %param.10) | copy-start | bytes 3145732
  7.2 3.4 %copy-start.2 = (f32[1024]{0:T(1024)S(1)}, f32[1024]{0:T(1024)}, u32[]{:S(2)}) copy-start(f32[1024]{0:T(1024)} %param.8) | copy-start | bytes 12292
  16.1 11.3 %all-to-all-start = ((bf16[8,2,6144]{2,1,0:T(2,128)(2,1)}), bf16[8,2,6144]{2,1,0:T(2,128)(2,1)S(1)}, u32[]{:S(2)}, u32[]{:S(2)}) async-start(bf16[8,2,6144]{2,1,0:T(2,128)(2,1)} %reshape.309), calls=%async_computation | async-start | bytes 393216 | tf_op jit(solution)/shard_map/all_to_all | solution.py:150
  27.3 13.4 %all-to-all-start.1 = ((bf16[8,192,128]{2,1,0:T(8,128)(2,1)}), bf16[8,192,128]{2,1,0:T(8,128)(2,1)S(1)}, u32[]{:S(2)}, u32[]{:S(2)}) async-start(bf16[8,192,128]{2,1,0:T(8,128)(2,1)} %copy.42), calls=%async_computation.1 | async-start | bytes 786432 | tf_op jit(solution)/shard_map/all_to_all | solution.py:151
  32.6 40.4 %reduce-scatter.2.cloned.1.call-start = ((), (), s32[]{:S(2)}) async-start(), calls=%async_computation.4 | async-start | bytes 589824 | tf_op jit(solution)/shard_map/reduce_scatter | solution.py:173
  61.2 1.5 %copy-start.3 = (f32[2,2,256]{2,1,0:T(2,128)S(1)}, f32[2,2,256]{2,1,0:T(2,128)}, u32[]{:S(2)}) copy-start(f32[2,2,256]{2,1,0:T(2,128)} %param.13) | copy-start | bytes 12292
  74.3 15.9 %copy-start.1 = (bf16[3,3,256,256]{3,2,1,0:T(8,128)(2,1)S(1)}, bf16[3,3,256,256]{3,2,1,0:T(8,128)(2,1)}, u32[]{:S(2)}) copy-start(bf16[3,3,256,256]{3,2,1,0:T(8,128)(2,1)} %get-tuple-element.18) | copy-start | bytes 3538948
  76.1 14.4 %collective-permute-start.4 = (bf16[1,24,256]{2,1,0:T(8,128)(2,1)S(1)}, bf16[1,24,256]{2,1,0:T(8,128)(2,1)S(1)}, u32[]{:S(2)}, u32[]{:S(2)}) collective-permute-start(bf16[1,24,256]{2,1,0:T(8,128)(2,1)S(1)} %fusion.115), channel_id=1, source_target_pairs={{0,2},{2,4},{4,6},{6,8},{8,10},{10,12},{12,14},{1,3},{3,5},{5,7},{... | collective-permute-start | bytes 36872 | tf_op jit(solution)/shard_map/ppermute | solution.py:21
  79.2 11.3 %collective-permute-start.5 = (bf16[1,24,256]{2,1,0:T(8,128)(2,1)S(1)}, bf16[1,24,256]{2,1,0:T(8,128)(2,1)S(1)}, u32[]{:S(2)}, u32[]{:S(2)}) collective-permute-start(bf16[1,24,256]{2,1,0:T(8,128)(2,1)S(1)} %fusion.115), channel_id=1, source_target_pairs={{2,0},{4,2},{6,4},{8,6},{10,8},{12,10},{14,12},{3,1},{5,3},{7,5},{... | collective-permute-start | bytes 36872 | tf_op jit(solution)/shard_map/ppermute | solution.py:23
  83.9 14.8 %collective-permute-start = (bf16[1,48,256]{2,1,0:T(8,128)(2,1)S(1)}, bf16[1,48,256]{2,1,0:T(8,128)(2,1)S(1)}, u32[]{:S(2)}, u32[]{:S(2)}) collective-permute-start(bf16[1,48,256]{2,1,0:T(8,128)(2,1)S(1)} %get-tuple-element.31), channel_id=1, source_target_pairs={{0,2},{2,4},{4,6},{6,8},{8,10},{10,12},{12,14},{1,3},{3,5},{5,7},{... | collective-permute-start | bytes 73736 | tf_op jit(solution)/shard_map/ppermute | solution.py:21
  86.1 12.6 %collective-permute-start.1 = (bf16[1,48,256]{2,1,0:T(8,128)(2,1)S(1)}, bf16[1,48,256]{2,1,0:T(8,128)(2,1)S(1)}, u32[]{:S(2)}, u32[]{:S(2)}) collective-permute-start(bf16[1,48,256]{2,1,0:T(8,128)(2,1)S(1)} %get-tuple-element.32), channel_id=1, source_target_pairs={{2,0},{4,2},{6,4},{8,6},{10,8},{12,10},{14,12},{3,1},{5,3},{7,5},{... | collective-permute-start | bytes 73736 | tf_op jit(solution)/shard_map/ppermute | solution.py:23
  90.5 6.5 %collective-permute-start.7 = (bf16[3,1,256]{2,1,0:T(2,128)(2,1)S(1)}, bf16[3,1,256]{2,1,0:T(2,128)(2,1)S(1)}, u32[]{:S(2)}, u32[]{:S(2)}) collective-permute-start(bf16[3,1,256]{2,1,0:T(2,128)(2,1)S(1)} %get-tuple-element.34), channel_id=1, source_target_pairs={{1,0},{3,2},{5,4},{7,6},{9,8},{11,10},{13,12},{15,14},{17,16},{19,... | collective-permute-start | bytes 4616 | tf_op jit(solution)/shard_map/ppermute | solution.py:23
  93.7 3.1 %collective-permute-start.6 = (bf16[3,1,256]{2,1,0:T(2,128)(2,1)S(1)}, bf16[3,1,256]{2,1,0:T(2,128)(2,1)S(1)}, u32[]{:S(2)}, u32[]{:S(2)}) collective-permute-start(bf16[3,1,256]{2,1,0:T(2,128)(2,1)S(1)} %get-tuple-element.33), channel_id=1, source_target_pairs={{0,1},{2,3},{4,5},{6,7},{8,9},{10,11},{12,13},{14,15},{16,17},{18,... | collective-permute-start | bytes 4616 | tf_op jit(solution)/shard_map/ppermute | solution.py:21
  98.7 4.7 %collective-permute-start.2 = (bf16[4,1,256]{2,1,0:T(2,128)(2,1)S(1)}, bf16[4,1,256]{2,1,0:T(2,128)(2,1)S(1)}, u32[]{:S(2)}, u32[]{:S(2)}) collective-permute-start(bf16[4,1,256]{2,1,0:T(2,128)(2,1)S(1)} %get-tuple-element.29), channel_id=1, source_target_pairs={{0,1},{2,3},{4,5},{6,7},{8,9},{10,11},{12,13},{14,15},{16,17},{18,... | collective-permute-start | bytes 6152 | tf_op jit(solution)/shard_map/ppermute | solution.py:21
  100.0 3.8 %collective-permute-start.3 = (bf16[4,1,256]{2,1,0:T(2,128)(2,1)S(1)}, bf16[4,1,256]{2,1,0:T(2,128)(2,1)S(1)}, u32[]{:S(2)}, u32[]{:S(2)}) collective-permute-start(bf16[4,1,256]{2,1,0:T(2,128)(2,1)S(1)} %get-tuple-element.30), channel_id=1, source_target_pairs={{1,0},{3,2},{5,4},{7,6},{9,8},{11,10},{13,12},{15,14},{17,16},{19,... | collective-permute-start | bytes 6152 | tf_op jit(solution)/shard_map/ppermute | solution.py:23
Sparse Core Ops, SparseCore 0:
  62.8 10.1 reduce-scatter.1
where the time goes:
time: 113 us
  starting transfers between devices  32.1 us (28%)
  waiting for transfers between devices  16.9 us (15%)
  blocking collectives  14.8 us (13%)
  matrix products  14.7 us (13%)
  between operations  14.5 us (13%)
  other arithmetic  11.5 us (10%)
  local copies, waits for them, and re-layouts  8.16 us (7%)
    ppermute x4, starting transfers between devices, padded_2(): lax.ppermute(head, axis, [((i + 1) % count, i) for i in range(ends)])  13.3 us
    all_to_all x1, blocking collectives, body(): lax.all_to_all(one_head.reshape(blk_count, slice_rows * HEAD_DIM), 'blk',...  11.7 us
    ppermute x4, starting transfers between devices, padded_2(): lax.ppermute(tail, axis, [(i, (i + 1) % count) for i in range(ends)])  7.87 us
    reduce_scatter x1, waiting for transfers between devices, body(): lax.psum_scatter(partial_value.astype(jnp.bfloat16), 'head', scatter_dime...  7.49 us
    all_to_all x1, waiting for transfers between devices, body(): lax.all_to_all(pair_send, 'blk', split_axis=0, concat_axis=0, tiled=True)  6.39 us
    all_to_all x1, starting transfers between devices, body(): lax.all_to_all(query_send, 'blk', split_axis=0, concat_axis=0, tiled=True)  5.69 us
    all_to_all x1, starting transfers between devices, body(): lax.all_to_all(pair_send, 'blk', split_axis=0, concat_axis=0, tiled=True)  5.28 us
    all_gather x1, blocking collectives, body(): gathered = lax.all_gather(tokens, 'head', axis=1, tiled=True)  3.01 us
  transfers between devices with their start and end apart: 11, of which 5 were waited for; matrix products, arithmetic and copies ran while one was open for 12% of the time, Pallas kernels for 0%

commit v1 on v0

v1 whole, which is shorter than its diff:
```python
import functools
import math

import jax
import jax.numpy as jnp
from jax import lax
from jax.experimental import pallas as pl
from jax.experimental.pallas import tpu as pltpu
from jax.sharding import PartitionSpec as P

HEAD_DIM = 64
LANES = 128
GRID_COLS = 96
EPS = 1e-06
BF16 = jnp.bfloat16
F32 = jnp.float32
VMEM_LIMIT = 48 * 1024 * 1024


def vmem_specs(count):
    return [pl.BlockSpec(memory_space=pltpu.VMEM)] * count


def kernel_params():
    return pltpu.CompilerParams(vmem_limit_bytes=VMEM_LIMIT)


def nbytes(*arrays):
    return sum(math.prod(a.shape) * jnp.dtype(a.dtype).itemsize for a in arrays)


def call(kernel, outs, args, scratch=(), flops=0, exps=0):
    outs = tuple(jax.ShapeDtypeStruct(shape, dtype) for shape, dtype in outs)
    return pl.pallas_call(
        kernel,
        out_shape=outs,
        in_specs=vmem_specs(len(args)),
        out_specs=tuple(vmem_specs(len(outs))),
        scratch_shapes=list(scratch),
        compiler_params=kernel_params(),
        cost_estimate=pl.CostEstimate(
            flops=flops, transcendentals=exps, bytes_accessed=nbytes(*args, *outs)
        ),
    )(*args)


def layer_norm(values_in, gain_row):
    mean_row = jnp.mean(values_in, axis=-1, keepdims=True)
    centred = values_in - mean_row
    spread = jnp.mean(centred * centred, axis=-1, keepdims=True)
    return centred * lax.rsqrt(spread + EPS) * gain_row


def dot(a, b):
    return jnp.dot(a, b, preferred_element_type=F32)


def low_lanes(shape):
    return lax.broadcasted_iota(jnp.int32, shape, len(shape) - 1) % LANES < HEAD_DIM


def half_turn(tile):
    return pltpu.roll(tile, HEAD_DIM, axis=1)


def project(mine_ref, other_ref, gain_ref, weight_ref):
    core = lax.axis_index("head")
    half = mine_ref.shape[1]
    width = 2 * half
    mine, other = mine_ref[...], other_ref[...]
    mean = (
        jnp.sum(mine, axis=-1, keepdims=True) + jnp.sum(other, axis=-1, keepdims=True)
    ) / width
    mine, other = mine - mean, other - mean
    spread = (
        jnp.sum(mine * mine, axis=-1, keepdims=True)
        + jnp.sum(other * other, axis=-1, keepdims=True)
    ) / width
    scale = lax.rsqrt(spread + EPS)
    mine = (mine * scale * gain_ref[pl.ds(core, 1), :]).astype(BF16)
    other = (other * scale * gain_ref[pl.ds(1 - core, 1), :]).astype(BF16)
    mine_at = pl.ds(pl.multiple_of(core * half, half), half)
    other_at = pl.ds(pl.multiple_of((1 - core) * half, half), half)
    return [
        dot(mine, weight_ref[part, mine_at, :]) + dot(other, weight_ref[part, other_at, :])
        for part in range(3)
    ]


def qkv_kernel(mine_ref, other_ref, gain_ref, weight_ref, send_ref):
    queries, keys, values = project(mine_ref, other_ref, gain_ref, weight_ref)
    rows = queries.shape[0]
    low = low_lanes((rows, LANES))
    low_q = low_lanes((rows // 2, LANES))
    for pair in range(queries.shape[1] // LANES):
        cols = slice(pair * LANES, (pair + 1) * LANES)
        key, value = keys[:, cols], values[:, cols]
        top, bottom = queries[: rows // 2, cols], queries[rows // 2 :, cols]
        send_ref[2 * pair, :rows] = jnp.where(low, key, half_turn(value)).astype(BF16)
        send_ref[2 * pair + 1, :rows] = jnp.where(low, half_turn(key), value).astype(BF16)
        send_ref[2 * pair, rows:] = jnp.where(low_q, top, half_turn(bottom)).astype(BF16)
        send_ref[2 * pair + 1, rows:] = jnp.where(low_q, half_turn(top), bottom).astype(BF16)


def plain_qkv_kernel(mine_ref, other_ref, gain_ref, weight_ref, q_ref, k_ref, v_ref):
    for ref, value in zip(
        (q_ref, k_ref, v_ref), project(mine_ref, other_ref, gain_ref, weight_ref)
    ):
        ref[...] = value.astype(BF16)


def attend_kernel(got_ref, out_ref, pair_ref):
    blocks, packed_rows = got_ref.shape[0], out_ref.shape[1]
    rows = 2 * packed_rows
    for block in range(blocks):
        pair_ref[block * rows : (block + 1) * rows] = got_ref[block, :rows]
    factor = HEAD_DIM ** (-0.5) * math.log2(math.e)
    low = low_lanes((packed_rows, LANES))
    for block in range(blocks):
        packed = got_ref[block, rows:].astype(F32)
        queries = jnp.concatenate(
            [jnp.where(low, packed, 0.0), jnp.where(low, half_turn(packed), 0.0)], axis=0
        ).astype(BF16)
        scores = lax.dot_general(
            queries, pair_ref[...], (((1,), (1,)), ((), ())), preferred_element_type=F32
        )
        top = jnp.max(scores, axis=-1, keepdims=True)
        weights = jnp.exp2((scores - top) * factor)
        total = jnp.sum(weights, axis=-1, keepdims=True)
        mixed = dot(weights.astype(BF16), pair_ref[...]) / total
        out_ref[block] = jnp.where(
            low, half_turn(mixed[:packed_rows]), mixed[packed_rows:]
        ).astype(BF16)


def out_terms(attended, weight_ref, mine_ref, other_ref, send_ref, keep_ref, full_ref):
    core = lax.axis_index("head")
    window = send_ref.shape[1]
    half = mine_ref.shape[1]
    shift = GRID_COLS - window
    full_ref[...] = dot(attended, weight_ref[...])
    for row in range(send_ref.shape[0]):
        there = pl.ds(pl.multiple_of(row * GRID_COLS + (1 - core) * shift, 8), window)
        send_ref[row] = full_ref[there, :].astype(BF16)
        here = pl.ds(pl.multiple_of(row * GRID_COLS + core * shift, 8), window)
        for part, ref in ((core, mine_ref), (1 - core, other_ref)):
            cols = pl.ds(pl.multiple_of(part * half, half), half)
            keep_ref[row, :, cols] = full_ref[here, cols] + ref[here, :]


def out_kernel(back_ref, weight_ref, mine_ref, other_ref, send_ref, keep_ref, full_ref, att_ref):
    packed_rows = back_ref.shape[1]
    low = low_lanes((packed_rows, LANES))
    for pair in range(back_ref.shape[0] // 2):
        cols = slice(pair * LANES, (pair + 1) * LANES)
        left = back_ref[2 * pair].astype(F32)
        right = back_ref[2 * pair + 1].astype(F32)
        att_ref[:packed_rows, cols] = jnp.where(low, left, half_turn(right)).astype(BF16)
        att_ref[packed_rows:, cols] = jnp.where(low, half_turn(left), right).astype(BF16)
    out_terms(att_ref[...], weight_ref, mine_ref, other_ref, send_ref, keep_ref, full_ref)


def plain_out_kernel(att_ref, weight_ref, mine_ref, other_ref, send_ref, keep_ref, full_ref):
    out_terms(att_ref[...], weight_ref, mine_ref, other_ref, send_ref, keep_ref, full_ref)


def lateral_kernel(keep_ref, got_ref, lateral_ref, gain_ref, up_ref, down_ref, pool_ref):
    window, features = keep_ref.shape[1], keep_ref.shape[2]
    cells = (keep_ref[...] + got_ref[...].astype(F32)).astype(BF16)
    fine = layer_norm(
        dot(cells.reshape(2 * window, features), lateral_ref[0]), gain_ref[0, 0][None, :]
    ).astype(BF16)
    up_ref[:window] = fine[:window]
    down_ref[:window] = fine[window:]
    tall = jnp.maximum(cells[0].astype(F32), cells[1].astype(F32))
    pooled = []
    for part in range(features // LANES):
        pool_ref[part] = tall[:, part * LANES : (part + 1) * LANES]
        even = pool_ref[part, pl.ds(0, window // 2, stride=2), :]
        odd = pool_ref[part, pl.ds(1, window // 2, stride=2), :]
        pooled.append(jnp.maximum(even, odd).astype(BF16))
    pooled = jnp.concatenate(pooled, axis=1)
    coarse = layer_norm(dot(pooled, lateral_ref[1]), gain_ref[1, 0][None, :]).astype(BF16)
    up_ref[window:] = coarse
    down_ref[window:] = coarse


def conv_level(stacked_ref, weight_ref, level, rows, window, sum_ref):
    block = rows * window
    place = lax.broadcasted_iota(jnp.int32, (block, weight_ref.shape[-1]), 0) % window
    taps = []
    for tap_col in range(3):
        total = None
        for tap_row in range(3):
            term = dot(
                stacked_ref[tap_row * window : tap_row * window + block],
                weight_ref[level, tap_row, tap_col],
            )
            total = term if total is None else total + term
        taps.append(total)
    left = jnp.where(place == 0, 0.0, pltpu.roll(taps[0], 1, axis=0))
    right = jnp.where(place == window - 1, 0.0, pltpu.roll(taps[2], block - 1, axis=0))
    sum_ref[...] = left + taps[1] + right


def conv_kernel(
    up_ref,
    down_ref,
    above_ref,
    below_ref,
    weight_ref,
    gain_ref,
    fine_ref,
    coarse_ref,
    fine_in,
    coarse_in,
    fine_sum,
    coarse_sum,
):
    core = lax.axis_index("head")
    window = fine_sum.shape[0] // 2
    half = window // 2
    has_above = lax.axis_index("blk") > 0
    has_below = lax.axis_index("blk") < lax.axis_size("blk") - 1
    fine_in[window : 2 * window] = up_ref[:window]
    fine_in[2 * window : 3 * window] = down_ref[:window]
    coarse_in[half : 2 * half] = up_ref[window:]
    above = jnp.where(has_above, above_ref[...].astype(F32), 0.0).astype(BF16)
    below = jnp.where(has_below, below_ref[...].astype(F32), 0.0).astype(BF16)
    fine_in[:window] = above[:window]
    fine_in[3 * window :] = below[:window]
    coarse_in[:half] = above[window:]
    coarse_in[2 * half :] = below[window:]
    conv_level(fine_in, weight_ref, 0, 2, window, fine_sum)
    conv_level(coarse_in, weight_ref, 1, 1, half, coarse_sum)
    cols = fine_ref.shape[1]
    shift = GRID_COLS - window
    inset = cols - shift
    for row in range(2):
        here = pl.ds(pl.multiple_of(row * window + core * inset, 8), cols)
        fine_ref[row] = layer_norm(fine_sum[here, :], gain_ref[0, 1][None, :]).astype(BF16)
    here = pl.ds(pl.multiple_of(core * (inset // 2), 8), cols // 2)
    coarse_ref[0] = layer_norm(coarse_sum[here, :], gain_ref[1, 1][None, :]).astype(BF16)


def attend_shared(queries, keys, values):
    factor = HEAD_DIM ** (-0.5)
    step = math.gcd(keys.shape[0], 1536)
    rows = queries.shape[0]

    def block(state, pair):
        running, totals, weighted = state
        key, value = pair
        scores = (
            lax.dot_general(queries, key, (((1,), (1,)), ((), ())), preferred_element_type=F32)
            * factor
        )
        newmax = jnp.maximum(running, jnp.max(scores, axis=-1, keepdims=True))
        weights = jnp.exp(scores - newmax)
        shrink = jnp.exp(running - newmax)
        totals = totals * shrink + jnp.sum(weights, axis=-1, keepdims=True)
        weighted = weighted * shrink + dot(weights.astype(BF16), value)
        return (newmax, totals, weighted), None

    state = (
        jnp.full((rows, 1), -jnp.inf, F32),
        jnp.zeros((rows, 1), F32),
        jnp.zeros((rows, HEAD_DIM), F32),
    )
    state, _ = lax.scan(
        block, state, (keys.reshape(-1, step, HEAD_DIM), values.reshape(-1, step, HEAD_DIM))
    )
    return (state[2] / state[1]).astype(BF16)


def exchange(value):
    return lax.all_to_all(value, "blk", split_axis=0, concat_axis=0, tiled=True)


def attention_shared(mine, other, gain_halves, qkv_weight, slices):
    rows = mine.shape[0]
    width = qkv_weight.shape[2]
    heads = width // HEAD_DIM
    blocks = heads * slices
    share = rows // slices
    queries, keys, values = call(
        plain_qkv_kernel, [((rows, width), BF16)] * 3, (mine, other, gain_halves, qkv_weight)
    )
    query_send = jnp.transpose(
        queries.reshape(slices, share, heads, HEAD_DIM), (2, 0, 1, 3)
    ).reshape(blocks, share * HEAD_DIM)
    pair = jnp.concatenate(
        (keys.reshape(rows, heads, HEAD_DIM), values.reshape(rows, heads, HEAD_DIM)), axis=2
    )
    pair = jnp.transpose(pair, (1, 0, 2))
    pair_send = jnp.broadcast_to(pair[:, None], (heads, slices, rows, 2 * HEAD_DIM)).reshape(
        blocks, rows, 2 * HEAD_DIM
    )
    query_got = exchange(query_send).reshape(blocks * share, HEAD_DIM)
    pair_got = exchange(pair_send).reshape(blocks * rows, 2 * HEAD_DIM)
    one_head = attend_shared(query_got, pair_got[:, :HEAD_DIM], pair_got[:, HEAD_DIM:])
    back = exchange(one_head.reshape(blocks, share * HEAD_DIM))
    return jnp.transpose(back.reshape(heads, slices, share, HEAD_DIM), (1, 2, 0, 3)).reshape(
        rows, width
    )


def body(tokens, norm_gain, qkv_weight, out_weight, lateral_weight, conv_weight, level_gains):
    rows, half = tokens.shape
    features = out_weight.shape[1]
    width = qkv_weight.shape[2]
    heads = width // HEAD_DIM
    blocks = lax.axis_size("blk")
    cores = lax.axis_size("head")
    grid_rows = rows // GRID_COLS
    cols = GRID_COLS // cores
    channels = lateral_weight.shape[2]
    window = 2 * GRID_COLS // 3
    swap = [(i, cores - 1 - i) for i in range(cores)]

    other = lax.ppermute(tokens, "head", swap)
    gain_halves = norm_gain.reshape(cores, half)
    tail = (out_weight, tokens, other)
    tail_outs = [
        ((grid_rows, window, features), BF16),
        ((grid_rows, window, features), F32),
    ]
    full = pltpu.VMEM((rows, features), F32)
    out_flops = 2 * rows * width * features
    if heads == blocks:
        (send,) = call(
            qkv_kernel,
            [((blocks, rows + rows // 2, LANES), BF16)],
            (tokens, other, gain_halves, qkv_weight),
            flops=6 * rows * features * width,
        )
        got = exchange(send)
        total = blocks * rows
        (one_head,) = call(
            attend_kernel,
            [((blocks, rows // 2, LANES), BF16)],
            (got,),
            [pltpu.VMEM((total, LANES), BF16)],
            flops=4 * total * total * LANES,
            exps=total * total,
        )
        back = exchange(one_head)
        peer_term, keep = call(
            out_kernel,
            tail_outs,
            (back,) + tail,
            [full, pltpu.VMEM((rows, width), BF16)],
            flops=out_flops,
        )
    else:
        attended = attention_shared(tokens, other, gain_halves, qkv_weight, blocks // heads)
        peer_term, keep = call(plain_out_kernel, tail_outs, (attended,) + tail, [full], out_flops)
    peer_term = lax.ppermute(peer_term, "head", swap)

    message = (window + window // 2, channels)
    up, down = call(
        lateral_kernel,
        [(message, BF16), (message, BF16)],
        (keep, peer_term, lateral_weight, level_gains),
        [pltpu.VMEM((features // LANES, window, LANES), F32)],
        flops=5 * window * features * channels,
    )
    above = lax.ppermute(down, "blk", [(i, (i + 1) % blocks) for i in range(blocks)])
    below = lax.ppermute(up, "blk", [((i + 1) % blocks, i) for i in range(blocks)])
    return call(
        conv_kernel,
        [((grid_rows, cols, channels), BF16), ((grid_rows // 2, cols // 2, channels), BF16)],
        (up, down, above, below, conv_weight, level_gains),
        [
            pltpu.VMEM((4 * window, channels), BF16),
            pltpu.VMEM((3 * window // 2, channels), BF16),
            pltpu.VMEM((2 * window, channels), F32),
            pltpu.VMEM((window // 2, channels), F32),
        ],
        flops=45 * window * channels * channels,
    )


def solution(mesh):
    in_specs = (
        P(("groups", "blk"), "head"),
        P(),
        P(None, None, "head"),
        P("head", None),
        P(),
        P(),
        P(),
    )
    out_specs = (P(("groups", "blk"), "head", None), P(("groups", "blk"), "head", None))
    return jax.shard_map(body, mesh=mesh, in_specs=in_specs, out_specs=out_specs, check_vma=False)
```

time: 113 us -> 58.8 us (0.52)
  the two profiles are of different devices: /device:TPU:9 before, /device:TPU:0 now
where the time goes in v1:
time: 58.8 us; the launch traced here: 58.5 us
  blocking collectives  34.7 us (59%)
  waiting for transfers between devices  9.02 us (15%)
  Pallas kernels  7.7 us (13%)
  local copies, waits for them, and re-layouts  3.6 us (6%)
  starting transfers between devices  2.71 us (5%)
  between operations  0.7 us (1%)
    all_to_all x2, blocking collectives, exchange(): return lax.all_to_all(value, 'blk', split_axis=0, concat_axis=0, tiled=True)  34.7 us
    pallas_call x5, Pallas kernels, call(): pl.pallas_call(kernel, out_shape=outs, in_specs=vmem_specs(len(args)), ou...  7.7 us
    ppermute x1, waiting for transfers between devices, body(): lax.ppermute(down, 'blk', [(i, (i + 1) % blocks) for i in range(blocks)])  4.57 us
    unnamed x14, local copies, waits for them, and re-layouts  2.91 us
    ppermute x1, waiting for transfers between devices, body(): lax.ppermute(up, 'blk', [((i + 1) % blocks, i) for i in range(blocks)])  2.06 us
    ppermute x1, starting transfers between devices, body(): lax.ppermute(up, 'blk', [((i + 1) % blocks, i) for i in range(blocks)])  1.93 us
    ppermute x1, waiting for transfers between devices, body(): peer_term = lax.ppermute(peer_term, 'head', swap)  1.52 us
  transfers between devices with their start and end apart: 4, of which 4 were waited for; matrix products, arithmetic and copies ran while one was open for 1% of the time, Pallas kernels for 0%

profile of v1, /device:TPU:0, one launch (start us, length us, event | category | flops | bytes accessed | tf_op | source)
XLA Modules:
  0.0 58.5 jit_solution(10311816773573843926)
XLA Ops:
  0.6 0.6 collective-permute-start
  1.2 0.7 %reshape.7.gain_ref = f32[2,512]{1,0:T(2,128)S(1)} reshape(f32[1024]{0:T(1024)} %param.8) | data formatting | bytes 8192 | tf_op jit(solution)/shard_map/reshape | solution.py:322
  1.9 0.9 %collective-permute-done.other_ref = f32[192,512]{1,0:T(8,128)S(1)} collective-permute-done((f32[192,512]{1,0:T(8,128)}, f32[192,512]{1,0:T(8,128)S(1)}, u32[]{:S(2)}, u32[]{:S(2)}) %collective-permute-start) | collective-permute-done | bytes 393248 | tf_op jit(solution)/shard_map/ppermute | solution.py:321
  2.7 0.0 copy-start
  2.8 1.9 %copy-done = bf16[3,1024,512]{2,1,0:T(8,128)(2,1)S(1)} copy-done((bf16[3,1024,512]{2,1,0:T(8,128)(2,1)S(1)}, bf16[3,1024,512]{2,1,0:T(8,128)(2,1)}, u32[]{:S(2)}) %copy-start) | copy-done | bytes 3145752
  4.6 0.0 copy-start.2
  4.6 1.0 %copy-done.2 = f32[192,512]{1,0:T(8,128)S(1)} copy-done((f32[192,512]{1,0:T(8,128)S(1)}, f32[192,512]{1,0:T(8,128)}, u32[]{:S(2)}) %copy-start.2) | copy-done | bytes 393240
  5.6 1.1 %shard_map.86 = bf16[8,288,128]{2,1,0:T(8,128)(2,1)S(1)} custom-call(f32[192,512]{1,0:T(8,128)S(1)} %copy-done.2, f32[192,512]{1,0:T(8,128)S(1)} %collective-permute-done.other_ref, f32[2,512]{1,0:T(2,128)S(1)} %reshape.7.gain_ref, bf16[3,1024,512]{2,1,0:T(8,128)(2,1)S(1)} %copy-done), custom_call_target="tpu_custom_call" | custom-call | flops 603979776 | bytes 4526080 | tf_op jit(solution)/shard_map/pallas_call | solution.py:34
  6.7 0.0 copy-start.3
  6.7 0.0 copy-start.5
  6.8 23.9 %all_to_all.10.got_ref = bf16[8,288,128]{2,1,0:T(8,128)(2,1)S(1)} all-to-all(bf16[8,288,128]{2,1,0:T(8,128)(2,1)S(1)} %shard_map.86), channel_id=1, replica_groups=mesh['groups'=2,'blk'=8,'head'=2] {'blk'}, dimensions={0} | all-to-all | bytes 1179648 | tf_op jit(solution)/shard_map/all_to_all | solution.py:277
  30.7 0.0 copy-start.4
  30.7 0.0 copy-start.6
  30.7 4.4 %shard_map.87 = bf16[8,96,128]{2,1,0:T(8,128)(2,1)S(1)} custom-call(bf16[8,288,128]{2,1,0:T(8,128)(2,1)S(1)} %all_to_all.10.got_ref), custom_call_target="tpu_custom_call" | custom-call | flops 1207959552 | bytes 786432 | tf_op jit(solution)/shard_map/pallas_call | solution.py:34
  35.1 0.0 copy-start.1
  35.1 10.8 %all_to_all.11.back_ref = bf16[8,96,128]{2,1,0:T(8,128)(2,1)S(1)} all-to-all(bf16[8,96,128]{2,1,0:T(8,128)(2,1)S(1)} %shard_map.87), channel_id=1, replica_groups=mesh['groups'=2,'blk'=8,'head'=2] {'blk'}, dimensions={0} | all-to-all | bytes 393216 | tf_op jit(solution)/shard_map/all_to_all | solution.py:277
  45.9 0.0 copy-done.3
  45.9 0.0 copy-done.5
  45.9 0.5 shard_map.88
  46.4 0.1 collective-permute-start.1
  46.5 1.5 %collective-permute-done.1.got_ref = bf16[2,64,1024]{2,1,0:T(8,128)(2,1)S(1)} collective-permute-done((bf16[2,64,1024]{2,1,0:T(8,128)(2,1)S(1)}, bf16[2,64,1024]{2,1,0:T(8,128)(2,1)S(1)}, u32[]{:S(2)}, u32[]{:S(2)}) %collective-permute-start.1) | collective-permute-done | bytes 262176 | tf_op jit(solution)/shard_map/ppermute | solution.py:358
  48.0 0.0 copy-done.4
  48.0 0.0 copy-done.6
  48.0 0.5 shard_map.89
  48.5 1.9 %collective-permute-start.3 = (bf16[96,256]{1,0:T(8,128)(2,1)S(1)}, bf16[96,256]{1,0:T(8,128)(2,1)S(1)}, u32[]{:S(2)}, u32[]{:S(2)}) collective-permute-start(bf16[96,256]{1,0:T(8,128)(2,1)S(1)} %get-tuple-element.8.up_ref), channel_id=1, source_target_pairs={{2,0},{4,2},{6,4},{8,6},{10,8},{12,10},{14,12},{0,14},{3,1},{5,3},... | collective-permute-start | bytes 147464 | tf_op jit(solution)/shard_map/ppermute | solution.py:369
  50.4 0.1 collective-permute-start.2
  50.6 2.1 %collective-permute-done.3.below_ref = bf16[96,256]{1,0:T(8,128)(2,1)S(1)} collective-permute-done((bf16[96,256]{1,0:T(8,128)(2,1)S(1)}, bf16[96,256]{1,0:T(8,128)(2,1)S(1)}, u32[]{:S(2)}, u32[]{:S(2)}) %collective-permute-start.3) | collective-permute-done | bytes 49184 | tf_op jit(solution)/shard_map/ppermute | solution.py:369
  52.6 4.6 %collective-permute-done.2.above_ref = bf16[96,256]{1,0:T(8,128)(2,1)S(1)} collective-permute-done((bf16[96,256]{1,0:T(8,128)(2,1)S(1)}, bf16[96,256]{1,0:T(8,128)(2,1)S(1)}, u32[]{:S(2)}, u32[]{:S(2)}) %collective-permute-start.2) | collective-permute-done | bytes 49184 | tf_op jit(solution)/shard_map/ppermute | solution.py:368
  57.2 0.0 copy-done.1
  57.2 1.3 %shard_map.90 = (bf16[2,48,256]{2,1,0:T(8,128)(2,1)}, bf16[1,24,256]{2,1,0:T(8,128)(2,1)}) custom-call(bf16[96,256]{1,0:T(8,128)(2,1)S(1)} %get-tuple-element.8.up_ref, bf16[96,256]{1,0:T(8,128)(2,1)S(1)} %get-tuple-element.9.down_ref, bf16[96,256]{1,0:T(8,128)(2,1)S(1)} %collective-permute-done.2.above_ref, ...), custom_call_target="tpu_custom_call" | custom-call | flops 188743680 | bytes 2621440 | tf_op jit(solution)/shard_map/pallas_call | solution.py:34
Async XLA Ops:
  0.6 2.1 %collective-permute-start = (f32[192,512]{1,0:T(8,128)}, f32[192,512]{1,0:T(8,128)S(1)}, u32[]{:S(2)}, u32[]{:S(2)}) collective-permute-start(f32[192,512]{1,0:T(8,128)} %mine_ref.3), channel_id=1, source_target_pairs={{0,1},{1,0},{2,3},{3,2},{4,5},{5,4},{6,7},{7,6},{8,9},{9,8},{10,11... | collective-permute-start | bytes 1179656 | tf_op jit(solution)/shard_map/ppermute | solution.py:321
  2.7 1.9 %copy-start = (bf16[3,1024,512]{2,1,0:T(8,128)(2,1)S(1)}, bf16[3,1024,512]{2,1,0:T(8,128)(2,1)}, u32[]{:S(2)}) copy-start(bf16[3,1024,512]{2,1,0:T(8,128)(2,1)} %weight_ref.3) | copy-start | bytes 9437188
  4.6 1.0 %copy-start.2 = (f32[192,512]{1,0:T(8,128)S(1)}, f32[192,512]{1,0:T(8,128)}, u32[]{:S(2)}) copy-start(f32[192,512]{1,0:T(8,128)} %mine_ref.3) | copy-start | bytes 1179652
  6.7 39.1 %copy-start.3 = (f32[192,512]{1,0:T(8,128)S(1)}, f32[192,512]{1,0:T(8,128)}, u32[]{:S(2)}) copy-start(f32[192,512]{1,0:T(8,128)} %mine_ref.3) | copy-start | bytes 1179652
  6.7 39.1 %copy-start.5 = (bf16[512,1024]{1,0:T(8,128)(2,1)S(1)}, bf16[512,1024]{1,0:T(8,128)(2,1)}, u32[]{:S(2)}) copy-start(bf16[512,1024]{1,0:T(8,128)(2,1)} %weight_ref.4) | copy-start | bytes 3145732
  30.7 17.3 %copy-start.4 = (bf16[2,1024,256]{2,1,0:T(8,128)(2,1)S(1)}, bf16[2,1024,256]{2,1,0:T(8,128)(2,1)}, u32[]{:S(2)}) copy-start(bf16[2,1024,256]{2,1,0:T(8,128)(2,1)} %lateral_ref.1) | copy-start | bytes 3145732
  30.7 17.3 %copy-start.6 = (f32[2,2,256]{2,1,0:T(2,128)S(1)}, f32[2,2,256]{2,1,0:T(2,128)}, u32[]{:S(2)}) copy-start(f32[2,2,256]{2,1,0:T(2,128)} %gain_ref.3) | copy-start | bytes 12292
  35.1 22.2 %copy-start.1 = (bf16[2,3,3,256,256]{4,3,2,1,0:T(8,128)(2,1)S(1)}, bf16[2,3,3,256,256]{4,3,2,1,0:T(8,128)(2,1)}, u32[]{:S(2)}) copy-start(bf16[2,3,3,256,256]{4,3,2,1,0:T(8,128)(2,1)} %weight_ref.5) | copy-start | bytes 7077892
  46.4 1.6 %collective-permute-start.1 = (bf16[2,64,1024]{2,1,0:T(8,128)(2,1)S(1)}, bf16[2,64,1024]{2,1,0:T(8,128)(2,1)S(1)}, u32[]{:S(2)}, u32[]{:S(2)}) collective-permute-start(bf16[2,64,1024]{2,1,0:T(8,128)(2,1)S(1)} %get-tuple-element.7), channel_id=1, source_target_pairs={{0,1},{1,0},{2,3},{3,2},{4,5},{5,4},{6,7},{7,6},{8,9},{9,8},{10,11... | collective-permute-start | bytes 786440 | tf_op jit(solution)/shard_map/ppermute | solution.py:358
  48.5 4.1 %collective-permute-start.3 = (bf16[96,256]{1,0:T(8,128)(2,1)S(1)}, bf16[96,256]{1,0:T(8,128)(2,1)S(1)}, u32[]{:S(2)}, u32[]{:S(2)}) collective-permute-start(bf16[96,256]{1,0:T(8,128)(2,1)S(1)} %get-tuple-element.8.up_ref), channel_id=1, source_target_pairs={{2,0},{4,2},{6,4},{8,6},{10,8},{12,10},{14,12},{0,14},{3,1},{5,3},... | collective-permute-start | bytes 147464 | tf_op jit(solution)/shard_map/ppermute | solution.py:369
  50.4 6.8 %collective-permute-start.2 = (bf16[96,256]{1,0:T(8,128)(2,1)S(1)}, bf16[96,256]{1,0:T(8,128)(2,1)S(1)}, u32[]{:S(2)}, u32[]{:S(2)}) collective-permute-start(bf16[96,256]{1,0:T(8,128)(2,1)S(1)} %get-tuple-element.9.down_ref), channel_id=1, source_target_pairs={{0,2},{2,4},{4,6},{6,8},{8,10},{10,12},{12,14},{14,0},{1,3},{3,5},... | collective-permute-start | bytes 147464 | tf_op jit(solution)/shard_map/ppermute | solution.py:368

commit v2 on v1

--- a/solution.py
+++ b/solution.py
@@ -17,8 +17,8 @@
 VMEM_LIMIT = 48 * 1024 * 1024
 
 
-def vmem_specs(count):
-    return [pl.BlockSpec(memory_space=pltpu.VMEM)] * count
+def specs(count, space=pltpu.VMEM):
+    return [pl.BlockSpec(memory_space=space)] * count
 
 
 def kernel_params():
@@ -29,13 +29,13 @@
     return sum(math.prod(a.shape) * jnp.dtype(a.dtype).itemsize for a in arrays)
 
 
-def call(kernel, outs, args, scratch=(), flops=0, exps=0):
+def call(kernel, outs, args, scratch=(), flops=0, exps=0, space=pltpu.VMEM):
     outs = tuple(jax.ShapeDtypeStruct(shape, dtype) for shape, dtype in outs)
     return pl.pallas_call(
         kernel,
         out_shape=outs,
-        in_specs=vmem_specs(len(args)),
-        out_specs=tuple(vmem_specs(len(outs))),
+        in_specs=specs(len(args), space),
+        out_specs=tuple(specs(len(outs))),
         scratch_shapes=list(scratch),
         compiler_params=kernel_params(),
         cost_estimate=pl.CostEstimate(
@@ -61,6 +61,17 @@
 
 def half_turn(tile):
     return pltpu.roll(tile, HEAD_DIM, axis=1)
+
+
+def fetch_kernel(weight_ref, out_ref, sems):
+    copies = [
+        pltpu.make_async_copy(weight_ref.at[part], out_ref.at[part], sems.at[part])
+        for part in range(weight_ref.shape[0])
+    ]
+    for copy in copies:
+        copy.start()
+    for copy in copies:
+        copy.wait()
 
 
 def project(mine_ref, other_ref, gain_ref, weight_ref):
@@ -77,8 +88,10 @@
         + jnp.sum(other * other, axis=-1, keepdims=True)
     ) / width
     scale = lax.rsqrt(spread + EPS)
-    mine = (mine * scale * gain_ref[pl.ds(core, 1), :]).astype(BF16)
-    other = (other * scale * gain_ref[pl.ds(1 - core, 1), :]).astype(BF16)
+    low_gain, high_gain = gain_ref[:half][None, :], gain_ref[half:][None, :]
+    first = core == 0
+    mine = (mine * scale * jnp.where(first, low_gain, high_gain)).astype(BF16)
+    other = (other * scale * jnp.where(first, high_gain, low_gain)).astype(BF16)
     mine_at = pl.ds(pl.multiple_of(core * half, half), half)
     other_at = pl.ds(pl.multiple_of((1 - core) * half, half), half)
     return [
@@ -109,28 +122,34 @@
         ref[...] = value.astype(BF16)
 
 
-def attend_kernel(got_ref, out_ref, pair_ref):
+def attend_kernel(got_ref, out_ref, pair_ref, query_ref, value_ref, mixed_ref):
     blocks, packed_rows = got_ref.shape[0], out_ref.shape[1]
     rows = 2 * packed_rows
+    share = blocks * packed_rows
+    low = low_lanes((packed_rows, LANES))
     for block in range(blocks):
         pair_ref[block * rows : (block + 1) * rows] = got_ref[block, :rows]
+        packed = got_ref[block, rows:].astype(F32)
+        here = block * packed_rows
+        query_ref[here : here + packed_rows] = jnp.where(low, packed, 0.0).astype(BF16)
+        query_ref[share + here : share + here + packed_rows] = jnp.where(
+            low, half_turn(packed), 0.0
+        ).astype(BF16)
+    value_ref[...] = pair_ref[...].astype(F32).T[HEAD_DIM:].astype(BF16)
     factor = HEAD_DIM ** (-0.5) * math.log2(math.e)
-    low = low_lanes((packed_rows, LANES))
-    for block in range(blocks):
-        packed = got_ref[block, rows:].astype(F32)
-        queries = jnp.concatenate(
-            [jnp.where(low, packed, 0.0), jnp.where(low, half_turn(packed), 0.0)], axis=0
-        ).astype(BF16)
-        scores = lax.dot_general(
-            queries, pair_ref[...], (((1,), (1,)), ((), ())), preferred_element_type=F32
-        )
-        top = jnp.max(scores, axis=-1, keepdims=True)
-        weights = jnp.exp2((scores - top) * factor)
-        total = jnp.sum(weights, axis=-1, keepdims=True)
-        mixed = dot(weights.astype(BF16), pair_ref[...]) / total
-        out_ref[block] = jnp.where(
-            low, half_turn(mixed[:packed_rows]), mixed[packed_rows:]
-        ).astype(BF16)
+    tile = math.gcd(share, 256)
+    for part in range(2):
+        for start in range(0, share, tile):
+            queries = query_ref[part * share + start : part * share + start + tile]
+            scores = lax.dot_general(
+                pair_ref[...], queries, (((1,), (1,)), ((), ())), preferred_element_type=F32
+            )
+            top = jnp.max(scores, axis=0, keepdims=True)
+            weights = jnp.exp2((scores - top) * factor)
+            total = jnp.sum(weights, axis=0, keepdims=True)
+            mixed = dot(value_ref[...], weights.astype(BF16)) / total
+            mixed_ref[part * HEAD_DIM : (part + 1) * HEAD_DIM, start : start + tile] = mixed
+    out_ref[...] = mixed_ref[...].T.astype(BF16).reshape(out_ref.shape)
 
 
 def out_terms(attended, weight_ref, mine_ref, other_ref, send_ref, keep_ref, full_ref):
@@ -164,14 +183,17 @@
     out_terms(att_ref[...], weight_ref, mine_ref, other_ref, send_ref, keep_ref, full_ref)
 
 
-def lateral_kernel(keep_ref, got_ref, lateral_ref, gain_ref, up_ref, down_ref, pool_ref):
+def lateral_kernel(
+    keep_ref, got_ref, lateral_ref, gain_ref, near_ref, far_ref, pool_ref, fine_ref
+):
+    odd = lax.axis_index("blk") % 2
     window, features = keep_ref.shape[1], keep_ref.shape[2]
     cells = (keep_ref[...] + got_ref[...].astype(F32)).astype(BF16)
-    fine = layer_norm(
+    fine_ref[...] = layer_norm(
         dot(cells.reshape(2 * window, features), lateral_ref[0]), gain_ref[0, 0][None, :]
     ).astype(BF16)
-    up_ref[:window] = fine[:window]
-    down_ref[:window] = fine[window:]
+    near_ref[:window] = fine_ref[pl.ds(pl.multiple_of((1 - odd) * window, window), window), :]
+    far_ref[:window] = fine_ref[pl.ds(pl.multiple_of(odd * window, window), window), :]
     tall = jnp.maximum(cells[0].astype(F32), cells[1].astype(F32))
     pooled = []
     for part in range(features // LANES):
@@ -181,8 +203,8 @@
         pooled.append(jnp.maximum(even, odd).astype(BF16))
     pooled = jnp.concatenate(pooled, axis=1)
     coarse = layer_norm(dot(pooled, lateral_ref[1]), gain_ref[1, 0][None, :]).astype(BF16)
-    up_ref[window:] = coarse
-    down_ref[window:] = coarse
+    near_ref[window:] = coarse
+    far_ref[window:] = coarse
 
 
 def conv_level(stacked_ref, weight_ref, level, rows, window, sum_ref):
@@ -204,10 +226,10 @@
 
 
 def conv_kernel(
-    up_ref,
-    down_ref,
-    above_ref,
-    below_ref,
+    near_ref,
+    far_ref,
+    got_near_ref,
+    got_far_ref,
     weight_ref,
     gain_ref,
     fine_ref,
@@ -218,19 +240,19 @@
     coarse_sum,
 ):
     core = lax.axis_index("head")
+    odd = lax.axis_index("blk") % 2
     window = fine_sum.shape[0] // 2
     half = window // 2
-    has_above = lax.axis_index("blk") > 0
-    has_below = lax.axis_index("blk") < lax.axis_size("blk") - 1
-    fine_in[window : 2 * window] = up_ref[:window]
-    fine_in[2 * window : 3 * window] = down_ref[:window]
-    coarse_in[half : 2 * half] = up_ref[window:]
-    above = jnp.where(has_above, above_ref[...].astype(F32), 0.0).astype(BF16)
-    below = jnp.where(has_below, below_ref[...].astype(F32), 0.0).astype(BF16)
-    fine_in[:window] = above[:window]
-    fine_in[3 * window :] = below[:window]
-    coarse_in[:half] = above[window:]
-    coarse_in[2 * half :] = below[window:]
+    for ref, place in (
+        (near_ref, 2 - odd),
+        (far_ref, 1 + odd),
+        (got_near_ref, 3 - 3 * odd),
+        (got_far_ref, 3 * odd),
+    ):
+        fine_in[pl.ds(pl.multiple_of(place * window, window), window), :] = ref[:window]
+    coarse_in[half : 2 * half] = near_ref[window:]
+    for ref, place in ((got_near_ref, 2 - 2 * odd), (got_far_ref, 2 * odd)):
+        coarse_in[pl.ds(pl.multiple_of(place * half, half), half), :] = ref[window:]
     conv_level(fine_in, weight_ref, 0, 2, window, fine_sum)
     conv_level(coarse_in, weight_ref, 1, 1, half, coarse_sum)
     cols = fine_ref.shape[1]
@@ -277,14 +299,14 @@
     return lax.all_to_all(value, "blk", split_axis=0, concat_axis=0, tiled=True)
 
 
-def attention_shared(mine, other, gain_halves, qkv_weight, slices):
+def attention_shared(mine, other, norm_gain, qkv_weight, slices):
     rows = mine.shape[0]
     width = qkv_weight.shape[2]
     heads = width // HEAD_DIM
     blocks = heads * slices
     share = rows // slices
     queries, keys, values = call(
-        plain_qkv_kernel, [((rows, width), BF16)] * 3, (mine, other, gain_halves, qkv_weight)
+        plain_qkv_kernel, [((rows, width), BF16)] * 3, (mine, other, norm_gain, qkv_weight)
     )
     query_send = jnp.transpose(
         queries.reshape(slices, share, heads, HEAD_DIM), (2, 0, 1, 3)
@@ -319,7 +341,13 @@
     swap = [(i, cores - 1 - i) for i in range(cores)]
 
     other = lax.ppermute(tokens, "head", swap)
-    gain_halves = norm_gain.reshape(cores, half)
+    (near_weight,) = call(
+        fetch_kernel,
+        [(qkv_weight.shape, BF16)],
+        (qkv_weight,),
+        [pltpu.SemaphoreType.DMA((qkv_weight.shape[0],))],
+        space=pltpu.HBM,
+    )
     tail = (out_weight, tokens, other)
     tail_outs = [
         ((grid_rows, window, features), BF16),
@@ -331,7 +359,7 @@
         (send,) = call(
             qkv_kernel,
             [((blocks, rows + rows // 2, LANES), BF16)],
-            (tokens, other, gain_halves, qkv_weight),
+            (tokens, other, norm_gain, near_weight),
             flops=6 * rows * features * width,
         )
         got = exchange(send)
@@ -340,7 +368,12 @@
             attend_kernel,
             [((blocks, rows // 2, LANES), BF16)],
             (got,),
-            [pltpu.VMEM((total, LANES), BF16)],
+            [
+                pltpu.VMEM((total, LANES), BF16),
+                pltpu.VMEM((total, LANES), BF16),
+                pltpu.VMEM((HEAD_DIM, total), BF16),
+                pltpu.VMEM((2 * HEAD_DIM, total // 2), F32),
+            ],
             flops=4 * total * total * LANES,
             exps=total * total,
         )
@@ -353,24 +386,31 @@
             flops=out_flops,
         )
     else:
-        attended = attention_shared(tokens, other, gain_halves, qkv_weight, blocks // heads)
+        attended = attention_shared(
+            tokens, other, norm_gain, near_weight, blocks // heads
+        )
         peer_term, keep = call(plain_out_kernel, tail_outs, (attended,) + tail, [full], out_flops)
     peer_term = lax.ppermute(peer_term, "head", swap)
 
     message = (window + window // 2, channels)
-    up, down = call(
+    near, far = call(
         lateral_kernel,
         [(message, BF16), (message, BF16)],
         (keep, peer_term, lateral_weight, level_gains),
-        [pltpu.VMEM((features // LANES, window, LANES), F32)],
+        [
+            pltpu.VMEM((features // LANES, window, LANES), F32),
+            pltpu.VMEM((2 * window, channels), BF16),
+        ],
         flops=5 * window * features * channels,
     )
-    above = lax.ppermute(down, "blk", [(i, (i + 1) % blocks) for i in range(blocks)])
-    below = lax.ppermute(up, "blk", [((i + 1) % blocks, i) for i in range(blocks)])
+    far_pairs = [(i, i + 1) for i in range(1, blocks - 1, 2)]
+    far_pairs += [(j, i) for i, j in far_pairs]
+    got_far = lax.ppermute(far, "blk", far_pairs)
+    got_near = lax.ppermute(near, "blk", [(i, i ^ 1) for i in range(blocks)])
     return call(
         conv_kernel,
         [((grid_rows, cols, channels), BF16), ((grid_rows // 2, cols // 2, channels), BF16)],
-        (up, down, above, below, conv_weight, level_gains),
+        (near, far, got_near, got_far, conv_weight, level_gains),
         [
             pltpu.VMEM((4 * window, channels), BF16),
             pltpu.VMEM((3 * window // 2, channels), BF16),

time: 58.8 us -> 54.8 us (0.932)
  the two profiles are of different devices: /device:TPU:0 before, /device:TPU:6 now
where the time goes in v2:
time: 54.8 us; the launch traced here: 54.6 us
  blocking collectives  33.3 us (61%)
  Pallas kernels  11 us (20%)
  waiting for transfers between devices  5.66 us (10%)
  starting transfers between devices  3.86 us (7%)
  between operations  0.74 us (1%)
    all_to_all x2, blocking collectives, exchange(): return lax.all_to_all(value, 'blk', split_axis=0, concat_axis=0, tiled=True)  33.3 us
    pallas_call x6, Pallas kernels, call(): pl.pallas_call(kernel, out_shape=outs, in_specs=specs(len(args), space),...  11 us
    ppermute x1, waiting for transfers between devices, body(): got_far = lax.ppermute(far, 'blk', far_pairs)  3.71 us
    ppermute x1, starting transfers between devices, body(): got_far = lax.ppermute(far, 'blk', far_pairs)  2.72 us
    ppermute x1, waiting for transfers between devices, body(): peer_term = lax.ppermute(peer_term, 'head', swap)  1.52 us
  transfers between devices with their start and end apart: 4, of which 3 were waited for; matrix products, arithmetic and copies ran while one was open for 0% of the time, Pallas kernels for 4%

profile of v2, /device:TPU:6, one launch (start us, length us, event | category | flops | bytes accessed | tf_op | source)
XLA Modules:
  0.0 54.6 jit_solution(17729285162105370169)
XLA Ops:
  0.6 0.0 copy-start.1
  0.6 0.0 copy-start.5
  0.6 0.1 collective-permute-start
  0.7 1.9 %shard_map.86.weight_ref = bf16[3,1024,512]{2,1,0:T(8,128)(2,1)S(1)} custom-call(bf16[3,1024,512]{2,1,0:T(8,128)(2,1)} %weight_ref.3), custom_call_target="tpu_custom_call" | custom-call | bytes 6291456 | tf_op jit(solution)/shard_map/pallas_call | solution.py:34
  2.7 0.0 collective-permute-done.other_ref
  2.7 0.0 copy-done.1
  2.7 0.0 copy-done.5
  2.7 1.1 %shard_map.87 = bf16[8,288,128]{2,1,0:T(8,128)(2,1)S(1)} custom-call(f32[192,512]{1,0:T(8,128)S(1)} %copy-done.1, f32[192,512]{1,0:T(8,128)S(1)} %collective-permute-done.other_ref, f32[1024]{0:T(1024)S(1)} %copy-done.5, bf16[3,1024,512]{2,1,0:T(8,128)(2,1)S(1)} %shard_map.86.weight_ref), custom_call_target="tpu_custom_call" | custom-call | flops 603979776 | bytes 4526080 | tf_op jit(solution)/shard_map/pallas_call | solution.py:34
  3.7 0.0 copy-start.3
  3.8 22.2 %all_to_all.10.got_ref = bf16[8,288,128]{2,1,0:T(8,128)(2,1)S(1)} all-to-all(bf16[8,288,128]{2,1,0:T(8,128)(2,1)S(1)} %shard_map.87), channel_id=1, replica_groups=mesh['groups'=2,'blk'=8,'head'=2] {'blk'}, dimensions={0} | all-to-all | bytes 1179648 | tf_op jit(solution)/shard_map/all_to_all | solution.py:299
  26.0 0.0 copy-start.2
  26.0 0.0 copy-start.4
  26.0 5.7 %shard_map.88 = bf16[8,96,128]{2,1,0:T(8,128)(2,1)S(1)} custom-call(bf16[8,288,128]{2,1,0:T(8,128)(2,1)S(1)} %all_to_all.10.got_ref), custom_call_target="tpu_custom_call" | custom-call | flops 1207959552 | bytes 786432 | tf_op jit(solution)/shard_map/pallas_call | solution.py:34
  31.7 0.0 copy-start
  31.7 11.1 %all_to_all.11.back_ref = bf16[8,96,128]{2,1,0:T(8,128)(2,1)S(1)} all-to-all(bf16[8,96,128]{2,1,0:T(8,128)(2,1)S(1)} %shard_map.88), channel_id=1, replica_groups=mesh['groups'=2,'blk'=8,'head'=2] {'blk'}, dimensions={0} | all-to-all | bytes 393216 | tf_op jit(solution)/shard_map/all_to_all | solution.py:299
  42.8 0.0 copy-done.3
  42.8 0.5 shard_map.89
  43.3 0.1 collective-permute-start.1
  43.4 1.5 %collective-permute-done.1.got_ref = bf16[2,64,1024]{2,1,0:T(8,128)(2,1)S(1)} collective-permute-done((bf16[2,64,1024]{2,1,0:T(8,128)(2,1)S(1)}, bf16[2,64,1024]{2,1,0:T(8,128)(2,1)S(1)}, u32[]{:S(2)}, u32[]{:S(2)}) %collective-permute-start.1) | collective-permute-done | bytes 262176 | tf_op jit(solution)/shard_map/ppermute | solution.py:393
  44.9 0.0 copy-done.2
  44.9 0.0 copy-done.4
  44.9 0.5 shard_map.90
  45.4 1.0 %collective-permute-start.2 = (bf16[96,256]{1,0:T(8,128)(2,1)S(1)}, bf16[96,256]{1,0:T(8,128)(2,1)S(1)}, u32[]{:S(2)}, u32[]{:S(2)}) collective-permute-start(bf16[96,256]{1,0:T(8,128)(2,1)S(1)} %get-tuple-element.8.near_ref), channel_id=1, source_target_pairs={{0,2},{2,0},{4,6},{6,4},{8,10},{10,8},{12,14},{14,12},{1,3},{3,1},... | collective-permute-start | bytes 147464 | tf_op jit(solution)/shard_map/ppermute | solution.py:409
  46.4 2.7 %collective-permute-start.3 = (bf16[96,256]{1,0:T(8,128)(2,1)S(1)}, bf16[96,256]{1,0:T(8,128)(2,1)S(1)}, u32[]{:S(2)}, u32[]{:S(2)}) collective-permute-start(bf16[96,256]{1,0:T(8,128)(2,1)S(1)} %get-tuple-element.9.far_ref), channel_id=1, source_target_pairs={{2,4},{6,8},{10,12},{4,2},{8,6},{12,10},{3,5},{7,9},{11,13},{5,3},... | collective-permute-start | bytes 147464 | tf_op jit(solution)/shard_map/ppermute | solution.py:408
  49.2 0.4 collective-permute-done.2.got_near_ref
  49.6 3.7 %collective-permute-done.3.got_far_ref = bf16[96,256]{1,0:T(8,128)(2,1)S(1)} collective-permute-done((bf16[96,256]{1,0:T(8,128)(2,1)S(1)}, bf16[96,256]{1,0:T(8,128)(2,1)S(1)}, u32[]{:S(2)}, u32[]{:S(2)}) %collective-permute-start.3) | collective-permute-done | bytes 49184 | tf_op jit(solution)/shard_map/ppermute | solution.py:408
  53.3 0.0 copy-done
  53.3 1.3 %shard_map.91 = (bf16[2,48,256]{2,1,0:T(8,128)(2,1)}, bf16[1,24,256]{2,1,0:T(8,128)(2,1)}) custom-call(bf16[96,256]{1,0:T(8,128)(2,1)S(1)} %get-tuple-element.8.near_ref, bf16[96,256]{1,0:T(8,128)(2,1)S(1)} %get-tuple-element.9.far_ref, bf16[96,256]{1,0:T(8,128)(2,1)S(1)} %collective-permute-done.2.got_near_ref, ...), custom_call_target="tpu_custom_call" | custom-call | flops 188743680 | bytes 2621440 | tf_op jit(solution)/shard_map/pallas_call | solution.py:34
Async XLA Ops:
  0.6 2.0 %copy-start.1 = (f32[192,512]{1,0:T(8,128)S(1)}, f32[192,512]{1,0:T(8,128)}, u32[]{:S(2)}) copy-start(f32[192,512]{1,0:T(8,128)} %mine_ref.3) | copy-start | bytes 1179652
  0.6 2.0 %copy-start.5 = (f32[1024]{0:T(1024)S(1)}, f32[1024]{0:T(1024)}, u32[]{:S(2)}) copy-start(f32[1024]{0:T(1024)} %gain_ref.3) | copy-start | bytes 12292
  0.6 2.0 %collective-permute-start = (f32[192,512]{1,0:T(8,128)}, f32[192,512]{1,0:T(8,128)S(1)}, u32[]{:S(2)}, u32[]{:S(2)}) collective-permute-start(f32[192,512]{1,0:T(8,128)} %mine_ref.3), channel_id=1, source_target_pairs={{0,1},{1,0},{2,3},{3,2},{4,5},{5,4},{6,7},{7,6},{8,9},{9,8},{10,11... | collective-permute-start | bytes 1179656 | tf_op jit(solution)/shard_map/ppermute | solution.py:343
  3.7 39.1 %copy-start.3 = (bf16[512,1024]{1,0:T(8,128)(2,1)S(1)}, bf16[512,1024]{1,0:T(8,128)(2,1)}, u32[]{:S(2)}) copy-start(bf16[512,1024]{1,0:T(8,128)(2,1)} %weight_ref.4) | copy-start | bytes 3145732
  26.0 18.9 %copy-start.2 = (bf16[2,1024,256]{2,1,0:T(8,128)(2,1)S(1)}, bf16[2,1024,256]{2,1,0:T(8,128)(2,1)}, u32[]{:S(2)}) copy-start(bf16[2,1024,256]{2,1,0:T(8,128)(2,1)} %lateral_ref.1) | copy-start | bytes 3145732
  26.0 18.9 %copy-start.4 = (f32[2,2,256]{2,1,0:T(2,128)S(1)}, f32[2,2,256]{2,1,0:T(2,128)}, u32[]{:S(2)}) copy-start(f32[2,2,256]{2,1,0:T(2,128)} %gain_ref.5) | copy-start | bytes 12292
  31.7 21.6 %copy-start = (bf16[2,3,3,256,256]{4,3,2,1,0:T(8,128)(2,1)S(1)}, bf16[2,3,3,256,256]{4,3,2,1,0:T(8,128)(2,1)}, u32[]{:S(2)}) copy-start(bf16[2,3,3,256,256]{4,3,2,1,0:T(8,128)(2,1)} %weight_ref.5) | copy-start | bytes 7077892
  43.3 1.6 %collective-permute-start.1 = (bf16[2,64,1024]{2,1,0:T(8,128)(2,1)S(1)}, bf16[2,64,1024]{2,1,0:T(8,128)(2,1)S(1)}, u32[]{:S(2)}, u32[]{:S(2)}) collective-permute-start(bf16[2,64,1024]{2,1,0:T(8,128)(2,1)S(1)} %get-tuple-element.7), channel_id=1, source_target_pairs={{0,1},{1,0},{2,3},{3,2},{4,5},{5,4},{6,7},{7,6},{8,9},{9,8},{10,11... | collective-permute-start | bytes 786440 | tf_op jit(solution)/shard_map/ppermute | solution.py:393
  45.4 4.2 %collective-permute-start.2 = (bf16[96,256]{1,0:T(8,128)(2,1)S(1)}, bf16[96,256]{1,0:T(8,128)(2,1)S(1)}, u32[]{:S(2)}, u32[]{:S(2)}) collective-permute-start(bf16[96,256]{1,0:T(8,128)(2,1)S(1)} %get-tuple-element.8.near_ref), channel_id=1, source_target_pairs={{0,2},{2,0},{4,6},{6,4},{8,10},{10,8},{12,14},{14,12},{1,3},{3,1},... | collective-permute-start | bytes 147464 | tf_op jit(solution)/shard_map/ppermute | solution.py:409
  46.4 6.9 %collective-permute-start.3 = (bf16[96,256]{1,0:T(8,128)(2,1)S(1)}, bf16[96,256]{1,0:T(8,128)(2,1)S(1)}, u32[]{:S(2)}, u32[]{:S(2)}) collective-permute-start(bf16[96,256]{1,0:T(8,128)(2,1)S(1)} %get-tuple-element.9.far_ref), channel_id=1, source_target_pairs={{2,4},{6,8},{10,12},{4,2},{8,6},{12,10},{3,5},{7,9},{11,13},{5,3},... | collective-permute-start | bytes 147464 | tf_op jit(solution)/shard_map/ppermute | solution.py:408

commit v3 on v2

--- a/solution.py
+++ b/solution.py
@@ -14,30 +14,26 @@
 EPS = 1e-06
 BF16 = jnp.bfloat16
 F32 = jnp.float32
-VMEM_LIMIT = 48 * 1024 * 1024
-
-
-def specs(count, space=pltpu.VMEM):
-    return [pl.BlockSpec(memory_space=space)] * count
-
-
-def kernel_params():
-    return pltpu.CompilerParams(vmem_limit_bytes=VMEM_LIMIT)
+MIB = 1024 * 1024
+
+
+def specs(count):
+    return [pl.BlockSpec(memory_space=pltpu.VMEM)] * count
 
 
 def nbytes(*arrays):
     return sum(math.prod(a.shape) * jnp.dtype(a.dtype).itemsize for a in arrays)
 
 
-def call(kernel, outs, args, scratch=(), flops=0, exps=0, space=pltpu.VMEM):
+def call(kernel, outs, args, scratch=(), flops=0, exps=0, limit=24):
     outs = tuple(jax.ShapeDtypeStruct(shape, dtype) for shape, dtype in outs)
     return pl.pallas_call(
         kernel,
         out_shape=outs,
-        in_specs=specs(len(args), space),
+        in_specs=specs(len(args)),
         out_specs=tuple(specs(len(outs))),
         scratch_shapes=list(scratch),
-        compiler_params=kernel_params(),
+        compiler_params=pltpu.CompilerParams(vmem_limit_bytes=limit * MIB),
         cost_estimate=pl.CostEstimate(
             flops=flops, transcendentals=exps, bytes_accessed=nbytes(*args, *outs)
         ),
@@ -63,19 +59,7 @@
     return pltpu.roll(tile, HEAD_DIM, axis=1)
 
 
-def fetch_kernel(weight_ref, out_ref, sems):
-    copies = [
-        pltpu.make_async_copy(weight_ref.at[part], out_ref.at[part], sems.at[part])
-        for part in range(weight_ref.shape[0])
-    ]
-    for copy in copies:
-        copy.start()
-    for copy in copies:
-        copy.wait()
-
-
-def project(mine_ref, other_ref, gain_ref, weight_ref):
-    core = lax.axis_index("head")
+def normalize(mine_ref, other_ref, gain_ref):
     half = mine_ref.shape[1]
     width = 2 * half
     mine, other = mine_ref[...], other_ref[...]
@@ -89,67 +73,110 @@
     ) / width
     scale = lax.rsqrt(spread + EPS)
     low_gain, high_gain = gain_ref[:half][None, :], gain_ref[half:][None, :]
-    first = core == 0
+    first = lax.axis_index("head") == 0
     mine = (mine * scale * jnp.where(first, low_gain, high_gain)).astype(BF16)
     other = (other * scale * jnp.where(first, high_gain, low_gain)).astype(BF16)
+    return mine, other
+
+
+def norm_kernel(mine_ref, other_ref, gain_ref, mine_out, other_out):
+    mine_out[...], other_out[...] = normalize(mine_ref, other_ref, gain_ref)
+
+
+def project(mine, other, weight_ref, part):
+    core = lax.axis_index("head")
+    half = mine.shape[1]
     mine_at = pl.ds(pl.multiple_of(core * half, half), half)
     other_at = pl.ds(pl.multiple_of((1 - core) * half, half), half)
-    return [
+    return (
         dot(mine, weight_ref[part, mine_at, :]) + dot(other, weight_ref[part, other_at, :])
-        for part in range(3)
-    ]
-
-
-def qkv_kernel(mine_ref, other_ref, gain_ref, weight_ref, send_ref):
-    queries, keys, values = project(mine_ref, other_ref, gain_ref, weight_ref)
-    rows = queries.shape[0]
+    ).astype(BF16)
+
+
+def plain_qkv_kernel(mine_ref, other_ref, gain_ref, weight_ref, *out_refs):
+    mine, other = normalize(mine_ref, other_ref, gain_ref)
+    for part, ref in enumerate(out_refs):
+        ref[...] = project(mine, other, weight_ref, part)
+
+
+def spread_lanes(column, width=LANES):
+    return jnp.broadcast_to(column, (column.shape[0], width))
+
+
+def across(lanes, width):
+    whole, rest = divmod(width, LANES)
+    return jnp.concatenate([lanes] * whole + ([lanes[:, :rest]] if rest else []), axis=1)
+
+
+def absorb(pair, queries, keys, values, old):
+    factor = HEAD_DIM ** (-0.5) * math.log2(math.e)
+    cols = slice(pair * LANES, (pair + 1) * LANES)
+    scores = lax.dot_general(
+        queries, keys[:, cols], (((1,), (1,)), ((), ())), preferred_element_type=F32
+    )
+    top = spread_lanes(jnp.max(scores, axis=-1, keepdims=True))
+    if old is not None:
+        old_top, old_total, old_mixed = old
+        top = jnp.maximum(top, old_top)
+    weights = jnp.exp2((scores - across(top, scores.shape[1])) * factor)
+    total = spread_lanes(jnp.sum(weights, axis=-1, keepdims=True))
+    mixed = dot(weights.astype(BF16), values[:, cols])
+    rows = mixed.shape[0] // 2
     low = low_lanes((rows, LANES))
-    low_q = low_lanes((rows // 2, LANES))
-    for pair in range(queries.shape[1] // LANES):
-        cols = slice(pair * LANES, (pair + 1) * LANES)
-        key, value = keys[:, cols], values[:, cols]
-        top, bottom = queries[: rows // 2, cols], queries[rows // 2 :, cols]
-        send_ref[2 * pair, :rows] = jnp.where(low, key, half_turn(value)).astype(BF16)
-        send_ref[2 * pair + 1, :rows] = jnp.where(low, half_turn(key), value).astype(BF16)
-        send_ref[2 * pair, rows:] = jnp.where(low_q, top, half_turn(bottom)).astype(BF16)
-        send_ref[2 * pair + 1, rows:] = jnp.where(low_q, half_turn(top), bottom).astype(BF16)
-
-
-def plain_qkv_kernel(mine_ref, other_ref, gain_ref, weight_ref, q_ref, k_ref, v_ref):
-    for ref, value in zip(
-        (q_ref, k_ref, v_ref), project(mine_ref, other_ref, gain_ref, weight_ref)
+    mixed = jnp.where(low, mixed[:rows], mixed[rows:])
+    if old is not None:
+        shrink = jnp.exp2((old_top - top) * factor)
+        total = total + old_total * shrink
+        mixed = mixed + old_mixed * jnp.where(low, shrink[:rows], shrink[rows:])
+    return top, total, mixed
+
+
+def own_kernel(
+    mine_ref, other_ref, weight_ref, query_ref, top_ref, total_ref, mixed_ref
+):
+    mine, other = mine_ref[...], other_ref[...]
+    rows = mine.shape[0]
+    queries = project(mine, other, weight_ref, 0)
+    keys = project(mine, other, weight_ref, 1)
+    values = project(mine, other, weight_ref, 2)
+    low = low_lanes((rows, LANES))
+    for pair in range(query_ref.shape[0]):
+        tile = queries[:, pair * LANES : (pair + 1) * LANES]
+        query_ref[pair, :rows] = jnp.where(low, tile, jnp.zeros_like(tile))
+        query_ref[pair, rows:] = jnp.where(low, jnp.zeros_like(tile), tile)
+        top_ref[pair], total_ref[pair], mixed_ref[pair] = absorb(
+            pair, query_ref[pair], keys, values, None
+        )
+
+
+def absorb_blocks(mine_refs, other_refs, weight_ref, query_ref, top_ref, total_ref, mixed_ref):
+    mine = jnp.concatenate([ref[...] for ref in mine_refs], axis=0)
+    other = jnp.concatenate([ref[...] for ref in other_refs], axis=0)
+    keys = project(mine, other, weight_ref, 1)
+    values = project(mine, other, weight_ref, 2)
+    for pair in range(query_ref.shape[0]):
+        old = top_ref[pair], total_ref[pair], mixed_ref[pair]
+        yield pair, absorb(pair, query_ref[pair], keys, values, old)
+
+
+def step_kernel(
+    mine_a,
+    mine_b,
+    other_a,
+    other_b,
+    weight_ref,
+    query_ref,
+    top_ref,
+    total_ref,
+    mixed_ref,
+    top_out,
+    total_out,
+    mixed_out,
+):
+    for pair, state in absorb_blocks(
+        (mine_a, mine_b), (other_a, other_b), weight_ref, query_ref, top_ref, total_ref, mixed_ref
     ):
-        ref[...] = value.astype(BF16)
-
-
-def attend_kernel(got_ref, out_ref, pair_ref, query_ref, value_ref, mixed_ref):
-    blocks, packed_rows = got_ref.shape[0], out_ref.shape[1]
-    rows = 2 * packed_rows
-    share = blocks * packed_rows
-    low = low_lanes((packed_rows, LANES))
-    for block in range(blocks):
-        pair_ref[block * rows : (block + 1) * rows] = got_ref[block, :rows]
-        packed = got_ref[block, rows:].astype(F32)
-        here = block * packed_rows
-        query_ref[here : here + packed_rows] = jnp.where(low, packed, 0.0).astype(BF16)
-        query_ref[share + here : share + here + packed_rows] = jnp.where(
-            low, half_turn(packed), 0.0
-        ).astype(BF16)
-    value_ref[...] = pair_ref[...].astype(F32).T[HEAD_DIM:].astype(BF16)
-    factor = HEAD_DIM ** (-0.5) * math.log2(math.e)
-    tile = math.gcd(share, 256)
-    for part in range(2):
-        for start in range(0, share, tile):
-            queries = query_ref[part * share + start : part * share + start + tile]
-            scores = lax.dot_general(
-                pair_ref[...], queries, (((1,), (1,)), ((), ())), preferred_element_type=F32
-            )
-            top = jnp.max(scores, axis=0, keepdims=True)
-            weights = jnp.exp2((scores - top) * factor)
-            total = jnp.sum(weights, axis=0, keepdims=True)
-            mixed = dot(value_ref[...], weights.astype(BF16)) / total
-            mixed_ref[part * HEAD_DIM : (part + 1) * HEAD_DIM, start : start + tile] = mixed
-    out_ref[...] = mixed_ref[...].T.astype(BF16).reshape(out_ref.shape)
+        top_out[pair], total_out[pair], mixed_out[pair] = state
 
 
 def out_terms(attended, weight_ref, mine_ref, other_ref, send_ref, keep_ref, full_ref):
@@ -167,16 +194,34 @@
             keep_ref[row, :, cols] = full_ref[here, cols] + ref[here, :]
 
 
-def out_kernel(back_ref, weight_ref, mine_ref, other_ref, send_ref, keep_ref, full_ref, att_ref):
-    packed_rows = back_ref.shape[1]
-    low = low_lanes((packed_rows, LANES))
-    for pair in range(back_ref.shape[0] // 2):
+def last_kernel(
+    mine_a,
+    mine_b,
+    other_a,
+    other_b,
+    weight_ref,
+    query_ref,
+    top_ref,
+    total_ref,
+    mixed_ref,
+    out_weight_ref,
+    tokens_ref,
+    other_tokens_ref,
+    send_ref,
+    keep_ref,
+    full_ref,
+    att_ref,
+):
+    rows = mixed_ref.shape[1]
+    low = low_lanes((rows, LANES))
+    for pair, (_, total, mixed) in absorb_blocks(
+        (mine_a, mine_b), (other_a, other_b), weight_ref, query_ref, top_ref, total_ref, mixed_ref
+    ):
         cols = slice(pair * LANES, (pair + 1) * LANES)
-        left = back_ref[2 * pair].astype(F32)
-        right = back_ref[2 * pair + 1].astype(F32)
-        att_ref[:packed_rows, cols] = jnp.where(low, left, half_turn(right)).astype(BF16)
-        att_ref[packed_rows:, cols] = jnp.where(low, half_turn(left), right).astype(BF16)
-    out_terms(att_ref[...], weight_ref, mine_ref, other_ref, send_ref, keep_ref, full_ref)
+        att_ref[:, cols] = (mixed / jnp.where(low, total[:rows], total[rows:])).astype(BF16)
+    out_terms(
+        att_ref[...], out_weight_ref, tokens_ref, other_tokens_ref, send_ref, keep_ref, full_ref
+    )
 
 
 def plain_out_kernel(att_ref, weight_ref, mine_ref, other_ref, send_ref, keep_ref, full_ref):
@@ -341,13 +386,6 @@
     swap = [(i, cores - 1 - i) for i in range(cores)]
 
     other = lax.ppermute(tokens, "head", swap)
-    (near_weight,) = call(
-        fetch_kernel,
-        [(qkv_weight.shape, BF16)],
-        (qkv_weight,),
-        [pltpu.SemaphoreType.DMA((qkv_weight.shape[0],))],
-        space=pltpu.HBM,
-    )
     tail = (out_weight, tokens, other)
     tail_outs = [
         ((grid_rows, window, features), BF16),
@@ -355,39 +393,60 @@
     ]
     full = pltpu.VMEM((rows, features), F32)
     out_flops = 2 * rows * width * features
-    if heads == blocks:
-        (send,) = call(
-            qkv_kernel,
-            [((blocks, rows + rows // 2, LANES), BF16)],
-            (tokens, other, norm_gain, near_weight),
-            flops=6 * rows * features * width,
-        )
-        got = exchange(send)
-        total = blocks * rows
-        (one_head,) = call(
-            attend_kernel,
-            [((blocks, rows // 2, LANES), BF16)],
-            (got,),
-            [
-                pltpu.VMEM((total, LANES), BF16),
-                pltpu.VMEM((total, LANES), BF16),
-                pltpu.VMEM((HEAD_DIM, total), BF16),
-                pltpu.VMEM((2 * HEAD_DIM, total // 2), F32),
-            ],
-            flops=4 * total * total * LANES,
-            exps=total * total,
-        )
-        back = exchange(one_head)
+    if blocks <= heads:
+        order = list(range(0, blocks, 2)) + list(range(blocks - 1, 0, -2))
+        forth = [(order[i - 1], order[i]) for i in range(blocks)]
+        back = [(target, source) for source, target in forth]
+        mine, across_core = call(
+            norm_kernel, [((rows, half), BF16)] * 2, (tokens, other, norm_gain)
+        )
+        pairs = width // LANES
+        state_outs = [
+            ((pairs, 2 * rows, LANES), F32),
+            ((pairs, 2 * rows, LANES), F32),
+            ((pairs, rows, LANES), F32),
+        ]
+        ahead = lax.ppermute(mine, "blk", forth)
+        behind = lax.ppermute(mine, "blk", back)
+        unit = 4 * rows * width * (features + rows)
+        queries, *state = call(
+            own_kernel,
+            [((pairs, 2 * rows, LANES), BF16)] + state_outs,
+            (mine, across_core, qkv_weight),
+            flops=unit + 2 * rows * width * features,
+            exps=heads * rows * rows,
+        )
+        ahead, behind, queries, state = lax.optimization_barrier((ahead, behind, queries, state))
+        for step in range(1, blocks // 2):
+            parts = (ahead, behind)
+            others = tuple(lax.ppermute(part, "head", swap) for part in parts)
+            if step == blocks // 2 - 1:
+                ahead = lax.ppermute(ahead[: rows // 2], "blk", forth)
+                behind = lax.ppermute(behind[rows // 2 :], "blk", back)
+            else:
+                ahead = lax.ppermute(ahead, "blk", forth)
+                behind = lax.ppermute(behind, "blk", back)
+            state = call(
+                step_kernel,
+                state_outs,
+                parts + others + (qkv_weight, queries) + tuple(state),
+                flops=2 * unit,
+                exps=2 * heads * rows * rows,
+            )
+            ahead, behind, state = lax.optimization_barrier((ahead, behind, state))
+        parts = (ahead, behind)
+        others = tuple(lax.ppermute(part, "head", swap) for part in parts)
         peer_term, keep = call(
-            out_kernel,
+            last_kernel,
             tail_outs,
-            (back,) + tail,
+            parts + others + (qkv_weight, queries) + tuple(state) + tail,
             [full, pltpu.VMEM((rows, width), BF16)],
-            flops=out_flops,
+            flops=unit + out_flops,
+            exps=heads * rows * rows,
         )
     else:
         attended = attention_shared(
-            tokens, other, norm_gain, near_weight, blocks // heads
+            tokens, other, norm_gain, qkv_weight, blocks // heads
         )
         peer_term, keep = call(plain_out_kernel, tail_outs, (attended,) + tail, [full], out_flops)
     peer_term = lax.ppermute(peer_term, "head", swap)

time: 54.8 us -> 51.1 us (0.932)
  blocking collectives: 33.3 us -> 0 us
  waiting for transfers between devices: 5.66 us -> 19.9 us
  starting transfers between devices: 3.86 us -> 14.6 us
  local copies, waits for them, and re-layouts: 0.03 us -> 3.61 us
  Pallas kernels: 11 us -> 12 us
    all_to_all x2 -> x0, blocking collectives: 33.3 us -> none  [exchange(): return lax.all_to_all(value, 'blk', split_axis=0, concat_axis=0, tiled=True)]
    ppermute x0 -> x16, waiting for transfers between devices: none -> 12.2 us  [the longest x2 4.94 us: body(): ahead = lax.ppermute(ahead, 'blk', forth)]
    ppermute x0 -> x16, starting transfers between devices: none -> 10.2 us  [the longest x2 3.15 us: body(): ahead = lax.ppermute(ahead, 'blk', forth)]
    unnamed x12 -> x18, local copies, waits for them, and re-layouts: 0.03 us -> 3.6 us
    ppermute x1, waiting for transfers between devices: 0.01 us -> 1.92 us  [body(): other = lax.ppermute(tokens, 'head', swap)]
    pallas_call x6 -> x8, Pallas kernels: 11 us -> 12 us  [call(): pl.pallas_call(kernel, out_shape=outs, in_specs=specs(len(args)), out_spe...]
    ppermute x1, starting transfers between devices: 1 us -> 1.56 us  [body(): got_near = lax.ppermute(near, 'blk', [(i, i ^ 1) for i in range(blocks)])]
    ppermute x1, waiting for transfers between devices: 3.71 us -> 4.28 us  [body(): got_far = lax.ppermute(far, 'blk', far_pairs)]
  transfers between devices with their start and end apart: 4 -> 20, of which waited for: 3 -> 14; matrix products, arithmetic and copies ran while one was open for 0% -> 0% of each run, Pallas kernels for 4% -> 16%
where the time goes in v3:
time: 51.1 us; the launch traced here: 50.9 us
  waiting for transfers between devices  19.9 us (39%)
  starting transfers between devices  14.6 us (29%)
  Pallas kernels  12 us (23%)
  local copies, waits for them, and re-layouts  3.61 us (7%)
  between operations  0.75 us (1%)
    pallas_call x8, Pallas kernels, call(): pl.pallas_call(kernel, out_shape=outs, in_specs=specs(len(args)), out_spe...  12 us
    ppermute x2, waiting for transfers between devices, body(): ahead = lax.ppermute(ahead, 'blk', forth)  4.94 us
    ppermute x1, waiting for transfers between devices, body(): got_far = lax.ppermute(far, 'blk', far_pairs)  4.28 us
    unnamed x18, local copies, waits for them, and re-layouts  3.6 us
    ppermute x2, starting transfers between devices, body(): ahead = lax.ppermute(ahead, 'blk', forth)  3.15 us
    ppermute x2, waiting for transfers between devices, body(): behind = lax.ppermute(behind, 'blk', back)  2.59 us
    ppermute x1, starting transfers between devices, body(): got_far = lax.ppermute(far, 'blk', far_pairs)  2.31 us
    ppermute x8, starting transfers between devices, body(): others = tuple((lax.ppermute(part, 'head', swap) for part in parts))  2.03 us
  transfers between devices with their start and end apart: 20, of which 14 were waited for; matrix products, arithmetic and copies ran while one was open for 0% of the time, Pallas kernels for 16%

profile of v3, /device:TPU:6, one launch (start us, length us, event | category | flops | bytes accessed | tf_op | source)
XLA Modules:
  0.0 50.9 jit_solution(553310862883967575)
XLA Ops:
  0.6 0.1 collective-permute-start
  0.7 1.9 %collective-permute-done.other_ref.other_tokens_ref = f32[192,512]{1,0:T(8,128)S(1)} collective-permute-done((f32[192,512]{1,0:T(8,128)}, f32[192,512]{1,0:T(8,128)S(1)}, u32[]{:S(2)}, u32[]{:S(2)}) %collective-permute-start) | collective-permute-done | bytes 393248 | tf_op jit(solution)/shard_map/ppermute | solution.py:388
  2.6 0.0 copy-start.3
  2.6 1.0 %copy-done.3 = f32[192,512]{1,0:T(8,128)S(1)} copy-done((f32[192,512]{1,0:T(8,128)S(1)}, f32[192,512]{1,0:T(8,128)}, u32[]{:S(2)}) %copy-start.3) | copy-done | bytes 393240
  3.6 0.0 copy-start.8
  3.6 0.7 %copy-done.8 = f32[1024]{0:T(1024)S(1)} copy-done((f32[1024]{0:T(1024)S(1)}, f32[1024]{0:T(1024)}, u32[]{:S(2)}) %copy-start.8) | copy-done | bytes 4120
  4.3 0.3 shard_map.86
  4.6 0.6 %collective-permute-start.1 = (bf16[192,512]{1,0:T(8,128)(2,1)S(1)}, bf16[192,512]{1,0:T(8,128)(2,1)S(1)}, u32[]{:S(2)}, u32[]{:S(2)}) collective-permute-start(bf16[192,512]{1,0:T(8,128)(2,1)S(1)} %get-tuple-element.42.mine_ref), channel_id=1, source_target_pairs={{2,0},{0,4},{4,8},{8,12},{12,14},{14,10},{10,6},{6,2},{3,1},{1,5},... | collective-permute-start | bytes 589832 | tf_op jit(solution)/shard_map/ppermute | solution.py:409
  5.2 1.5 %collective-permute-start.2 = (bf16[192,512]{1,0:T(8,128)(2,1)S(1)}, bf16[192,512]{1,0:T(8,128)(2,1)S(1)}, u32[]{:S(2)}, u32[]{:S(2)}) collective-permute-start(bf16[192,512]{1,0:T(8,128)(2,1)S(1)} %get-tuple-element.42.mine_ref), channel_id=1, source_target_pairs={{0,2},{4,0},{8,4},{12,8},{14,12},{10,14},{6,10},{2,6},{1,3},{5,1},... | collective-permute-start | bytes 589832 | tf_op jit(solution)/shard_map/ppermute | solution.py:410
  6.7 0.0 copy-start
  6.7 1.9 %copy-done = bf16[3,1024,512]{2,1,0:T(8,128)(2,1)S(1)} copy-done((bf16[3,1024,512]{2,1,0:T(8,128)(2,1)S(1)}, bf16[3,1024,512]{2,1,0:T(8,128)(2,1)}, u32[]{:S(2)}) %copy-start) | copy-done | bytes 3145752
  8.6 0.0 copy-start.1
  8.6 1.4 %shard_map.87 = (bf16[4,384,128]{2,1,0:T(8,128)(2,1)S(1)}, f32[4,384,128]{2,1,0:T(8,128)S(1)}, f32[4,384,128]{2,1,0:T(8,128)S(1)}, f32[4,192,128]{2,1,0:T(8,128)S(1)}) custom-call(bf16[192,512]{1,0:T(8,128)(2,1)S(1)} %get-tuple-element.42.mine_ref, bf16[192,512]{1,0:T(8,128)(2,1)S(1)} %get-tuple-element.43.other_ref, bf16[3,1024,512]{2,1,0:T(8,128)(2,1)S(1)} %copy-done), custom_call_target="tpu_custom_call" | custom-call | flops 679477248 | bytes 5898240 | tf_op jit(solution)/shard_map/pallas_call | solution.py:30
  10.0 1.6 %collective-permute-done.1.mine_a = bf16[192,512]{1,0:T(8,128)(2,1)S(1)} collective-permute-done((bf16[192,512]{1,0:T(8,128)(2,1)S(1)}, bf16[192,512]{1,0:T(8,128)(2,1)S(1)}, u32[]{:S(2)}, u32[]{:S(2)}) %collective-permute-start.1) | collective-permute-done | bytes 196640 | tf_op jit(solution)/shard_map/ppermute | solution.py:409
  11.6 0.3 collective-permute-done.2.mine_b
  11.9 0.0 collective-permute-start.5
  11.9 0.5 collective-permute-start.6
  12.4 1.6 %collective-permute-start.3 = (bf16[192,512]{1,0:T(8,128)(2,1)S(1)}, bf16[192,512]{1,0:T(8,128)(2,1)S(1)}, u32[]{:S(2)}, u32[]{:S(2)}) collective-permute-start(bf16[192,512]{1,0:T(8,128)(2,1)S(1)} %collective-permute-done.1.mine_a), channel_id=1, source_target_pairs={{2,0},{0,4},{4,8},{8,12},{12,14},{14,10},{10,6},{6,2},{3,1},{1,5},... | collective-permute-start | bytes 589832 | tf_op jit(solution)/shard_map/ppermute | solution.py:427
  14.0 0.4 collective-permute-start.4
  14.4 0.0 collective-permute-done.5.other_a
  14.4 0.0 collective-permute-done.6.other_b
  14.4 0.0 copy-done.1
  14.4 2.3 %shard_map.88 = (f32[4,384,128]{2,1,0:T(8,128)S(1)}, f32[4,384,128]{2,1,0:T(8,128)S(1)}, f32[4,192,128]{2,1,0:T(8,128)S(1)}) custom-call(bf16[192,512]{1,0:T(8,128)(2,1)S(1)} %collective-permute-done.1.mine_a, bf16[192,512]{1,0:T(8,128)(2,1)S(1)} %collective-permute-done.2.mine_b, bf16[192,512]{1,0:T(8,128)(2,1)S(1)} %collective-permute-done.5.other_a, ...), custom_call_target="tpu_custom_call" | custom-call | flops 956301312 | bytes 8257536 | tf_op jit(solution)/shard_map/pallas_call | solution.py:30
  16.8 2.5 %collective-permute-done.3.mine_a = bf16[192,512]{1,0:T(8,128)(2,1)S(1)} collective-permute-done((bf16[192,512]{1,0:T(8,128)(2,1)S(1)}, bf16[192,512]{1,0:T(8,128)(2,1)S(1)}, u32[]{:S(2)}, u32[]{:S(2)}) %collective-permute-start.3) | collective-permute-done | bytes 196640 | tf_op jit(solution)/shard_map/ppermute | solution.py:427
  19.2 1.3 %collective-permute-done.4.mine_b = bf16[192,512]{1,0:T(8,128)(2,1)S(1)} collective-permute-done((bf16[192,512]{1,0:T(8,128)(2,1)S(1)}, bf16[192,512]{1,0:T(8,128)(2,1)S(1)}, u32[]{:S(2)}, u32[]{:S(2)}) %collective-permute-start.4) | collective-permute-done | bytes 196640 | tf_op jit(solution)/shard_map/ppermute | solution.py:428
  20.5 0.0 collective-permute-start.10
  20.5 0.5 collective-permute-start.9
  21.0 1.6 %collective-permute-start.7 = (bf16[192,512]{1,0:T(8,128)(2,1)S(1)}, bf16[192,512]{1,0:T(8,128)(2,1)S(1)}, u32[]{:S(2)}, u32[]{:S(2)}) collective-permute-start(bf16[192,512]{1,0:T(8,128)(2,1)S(1)} %collective-permute-done.3.mine_a), channel_id=1, source_target_pairs={{2,0},{0,4},{4,8},{8,12},{12,14},{14,10},{10,6},{6,2},{3,1},{1,5},... | collective-permute-start | bytes 589832 | tf_op jit(solution)/shard_map/ppermute | solution.py:427
  22.6 0.4 collective-permute-start.8
  23.1 0.0 collective-permute-done.10.other_b
  23.1 0.0 collective-permute-done.9.other_a
  23.1 2.3 %shard_map.89 = (f32[4,384,128]{2,1,0:T(8,128)S(1)}, f32[4,384,128]{2,1,0:T(8,128)S(1)}, f32[4,192,128]{2,1,0:T(8,128)S(1)}) custom-call(bf16[192,512]{1,0:T(8,128)(2,1)S(1)} %collective-permute-done.3.mine_a, bf16[192,512]{1,0:T(8,128)(2,1)S(1)} %collective-permute-done.4.mine_b, bf16[192,512]{1,0:T(8,128)(2,1)S(1)} %collective-permute-done.9.other_a, ...), custom_call_target="tpu_custom_call" | custom-call | flops 956301312 | bytes 8257536 | tf_op jit(solution)/shard_map/pallas_call | solution.py:30
  25.4 2.5 %collective-permute-done.7.mine_a = bf16[192,512]{1,0:T(8,128)(2,1)S(1)} collective-permute-done((bf16[192,512]{1,0:T(8,128)(2,1)S(1)}, bf16[192,512]{1,0:T(8,128)(2,1)S(1)}, u32[]{:S(2)}, u32[]{:S(2)}) %collective-permute-start.7) | collective-permute-done | bytes 196640 | tf_op jit(solution)/shard_map/ppermute | solution.py:427
  27.8 1.3 %collective-permute-done.8.mine_b = bf16[192,512]{1,0:T(8,128)(2,1)S(1)} collective-permute-done((bf16[192,512]{1,0:T(8,128)(2,1)S(1)}, bf16[192,512]{1,0:T(8,128)(2,1)S(1)}, u32[]{:S(2)}, u32[]{:S(2)}) %collective-permute-start.8) | collective-permute-done | bytes 196640 | tf_op jit(solution)/shard_map/ppermute | solution.py:428
  29.1 0.0 collective-permute-start.13
  29.1 0.5 collective-permute-start.14
  29.7 0.0 copy-start.4
  29.7 0.0 copy-start.6
  29.7 1.6 %collective-permute-start.11 = (bf16[96,512]{1,0:T(8,128)(2,1)S(1)}, bf16[96,512]{1,0:T(8,128)(2,1)S(1)}, u32[]{:S(2)}, u32[]{:S(2)}) collective-permute-start(bf16[96,512]{1,0:T(8,128)(2,1)S(1)} %slice.6), channel_id=1, source_target_pairs={{2,0},{0,4},{4,8},{8,12},{12,14},{14,10},{10,6},{6,2},{3,1},{1,5},... | collective-permute-start | bytes 294920 | tf_op jit(solution)/shard_map/ppermute | solution.py:424
  31.3 0.4 collective-permute-start.12
  31.8 0.0 collective-permute-done.13.other_a
  31.8 0.0 collective-permute-done.14.other_b
  31.8 2.3 %shard_map.90 = (f32[4,384,128]{2,1,0:T(8,128)S(1)}, f32[4,384,128]{2,1,0:T(8,128)S(1)}, f32[4,192,128]{2,1,0:T(8,128)S(1)}) custom-call(bf16[192,512]{1,0:T(8,128)(2,1)S(1)} %collective-permute-done.7.mine_a, bf16[192,512]{1,0:T(8,128)(2,1)S(1)} %collective-permute-done.8.mine_b, bf16[192,512]{1,0:T(8,128)(2,1)S(1)} %collective-permute-done.13.other_a, ...), custom_call_target="tpu_custom_call" | custom-call | flops 956301312 | bytes 8257536 | tf_op jit(solution)/shard_map/pallas_call | solution.py:30
  34.1 0.4 collective-permute-done.11.mine_a
  34.5 1.5 %collective-permute-done.12.mine_b = bf16[96,512]{1,0:T(8,128)(2,1)S(1)} collective-permute-done((bf16[96,512]{1,0:T(8,128)(2,1)S(1)}, bf16[96,512]{1,0:T(8,128)(2,1)S(1)}, u32[]{:S(2)}, u32[]{:S(2)}) %collective-permute-start.12) | collective-permute-done | bytes 98336 | tf_op jit(solution)/shard_map/ppermute | solution.py:425
  35.9 0.0 copy-start.5
  35.9 0.0 collective-permute-start.15
  36.0 0.5 collective-permute-start.16
  36.5 0.8 %collective-permute-done.15.other_a = bf16[96,512]{1,0:T(8,128)(2,1)S(1)} collective-permute-done((bf16[96,512]{1,0:T(8,128)(2,1)S(1)}, bf16[96,512]{1,0:T(8,128)(2,1)S(1)}, u32[]{:S(2)}, u32[]{:S(2)}) %collective-permute-start.15) | collective-permute-done | bytes 98336 | tf_op jit(solution)/shard_map/ppermute | solution.py:438
  37.2 0.2 collective-permute-done.16.other_b
  37.4 0.0 copy-done.4
  37.4 0.0 copy-done.6
  37.4 1.7 %shard_map.91 = (bf16[2,64,1024]{2,1,0:T(8,128)(2,1)S(1)}, f32[2,64,1024]{2,1,0:T(8,128)S(1)}) custom-call(bf16[96,512]{1,0:T(8,128)(2,1)S(1)} %collective-permute-done.11.mine_a, bf16[96,512]{1,0:T(8,128)(2,1)S(1)} %collective-permute-done.12.mine_b, bf16[96,512]{1,0:T(8,128)(2,1)S(1)} %collective-permute-done.15.other_a, ...), custom_call_target="tpu_custom_call" | custom-call | flops 679477248 | bytes 8519680 | tf_op jit(solution)/shard_map/pallas_call | solution.py:30
  39.1 0.4 collective-permute-start.17
  39.5 1.2 %collective-permute-done.17.got_ref = bf16[2,64,1024]{2,1,0:T(8,128)(2,1)S(1)} collective-permute-done((bf16[2,64,1024]{2,1,0:T(8,128)(2,1)S(1)}, bf16[2,64,1024]{2,1,0:T(8,128)(2,1)S(1)}, u32[]{:S(2)}, u32[]{:S(2)}) %collective-permute-start.17) | collective-permute-done | bytes 262176 | tf_op jit(solution)/shard_map/ppermute | solution.py:452
  40.7 0.0 copy-done.5
  40.7 0.0 copy-done.7
  40.7 0.5 shard_map.92
  41.2 1.6 %collective-permute-start.18 = (bf16[96,256]{1,0:T(8,128)(2,1)S(1)}, bf16[96,256]{1,0:T(8,128)(2,1)S(1)}, u32[]{:S(2)}, u32[]{:S(2)}) collective-permute-start(bf16[96,256]{1,0:T(8,128)(2,1)S(1)} %get-tuple-element.80.near_ref), channel_id=1, source_target_pairs={{0,2},{2,0},{4,6},{6,4},{8,10},{10,8},{12,14},{14,12},{1,3},{3,1},... | collective-permute-start | bytes 147464 | tf_op jit(solution)/shard_map/ppermute | solution.py:468
  42.7 2.3 %collective-permute-start.19 = (bf16[96,256]{1,0:T(8,128)(2,1)S(1)}, bf16[96,256]{1,0:T(8,128)(2,1)S(1)}, u32[]{:S(2)}, u32[]{:S(2)}) collective-permute-start(bf16[96,256]{1,0:T(8,128)(2,1)S(1)} %get-tuple-element.81.far_ref), channel_id=1, source_target_pairs={{2,4},{6,8},{10,12},{4,2},{8,6},{12,10},{3,5},{7,9},{11,13},{5,3},... | collective-permute-start | bytes 147464 | tf_op jit(solution)/shard_map/ppermute | solution.py:467
  45.1 0.3 collective-permute-done.18.got_near_ref
  45.3 4.3 %collective-permute-done.19.got_far_ref = bf16[96,256]{1,0:T(8,128)(2,1)S(1)} collective-permute-done((bf16[96,256]{1,0:T(8,128)(2,1)S(1)}, bf16[96,256]{1,0:T(8,128)(2,1)S(1)}, u32[]{:S(2)}, u32[]{:S(2)}) %collective-permute-start.19) | collective-permute-done | bytes 49184 | tf_op jit(solution)/shard_map/ppermute | solution.py:467
  49.6 0.0 copy-done.2
  49.6 1.2 %shard_map.93 = (bf16[2,48,256]{2,1,0:T(8,128)(2,1)}, bf16[1,24,256]{2,1,0:T(8,128)(2,1)}) custom-call(bf16[96,256]{1,0:T(8,128)(2,1)S(1)} %get-tuple-element.80.near_ref, bf16[96,256]{1,0:T(8,128)(2,1)S(1)} %get-tuple-element.81.far_ref, bf16[96,256]{1,0:T(8,128)(2,1)S(1)} %collective-permute-done.18.got_near_ref, ...), custom_call_target="tpu_custom_call" | custom-call | flops 188743680 | bytes 2621440 | tf_op jit(solution)/shard_map/pallas_call | solution.py:30
  (4 shorter events, 0.0 us)
Async XLA Ops:
  0.6 2.0 %collective-permute-start = (f32[192,512]{1,0:T(8,128)}, f32[192,512]{1,0:T(8,128)S(1)}, u32[]{:S(2)}, u32[]{:S(2)}) collective-permute-start(f32[192,512]{1,0:T(8,128)} %tokens_ref.1), channel_id=1, source_target_pairs={{0,1},{1,0},{2,3},{3,2},{4,5},{5,4},{6,7},{7,6},{8,9},{9,8},{10,11... | collective-permute-start | bytes 1179656 | tf_op jit(solution)/shard_map/ppermute | solution.py:388
  2.6 1.0 %copy-start.3 = (f32[192,512]{1,0:T(8,128)S(1)}, f32[192,512]{1,0:T(8,128)}, u32[]{:S(2)}) copy-start(f32[192,512]{1,0:T(8,128)} %tokens_ref.1) | copy-start | bytes 1179652
  3.6 0.7 %copy-start.8 = (f32[1024]{0:T(1024)S(1)}, f32[1024]{0:T(1024)}, u32[]{:S(2)}) copy-start(f32[1024]{0:T(1024)} %gain_ref.3) | copy-start | bytes 12292
  4.6 7.0 %collective-permute-start.1 = (bf16[192,512]{1,0:T(8,128)(2,1)S(1)}, bf16[192,512]{1,0:T(8,128)(2,1)S(1)}, u32[]{:S(2)}, u32[]{:S(2)}) collective-permute-start(bf16[192,512]{1,0:T(8,128)(2,1)S(1)} %get-tuple-element.42.mine_ref), channel_id=1, source_target_pairs={{2,0},{0,4},{4,8},{8,12},{12,14},{14,10},{10,6},{6,2},{3,1},{1,5},... | collective-permute-start | bytes 589832 | tf_op jit(solution)/shard_map/ppermute | solution.py:409
  5.2 6.7 %collective-permute-start.2 = (bf16[192,512]{1,0:T(8,128)(2,1)S(1)}, bf16[192,512]{1,0:T(8,128)(2,1)S(1)}, u32[]{:S(2)}, u32[]{:S(2)}) collective-permute-start(bf16[192,512]{1,0:T(8,128)(2,1)S(1)} %get-tuple-element.42.mine_ref), channel_id=1, source_target_pairs={{0,2},{4,0},{8,4},{12,8},{14,12},{10,14},{6,10},{2,6},{1,3},{5,1},... | collective-permute-start | bytes 589832 | tf_op jit(solution)/shard_map/ppermute | solution.py:410
  6.7 1.9 %copy-start = (bf16[3,1024,512]{2,1,0:T(8,128)(2,1)S(1)}, bf16[3,1024,512]{2,1,0:T(8,128)(2,1)}, u32[]{:S(2)}) copy-start(bf16[3,1024,512]{2,1,0:T(8,128)(2,1)} %weight_ref.10) | copy-start | bytes 9437188
  8.6 5.8 %copy-start.1 = (bf16[3,1024,512]{2,1,0:T(8,128)(2,1)S(1)}, bf16[3,1024,512]{2,1,0:T(8,128)(2,1)}, u32[]{:S(2)}) copy-start(bf16[3,1024,512]{2,1,0:T(8,128)(2,1)} %weight_ref.10) | copy-start | bytes 9437188
  11.9 2.5 %collective-permute-start.5 = (bf16[192,512]{1,0:T(8,128)(2,1)S(1)}, bf16[192,512]{1,0:T(8,128)(2,1)S(1)}, u32[]{:S(2)}, u32[]{:S(2)}) collective-permute-start(bf16[192,512]{1,0:T(8,128)(2,1)S(1)} %collective-permute-done.1.mine_a), channel_id=1, source_target_pairs={{0,1},{1,0},{2,3},{3,2},{4,5},{5,4},{6,7},{7,6},{8,9},{9,8},{10,11... | collective-permute-start | bytes 589832 | tf_op jit(solution)/shard_map/ppermute | solution.py:422
  11.9 2.5 %collective-permute-start.6 = (bf16[192,512]{1,0:T(8,128)(2,1)S(1)}, bf16[192,512]{1,0:T(8,128)(2,1)S(1)}, u32[]{:S(2)}, u32[]{:S(2)}) collective-permute-start(bf16[192,512]{1,0:T(8,128)(2,1)S(1)} %collective-permute-done.2.mine_b), channel_id=1, source_target_pairs={{0,1},{1,0},{2,3},{3,2},{4,5},{5,4},{6,7},{7,6},{8,9},{9,8},{10,11... | collective-permute-start | bytes 589832 | tf_op jit(solution)/shard_map/ppermute | solution.py:422
  12.4 6.8 %collective-permute-start.3 = (bf16[192,512]{1,0:T(8,128)(2,1)S(1)}, bf16[192,512]{1,0:T(8,128)(2,1)S(1)}, u32[]{:S(2)}, u32[]{:S(2)}) collective-permute-start(bf16[192,512]{1,0:T(8,128)(2,1)S(1)} %collective-permute-done.1.mine_a), channel_id=1, source_target_pairs={{2,0},{0,4},{4,8},{8,12},{12,14},{14,10},{10,6},{6,2},{3,1},{1,5},... | collective-permute-start | bytes 589832 | tf_op jit(solution)/shard_map/ppermute | solution.py:427
  14.0 6.5 %collective-permute-start.4 = (bf16[192,512]{1,0:T(8,128)(2,1)S(1)}, bf16[192,512]{1,0:T(8,128)(2,1)S(1)}, u32[]{:S(2)}, u32[]{:S(2)}) collective-permute-start(bf16[192,512]{1,0:T(8,128)(2,1)S(1)} %collective-permute-done.2.mine_b), channel_id=1, source_target_pairs={{0,2},{4,0},{8,4},{12,8},{14,12},{10,14},{6,10},{2,6},{1,3},{5,1},... | collective-permute-start | bytes 589832 | tf_op jit(solution)/shard_map/ppermute | solution.py:428
  20.5 2.5 %collective-permute-start.10 = (bf16[192,512]{1,0:T(8,128)(2,1)S(1)}, bf16[192,512]{1,0:T(8,128)(2,1)S(1)}, u32[]{:S(2)}, u32[]{:S(2)}) collective-permute-start(bf16[192,512]{1,0:T(8,128)(2,1)S(1)} %collective-permute-done.4.mine_b), channel_id=1, source_target_pairs={{0,1},{1,0},{2,3},{3,2},{4,5},{5,4},{6,7},{7,6},{8,9},{9,8},{10,11... | collective-permute-start | bytes 589832 | tf_op jit(solution)/shard_map/ppermute | solution.py:422
  20.5 2.5 %collective-permute-start.9 = (bf16[192,512]{1,0:T(8,128)(2,1)S(1)}, bf16[192,512]{1,0:T(8,128)(2,1)S(1)}, u32[]{:S(2)}, u32[]{:S(2)}) collective-permute-start(bf16[192,512]{1,0:T(8,128)(2,1)S(1)} %collective-permute-done.3.mine_a), channel_id=1, source_target_pairs={{0,1},{1,0},{2,3},{3,2},{4,5},{5,4},{6,7},{7,6},{8,9},{9,8},{10,11... | collective-permute-start | bytes 589832 | tf_op jit(solution)/shard_map/ppermute | solution.py:422
  21.0 6.8 %collective-permute-start.7 = (bf16[192,512]{1,0:T(8,128)(2,1)S(1)}, bf16[192,512]{1,0:T(8,128)(2,1)S(1)}, u32[]{:S(2)}, u32[]{:S(2)}) collective-permute-start(bf16[192,512]{1,0:T(8,128)(2,1)S(1)} %collective-permute-done.3.mine_a), channel_id=1, source_target_pairs={{2,0},{0,4},{4,8},{8,12},{12,14},{14,10},{10,6},{6,2},{3,1},{1,5},... | collective-permute-start | bytes 589832 | tf_op jit(solution)/shard_map/ppermute | solution.py:427
  22.6 6.5 %collective-permute-start.8 = (bf16[192,512]{1,0:T(8,128)(2,1)S(1)}, bf16[192,512]{1,0:T(8,128)(2,1)S(1)}, u32[]{:S(2)}, u32[]{:S(2)}) collective-permute-start(bf16[192,512]{1,0:T(8,128)(2,1)S(1)} %collective-permute-done.4.mine_b), channel_id=1, source_target_pairs={{0,2},{4,0},{8,4},{12,8},{14,12},{10,14},{6,10},{2,6},{1,3},{5,1},... | collective-permute-start | bytes 589832 | tf_op jit(solution)/shard_map/ppermute | solution.py:428
  29.1 2.6 %collective-permute-start.13 = (bf16[192,512]{1,0:T(8,128)(2,1)S(1)}, bf16[192,512]{1,0:T(8,128)(2,1)S(1)}, u32[]{:S(2)}, u32[]{:S(2)}) collective-permute-start(bf16[192,512]{1,0:T(8,128)(2,1)S(1)} %collective-permute-done.7.mine_a), channel_id=1, source_target_pairs={{0,1},{1,0},{2,3},{3,2},{4,5},{5,4},{6,7},{7,6},{8,9},{9,8},{10,11... | collective-permute-start | bytes 589832 | tf_op jit(solution)/shard_map/ppermute | solution.py:422
  29.1 2.6 %collective-permute-start.14 = (bf16[192,512]{1,0:T(8,128)(2,1)S(1)}, bf16[192,512]{1,0:T(8,128)(2,1)S(1)}, u32[]{:S(2)}, u32[]{:S(2)}) collective-permute-start(bf16[192,512]{1,0:T(8,128)(2,1)S(1)} %collective-permute-done.8.mine_b), channel_id=1, source_target_pairs={{0,1},{1,0},{2,3},{3,2},{4,5},{5,4},{6,7},{7,6},{8,9},{9,8},{10,11... | collective-permute-start | bytes 589832 | tf_op jit(solution)/shard_map/ppermute | solution.py:422
  29.7 7.7 %copy-start.4 = (f32[192,512]{1,0:T(8,128)S(1)}, f32[192,512]{1,0:T(8,128)}, u32[]{:S(2)}) copy-start(f32[192,512]{1,0:T(8,128)} %tokens_ref.1) | copy-start | bytes 1179652
  29.7 7.7 %copy-start.6 = (bf16[512,1024]{1,0:T(8,128)(2,1)S(1)}, bf16[512,1024]{1,0:T(8,128)(2,1)}, u32[]{:S(2)}) copy-start(bf16[512,1024]{1,0:T(8,128)(2,1)} %out_weight_ref.1) | copy-start | bytes 3145732
  29.7 4.8 %collective-permute-start.11 = (bf16[96,512]{1,0:T(8,128)(2,1)S(1)}, bf16[96,512]{1,0:T(8,128)(2,1)S(1)}, u32[]{:S(2)}, u32[]{:S(2)}) collective-permute-start(bf16[96,512]{1,0:T(8,128)(2,1)S(1)} %slice.6), channel_id=1, source_target_pairs={{2,0},{0,4},{4,8},{8,12},{12,14},{14,10},{10,6},{6,2},{3,1},{1,5},... | collective-permute-start | bytes 294920 | tf_op jit(solution)/shard_map/ppermute | solution.py:424
  31.3 4.6 %collective-permute-start.12 = (bf16[96,512]{1,0:T(8,128)(2,1)S(1)}, bf16[96,512]{1,0:T(8,128)(2,1)S(1)}, u32[]{:S(2)}, u32[]{:S(2)}) collective-permute-start(bf16[96,512]{1,0:T(8,128)(2,1)S(1)} %slice.7), channel_id=1, source_target_pairs={{0,2},{4,0},{8,4},{12,8},{14,12},{10,14},{6,10},{2,6},{1,3},{5,1},... | collective-permute-start | bytes 294920 | tf_op jit(solution)/shard_map/ppermute | solution.py:425
  35.9 4.7 %copy-start.5 = (bf16[2,1024,256]{2,1,0:T(8,128)(2,1)S(1)}, bf16[2,1024,256]{2,1,0:T(8,128)(2,1)}, u32[]{:S(2)}) copy-start(bf16[2,1024,256]{2,1,0:T(8,128)(2,1)} %lateral_ref.1) | copy-start | bytes 3145732
  35.9 4.7 %copy-start.7 = (f32[2,2,256]{2,1,0:T(2,128)S(1)}, f32[2,2,256]{2,1,0:T(2,128)}, u32[]{:S(2)}) copy-start(f32[2,2,256]{2,1,0:T(2,128)} %gain_ref.5) | copy-start | bytes 12292
  35.9 13.7 %copy-start.2 = (bf16[2,3,3,256,256]{4,3,2,1,0:T(8,128)(2,1)S(1)}, bf16[2,3,3,256,256]{4,3,2,1,0:T(8,128)(2,1)}, u32[]{:S(2)}) copy-start(bf16[2,3,3,256,256]{4,3,2,1,0:T(8,128)(2,1)} %weight_ref.11) | copy-start | bytes 7077892
  35.9 1.3 %collective-permute-start.15 = (bf16[96,512]{1,0:T(8,128)(2,1)S(1)}, bf16[96,512]{1,0:T(8,128)(2,1)S(1)}, u32[]{:S(2)}, u32[]{:S(2)}) collective-permute-start(bf16[96,512]{1,0:T(8,128)(2,1)S(1)} %collective-permute-done.11.mine_a), channel_id=1, source_target_pairs={{0,1},{1,0},{2,3},{3,2},{4,5},{5,4},{6,7},{7,6},{8,9},{9,8},{10,11... | collective-permute-start | bytes 294920 | tf_op jit(solution)/shard_map/ppermute | solution.py:438
  36.0 1.4 %collective-permute-start.16 = (bf16[96,512]{1,0:T(8,128)(2,1)S(1)}, bf16[96,512]{1,0:T(8,128)(2,1)S(1)}, u32[]{:S(2)}, u32[]{:S(2)}) collective-permute-start(bf16[96,512]{1,0:T(8,128)(2,1)S(1)} %collective-permute-done.12.mine_b), channel_id=1, source_target_pairs={{0,1},{1,0},{2,3},{3,2},{4,5},{5,4},{6,7},{7,6},{8,9},{9,8},{10,11... | collective-permute-start | bytes 294920 | tf_op jit(solution)/shard_map/ppermute | solution.py:438
  39.1 1.6 %collective-permute-start.17 = (bf16[2,64,1024]{2,1,0:T(8,128)(2,1)S(1)}, bf16[2,64,1024]{2,1,0:T(8,128)(2,1)S(1)}, u32[]{:S(2)}, u32[]{:S(2)}) collective-permute-start(bf16[2,64,1024]{2,1,0:T(8,128)(2,1)S(1)} %get-tuple-element.79), channel_id=1, source_target_pairs={{0,1},{1,0},{2,3},{3,2},{4,5},{5,4},{6,7},{7,6},{8,9},{9,8},{10,11... | collective-permute-start | bytes 786440 | tf_op jit(solution)/shard_map/ppermute | solution.py:452
  41.2 4.2 %collective-permute-start.18 = (bf16[96,256]{1,0:T(8,128)(2,1)S(1)}, bf16[96,256]{1,0:T(8,128)(2,1)S(1)}, u32[]{:S(2)}, u32[]{:S(2)}) collective-permute-start(bf16[96,256]{1,0:T(8,128)(2,1)S(1)} %get-tuple-element.80.near_ref), channel_id=1, source_target_pairs={{0,2},{2,0},{4,6},{6,4},{8,10},{10,8},{12,14},{14,12},{1,3},{3,1},... | collective-permute-start | bytes 147464 | tf_op jit(solution)/shard_map/ppermute | solution.py:468
  42.7 6.9 %collective-permute-start.19 = (bf16[96,256]{1,0:T(8,128)(2,1)S(1)}, bf16[96,256]{1,0:T(8,128)(2,1)S(1)}, u32[]{:S(2)}, u32[]{:S(2)}) collective-permute-start(bf16[96,256]{1,0:T(8,128)(2,1)S(1)} %get-tuple-element.81.far_ref), channel_id=1, source_target_pairs={{2,4},{6,8},{10,12},{4,2},{8,6},{12,10},{3,5},{7,9},{11,13},{5,3},... | collective-permute-start | bytes 147464 | tf_op jit(solution)/shard_map/ppermute | solution.py:467

commit v4 on v3

--- a/solution.py
+++ b/solution.py
@@ -1,4 +1,3 @@
-import functools
 import math
 
 import jax
@@ -53,10 +52,6 @@
 
 def low_lanes(shape):
     return lax.broadcasted_iota(jnp.int32, shape, len(shape) - 1) % LANES < HEAD_DIM
-
-
-def half_turn(tile):
-    return pltpu.roll(tile, HEAD_DIM, axis=1)
 
 
 def normalize(mine_ref, other_ref, gain_ref):
@@ -79,6 +74,11 @@
     return mine, other
 
 
+def intake_kernel(tokens_ref, gain_ref, tokens_out, gain_out):
+    tokens_out[...] = tokens_ref[...]
+    gain_out[...] = gain_ref[...]
+
+
 def norm_kernel(mine_ref, other_ref, gain_ref, mine_out, other_out):
     mine_out[...], other_out[...] = normalize(mine_ref, other_ref, gain_ref)
 
@@ -159,6 +159,10 @@
         yield pair, absorb(pair, query_ref[pair], keys, values, old)
 
 
+def mark_kernel(block_ref, mark_ref):
+    mark_ref[...] = block_ref[: mark_ref.shape[0], : mark_ref.shape[1]]
+
+
 def step_kernel(
     mine_a,
     mine_b,
@@ -169,6 +173,7 @@
     top_ref,
     total_ref,
     mixed_ref,
+    mark_ref,
     top_out,
     total_out,
     mixed_out,
@@ -386,6 +391,13 @@
     swap = [(i, cores - 1 - i) for i in range(cores)]
 
     other = lax.ppermute(tokens, "head", swap)
+    tokens, norm_gain = call(
+        intake_kernel,
+        [(tokens.shape, F32), (norm_gain.shape, F32)],
+        (tokens, norm_gain),
+        flops=MIB * 1024,
+    )
+    other, tokens, norm_gain = lax.optimization_barrier((other, tokens, norm_gain))
     tail = (out_weight, tokens, other)
     tail_outs = [
         ((grid_rows, window, features), BF16),
@@ -416,24 +428,25 @@
             flops=unit + 2 * rows * width * features,
             exps=heads * rows * rows,
         )
-        ahead, behind, queries, state = lax.optimization_barrier((ahead, behind, queries, state))
         for step in range(1, blocks // 2):
+            ahead, state[0] = lax.optimization_barrier((ahead, state[0]))
+            behind, state[0] = lax.optimization_barrier((behind, state[0]))
             parts = (ahead, behind)
-            others = tuple(lax.ppermute(part, "head", swap) for part in parts)
+            (mark,) = call(mark_kernel, [((16, LANES), BF16)], (ahead,))
             if step == blocks // 2 - 1:
-                ahead = lax.ppermute(ahead[: rows // 2], "blk", forth)
-                behind = lax.ppermute(behind[rows // 2 :], "blk", back)
-            else:
-                ahead = lax.ppermute(ahead, "blk", forth)
-                behind = lax.ppermute(behind, "blk", back)
+                ahead, behind = ahead[: rows // 2], behind[rows // 2 :]
+            ahead = lax.ppermute(ahead, "blk", forth)
+            behind = lax.ppermute(behind, "blk", back)
+            others = (lax.ppermute(parts[0], "head", swap), lax.ppermute(parts[1], "head", swap))
             state = call(
                 step_kernel,
                 state_outs,
-                parts + others + (qkv_weight, queries) + tuple(state),
+                parts + others + (qkv_weight, queries) + tuple(state) + (mark,),
                 flops=2 * unit,
                 exps=2 * heads * rows * rows,
             )
-            ahead, behind, state = lax.optimization_barrier((ahead, behind, state))
+            state = list(state)
+        ahead, behind, state = lax.optimization_barrier((ahead, behind, state))
         parts = (ahead, behind)
         others = tuple(lax.ppermute(part, "head", swap) for part in parts)
         peer_term, keep = call(

time: 51.1 us -> 48.7 us (0.953)
  local copies, waits for them, and re-layouts: 3.61 us -> 1.86 us
  waiting for transfers between devices: 19.9 us -> 18.3 us
  starting transfers between devices: 14.6 us -> 15.3 us
    ppermute x1, waiting for transfers between devices: 1.62 us -> 3.86 us  [body(): ahead = lax.ppermute(mine, 'blk', forth)]
    ppermute x1, waiting for transfers between devices: 1.92 us -> 0.06 us  [body(): other = lax.ppermute(tokens, 'head', swap)]
    ppermute x2 -> x6, waiting for transfers between devices: 1.86 us -> 0.02 us  [the longest x3 0.01 us: body(): lax.ppermute(parts[0], 'head', swap)]
    unnamed x18 -> x14, local copies, waits for them, and re-layouts: 3.6 us -> 1.85 us
    ppermute x2 -> x3, starting transfers between devices: 3.15 us -> 4.73 us  [body(): ahead = lax.ppermute(ahead, 'blk', forth)]
    ppermute x8 -> x2, starting transfers between devices: 2.03 us -> 0.5 us  [body(): others = tuple((lax.ppermute(part, 'head', swap) for part in parts))]
    ppermute x1, starting transfers between devices: 2.31 us -> 2.93 us  [body(): got_far = lax.ppermute(far, 'blk', far_pairs)]
    ppermute x2 -> x6, starting transfers between devices: 2.08 us -> 1.53 us  [the longest x3 1.52 us: body(): lax.ppermute(parts[0], 'head', swap)]
  transfers between devices with their start and end apart: 20 -> 20, of which waited for: 14 -> 13; matrix products, arithmetic and copies ran while one was open for 0% -> 0% of each run, Pallas kernels for 16% -> 17%
where the time goes in v4:
time: 48.7 us; the launch traced here: 48.5 us
  waiting for transfers between devices  18.3 us (38%)
  starting transfers between devices  15.3 us (31%)
  Pallas kernels  12.2 us (25%)
  local copies, waits for them, and re-layouts  1.86 us (4%)
  between operations  0.77 us (2%)
    pallas_call x12, Pallas kernels, call(): pl.pallas_call(kernel, out_shape=outs, in_specs=specs(len(args)), out_spe...  12.2 us
    ppermute x3, waiting for transfers between devices, body(): ahead = lax.ppermute(ahead, 'blk', forth)  5.2 us
    ppermute x3, starting transfers between devices, body(): ahead = lax.ppermute(ahead, 'blk', forth)  4.73 us
    ppermute x1, waiting for transfers between devices, body(): got_far = lax.ppermute(far, 'blk', far_pairs)  3.92 us
    ppermute x1, waiting for transfers between devices, body(): ahead = lax.ppermute(mine, 'blk', forth)  3.86 us
    ppermute x1, starting transfers between devices, body(): got_far = lax.ppermute(far, 'blk', far_pairs)  2.93 us
    ppermute x3, waiting for transfers between devices, body(): behind = lax.ppermute(behind, 'blk', back)  2.92 us
    unnamed x14, local copies, waits for them, and re-layouts  1.85 us
  transfers between devices with their start and end apart: 20, of which 13 were waited for; matrix products, arithmetic and copies ran while one was open for 0% of the time, Pallas kernels for 17%

profile of v4, /device:TPU:6, one launch (start us, length us, event | category | flops | bytes accessed | tf_op | source)
XLA Modules:
  0.0 48.5 jit_solution(10797102802756671042)
XLA Ops:
  0.6 0.0 copy-start
  0.6 0.1 collective-permute-start
  0.7 0.0 copy-start.5
  0.7 1.1 %copy-done.5 = f32[192,512]{1,0:T(8,128)S(1)} copy-done((f32[192,512]{1,0:T(8,128)S(1)}, f32[192,512]{1,0:T(8,128)}, u32[]{:S(2)}) %copy-start.5) | copy-done | bytes 393240
  1.9 0.0 copy-start.6
  1.9 0.7 %copy-done.6 = f32[1024]{0:T(1024)S(1)} copy-done((f32[1024]{0:T(1024)S(1)}, f32[1024]{0:T(1024)}, u32[]{:S(2)}) %copy-start.6) | copy-done | bytes 4120
  2.6 0.1 collective-permute-done.other_ref.other_tokens_ref
  2.6 0.3 shard_map.87
  3.0 0.6 %collective-permute-start.1 = (bf16[192,512]{1,0:T(8,128)(2,1)S(1)}, bf16[192,512]{1,0:T(8,128)(2,1)S(1)}, u32[]{:S(2)}, u32[]{:S(2)}) collective-permute-start(bf16[192,512]{1,0:T(8,128)(2,1)S(1)} %get-tuple-element.48.mine_ref), channel_id=1, source_target_pairs={{2,0},{0,4},{4,8},{8,12},{12,14},{14,10},{10,6},{6,2},{3,1},{1,5},... | collective-permute-start | bytes 589832 | tf_op jit(solution)/shard_map/ppermute | solution.py:421
  3.6 1.5 %collective-permute-start.3 = (bf16[192,512]{1,0:T(8,128)(2,1)S(1)}, bf16[192,512]{1,0:T(8,128)(2,1)S(1)}, u32[]{:S(2)}, u32[]{:S(2)}) collective-permute-start(bf16[192,512]{1,0:T(8,128)(2,1)S(1)} %get-tuple-element.48.mine_ref), channel_id=1, source_target_pairs={{0,2},{4,0},{8,4},{12,8},{14,12},{10,14},{6,10},{2,6},{1,3},{5,1},... | collective-permute-start | bytes 589832 | tf_op jit(solution)/shard_map/ppermute | solution.py:422
  5.1 0.0 copy-done
  5.1 1.4 %shard_map.88 = (bf16[4,384,128]{2,1,0:T(8,128)(2,1)S(1)}, f32[4,384,128]{2,1,0:T(8,128)S(1)}, f32[4,384,128]{2,1,0:T(8,128)S(1)}, f32[4,192,128]{2,1,0:T(8,128)S(1)}) custom-call(bf16[192,512]{1,0:T(8,128)(2,1)S(1)} %get-tuple-element.48.mine_ref, bf16[192,512]{1,0:T(8,128)(2,1)S(1)} %get-tuple-element.49.other_ref, bf16[3,1024,512]{2,1,0:T(8,128)(2,1)S(1)} %copy-done), custom_call_target="tpu_custom_call" | custom-call | flops 679477248 | bytes 5898240 | tf_op jit(solution)/shard_map/pallas_call | solution.py:29
  6.5 3.9 %collective-permute-done.1.block_ref.mine_a = bf16[192,512]{1,0:T(8,128)(2,1)S(1)} collective-permute-done((bf16[192,512]{1,0:T(8,128)(2,1)S(1)}, bf16[192,512]{1,0:T(8,128)(2,1)S(1)}, u32[]{:S(2)}, u32[]{:S(2)}) %collective-permute-start.1) | collective-permute-done | bytes 196640 | tf_op jit(solution)/shard_map/ppermute | solution.py:421
  10.3 0.3 collective-permute-done.3.mine_b
  10.6 0.0 collective-permute-start.5
  10.6 0.5 %collective-permute-start.4 = (bf16[192,512]{1,0:T(8,128)(2,1)S(1)}, bf16[192,512]{1,0:T(8,128)(2,1)S(1)}, u32[]{:S(2)}, u32[]{:S(2)}) collective-permute-start(bf16[192,512]{1,0:T(8,128)(2,1)S(1)} %collective-permute-done.1.block_ref.mine_a), channel_id=1, source_target_pairs={{0,1},{1,0},{2,3},{3,2},{4,5},{5,4},{6,7},{7,6},{8,9},{9,8},{10,11... | collective-permute-start | bytes 589832 | tf_op jit(solution)/shard_map/ppermute | solution.py:440
  11.1 1.6 %collective-permute-start.2 = (bf16[192,512]{1,0:T(8,128)(2,1)S(1)}, bf16[192,512]{1,0:T(8,128)(2,1)S(1)}, u32[]{:S(2)}, u32[]{:S(2)}) collective-permute-start(bf16[192,512]{1,0:T(8,128)(2,1)S(1)} %collective-permute-done.1.block_ref.mine_a), channel_id=1, source_target_pairs={{2,0},{0,4},{4,8},{8,12},{12,14},{14,10},{10,6},{6,2},{3,1},{1,5},... | collective-permute-start | bytes 589832 | tf_op jit(solution)/shard_map/ppermute | solution.py:438
  12.7 0.4 collective-permute-start.7
  13.1 0.0 collective-permute-done.5.other_b
  13.1 0.0 collective-permute-done.4.other_a
  13.1 2.3 %shard_map.90 = (f32[4,384,128]{2,1,0:T(8,128)S(1)}, f32[4,384,128]{2,1,0:T(8,128)S(1)}, f32[4,192,128]{2,1,0:T(8,128)S(1)}) custom-call(bf16[192,512]{1,0:T(8,128)(2,1)S(1)} %collective-permute-done.1.block_ref.mine_a, bf16[192,512]{1,0:T(8,128)(2,1)S(1)} %collective-permute-done.3.mine_b, bf16[192,512]{1,0:T(8,128)(2,1)S(1)} %collective-permute-done.4.other_a, ...), custom_call_target="tpu_custom_call" | custom-call | flops 956301312 | bytes 8261632 | tf_op jit(solution)/shard_map/pallas_call | solution.py:29
  15.5 2.4 %collective-permute-done.2.block_ref.mine_a = bf16[192,512]{1,0:T(8,128)(2,1)S(1)} collective-permute-done((bf16[192,512]{1,0:T(8,128)(2,1)S(1)}, bf16[192,512]{1,0:T(8,128)(2,1)S(1)}, u32[]{:S(2)}, u32[]{:S(2)}) %collective-permute-start.2) | collective-permute-done | bytes 196640 | tf_op jit(solution)/shard_map/ppermute | solution.py:438
  17.9 1.3 %collective-permute-done.7.mine_b = bf16[192,512]{1,0:T(8,128)(2,1)S(1)} collective-permute-done((bf16[192,512]{1,0:T(8,128)(2,1)S(1)}, bf16[192,512]{1,0:T(8,128)(2,1)S(1)}, u32[]{:S(2)}, u32[]{:S(2)}) %collective-permute-start.7) | collective-permute-done | bytes 196640 | tf_op jit(solution)/shard_map/ppermute | solution.py:439
  19.2 0.0 collective-permute-start.9
  19.2 0.5 %collective-permute-start.8 = (bf16[192,512]{1,0:T(8,128)(2,1)S(1)}, bf16[192,512]{1,0:T(8,128)(2,1)S(1)}, u32[]{:S(2)}, u32[]{:S(2)}) collective-permute-start(bf16[192,512]{1,0:T(8,128)(2,1)S(1)} %collective-permute-done.2.block_ref.mine_a), channel_id=1, source_target_pairs={{0,1},{1,0},{2,3},{3,2},{4,5},{5,4},{6,7},{7,6},{8,9},{9,8},{10,11... | collective-permute-start | bytes 589832 | tf_op jit(solution)/shard_map/ppermute | solution.py:440
  19.7 1.6 %collective-permute-start.6 = (bf16[192,512]{1,0:T(8,128)(2,1)S(1)}, bf16[192,512]{1,0:T(8,128)(2,1)S(1)}, u32[]{:S(2)}, u32[]{:S(2)}) collective-permute-start(bf16[192,512]{1,0:T(8,128)(2,1)S(1)} %collective-permute-done.2.block_ref.mine_a), channel_id=1, source_target_pairs={{2,0},{0,4},{4,8},{8,12},{12,14},{14,10},{10,6},{6,2},{3,1},{1,5},... | collective-permute-start | bytes 589832 | tf_op jit(solution)/shard_map/ppermute | solution.py:438
  21.3 0.4 collective-permute-start.11
  21.7 0.0 collective-permute-done.9.other_b
  21.8 0.0 collective-permute-done.8.other_a
  21.8 2.3 %shard_map.92 = (f32[4,384,128]{2,1,0:T(8,128)S(1)}, f32[4,384,128]{2,1,0:T(8,128)S(1)}, f32[4,192,128]{2,1,0:T(8,128)S(1)}) custom-call(bf16[192,512]{1,0:T(8,128)(2,1)S(1)} %collective-permute-done.2.block_ref.mine_a, bf16[192,512]{1,0:T(8,128)(2,1)S(1)} %collective-permute-done.7.mine_b, bf16[192,512]{1,0:T(8,128)(2,1)S(1)} %collective-permute-done.8.other_a, ...), custom_call_target="tpu_custom_call" | custom-call | flops 956301312 | bytes 8261632 | tf_op jit(solution)/shard_map/pallas_call | solution.py:29
  24.1 2.4 %collective-permute-done.6.block_ref.mine_a = bf16[192,512]{1,0:T(8,128)(2,1)S(1)} collective-permute-done((bf16[192,512]{1,0:T(8,128)(2,1)S(1)}, bf16[192,512]{1,0:T(8,128)(2,1)S(1)}, u32[]{:S(2)}, u32[]{:S(2)}) %collective-permute-start.6) | collective-permute-done | bytes 196640 | tf_op jit(solution)/shard_map/ppermute | solution.py:438
  26.5 1.3 %collective-permute-done.11.mine_b = bf16[192,512]{1,0:T(8,128)(2,1)S(1)} collective-permute-done((bf16[192,512]{1,0:T(8,128)(2,1)S(1)}, bf16[192,512]{1,0:T(8,128)(2,1)S(1)}, u32[]{:S(2)}, u32[]{:S(2)}) %collective-permute-start.11) | collective-permute-done | bytes 196640 | tf_op jit(solution)/shard_map/ppermute | solution.py:439
  27.8 0.0 collective-permute-start.14
  27.8 0.5 %collective-permute-start.13 = (bf16[192,512]{1,0:T(8,128)(2,1)S(1)}, bf16[192,512]{1,0:T(8,128)(2,1)S(1)}, u32[]{:S(2)}, u32[]{:S(2)}) collective-permute-start(bf16[192,512]{1,0:T(8,128)(2,1)S(1)} %collective-permute-done.6.block_ref.mine_a), channel_id=1, source_target_pairs={{0,1},{1,0},{2,3},{3,2},{4,5},{5,4},{6,7},{7,6},{8,9},{9,8},{10,11... | collective-permute-start | bytes 589832 | tf_op jit(solution)/shard_map/ppermute | solution.py:440
  28.4 0.5 %collective-permute-start.12 = (bf16[96,512]{1,0:T(8,128)(2,1)S(1)}, bf16[96,512]{1,0:T(8,128)(2,1)S(1)}, u32[]{:S(2)}, u32[]{:S(2)}) collective-permute-start(bf16[96,512]{1,0:T(8,128)(2,1)S(1)} %slice.7), channel_id=1, source_target_pairs={{0,2},{4,0},{8,4},{12,8},{14,12},{10,14},{6,10},{2,6},{1,3},{5,1},... | collective-permute-start | bytes 294920 | tf_op jit(solution)/shard_map/ppermute | solution.py:439
  28.9 1.6 %collective-permute-start.10 = (bf16[96,512]{1,0:T(8,128)(2,1)S(1)}, bf16[96,512]{1,0:T(8,128)(2,1)S(1)}, u32[]{:S(2)}, u32[]{:S(2)}) collective-permute-start(bf16[96,512]{1,0:T(8,128)(2,1)S(1)} %slice.6), channel_id=1, source_target_pairs={{2,0},{0,4},{4,8},{8,12},{12,14},{14,10},{10,6},{6,2},{3,1},{1,5},... | collective-permute-start | bytes 294920 | tf_op jit(solution)/shard_map/ppermute | solution.py:438
  30.4 0.0 collective-permute-done.14.other_b
  30.4 0.0 collective-permute-done.13.other_a
  30.4 0.0 copy-start.3
  30.5 2.3 %shard_map.94 = (f32[4,384,128]{2,1,0:T(8,128)S(1)}, f32[4,384,128]{2,1,0:T(8,128)S(1)}, f32[4,192,128]{2,1,0:T(8,128)S(1)}) custom-call(bf16[192,512]{1,0:T(8,128)(2,1)S(1)} %collective-permute-done.6.block_ref.mine_a, bf16[192,512]{1,0:T(8,128)(2,1)S(1)} %collective-permute-done.11.mine_b, bf16[192,512]{1,0:T(8,128)(2,1)S(1)} %collective-permute-done.13.other_a, ...), custom_call_target="tpu_custom_call" | custom-call | flops 956301312 | bytes 8261632 | tf_op jit(solution)/shard_map/pallas_call | solution.py:29
  32.8 0.3 collective-permute-done.12.mine_b
  33.1 0.4 collective-permute-done.10.mine_a
  33.5 0.0 copy-start.2
  33.5 0.0 copy-start.4
  33.5 0.0 copy-start.1
  33.5 0.0 collective-permute-start.15
  33.5 0.5 %collective-permute-start.16 = (bf16[96,512]{1,0:T(8,128)(2,1)S(1)}, bf16[96,512]{1,0:T(8,128)(2,1)S(1)}, u32[]{:S(2)}, u32[]{:S(2)}) collective-permute-start(bf16[96,512]{1,0:T(8,128)(2,1)S(1)} %collective-permute-done.12.mine_b), channel_id=1, source_target_pairs={{0,1},{1,0},{2,3},{3,2},{4,5},{5,4},{6,7},{7,6},{8,9},{9,8},{10,11... | collective-permute-start | bytes 294920 | tf_op jit(solution)/shard_map/ppermute | solution.py:451
  34.0 0.8 %collective-permute-done.15.other_a = bf16[96,512]{1,0:T(8,128)(2,1)S(1)} collective-permute-done((bf16[96,512]{1,0:T(8,128)(2,1)S(1)}, bf16[96,512]{1,0:T(8,128)(2,1)S(1)}, u32[]{:S(2)}, u32[]{:S(2)}) %collective-permute-start.15) | collective-permute-done | bytes 98336 | tf_op jit(solution)/shard_map/ppermute | solution.py:451
  34.8 0.2 collective-permute-done.16.other_b
  34.9 0.0 copy-done.3
  34.9 1.7 %shard_map.95 = (bf16[2,64,1024]{2,1,0:T(8,128)(2,1)S(1)}, f32[2,64,1024]{2,1,0:T(8,128)S(1)}) custom-call(bf16[96,512]{1,0:T(8,128)(2,1)S(1)} %collective-permute-done.10.mine_a, bf16[96,512]{1,0:T(8,128)(2,1)S(1)} %collective-permute-done.12.mine_b, bf16[96,512]{1,0:T(8,128)(2,1)S(1)} %collective-permute-done.15.other_a, ...), custom_call_target="tpu_custom_call" | custom-call | flops 679477248 | bytes 8519680 | tf_op jit(solution)/shard_map/pallas_call | solution.py:29
  36.6 0.4 collective-permute-start.17
  37.0 1.2 %collective-permute-done.17.got_ref = bf16[2,64,1024]{2,1,0:T(8,128)(2,1)S(1)} collective-permute-done((bf16[2,64,1024]{2,1,0:T(8,128)(2,1)S(1)}, bf16[2,64,1024]{2,1,0:T(8,128)(2,1)S(1)}, u32[]{:S(2)}, u32[]{:S(2)}) %collective-permute-start.17) | collective-permute-done | bytes 262176 | tf_op jit(solution)/shard_map/ppermute | solution.py:465
  38.2 0.0 copy-done.2
  38.2 0.0 copy-done.4
  38.2 0.5 %shard_map.96 = (bf16[96,256]{1,0:T(8,128)(2,1)S(1)}, bf16[96,256]{1,0:T(8,128)(2,1)S(1)}) custom-call(f32[2,64,1024]{2,1,0:T(8,128)S(1)} %get-tuple-element.80.keep_ref, bf16[2,64,1024]{2,1,0:T(8,128)(2,1)S(1)} %collective-permute-done.17.got_ref, bf16[2,1024,256]{2,1,0:T(8,128)(2,1)S(1)} %copy-done.2, f32[2,2,256]{2,1,0:T(2,128)S(1)} %copy-done.4), custom_call_target="tpu_custom_call" | custom-call | flops 83886080 | bytes 1937408 | tf_op jit(solution)/shard_map/pallas_call | solution.py:29
  38.7 1.6 %collective-permute-start.18 = (bf16[96,256]{1,0:T(8,128)(2,1)S(1)}, bf16[96,256]{1,0:T(8,128)(2,1)S(1)}, u32[]{:S(2)}, u32[]{:S(2)}) collective-permute-start(bf16[96,256]{1,0:T(8,128)(2,1)S(1)} %get-tuple-element.82.near_ref), channel_id=1, source_target_pairs={{0,2},{2,0},{4,6},{6,4},{8,10},{10,8},{12,14},{14,12},{1,3},{3,1},... | collective-permute-start | bytes 147464 | tf_op jit(solution)/shard_map/ppermute | solution.py:481
  40.3 2.9 %collective-permute-start.19 = (bf16[96,256]{1,0:T(8,128)(2,1)S(1)}, bf16[96,256]{1,0:T(8,128)(2,1)S(1)}, u32[]{:S(2)}, u32[]{:S(2)}) collective-permute-start(bf16[96,256]{1,0:T(8,128)(2,1)S(1)} %get-tuple-element.83.far_ref), channel_id=1, source_target_pairs={{2,4},{6,8},{10,12},{4,2},{8,6},{12,10},{3,5},{7,9},{11,13},{5,3},... | collective-permute-start | bytes 147464 | tf_op jit(solution)/shard_map/ppermute | solution.py:480
  43.3 0.0 collective-permute-done.18.got_near_ref
  43.3 3.9 %collective-permute-done.19.got_far_ref = bf16[96,256]{1,0:T(8,128)(2,1)S(1)} collective-permute-done((bf16[96,256]{1,0:T(8,128)(2,1)S(1)}, bf16[96,256]{1,0:T(8,128)(2,1)S(1)}, u32[]{:S(2)}, u32[]{:S(2)}) %collective-permute-start.19) | collective-permute-done | bytes 49184 | tf_op jit(solution)/shard_map/ppermute | solution.py:480
  47.2 0.0 copy-done.1
  47.2 1.2 %shard_map.97 = (bf16[2,48,256]{2,1,0:T(8,128)(2,1)}, bf16[1,24,256]{2,1,0:T(8,128)(2,1)}) custom-call(bf16[96,256]{1,0:T(8,128)(2,1)S(1)} %get-tuple-element.82.near_ref, bf16[96,256]{1,0:T(8,128)(2,1)S(1)} %get-tuple-element.83.far_ref, bf16[96,256]{1,0:T(8,128)(2,1)S(1)} %collective-permute-done.18.got_near_ref, ...), custom_call_target="tpu_custom_call" | custom-call | flops 188743680 | bytes 2621440 | tf_op jit(solution)/shard_map/pallas_call | solution.py:29
  (6 shorter events, 0.0 us)
Async XLA Ops:
  0.6 4.4 %copy-start = (bf16[3,1024,512]{2,1,0:T(8,128)(2,1)S(1)}, bf16[3,1024,512]{2,1,0:T(8,128)(2,1)}, u32[]{:S(2)}) copy-start(bf16[3,1024,512]{2,1,0:T(8,128)(2,1)} %weight_ref.10) | copy-start | bytes 9437188
  0.6 2.0 %collective-permute-start = (f32[192,512]{1,0:T(8,128)}, f32[192,512]{1,0:T(8,128)S(1)}, u32[]{:S(2)}, u32[]{:S(2)}) collective-permute-start(f32[192,512]{1,0:T(8,128)} %tokens_ref.1), channel_id=1, source_target_pairs={{0,1},{1,0},{2,3},{3,2},{4,5},{5,4},{6,7},{7,6},{8,9},{9,8},{10,11... | collective-permute-start | bytes 1179656 | tf_op jit(solution)/shard_map/ppermute | solution.py:393
  0.7 1.1 %copy-start.5 = (f32[192,512]{1,0:T(8,128)S(1)}, f32[192,512]{1,0:T(8,128)}, u32[]{:S(2)}) copy-start(f32[192,512]{1,0:T(8,128)} %tokens_ref.1) | copy-start | bytes 1179652
  1.9 0.7 %copy-start.6 = (f32[1024]{0:T(1024)S(1)}, f32[1024]{0:T(1024)}, u32[]{:S(2)}) copy-start(f32[1024]{0:T(1024)} %gain_ref.3) | copy-start | bytes 12292
  3.0 7.4 %collective-permute-start.1 = (bf16[192,512]{1,0:T(8,128)(2,1)S(1)}, bf16[192,512]{1,0:T(8,128)(2,1)S(1)}, u32[]{:S(2)}, u32[]{:S(2)}) collective-permute-start(bf16[192,512]{1,0:T(8,128)(2,1)S(1)} %get-tuple-element.48.mine_ref), channel_id=1, source_target_pairs={{2,0},{0,4},{4,8},{8,12},{12,14},{14,10},{10,6},{6,2},{3,1},{1,5},... | collective-permute-start | bytes 589832 | tf_op jit(solution)/shard_map/ppermute | solution.py:421
  3.6 7.0 %collective-permute-start.3 = (bf16[192,512]{1,0:T(8,128)(2,1)S(1)}, bf16[192,512]{1,0:T(8,128)(2,1)S(1)}, u32[]{:S(2)}, u32[]{:S(2)}) collective-permute-start(bf16[192,512]{1,0:T(8,128)(2,1)S(1)} %get-tuple-element.48.mine_ref), channel_id=1, source_target_pairs={{0,2},{4,0},{8,4},{12,8},{14,12},{10,14},{6,10},{2,6},{1,3},{5,1},... | collective-permute-start | bytes 589832 | tf_op jit(solution)/shard_map/ppermute | solution.py:422
  10.6 2.5 %collective-permute-start.5 = (bf16[192,512]{1,0:T(8,128)(2,1)S(1)}, bf16[192,512]{1,0:T(8,128)(2,1)S(1)}, u32[]{:S(2)}, u32[]{:S(2)}) collective-permute-start(bf16[192,512]{1,0:T(8,128)(2,1)S(1)} %collective-permute-done.3.mine_b), channel_id=1, source_target_pairs={{0,1},{1,0},{2,3},{3,2},{4,5},{5,4},{6,7},{7,6},{8,9},{9,8},{10,11... | collective-permute-start | bytes 589832 | tf_op jit(solution)/shard_map/ppermute | solution.py:440
  10.6 2.5 %collective-permute-start.4 = (bf16[192,512]{1,0:T(8,128)(2,1)S(1)}, bf16[192,512]{1,0:T(8,128)(2,1)S(1)}, u32[]{:S(2)}, u32[]{:S(2)}) collective-permute-start(bf16[192,512]{1,0:T(8,128)(2,1)S(1)} %collective-permute-done.1.block_ref.mine_a), channel_id=1, source_target_pairs={{0,1},{1,0},{2,3},{3,2},{4,5},{5,4},{6,7},{7,6},{8,9},{9,8},{10,11... | collective-permute-start | bytes 589832 | tf_op jit(solution)/shard_map/ppermute | solution.py:440
  11.1 6.8 %collective-permute-start.2 = (bf16[192,512]{1,0:T(8,128)(2,1)S(1)}, bf16[192,512]{1,0:T(8,128)(2,1)S(1)}, u32[]{:S(2)}, u32[]{:S(2)}) collective-permute-start(bf16[192,512]{1,0:T(8,128)(2,1)S(1)} %collective-permute-done.1.block_ref.mine_a), channel_id=1, source_target_pairs={{2,0},{0,4},{4,8},{8,12},{12,14},{14,10},{10,6},{6,2},{3,1},{1,5},... | collective-permute-start | bytes 589832 | tf_op jit(solution)/shard_map/ppermute | solution.py:438
  12.7 6.5 %collective-permute-start.7 = (bf16[192,512]{1,0:T(8,128)(2,1)S(1)}, bf16[192,512]{1,0:T(8,128)(2,1)S(1)}, u32[]{:S(2)}, u32[]{:S(2)}) collective-permute-start(bf16[192,512]{1,0:T(8,128)(2,1)S(1)} %collective-permute-done.3.mine_b), channel_id=1, source_target_pairs={{0,2},{4,0},{8,4},{12,8},{14,12},{10,14},{6,10},{2,6},{1,3},{5,1},... | collective-permute-start | bytes 589832 | tf_op jit(solution)/shard_map/ppermute | solution.py:439
  19.2 2.5 %collective-permute-start.9 = (bf16[192,512]{1,0:T(8,128)(2,1)S(1)}, bf16[192,512]{1,0:T(8,128)(2,1)S(1)}, u32[]{:S(2)}, u32[]{:S(2)}) collective-permute-start(bf16[192,512]{1,0:T(8,128)(2,1)S(1)} %collective-permute-done.7.mine_b), channel_id=1, source_target_pairs={{0,1},{1,0},{2,3},{3,2},{4,5},{5,4},{6,7},{7,6},{8,9},{9,8},{10,11... | collective-permute-start | bytes 589832 | tf_op jit(solution)/shard_map/ppermute | solution.py:440
  19.2 2.5 %collective-permute-start.8 = (bf16[192,512]{1,0:T(8,128)(2,1)S(1)}, bf16[192,512]{1,0:T(8,128)(2,1)S(1)}, u32[]{:S(2)}, u32[]{:S(2)}) collective-permute-start(bf16[192,512]{1,0:T(8,128)(2,1)S(1)} %collective-permute-done.2.block_ref.mine_a), channel_id=1, source_target_pairs={{0,1},{1,0},{2,3},{3,2},{4,5},{5,4},{6,7},{7,6},{8,9},{9,8},{10,11... | collective-permute-start | bytes 589832 | tf_op jit(solution)/shard_map/ppermute | solution.py:440
  19.7 6.8 %collective-permute-start.6 = (bf16[192,512]{1,0:T(8,128)(2,1)S(1)}, bf16[192,512]{1,0:T(8,128)(2,1)S(1)}, u32[]{:S(2)}, u32[]{:S(2)}) collective-permute-start(bf16[192,512]{1,0:T(8,128)(2,1)S(1)} %collective-permute-done.2.block_ref.mine_a), channel_id=1, source_target_pairs={{2,0},{0,4},{4,8},{8,12},{12,14},{14,10},{10,6},{6,2},{3,1},{1,5},... | collective-permute-start | bytes 589832 | tf_op jit(solution)/shard_map/ppermute | solution.py:438
  21.3 6.5 %collective-permute-start.11 = (bf16[192,512]{1,0:T(8,128)(2,1)S(1)}, bf16[192,512]{1,0:T(8,128)(2,1)S(1)}, u32[]{:S(2)}, u32[]{:S(2)}) collective-permute-start(bf16[192,512]{1,0:T(8,128)(2,1)S(1)} %collective-permute-done.7.mine_b), channel_id=1, source_target_pairs={{0,2},{4,0},{8,4},{12,8},{14,12},{10,14},{6,10},{2,6},{1,3},{5,1},... | collective-permute-start | bytes 589832 | tf_op jit(solution)/shard_map/ppermute | solution.py:439
  27.8 2.6 %collective-permute-start.14 = (bf16[192,512]{1,0:T(8,128)(2,1)S(1)}, bf16[192,512]{1,0:T(8,128)(2,1)S(1)}, u32[]{:S(2)}, u32[]{:S(2)}) collective-permute-start(bf16[192,512]{1,0:T(8,128)(2,1)S(1)} %collective-permute-done.11.mine_b), channel_id=1, source_target_pairs={{0,1},{1,0},{2,3},{3,2},{4,5},{5,4},{6,7},{7,6},{8,9},{9,8},{10,11... | collective-permute-start | bytes 589832 | tf_op jit(solution)/shard_map/ppermute | solution.py:440
  27.8 2.6 %collective-permute-start.13 = (bf16[192,512]{1,0:T(8,128)(2,1)S(1)}, bf16[192,512]{1,0:T(8,128)(2,1)S(1)}, u32[]{:S(2)}, u32[]{:S(2)}) collective-permute-start(bf16[192,512]{1,0:T(8,128)(2,1)S(1)} %collective-permute-done.6.block_ref.mine_a), channel_id=1, source_target_pairs={{0,1},{1,0},{2,3},{3,2},{4,5},{5,4},{6,7},{7,6},{8,9},{9,8},{10,11... | collective-permute-start | bytes 589832 | tf_op jit(solution)/shard_map/ppermute | solution.py:440
  28.4 4.8 %collective-permute-start.12 = (bf16[96,512]{1,0:T(8,128)(2,1)S(1)}, bf16[96,512]{1,0:T(8,128)(2,1)S(1)}, u32[]{:S(2)}, u32[]{:S(2)}) collective-permute-start(bf16[96,512]{1,0:T(8,128)(2,1)S(1)} %slice.7), channel_id=1, source_target_pairs={{0,2},{4,0},{8,4},{12,8},{14,12},{10,14},{6,10},{2,6},{1,3},{5,1},... | collective-permute-start | bytes 294920 | tf_op jit(solution)/shard_map/ppermute | solution.py:439
  28.9 4.6 %collective-permute-start.10 = (bf16[96,512]{1,0:T(8,128)(2,1)S(1)}, bf16[96,512]{1,0:T(8,128)(2,1)S(1)}, u32[]{:S(2)}, u32[]{:S(2)}) collective-permute-start(bf16[96,512]{1,0:T(8,128)(2,1)S(1)} %slice.6), channel_id=1, source_target_pairs={{2,0},{0,4},{4,8},{8,12},{12,14},{14,10},{10,6},{6,2},{3,1},{1,5},... | collective-permute-start | bytes 294920 | tf_op jit(solution)/shard_map/ppermute | solution.py:438
  30.4 4.5 %copy-start.3 = (bf16[512,1024]{1,0:T(8,128)(2,1)S(1)}, bf16[512,1024]{1,0:T(8,128)(2,1)}, u32[]{:S(2)}) copy-start(bf16[512,1024]{1,0:T(8,128)(2,1)} %out_weight_ref.1) | copy-start | bytes 3145732
  33.5 4.7 %copy-start.2 = (bf16[2,1024,256]{2,1,0:T(8,128)(2,1)S(1)}, bf16[2,1024,256]{2,1,0:T(8,128)(2,1)}, u32[]{:S(2)}) copy-start(bf16[2,1024,256]{2,1,0:T(8,128)(2,1)} %lateral_ref.1) | copy-start | bytes 3145732
  33.5 4.7 %copy-start.4 = (f32[2,2,256]{2,1,0:T(2,128)S(1)}, f32[2,2,256]{2,1,0:T(2,128)}, u32[]{:S(2)}) copy-start(f32[2,2,256]{2,1,0:T(2,128)} %gain_ref.5) | copy-start | bytes 12292
  33.5 13.7 %copy-start.1 = (bf16[2,3,3,256,256]{4,3,2,1,0:T(8,128)(2,1)S(1)}, bf16[2,3,3,256,256]{4,3,2,1,0:T(8,128)(2,1)}, u32[]{:S(2)}) copy-start(bf16[2,3,3,256,256]{4,3,2,1,0:T(8,128)(2,1)} %weight_ref.11) | copy-start | bytes 7077892
  33.5 1.3 %collective-permute-start.15 = (bf16[96,512]{1,0:T(8,128)(2,1)S(1)}, bf16[96,512]{1,0:T(8,128)(2,1)S(1)}, u32[]{:S(2)}, u32[]{:S(2)}) collective-permute-start(bf16[96,512]{1,0:T(8,128)(2,1)S(1)} %collective-permute-done.10.mine_a), channel_id=1, source_target_pairs={{0,1},{1,0},{2,3},{3,2},{4,5},{5,4},{6,7},{7,6},{8,9},{9,8},{10,11... | collective-permute-start | bytes 294920 | tf_op jit(solution)/shard_map/ppermute | solution.py:451
  33.5 1.4 %collective-permute-start.16 = (bf16[96,512]{1,0:T(8,128)(2,1)S(1)}, bf16[96,512]{1,0:T(8,128)(2,1)S(1)}, u32[]{:S(2)}, u32[]{:S(2)}) collective-permute-start(bf16[96,512]{1,0:T(8,128)(2,1)S(1)} %collective-permute-done.12.mine_b), channel_id=1, source_target_pairs={{0,1},{1,0},{2,3},{3,2},{4,5},{5,4},{6,7},{7,6},{8,9},{9,8},{10,11... | collective-permute-start | bytes 294920 | tf_op jit(solution)/shard_map/ppermute | solution.py:451
  36.6 1.6 %collective-permute-start.17 = (bf16[2,64,1024]{2,1,0:T(8,128)(2,1)S(1)}, bf16[2,64,1024]{2,1,0:T(8,128)(2,1)S(1)}, u32[]{:S(2)}, u32[]{:S(2)}) collective-permute-start(bf16[2,64,1024]{2,1,0:T(8,128)(2,1)S(1)} %get-tuple-element.81), channel_id=1, source_target_pairs={{0,1},{1,0},{2,3},{3,2},{4,5},{5,4},{6,7},{7,6},{8,9},{9,8},{10,11... | collective-permute-start | bytes 786440 | tf_op jit(solution)/shard_map/ppermute | solution.py:465
  38.7 4.6 %collective-permute-start.18 = (bf16[96,256]{1,0:T(8,128)(2,1)S(1)}, bf16[96,256]{1,0:T(8,128)(2,1)S(1)}, u32[]{:S(2)}, u32[]{:S(2)}) collective-permute-start(bf16[96,256]{1,0:T(8,128)(2,1)S(1)} %get-tuple-element.82.near_ref), channel_id=1, source_target_pairs={{0,2},{2,0},{4,6},{6,4},{8,10},{10,8},{12,14},{14,12},{1,3},{3,1},... | collective-permute-start | bytes 147464 | tf_op jit(solution)/shard_map/ppermute | solution.py:481
  40.3 6.9 %collective-permute-start.19 = (bf16[96,256]{1,0:T(8,128)(2,1)S(1)}, bf16[96,256]{1,0:T(8,128)(2,1)S(1)}, u32[]{:S(2)}, u32[]{:S(2)}) collective-permute-start(bf16[96,256]{1,0:T(8,128)(2,1)S(1)} %get-tuple-element.83.far_ref), channel_id=1, source_target_pairs={{2,4},{6,8},{10,12},{4,2},{8,6},{12,10},{3,5},{7,9},{11,13},{5,3},... | collective-permute-start | bytes 147464 | tf_op jit(solution)/shard_map/ppermute | solution.py:480

commit v5 on v4

--- a/solution.py
+++ b/solution.py
@@ -74,9 +74,8 @@
     return mine, other
 
 
-def intake_kernel(tokens_ref, gain_ref, tokens_out, gain_out):
+def intake_kernel(tokens_ref, tokens_out):
     tokens_out[...] = tokens_ref[...]
-    gain_out[...] = gain_ref[...]
 
 
 def norm_kernel(mine_ref, other_ref, gain_ref, mine_out, other_out):
@@ -164,10 +163,8 @@
 
 
 def step_kernel(
-    mine_a,
-    mine_b,
-    other_a,
-    other_b,
+    mine_ref,
+    other_ref,
     weight_ref,
     query_ref,
     top_ref,
@@ -179,7 +176,7 @@
     mixed_out,
 ):
     for pair, state in absorb_blocks(
-        (mine_a, mine_b), (other_a, other_b), weight_ref, query_ref, top_ref, total_ref, mixed_ref
+        (mine_ref,), (other_ref,), weight_ref, query_ref, top_ref, total_ref, mixed_ref
     ):
         top_out[pair], total_out[pair], mixed_out[pair] = state
 
@@ -391,13 +388,8 @@
     swap = [(i, cores - 1 - i) for i in range(cores)]
 
     other = lax.ppermute(tokens, "head", swap)
-    tokens, norm_gain = call(
-        intake_kernel,
-        [(tokens.shape, F32), (norm_gain.shape, F32)],
-        (tokens, norm_gain),
-        flops=MIB * 1024,
-    )
-    other, tokens, norm_gain = lax.optimization_barrier((other, tokens, norm_gain))
+    (tokens,) = call(intake_kernel, [(tokens.shape, F32)], (tokens,), flops=MIB * 1024)
+    other, tokens = lax.optimization_barrier((other, tokens))
     tail = (out_weight, tokens, other)
     tail_outs = [
         ((grid_rows, window, features), BF16),
@@ -438,13 +430,14 @@
             ahead = lax.ppermute(ahead, "blk", forth)
             behind = lax.ppermute(behind, "blk", back)
             others = (lax.ppermute(parts[0], "head", swap), lax.ppermute(parts[1], "head", swap))
-            state = call(
-                step_kernel,
-                state_outs,
-                parts + others + (qkv_weight, queries) + tuple(state) + (mark,),
-                flops=2 * unit,
-                exps=2 * heads * rows * rows,
-            )
+            for block in zip(parts, others):
+                state = call(
+                    step_kernel,
+                    state_outs,
+                    block + (qkv_weight, queries) + tuple(state) + (mark,),
+                    flops=unit,
+                    exps=heads * rows * rows,
+                )
             state = list(state)
         ahead, behind, state = lax.optimization_barrier((ahead, behind, state))
         parts = (ahead, behind)

time: 48.7 us -> 48.2 us (0.990)
  starting transfers between devices: 15.3 us -> 14 us
  Pallas kernels: 12.2 us -> 13.1 us
  local copies, waits for them, and re-layouts: 1.86 us -> 1.18 us
  waiting for transfers between devices: 18.3 us -> 18.9 us
    ppermute x3, starting transfers between devices: 1.52 us -> 0.01 us  [body(): lax.ppermute(parts[0], 'head', swap)]
    pallas_call x12 -> x15, Pallas kernels: 12.2 us -> 13.1 us  [call(): pl.pallas_call(kernel, out_shape=outs, in_specs=specs(len(args)), out_spe...]
    ppermute x1, waiting for transfers between devices: 0.06 us -> 0.74 us  [body(): other = lax.ppermute(tokens, 'head', swap)]
    unnamed x14, local copies, waits for them, and re-layouts: 1.85 us -> 1.16 us
  transfers between devices with their start and end apart: 20 -> 20, of which waited for: 13 -> 13; matrix products, arithmetic and copies ran while one was open for 0% -> 0% of each run, Pallas kernels for 17% -> 19%
where the time goes in v5:
time: 48.2 us; the launch traced here: 48 us
  waiting for transfers between devices  18.9 us (39%)
  starting transfers between devices  14 us (29%)
  Pallas kernels  13.1 us (27%)
  local copies, waits for them, and re-layouts  1.18 us (2%)
  between operations  0.82 us (2%)
    pallas_call x15, Pallas kernels, call(): pl.pallas_call(kernel, out_shape=outs, in_specs=specs(len(args)), out_spe...  13.1 us
    ppermute x3, waiting for transfers between devices, body(): ahead = lax.ppermute(ahead, 'blk', forth)  5.22 us
    ppermute x3, starting transfers between devices, body(): ahead = lax.ppermute(ahead, 'blk', forth)  4.48 us
    ppermute x1, waiting for transfers between devices, body(): got_far = lax.ppermute(far, 'blk', far_pairs)  3.99 us
    ppermute x1, waiting for transfers between devices, body(): ahead = lax.ppermute(mine, 'blk', forth)  3.5 us
    ppermute x3, waiting for transfers between devices, body(): behind = lax.ppermute(behind, 'blk', back)  3.09 us
    ppermute x1, starting transfers between devices, body(): got_far = lax.ppermute(far, 'blk', far_pairs)  2.86 us
    ppermute x3, starting transfers between devices, body(): behind = lax.ppermute(behind, 'blk', back)  1.66 us
  transfers between devices with their start and end apart: 20, of which 13 were waited for; matrix products, arithmetic and copies ran while one was open for 0% of the time, Pallas kernels for 19%

profile of v5, /device:TPU:6, one launch (start us, length us, event | category | flops | bytes accessed | tf_op | source)
XLA Modules:
  0.0 48.0 jit_solution(13590976290461067236)
XLA Ops:
  0.6 0.0 copy-start.5
  0.6 0.0 copy-start
  0.6 0.1 collective-permute-start
  0.7 0.0 copy-start.6
  0.7 1.1 %copy-done.6 = f32[192,512]{1,0:T(8,128)S(1)} copy-done((f32[192,512]{1,0:T(8,128)S(1)}, f32[192,512]{1,0:T(8,128)}, u32[]{:S(2)}) %copy-start.6) | copy-done | bytes 393240
  1.9 0.7 %collective-permute-done.other_ref.other_tokens_ref = f32[192,512]{1,0:T(8,128)S(1)} collective-permute-done((f32[192,512]{1,0:T(8,128)}, f32[192,512]{1,0:T(8,128)S(1)}, u32[]{:S(2)}, u32[]{:S(2)}) %collective-permute-start) | collective-permute-done | bytes 393248 | tf_op jit(solution)/shard_map/ppermute | solution.py:390
  2.6 0.0 copy-done.5
  2.7 0.3 shard_map.87
  3.0 0.6 %collective-permute-start.1 = (bf16[192,512]{1,0:T(8,128)(2,1)S(1)}, bf16[192,512]{1,0:T(8,128)(2,1)S(1)}, u32[]{:S(2)}, u32[]{:S(2)}) collective-permute-start(bf16[192,512]{1,0:T(8,128)(2,1)S(1)} %get-tuple-element.51.mine_ref), channel_id=1, source_target_pairs={{2,0},{0,4},{4,8},{8,12},{12,14},{14,10},{10,6},{6,2},{3,1},{1,5},... | collective-permute-start | bytes 589832 | tf_op jit(solution)/shard_map/ppermute | solution.py:413
  3.6 1.5 %collective-permute-start.3 = (bf16[192,512]{1,0:T(8,128)(2,1)S(1)}, bf16[192,512]{1,0:T(8,128)(2,1)S(1)}, u32[]{:S(2)}, u32[]{:S(2)}) collective-permute-start(bf16[192,512]{1,0:T(8,128)(2,1)S(1)} %get-tuple-element.51.mine_ref), channel_id=1, source_target_pairs={{0,2},{4,0},{8,4},{12,8},{14,12},{10,14},{6,10},{2,6},{1,3},{5,1},... | collective-permute-start | bytes 589832 | tf_op jit(solution)/shard_map/ppermute | solution.py:414
  5.1 0.0 copy-done
  5.1 1.4 %shard_map.88 = (bf16[4,384,128]{2,1,0:T(8,128)(2,1)S(1)}, f32[4,384,128]{2,1,0:T(8,128)S(1)}, f32[4,384,128]{2,1,0:T(8,128)S(1)}, f32[4,192,128]{2,1,0:T(8,128)S(1)}) custom-call(bf16[192,512]{1,0:T(8,128)(2,1)S(1)} %get-tuple-element.51.mine_ref, bf16[192,512]{1,0:T(8,128)(2,1)S(1)} %get-tuple-element.52.other_ref, bf16[3,1024,512]{2,1,0:T(8,128)(2,1)S(1)} %copy-done), custom_call_target="tpu_custom_call" | custom-call | flops 679477248 | bytes 5898240 | tf_op jit(solution)/shard_map/pallas_call | solution.py:29
  6.5 3.5 %collective-permute-done.1.block_ref.mine_ref = bf16[192,512]{1,0:T(8,128)(2,1)S(1)} collective-permute-done((bf16[192,512]{1,0:T(8,128)(2,1)S(1)}, bf16[192,512]{1,0:T(8,128)(2,1)S(1)}, u32[]{:S(2)}, u32[]{:S(2)}) %collective-permute-start.1) | collective-permute-done | bytes 196640 | tf_op jit(solution)/shard_map/ppermute | solution.py:413
  10.0 0.0 collective-permute-start.5
  10.0 0.3 collective-permute-done.3.mine_ref
  10.2 0.3 collective-permute-start.4
  10.5 1.3 %collective-permute-start.2 = (bf16[192,512]{1,0:T(8,128)(2,1)S(1)}, bf16[192,512]{1,0:T(8,128)(2,1)S(1)}, u32[]{:S(2)}, u32[]{:S(2)}) collective-permute-start(bf16[192,512]{1,0:T(8,128)(2,1)S(1)} %collective-permute-done.1.block_ref.mine_ref), channel_id=1, source_target_pairs={{2,0},{0,4},{4,8},{8,12},{12,14},{14,10},{10,6},{6,2},{3,1},{1,5},... | collective-permute-start | bytes 589832 | tf_op jit(solution)/shard_map/ppermute | solution.py:430
  11.8 0.7 %collective-permute-start.7 = (bf16[192,512]{1,0:T(8,128)(2,1)S(1)}, bf16[192,512]{1,0:T(8,128)(2,1)S(1)}, u32[]{:S(2)}, u32[]{:S(2)}) collective-permute-start(bf16[192,512]{1,0:T(8,128)(2,1)S(1)} %collective-permute-done.3.mine_ref), channel_id=1, source_target_pairs={{0,2},{4,0},{8,4},{12,8},{14,12},{10,14},{6,10},{2,6},{1,3},{5,1},... | collective-permute-start | bytes 589832 | tf_op jit(solution)/shard_map/ppermute | solution.py:431
  12.5 0.0 collective-permute-done.5.other_ref
  12.5 1.3 %shard_map.90 = (f32[4,384,128]{2,1,0:T(8,128)S(1)}, f32[4,384,128]{2,1,0:T(8,128)S(1)}, f32[4,192,128]{2,1,0:T(8,128)S(1)}) custom-call(bf16[192,512]{1,0:T(8,128)(2,1)S(1)} %collective-permute-done.1.block_ref.mine_ref, bf16[192,512]{1,0:T(8,128)(2,1)S(1)} %collective-permute-done.5.other_ref, bf16[3,1024,512]{2,1,0:T(8,128)(2,1)S(1)} %copy-done, ...), custom_call_target="tpu_custom_call" | custom-call | flops 478150656 | bytes 7868416 | tf_op jit(solution)/shard_map/pallas_call | solution.py:29
  13.9 0.0 collective-permute-done.4.other_ref
  13.9 1.3 %shard_map.91 = (f32[4,384,128]{2,1,0:T(8,128)S(1)}, f32[4,384,128]{2,1,0:T(8,128)S(1)}, f32[4,192,128]{2,1,0:T(8,128)S(1)}) custom-call(bf16[192,512]{1,0:T(8,128)(2,1)S(1)} %collective-permute-done.3.mine_ref, bf16[192,512]{1,0:T(8,128)(2,1)S(1)} %collective-permute-done.4.other_ref, bf16[3,1024,512]{2,1,0:T(8,128)(2,1)S(1)} %copy-done, ...), custom_call_target="tpu_custom_call" | custom-call | flops 478150656 | bytes 7868416 | tf_op jit(solution)/shard_map/pallas_call | solution.py:29
  15.2 2.4 %collective-permute-done.2.block_ref.mine_ref = bf16[192,512]{1,0:T(8,128)(2,1)S(1)} collective-permute-done((bf16[192,512]{1,0:T(8,128)(2,1)S(1)}, bf16[192,512]{1,0:T(8,128)(2,1)S(1)}, u32[]{:S(2)}, u32[]{:S(2)}) %collective-permute-start.2) | collective-permute-done | bytes 196640 | tf_op jit(solution)/shard_map/ppermute | solution.py:430
  17.6 0.0 collective-permute-start.9
  17.6 1.3 %collective-permute-done.7.mine_ref = bf16[192,512]{1,0:T(8,128)(2,1)S(1)} collective-permute-done((bf16[192,512]{1,0:T(8,128)(2,1)S(1)}, bf16[192,512]{1,0:T(8,128)(2,1)S(1)}, u32[]{:S(2)}, u32[]{:S(2)}) %collective-permute-start.7) | collective-permute-done | bytes 196640 | tf_op jit(solution)/shard_map/ppermute | solution.py:431
  18.9 0.0 collective-permute-start.8
  18.9 1.6 %collective-permute-start.6 = (bf16[192,512]{1,0:T(8,128)(2,1)S(1)}, bf16[192,512]{1,0:T(8,128)(2,1)S(1)}, u32[]{:S(2)}, u32[]{:S(2)}) collective-permute-start(bf16[192,512]{1,0:T(8,128)(2,1)S(1)} %collective-permute-done.2.block_ref.mine_ref), channel_id=1, source_target_pairs={{2,0},{0,4},{4,8},{8,12},{12,14},{14,10},{10,6},{6,2},{3,1},{1,5},... | collective-permute-start | bytes 589832 | tf_op jit(solution)/shard_map/ppermute | solution.py:430
  20.4 0.4 collective-permute-start.11
  20.9 0.0 collective-permute-done.9.other_ref
  20.9 1.3 %shard_map.93 = (f32[4,384,128]{2,1,0:T(8,128)S(1)}, f32[4,384,128]{2,1,0:T(8,128)S(1)}, f32[4,192,128]{2,1,0:T(8,128)S(1)}) custom-call(bf16[192,512]{1,0:T(8,128)(2,1)S(1)} %collective-permute-done.2.block_ref.mine_ref, bf16[192,512]{1,0:T(8,128)(2,1)S(1)} %collective-permute-done.9.other_ref, bf16[3,1024,512]{2,1,0:T(8,128)(2,1)S(1)} %copy-done, ...), custom_call_target="tpu_custom_call" | custom-call | flops 478150656 | bytes 7868416 | tf_op jit(solution)/shard_map/pallas_call | solution.py:29
  22.2 0.0 collective-permute-done.8.other_ref
  22.2 1.3 %shard_map.94 = (f32[4,384,128]{2,1,0:T(8,128)S(1)}, f32[4,384,128]{2,1,0:T(8,128)S(1)}, f32[4,192,128]{2,1,0:T(8,128)S(1)}) custom-call(bf16[192,512]{1,0:T(8,128)(2,1)S(1)} %collective-permute-done.7.mine_ref, bf16[192,512]{1,0:T(8,128)(2,1)S(1)} %collective-permute-done.8.other_ref, bf16[3,1024,512]{2,1,0:T(8,128)(2,1)S(1)} %copy-done, ...), custom_call_target="tpu_custom_call" | custom-call | flops 478150656 | bytes 7868416 | tf_op jit(solution)/shard_map/pallas_call | solution.py:29
  23.6 2.6 %collective-permute-done.6.block_ref.mine_ref = bf16[192,512]{1,0:T(8,128)(2,1)S(1)} collective-permute-done((bf16[192,512]{1,0:T(8,128)(2,1)S(1)}, bf16[192,512]{1,0:T(8,128)(2,1)S(1)}, u32[]{:S(2)}, u32[]{:S(2)}) %collective-permute-start.6) | collective-permute-done | bytes 196640 | tf_op jit(solution)/shard_map/ppermute | solution.py:430
  26.2 0.0 collective-permute-start.14
  26.2 1.3 %collective-permute-done.11.mine_ref = bf16[192,512]{1,0:T(8,128)(2,1)S(1)} collective-permute-done((bf16[192,512]{1,0:T(8,128)(2,1)S(1)}, bf16[192,512]{1,0:T(8,128)(2,1)S(1)}, u32[]{:S(2)}, u32[]{:S(2)}) %collective-permute-start.11) | collective-permute-done | bytes 196640 | tf_op jit(solution)/shard_map/ppermute | solution.py:431
  27.5 0.0 collective-permute-start.13
  27.5 0.5 %collective-permute-start.12 = (bf16[96,512]{1,0:T(8,128)(2,1)S(1)}, bf16[96,512]{1,0:T(8,128)(2,1)S(1)}, u32[]{:S(2)}, u32[]{:S(2)}) collective-permute-start(bf16[96,512]{1,0:T(8,128)(2,1)S(1)} %slice.7), channel_id=1, source_target_pairs={{0,2},{4,0},{8,4},{12,8},{14,12},{10,14},{6,10},{2,6},{1,3},{5,1},... | collective-permute-start | bytes 294920 | tf_op jit(solution)/shard_map/ppermute | solution.py:431
  28.0 1.6 %collective-permute-start.10 = (bf16[96,512]{1,0:T(8,128)(2,1)S(1)}, bf16[96,512]{1,0:T(8,128)(2,1)S(1)}, u32[]{:S(2)}, u32[]{:S(2)}) collective-permute-start(bf16[96,512]{1,0:T(8,128)(2,1)S(1)} %slice.6), channel_id=1, source_target_pairs={{2,0},{0,4},{4,8},{8,12},{12,14},{14,10},{10,6},{6,2},{3,1},{1,5},... | collective-permute-start | bytes 294920 | tf_op jit(solution)/shard_map/ppermute | solution.py:430
  29.6 0.0 collective-permute-done.14.other_ref
  29.6 1.3 %shard_map.96 = (f32[4,384,128]{2,1,0:T(8,128)S(1)}, f32[4,384,128]{2,1,0:T(8,128)S(1)}, f32[4,192,128]{2,1,0:T(8,128)S(1)}) custom-call(bf16[192,512]{1,0:T(8,128)(2,1)S(1)} %collective-permute-done.6.block_ref.mine_ref, bf16[192,512]{1,0:T(8,128)(2,1)S(1)} %collective-permute-done.14.other_ref, bf16[3,1024,512]{2,1,0:T(8,128)(2,1)S(1)} %copy-done, ...), custom_call_target="tpu_custom_call" | custom-call | flops 478150656 | bytes 7868416 | tf_op jit(solution)/shard_map/pallas_call | solution.py:29
  30.9 0.0 copy-start.3
  30.9 0.0 collective-permute-done.13.other_ref
  30.9 1.3 %shard_map.97 = (f32[4,384,128]{2,1,0:T(8,128)S(1)}, f32[4,384,128]{2,1,0:T(8,128)S(1)}, f32[4,192,128]{2,1,0:T(8,128)S(1)}) custom-call(bf16[192,512]{1,0:T(8,128)(2,1)S(1)} %collective-permute-done.11.mine_ref, bf16[192,512]{1,0:T(8,128)(2,1)S(1)} %collective-permute-done.13.other_ref, bf16[3,1024,512]{2,1,0:T(8,128)(2,1)S(1)} %copy-done, ...), custom_call_target="tpu_custom_call" | custom-call | flops 478150656 | bytes 7868416 | tf_op jit(solution)/shard_map/pallas_call | solution.py:29
  32.2 0.5 %collective-permute-done.12.mine_b = bf16[96,512]{1,0:T(8,128)(2,1)S(1)} collective-permute-done((bf16[96,512]{1,0:T(8,128)(2,1)S(1)}, bf16[96,512]{1,0:T(8,128)(2,1)S(1)}, u32[]{:S(2)}, u32[]{:S(2)}) %collective-permute-start.12) | collective-permute-done | bytes 98336 | tf_op jit(solution)/shard_map/ppermute | solution.py:431
  32.8 0.2 collective-permute-done.10.mine_a
  33.0 0.0 copy-start.2
  33.0 0.0 copy-start.4
  33.0 0.0 collective-permute-start.15
  33.0 0.5 %collective-permute-start.16 = (bf16[96,512]{1,0:T(8,128)(2,1)S(1)}, bf16[96,512]{1,0:T(8,128)(2,1)S(1)}, u32[]{:S(2)}, u32[]{:S(2)}) collective-permute-start(bf16[96,512]{1,0:T(8,128)(2,1)S(1)} %collective-permute-done.12.mine_b), channel_id=1, source_target_pairs={{0,1},{1,0},{2,3},{3,2},{4,5},{5,4},{6,7},{7,6},{8,9},{9,8},{10,11... | collective-permute-start | bytes 294920 | tf_op jit(solution)/shard_map/ppermute | solution.py:444
  33.5 0.8 %collective-permute-done.15.other_a = bf16[96,512]{1,0:T(8,128)(2,1)S(1)} collective-permute-done((bf16[96,512]{1,0:T(8,128)(2,1)S(1)}, bf16[96,512]{1,0:T(8,128)(2,1)S(1)}, u32[]{:S(2)}, u32[]{:S(2)}) %collective-permute-start.15) | collective-permute-done | bytes 98336 | tf_op jit(solution)/shard_map/ppermute | solution.py:444
  34.3 0.2 collective-permute-done.16.other_b
  34.5 0.0 copy-done.3
  34.5 1.7 %shard_map.98 = (bf16[2,64,1024]{2,1,0:T(8,128)(2,1)S(1)}, f32[2,64,1024]{2,1,0:T(8,128)S(1)}) custom-call(bf16[96,512]{1,0:T(8,128)(2,1)S(1)} %collective-permute-done.10.mine_a, bf16[96,512]{1,0:T(8,128)(2,1)S(1)} %collective-permute-done.12.mine_b, bf16[96,512]{1,0:T(8,128)(2,1)S(1)} %collective-permute-done.15.other_a, ...), custom_call_target="tpu_custom_call" | custom-call | flops 679477248 | bytes 8519680 | tf_op jit(solution)/shard_map/pallas_call | solution.py:29
  36.1 0.4 collective-permute-start.17
  36.5 1.2 %collective-permute-done.17.got_ref = bf16[2,64,1024]{2,1,0:T(8,128)(2,1)S(1)} collective-permute-done((bf16[2,64,1024]{2,1,0:T(8,128)(2,1)S(1)}, bf16[2,64,1024]{2,1,0:T(8,128)(2,1)S(1)}, u32[]{:S(2)}, u32[]{:S(2)}) %collective-permute-start.17) | collective-permute-done | bytes 262176 | tf_op jit(solution)/shard_map/ppermute | solution.py:458
  37.7 0.0 copy-done.2
  37.7 0.0 copy-done.4
  37.7 0.5 %shard_map.99 = (bf16[96,256]{1,0:T(8,128)(2,1)S(1)}, bf16[96,256]{1,0:T(8,128)(2,1)S(1)}) custom-call(f32[2,64,1024]{2,1,0:T(8,128)S(1)} %get-tuple-element.92.keep_ref, bf16[2,64,1024]{2,1,0:T(8,128)(2,1)S(1)} %collective-permute-done.17.got_ref, bf16[2,1024,256]{2,1,0:T(8,128)(2,1)S(1)} %copy-done.2, f32[2,2,256]{2,1,0:T(2,128)S(1)} %copy-done.4), custom_call_target="tpu_custom_call" | custom-call | flops 83886080 | bytes 1937408 | tf_op jit(solution)/shard_map/pallas_call | solution.py:29
  38.2 1.6 %collective-permute-start.18 = (bf16[96,256]{1,0:T(8,128)(2,1)S(1)}, bf16[96,256]{1,0:T(8,128)(2,1)S(1)}, u32[]{:S(2)}, u32[]{:S(2)}) collective-permute-start(bf16[96,256]{1,0:T(8,128)(2,1)S(1)} %get-tuple-element.94.near_ref), channel_id=1, source_target_pairs={{0,2},{2,0},{4,6},{6,4},{8,10},{10,8},{12,14},{14,12},{1,3},{3,1},... | collective-permute-start | bytes 147464 | tf_op jit(solution)/shard_map/ppermute | solution.py:474
  39.9 2.9 %collective-permute-start.19 = (bf16[96,256]{1,0:T(8,128)(2,1)S(1)}, bf16[96,256]{1,0:T(8,128)(2,1)S(1)}, u32[]{:S(2)}, u32[]{:S(2)}) collective-permute-start(bf16[96,256]{1,0:T(8,128)(2,1)S(1)} %get-tuple-element.95.far_ref), channel_id=1, source_target_pairs={{2,4},{6,8},{10,12},{4,2},{8,6},{12,10},{3,5},{7,9},{11,13},{5,3},... | collective-permute-start | bytes 147464 | tf_op jit(solution)/shard_map/ppermute | solution.py:473
  42.7 0.0 collective-permute-done.18.got_near_ref
  42.7 4.0 %collective-permute-done.19.got_far_ref = bf16[96,256]{1,0:T(8,128)(2,1)S(1)} collective-permute-done((bf16[96,256]{1,0:T(8,128)(2,1)S(1)}, bf16[96,256]{1,0:T(8,128)(2,1)S(1)}, u32[]{:S(2)}, u32[]{:S(2)}) %collective-permute-start.19) | collective-permute-done | bytes 49184 | tf_op jit(solution)/shard_map/ppermute | solution.py:473
  46.7 0.0 copy-done.1
  46.7 1.2 %shard_map.100 = (bf16[2,48,256]{2,1,0:T(8,128)(2,1)}, bf16[1,24,256]{2,1,0:T(8,128)(2,1)}) custom-call(bf16[96,256]{1,0:T(8,128)(2,1)S(1)} %get-tuple-element.94.near_ref, bf16[96,256]{1,0:T(8,128)(2,1)S(1)} %get-tuple-element.95.far_ref, bf16[96,256]{1,0:T(8,128)(2,1)S(1)} %collective-permute-done.18.got_near_ref, ...), custom_call_target="tpu_custom_call" | custom-call | flops 188743680 | bytes 2621440 | tf_op jit(solution)/shard_map/pallas_call | solution.py:29
  (7 shorter events, 0.0 us)
Async XLA Ops:
  0.6 2.0 %copy-start.5 = (f32[1024]{0:T(1024)S(1)}, f32[1024]{0:T(1024)}, u32[]{:S(2)}) copy-start(f32[1024]{0:T(1024)} %gain_ref.3) | copy-start | bytes 12292
  0.6 4.4 %copy-start = (bf16[3,1024,512]{2,1,0:T(8,128)(2,1)S(1)}, bf16[3,1024,512]{2,1,0:T(8,128)(2,1)}, u32[]{:S(2)}) copy-start(bf16[3,1024,512]{2,1,0:T(8,128)(2,1)} %weight_ref.16) | copy-start | bytes 9437188
  0.6 2.0 %collective-permute-start = (f32[192,512]{1,0:T(8,128)}, f32[192,512]{1,0:T(8,128)S(1)}, u32[]{:S(2)}, u32[]{:S(2)}) collective-permute-start(f32[192,512]{1,0:T(8,128)} %tokens_ref.1), channel_id=1, source_target_pairs={{0,1},{1,0},{2,3},{3,2},{4,5},{5,4},{6,7},{7,6},{8,9},{9,8},{10,11... | collective-permute-start | bytes 1179656 | tf_op jit(solution)/shard_map/ppermute | solution.py:390
  0.7 1.1 %copy-start.6 = (f32[192,512]{1,0:T(8,128)S(1)}, f32[192,512]{1,0:T(8,128)}, u32[]{:S(2)}) copy-start(f32[192,512]{1,0:T(8,128)} %tokens_ref.1) | copy-start | bytes 1179652
  3.0 7.0 %collective-permute-start.1 = (bf16[192,512]{1,0:T(8,128)(2,1)S(1)}, bf16[192,512]{1,0:T(8,128)(2,1)S(1)}, u32[]{:S(2)}, u32[]{:S(2)}) collective-permute-start(bf16[192,512]{1,0:T(8,128)(2,1)S(1)} %get-tuple-element.51.mine_ref), channel_id=1, source_target_pairs={{2,0},{0,4},{4,8},{8,12},{12,14},{14,10},{10,6},{6,2},{3,1},{1,5},... | collective-permute-start | bytes 589832 | tf_op jit(solution)/shard_map/ppermute | solution.py:413
  3.6 6.7 %collective-permute-start.3 = (bf16[192,512]{1,0:T(8,128)(2,1)S(1)}, bf16[192,512]{1,0:T(8,128)(2,1)S(1)}, u32[]{:S(2)}, u32[]{:S(2)}) collective-permute-start(bf16[192,512]{1,0:T(8,128)(2,1)S(1)} %get-tuple-element.51.mine_ref), channel_id=1, source_target_pairs={{0,2},{4,0},{8,4},{12,8},{14,12},{10,14},{6,10},{2,6},{1,3},{5,1},... | collective-permute-start | bytes 589832 | tf_op jit(solution)/shard_map/ppermute | solution.py:414
  10.0 2.5 %collective-permute-start.5 = (bf16[192,512]{1,0:T(8,128)(2,1)S(1)}, bf16[192,512]{1,0:T(8,128)(2,1)S(1)}, u32[]{:S(2)}, u32[]{:S(2)}) collective-permute-start(bf16[192,512]{1,0:T(8,128)(2,1)S(1)} %collective-permute-done.1.block_ref.mine_ref), channel_id=1, source_target_pairs={{0,1},{1,0},{2,3},{3,2},{4,5},{5,4},{6,7},{7,6},{8,9},{9,8},{10,11... | collective-permute-start | bytes 589832 | tf_op jit(solution)/shard_map/ppermute | solution.py:432
  10.2 3.6 %collective-permute-start.4 = (bf16[192,512]{1,0:T(8,128)(2,1)S(1)}, bf16[192,512]{1,0:T(8,128)(2,1)S(1)}, u32[]{:S(2)}, u32[]{:S(2)}) collective-permute-start(bf16[192,512]{1,0:T(8,128)(2,1)S(1)} %collective-permute-done.3.mine_ref), channel_id=1, source_target_pairs={{0,1},{1,0},{2,3},{3,2},{4,5},{5,4},{6,7},{7,6},{8,9},{9,8},{10,11... | collective-permute-start | bytes 589832 | tf_op jit(solution)/shard_map/ppermute | solution.py:432
  10.5 7.1 %collective-permute-start.2 = (bf16[192,512]{1,0:T(8,128)(2,1)S(1)}, bf16[192,512]{1,0:T(8,128)(2,1)S(1)}, u32[]{:S(2)}, u32[]{:S(2)}) collective-permute-start(bf16[192,512]{1,0:T(8,128)(2,1)S(1)} %collective-permute-done.1.block_ref.mine_ref), channel_id=1, source_target_pairs={{2,0},{0,4},{4,8},{8,12},{12,14},{14,10},{10,6},{6,2},{3,1},{1,5},... | collective-permute-start | bytes 589832 | tf_op jit(solution)/shard_map/ppermute | solution.py:430
  11.8 7.0 %collective-permute-start.7 = (bf16[192,512]{1,0:T(8,128)(2,1)S(1)}, bf16[192,512]{1,0:T(8,128)(2,1)S(1)}, u32[]{:S(2)}, u32[]{:S(2)}) collective-permute-start(bf16[192,512]{1,0:T(8,128)(2,1)S(1)} %collective-permute-done.3.mine_ref), channel_id=1, source_target_pairs={{0,2},{4,0},{8,4},{12,8},{14,12},{10,14},{6,10},{2,6},{1,3},{5,1},... | collective-permute-start | bytes 589832 | tf_op jit(solution)/shard_map/ppermute | solution.py:431
  17.6 3.3 %collective-permute-start.9 = (bf16[192,512]{1,0:T(8,128)(2,1)S(1)}, bf16[192,512]{1,0:T(8,128)(2,1)S(1)}, u32[]{:S(2)}, u32[]{:S(2)}) collective-permute-start(bf16[192,512]{1,0:T(8,128)(2,1)S(1)} %collective-permute-done.2.block_ref.mine_ref), channel_id=1, source_target_pairs={{0,1},{1,0},{2,3},{3,2},{4,5},{5,4},{6,7},{7,6},{8,9},{9,8},{10,11... | collective-permute-start | bytes 589832 | tf_op jit(solution)/shard_map/ppermute | solution.py:432
  18.9 3.4 %collective-permute-start.8 = (bf16[192,512]{1,0:T(8,128)(2,1)S(1)}, bf16[192,512]{1,0:T(8,128)(2,1)S(1)}, u32[]{:S(2)}, u32[]{:S(2)}) collective-permute-start(bf16[192,512]{1,0:T(8,128)(2,1)S(1)} %collective-permute-done.7.mine_ref), channel_id=1, source_target_pairs={{0,1},{1,0},{2,3},{3,2},{4,5},{5,4},{6,7},{7,6},{8,9},{9,8},{10,11... | collective-permute-start | bytes 589832 | tf_op jit(solution)/shard_map/ppermute | solution.py:432
  18.9 7.3 %collective-permute-start.6 = (bf16[192,512]{1,0:T(8,128)(2,1)S(1)}, bf16[192,512]{1,0:T(8,128)(2,1)S(1)}, u32[]{:S(2)}, u32[]{:S(2)}) collective-permute-start(bf16[192,512]{1,0:T(8,128)(2,1)S(1)} %collective-permute-done.2.block_ref.mine_ref), channel_id=1, source_target_pairs={{2,0},{0,4},{4,8},{8,12},{12,14},{14,10},{10,6},{6,2},{3,1},{1,5},... | collective-permute-start | bytes 589832 | tf_op jit(solution)/shard_map/ppermute | solution.py:430
  20.4 7.0 %collective-permute-start.11 = (bf16[192,512]{1,0:T(8,128)(2,1)S(1)}, bf16[192,512]{1,0:T(8,128)(2,1)S(1)}, u32[]{:S(2)}, u32[]{:S(2)}) collective-permute-start(bf16[192,512]{1,0:T(8,128)(2,1)S(1)} %collective-permute-done.7.mine_ref), channel_id=1, source_target_pairs={{0,2},{4,0},{8,4},{12,8},{14,12},{10,14},{6,10},{2,6},{1,3},{5,1},... | collective-permute-start | bytes 589832 | tf_op jit(solution)/shard_map/ppermute | solution.py:431
  26.2 3.4 %collective-permute-start.14 = (bf16[192,512]{1,0:T(8,128)(2,1)S(1)}, bf16[192,512]{1,0:T(8,128)(2,1)S(1)}, u32[]{:S(2)}, u32[]{:S(2)}) collective-permute-start(bf16[192,512]{1,0:T(8,128)(2,1)S(1)} %collective-permute-done.6.block_ref.mine_ref), channel_id=1, source_target_pairs={{0,1},{1,0},{2,3},{3,2},{4,5},{5,4},{6,7},{7,6},{8,9},{9,8},{10,11... | collective-permute-start | bytes 589832 | tf_op jit(solution)/shard_map/ppermute | solution.py:432
  27.5 3.5 %collective-permute-start.13 = (bf16[192,512]{1,0:T(8,128)(2,1)S(1)}, bf16[192,512]{1,0:T(8,128)(2,1)S(1)}, u32[]{:S(2)}, u32[]{:S(2)}) collective-permute-start(bf16[192,512]{1,0:T(8,128)(2,1)S(1)} %collective-permute-done.11.mine_ref), channel_id=1, source_target_pairs={{0,1},{1,0},{2,3},{3,2},{4,5},{5,4},{6,7},{7,6},{8,9},{9,8},{10,11... | collective-permute-start | bytes 589832 | tf_op jit(solution)/shard_map/ppermute | solution.py:432
  27.5 5.3 %collective-permute-start.12 = (bf16[96,512]{1,0:T(8,128)(2,1)S(1)}, bf16[96,512]{1,0:T(8,128)(2,1)S(1)}, u32[]{:S(2)}, u32[]{:S(2)}) collective-permute-start(bf16[96,512]{1,0:T(8,128)(2,1)S(1)} %slice.7), channel_id=1, source_target_pairs={{0,2},{4,0},{8,4},{12,8},{14,12},{10,14},{6,10},{2,6},{1,3},{5,1},... | collective-permute-start | bytes 294920 | tf_op jit(solution)/shard_map/ppermute | solution.py:431
  28.0 5.0 %collective-permute-start.10 = (bf16[96,512]{1,0:T(8,128)(2,1)S(1)}, bf16[96,512]{1,0:T(8,128)(2,1)S(1)}, u32[]{:S(2)}, u32[]{:S(2)}) collective-permute-start(bf16[96,512]{1,0:T(8,128)(2,1)S(1)} %slice.6), channel_id=1, source_target_pairs={{2,0},{0,4},{4,8},{8,12},{12,14},{14,10},{10,6},{6,2},{3,1},{1,5},... | collective-permute-start | bytes 294920 | tf_op jit(solution)/shard_map/ppermute | solution.py:430
  30.9 3.6 %copy-start.3 = (bf16[512,1024]{1,0:T(8,128)(2,1)S(1)}, bf16[512,1024]{1,0:T(8,128)(2,1)}, u32[]{:S(2)}) copy-start(bf16[512,1024]{1,0:T(8,128)(2,1)} %out_weight_ref.1) | copy-start | bytes 3145732
  33.0 4.7 %copy-start.2 = (bf16[2,1024,256]{2,1,0:T(8,128)(2,1)S(1)}, bf16[2,1024,256]{2,1,0:T(8,128)(2,1)}, u32[]{:S(2)}) copy-start(bf16[2,1024,256]{2,1,0:T(8,128)(2,1)} %lateral_ref.1) | copy-start | bytes 3145732
  33.0 4.7 %copy-start.4 = (f32[2,2,256]{2,1,0:T(2,128)S(1)}, f32[2,2,256]{2,1,0:T(2,128)}, u32[]{:S(2)}) copy-start(f32[2,2,256]{2,1,0:T(2,128)} %gain_ref.5) | copy-start | bytes 12292
  33.0 13.7 %copy-start.1 = (bf16[2,3,3,256,256]{4,3,2,1,0:T(8,128)(2,1)S(1)}, bf16[2,3,3,256,256]{4,3,2,1,0:T(8,128)(2,1)}, u32[]{:S(2)}) copy-start(bf16[2,3,3,256,256]{4,3,2,1,0:T(8,128)(2,1)} %weight_ref.17) | copy-start | bytes 7077892
  33.0 1.3 %collective-permute-start.15 = (bf16[96,512]{1,0:T(8,128)(2,1)S(1)}, bf16[96,512]{1,0:T(8,128)(2,1)S(1)}, u32[]{:S(2)}, u32[]{:S(2)}) collective-permute-start(bf16[96,512]{1,0:T(8,128)(2,1)S(1)} %collective-permute-done.10.mine_a), channel_id=1, source_target_pairs={{0,1},{1,0},{2,3},{3,2},{4,5},{5,4},{6,7},{7,6},{8,9},{9,8},{10,11... | collective-permute-start | bytes 294920 | tf_op jit(solution)/shard_map/ppermute | solution.py:444
  33.0 1.4 %collective-permute-start.16 = (bf16[96,512]{1,0:T(8,128)(2,1)S(1)}, bf16[96,512]{1,0:T(8,128)(2,1)S(1)}, u32[]{:S(2)}, u32[]{:S(2)}) collective-permute-start(bf16[96,512]{1,0:T(8,128)(2,1)S(1)} %collective-permute-done.12.mine_b), channel_id=1, source_target_pairs={{0,1},{1,0},{2,3},{3,2},{4,5},{5,4},{6,7},{7,6},{8,9},{9,8},{10,11... | collective-permute-start | bytes 294920 | tf_op jit(solution)/shard_map/ppermute | solution.py:444
  36.1 1.6 %collective-permute-start.17 = (bf16[2,64,1024]{2,1,0:T(8,128)(2,1)S(1)}, bf16[2,64,1024]{2,1,0:T(8,128)(2,1)S(1)}, u32[]{:S(2)}, u32[]{:S(2)}) collective-permute-start(bf16[2,64,1024]{2,1,0:T(8,128)(2,1)S(1)} %get-tuple-element.93), channel_id=1, source_target_pairs={{0,1},{1,0},{2,3},{3,2},{4,5},{5,4},{6,7},{7,6},{8,9},{9,8},{10,11... | collective-permute-start | bytes 786440 | tf_op jit(solution)/shard_map/ppermute | solution.py:458
  38.2 4.5 %collective-permute-start.18 = (bf16[96,256]{1,0:T(8,128)(2,1)S(1)}, bf16[96,256]{1,0:T(8,128)(2,1)S(1)}, u32[]{:S(2)}, u32[]{:S(2)}) collective-permute-start(bf16[96,256]{1,0:T(8,128)(2,1)S(1)} %get-tuple-element.94.near_ref), channel_id=1, source_target_pairs={{0,2},{2,0},{4,6},{6,4},{8,10},{10,8},{12,14},{14,12},{1,3},{3,1},... | collective-permute-start | bytes 147464 | tf_op jit(solution)/shard_map/ppermute | solution.py:474
  39.9 6.9 %collective-permute-start.19 = (bf16[96,256]{1,0:T(8,128)(2,1)S(1)}, bf16[96,256]{1,0:T(8,128)(2,1)S(1)}, u32[]{:S(2)}, u32[]{:S(2)}) collective-permute-start(bf16[96,256]{1,0:T(8,128)(2,1)S(1)} %get-tuple-element.95.far_ref), channel_id=1, source_target_pairs={{2,4},{6,8},{10,12},{4,2},{8,6},{12,10},{3,5},{7,9},{11,13},{5,3},... | collective-permute-start | bytes 147464 | tf_op jit(solution)/shard_map/ppermute | solution.py:473

commit v6 on v5

--- a/solution.py
+++ b/solution.py
@@ -181,53 +181,60 @@
         top_out[pair], total_out[pair], mixed_out[pair] = state
 
 
-def out_terms(attended, weight_ref, mine_ref, other_ref, send_ref, keep_ref, full_ref):
+def send_terms(att_ref, weight_ref, send_ref):
+    grid_rows, window = send_ref.shape[:2]
+    shift = (1 - lax.axis_index("head")) * (GRID_COLS - window)
+    cells = jnp.concatenate(
+        [
+            att_ref[pl.ds(pl.multiple_of(row * GRID_COLS + shift, 32), window), :]
+            for row in range(grid_rows)
+        ],
+        axis=0,
+    )
+    send_ref[...] = dot(cells, weight_ref[...]).astype(BF16).reshape(send_ref.shape)
+
+
+def keep_kernel(att_ref, weight_ref, mine_ref, other_ref, keep_ref, full_ref):
     core = lax.axis_index("head")
-    window = send_ref.shape[1]
+    grid_rows, window = keep_ref.shape[:2]
     half = mine_ref.shape[1]
-    shift = GRID_COLS - window
-    full_ref[...] = dot(attended, weight_ref[...])
-    for row in range(send_ref.shape[0]):
-        there = pl.ds(pl.multiple_of(row * GRID_COLS + (1 - core) * shift, 8), window)
-        send_ref[row] = full_ref[there, :].astype(BF16)
-        here = pl.ds(pl.multiple_of(row * GRID_COLS + core * shift, 8), window)
+    shift = core * (GRID_COLS - window)
+    places = [
+        pl.ds(pl.multiple_of(row * GRID_COLS + shift, 32), window) for row in range(grid_rows)
+    ]
+    cells = jnp.concatenate([att_ref[here, :] for here in places], axis=0)
+    full_ref[...] = dot(cells, weight_ref[...])
+    for row, here in enumerate(places):
+        there = slice(row * window, (row + 1) * window)
         for part, ref in ((core, mine_ref), (1 - core, other_ref)):
             cols = pl.ds(pl.multiple_of(part * half, half), half)
-            keep_ref[row, :, cols] = full_ref[here, cols] + ref[here, :]
+            keep_ref[row, :, cols] = full_ref[there, cols] + ref[here, :]
 
 
 def last_kernel(
-    mine_a,
-    mine_b,
-    other_a,
-    other_b,
+    mine_ref,
+    other_ref,
     weight_ref,
     query_ref,
     top_ref,
     total_ref,
     mixed_ref,
     out_weight_ref,
-    tokens_ref,
-    other_tokens_ref,
     send_ref,
-    keep_ref,
-    full_ref,
     att_ref,
 ):
     rows = mixed_ref.shape[1]
     low = low_lanes((rows, LANES))
     for pair, (_, total, mixed) in absorb_blocks(
-        (mine_a, mine_b), (other_a, other_b), weight_ref, query_ref, top_ref, total_ref, mixed_ref
+        (mine_ref,), (other_ref,), weight_ref, query_ref, top_ref, total_ref, mixed_ref
     ):
         cols = slice(pair * LANES, (pair + 1) * LANES)
         att_ref[:, cols] = (mixed / jnp.where(low, total[:rows], total[rows:])).astype(BF16)
-    out_terms(
-        att_ref[...], out_weight_ref, tokens_ref, other_tokens_ref, send_ref, keep_ref, full_ref
-    )
-
-
-def plain_out_kernel(att_ref, weight_ref, mine_ref, other_ref, send_ref, keep_ref, full_ref):
-    out_terms(att_ref[...], weight_ref, mine_ref, other_ref, send_ref, keep_ref, full_ref)
+    send_terms(att_ref, out_weight_ref, send_ref)
+
+
+def plain_out_kernel(att_ref, weight_ref, send_ref):
+    send_terms(att_ref, weight_ref, send_ref)
 
 
 def lateral_kernel(
@@ -254,54 +261,69 @@
     far_ref[window:] = coarse
 
 
-def conv_level(stacked_ref, weight_ref, level, rows, window, sum_ref):
-    block = rows * window
-    place = lax.broadcasted_iota(jnp.int32, (block, weight_ref.shape[-1]), 0) % window
-    taps = []
-    for tap_col in range(3):
-        total = None
-        for tap_row in range(3):
-            term = dot(
-                stacked_ref[tap_row * window : tap_row * window + block],
-                weight_ref[level, tap_row, tap_col],
-            )
-            total = term if total is None else total + term
-        taps.append(total)
-    left = jnp.where(place == 0, 0.0, pltpu.roll(taps[0], 1, axis=0))
-    right = jnp.where(place == window - 1, 0.0, pltpu.roll(taps[2], block - 1, axis=0))
-    sum_ref[...] = left + taps[1] + right
+def joined(terms, window):
+    left, middle, right = (terms(tap_col) for tap_col in range(3))
+    block = middle.shape[0]
+    place = lax.broadcasted_iota(jnp.int32, middle.shape, 0) % window
+    left = jnp.where(place == 0, 0.0, pltpu.roll(left, 1, axis=0))
+    right = jnp.where(place == window - 1, 0.0, pltpu.roll(right, block - 1, axis=0))
+    return left + middle + right
+
+
+def own_conv_kernel(near_ref, far_ref, weight_ref, fine_ref, coarse_ref, fine_in):
+    odd = lax.axis_index("blk") % 2
+    window = fine_ref.shape[0] // 2
+    for ref, place in ((near_ref, 1 - odd), (far_ref, odd)):
+        fine_in[pl.ds(pl.multiple_of(place * window, window), window), :] = ref[:window]
+    coarse = near_ref[window:]
+
+    def fine_terms(tap_col):
+        to_lower = dot(fine_in[:window], weight_ref[0, 0, tap_col])
+        to_upper = dot(fine_in[window:], weight_ref[0, 2, tap_col])
+        return dot(fine_in[...], weight_ref[0, 1, tap_col]) + jnp.concatenate(
+            [to_upper, to_lower], axis=0
+        )
+
+    fine_ref[...] = joined(fine_terms, window)
+    coarse_ref[...] = joined(lambda tap_col: dot(coarse, weight_ref[1, 1, tap_col]), window // 2)
 
 
 def conv_kernel(
-    near_ref,
-    far_ref,
     got_near_ref,
     got_far_ref,
+    own_fine_ref,
+    own_coarse_ref,
     weight_ref,
     gain_ref,
     fine_ref,
     coarse_ref,
-    fine_in,
-    coarse_in,
+    edge_in,
     fine_sum,
     coarse_sum,
 ):
     core = lax.axis_index("head")
     odd = lax.axis_index("blk") % 2
     window = fine_sum.shape[0] // 2
-    half = window // 2
-    for ref, place in (
-        (near_ref, 2 - odd),
-        (far_ref, 1 + odd),
-        (got_near_ref, 3 - 3 * odd),
-        (got_far_ref, 3 * odd),
-    ):
-        fine_in[pl.ds(pl.multiple_of(place * window, window), window), :] = ref[:window]
-    coarse_in[half : 2 * half] = near_ref[window:]
-    for ref, place in ((got_near_ref, 2 - 2 * odd), (got_far_ref, 2 * odd)):
-        coarse_in[pl.ds(pl.multiple_of(place * half, half), half), :] = ref[window:]
-    conv_level(fine_in, weight_ref, 0, 2, window, fine_sum)
-    conv_level(coarse_in, weight_ref, 1, 1, half, coarse_sum)
+    rows = got_near_ref.shape[0]
+    for ref, place in ((got_near_ref, 1 - odd), (got_far_ref, odd)):
+        edge_in[pl.ds(pl.multiple_of(place * rows, 32), rows), :] = ref[...]
+
+    def fine_terms(tap_col):
+        return jnp.concatenate(
+            [
+                dot(edge_in[:window], weight_ref[0, 0, tap_col]),
+                dot(edge_in[rows : rows + window], weight_ref[0, 2, tap_col]),
+            ],
+            axis=0,
+        )
+
+    def coarse_terms(tap_col):
+        return dot(edge_in[window:rows], weight_ref[1, 0, tap_col]) + dot(
+            edge_in[rows + window :], weight_ref[1, 2, tap_col]
+        )
+
+    fine_sum[...] = own_fine_ref[...] + joined(fine_terms, window)
+    coarse_sum[...] = own_coarse_ref[...] + joined(coarse_terms, window // 2)
     cols = fine_ref.shape[1]
     shift = GRID_COLS - window
     inset = cols - shift
@@ -390,13 +412,8 @@
     other = lax.ppermute(tokens, "head", swap)
     (tokens,) = call(intake_kernel, [(tokens.shape, F32)], (tokens,), flops=MIB * 1024)
     other, tokens = lax.optimization_barrier((other, tokens))
-    tail = (out_weight, tokens, other)
-    tail_outs = [
-        ((grid_rows, window, features), BF16),
-        ((grid_rows, window, features), F32),
-    ]
-    full = pltpu.VMEM((rows, features), F32)
-    out_flops = 2 * rows * width * features
+    term_out = ((grid_rows, window, features), BF16)
+    out_flops = 2 * grid_rows * window * width * features
     if blocks <= heads:
         order = list(range(0, blocks, 2)) + list(range(blocks - 1, 0, -2))
         forth = [(order[i - 1], order[i]) for i in range(blocks)]
@@ -439,23 +456,35 @@
                     exps=heads * rows * rows,
                 )
             state = list(state)
-        ahead, behind, state = lax.optimization_barrier((ahead, behind, state))
-        parts = (ahead, behind)
-        others = tuple(lax.ppermute(part, "head", swap) for part in parts)
-        peer_term, keep = call(
+        ahead, state[0] = lax.optimization_barrier((ahead, state[0]))
+        behind, state[0] = lax.optimization_barrier((behind, state[0]))
+        (mark,) = call(mark_kernel, [((16, LANES), BF16)], (ahead,))
+        others = (lax.ppermute(ahead, "head", swap), lax.ppermute(behind, "head", swap))
+        state = call(
+            step_kernel,
+            state_outs,
+            (ahead, others[0], qkv_weight, queries) + tuple(state) + (mark,),
+            flops=unit // 2,
+            exps=heads * rows * rows // 2,
+        )
+        peer_term, attended = call(
             last_kernel,
-            tail_outs,
-            parts + others + (qkv_weight, queries) + tuple(state) + tail,
-            [full, pltpu.VMEM((rows, width), BF16)],
-            flops=unit + out_flops,
-            exps=heads * rows * rows,
+            [term_out, ((rows, width), BF16)],
+            (behind, others[1], qkv_weight, queries) + tuple(state) + (out_weight,),
+            flops=unit // 2 + out_flops,
+            exps=heads * rows * rows // 2,
         )
     else:
-        attended = attention_shared(
-            tokens, other, norm_gain, qkv_weight, blocks // heads
-        )
-        peer_term, keep = call(plain_out_kernel, tail_outs, (attended,) + tail, [full], out_flops)
+        attended = attention_shared(tokens, other, norm_gain, qkv_weight, blocks // heads)
+        (peer_term,) = call(plain_out_kernel, [term_out], (attended, out_weight), flops=out_flops)
     peer_term = lax.ppermute(peer_term, "head", swap)
+    (keep,) = call(
+        keep_kernel,
+        [((grid_rows, window, features), F32)],
+        (attended, out_weight, tokens, other),
+        [pltpu.VMEM((grid_rows * window, features), F32)],
+        flops=out_flops,
+    )
 
     message = (window + window // 2, channels)
     near, far = call(
@@ -472,17 +501,21 @@
     far_pairs += [(j, i) for i, j in far_pairs]
     got_far = lax.ppermute(far, "blk", far_pairs)
     got_near = lax.ppermute(near, "blk", [(i, i ^ 1) for i in range(blocks)])
+    sums = [((2 * window, channels), F32), ((window // 2, channels), F32)]
+    own_sums = call(
+        own_conv_kernel,
+        sums,
+        (near, far, conv_weight),
+        [pltpu.VMEM((2 * window, channels), BF16)],
+        flops=27 * window * channels * channels,
+    )
     return call(
         conv_kernel,
         [((grid_rows, cols, channels), BF16), ((grid_rows // 2, cols // 2, channels), BF16)],
-        (near, far, got_near, got_far, conv_weight, level_gains),
-        [
-            pltpu.VMEM((4 * window, channels), BF16),
-            pltpu.VMEM((3 * window // 2, channels), BF16),
-            pltpu.VMEM((2 * window, channels), F32),
-            pltpu.VMEM((window // 2, channels), F32),
-        ],
-        flops=45 * window * channels * channels,
+        (got_near, got_far, *own_sums, conv_weight, level_gains),
+        [pltpu.VMEM((2 * message[0], channels), BF16)]
+        + [pltpu.VMEM(shape, dtype) for shape, dtype in sums],
+        flops=18 * window * channels * channels,
     )
 
 

time: 48.2 us -> 48.8 us (1.012)
  Pallas kernels: 13.1 us -> 14.5 us
  starting transfers between devices: 14 us -> 13.3 us
    pallas_call x15 -> x19, Pallas kernels: 13.1 us -> 14.5 us  [call(): pl.pallas_call(kernel, out_shape=outs, in_specs=specs(len(args)), out_spe...]
    ppermute x3, waiting for transfers between devices: 3.09 us -> 4.13 us  [body(): behind = lax.ppermute(behind, 'blk', back)]
    ppermute x2, waiting for transfers between devices: 0.94 us -> 0.2 us  [the longest x1 0.19 us: body(): lax.ppermute(behind, 'head', swap)]
    ppermute x2, starting transfers between devices: 0.5 us -> 0.01 us  [the longest x1 0.01 us: body(): lax.ppermute(behind, 'head', swap)]
  transfers between devices with their start and end apart: 20 -> 20, of which waited for: 13 -> 12; matrix products, arithmetic and copies ran while one was open for 0% -> 0% of each run, Pallas kernels for 19% -> 23%
where the time goes in v6:
time: 48.8 us; the launch traced here: 48.6 us
  waiting for transfers between devices  18.8 us (39%)
  Pallas kernels  14.5 us (30%)
  starting transfers between devices  13.3 us (27%)
  local copies, waits for them, and re-layouts  1.18 us (2%)
  between operations  0.85 us (2%)
    pallas_call x19, Pallas kernels, call(): pl.pallas_call(kernel, out_shape=outs, in_specs=specs(len(args)), out_spe...  14.5 us
    ppermute x3, waiting for transfers between devices, body(): ahead = lax.ppermute(ahead, 'blk', forth)  5.26 us
    ppermute x3, starting transfers between devices, body(): ahead = lax.ppermute(ahead, 'blk', forth)  4.53 us
    ppermute x3, waiting for transfers between devices, body(): behind = lax.ppermute(behind, 'blk', back)  4.13 us
    ppermute x1, waiting for transfers between devices, body(): got_far = lax.ppermute(far, 'blk', far_pairs)  3.94 us
    ppermute x1, waiting for transfers between devices, body(): ahead = lax.ppermute(mine, 'blk', forth)  3.51 us
    ppermute x1, starting transfers between devices, body(): got_far = lax.ppermute(far, 'blk', far_pairs)  2.52 us
    ppermute x3, starting transfers between devices, body(): behind = lax.ppermute(behind, 'blk', back)  1.84 us
  transfers between devices with their start and end apart: 20, of which 12 were waited for; matrix products, arithmetic and copies ran while one was open for 0% of the time, Pallas kernels for 23%

profile of v6, /device:TPU:6, one launch (start us, length us, event | category | flops | bytes accessed | tf_op | source)
XLA Modules:
  0.0 48.6 jit_solution(15948646884118006638)
XLA Ops:
  0.6 0.0 copy-start.5
  0.6 0.0 copy-start
  0.6 0.1 collective-permute-start
  0.7 0.0 copy-start.6
  0.7 1.1 %copy-done.6 = f32[192,512]{1,0:T(8,128)S(1)} copy-done((f32[192,512]{1,0:T(8,128)S(1)}, f32[192,512]{1,0:T(8,128)}, u32[]{:S(2)}) %copy-start.6) | copy-done | bytes 393240
  1.9 0.7 %collective-permute-done.other_ref = f32[192,512]{1,0:T(8,128)S(1)} collective-permute-done((f32[192,512]{1,0:T(8,128)}, f32[192,512]{1,0:T(8,128)S(1)}, u32[]{:S(2)}, u32[]{:S(2)}) %collective-permute-start) | collective-permute-done | bytes 393248 | tf_op jit(solution)/shard_map/ppermute | solution.py:412
  2.6 0.0 copy-done.5
  2.7 0.3 shard_map.87
  3.0 0.6 %collective-permute-start.2 = (bf16[192,512]{1,0:T(8,128)(2,1)S(1)}, bf16[192,512]{1,0:T(8,128)(2,1)S(1)}, u32[]{:S(2)}, u32[]{:S(2)}) collective-permute-start(bf16[192,512]{1,0:T(8,128)(2,1)S(1)} %get-tuple-element.55.mine_ref), channel_id=1, source_target_pairs={{2,0},{0,4},{4,8},{8,12},{12,14},{14,10},{10,6},{6,2},{3,1},{1,5},... | collective-permute-start | bytes 589832 | tf_op jit(solution)/shard_map/ppermute | solution.py:430
  3.6 1.5 %collective-permute-start.1 = (bf16[192,512]{1,0:T(8,128)(2,1)S(1)}, bf16[192,512]{1,0:T(8,128)(2,1)S(1)}, u32[]{:S(2)}, u32[]{:S(2)}) collective-permute-start(bf16[192,512]{1,0:T(8,128)(2,1)S(1)} %get-tuple-element.55.mine_ref), channel_id=1, source_target_pairs={{0,2},{4,0},{8,4},{12,8},{14,12},{10,14},{6,10},{2,6},{1,3},{5,1},... | collective-permute-start | bytes 589832 | tf_op jit(solution)/shard_map/ppermute | solution.py:431
  5.1 0.0 copy-done
  5.1 1.4 %shard_map.88 = (bf16[4,384,128]{2,1,0:T(8,128)(2,1)S(1)}, f32[4,384,128]{2,1,0:T(8,128)S(1)}, f32[4,384,128]{2,1,0:T(8,128)S(1)}, f32[4,192,128]{2,1,0:T(8,128)S(1)}) custom-call(bf16[192,512]{1,0:T(8,128)(2,1)S(1)} %get-tuple-element.55.mine_ref, bf16[192,512]{1,0:T(8,128)(2,1)S(1)} %get-tuple-element.56.other_ref, bf16[3,1024,512]{2,1,0:T(8,128)(2,1)S(1)} %copy-done), custom_call_target="tpu_custom_call" | custom-call | flops 679477248 | bytes 5898240 | tf_op jit(solution)/shard_map/pallas_call | solution.py:29
  6.5 3.5 %collective-permute-done.2.block_ref.mine_ref = bf16[192,512]{1,0:T(8,128)(2,1)S(1)} collective-permute-done((bf16[192,512]{1,0:T(8,128)(2,1)S(1)}, bf16[192,512]{1,0:T(8,128)(2,1)S(1)}, u32[]{:S(2)}, u32[]{:S(2)}) %collective-permute-start.2) | collective-permute-done | bytes 196640 | tf_op jit(solution)/shard_map/ppermute | solution.py:430
  10.0 0.0 collective-permute-start.6
  10.0 0.3 collective-permute-done.1.mine_ref
  10.2 0.3 collective-permute-start.5
  10.5 1.3 %collective-permute-start.4 = (bf16[192,512]{1,0:T(8,128)(2,1)S(1)}, bf16[192,512]{1,0:T(8,128)(2,1)S(1)}, u32[]{:S(2)}, u32[]{:S(2)}) collective-permute-start(bf16[192,512]{1,0:T(8,128)(2,1)S(1)} %collective-permute-done.2.block_ref.mine_ref), channel_id=1, source_target_pairs={{2,0},{0,4},{4,8},{8,12},{12,14},{14,10},{10,6},{6,2},{3,1},{1,5},... | collective-permute-start | bytes 589832 | tf_op jit(solution)/shard_map/ppermute | solution.py:447
  11.8 0.7 %collective-permute-start.3 = (bf16[192,512]{1,0:T(8,128)(2,1)S(1)}, bf16[192,512]{1,0:T(8,128)(2,1)S(1)}, u32[]{:S(2)}, u32[]{:S(2)}) collective-permute-start(bf16[192,512]{1,0:T(8,128)(2,1)S(1)} %collective-permute-done.1.mine_ref), channel_id=1, source_target_pairs={{0,2},{4,0},{8,4},{12,8},{14,12},{10,14},{6,10},{2,6},{1,3},{5,1},... | collective-permute-start | bytes 589832 | tf_op jit(solution)/shard_map/ppermute | solution.py:448
  12.5 0.0 collective-permute-done.6.other_ref
  12.5 1.3 %shard_map.90 = (f32[4,384,128]{2,1,0:T(8,128)S(1)}, f32[4,384,128]{2,1,0:T(8,128)S(1)}, f32[4,192,128]{2,1,0:T(8,128)S(1)}) custom-call(bf16[192,512]{1,0:T(8,128)(2,1)S(1)} %collective-permute-done.2.block_ref.mine_ref, bf16[192,512]{1,0:T(8,128)(2,1)S(1)} %collective-permute-done.6.other_ref, bf16[3,1024,512]{2,1,0:T(8,128)(2,1)S(1)} %copy-done, ...), custom_call_target="tpu_custom_call" | custom-call | flops 478150656 | bytes 7868416 | tf_op jit(solution)/shard_map/pallas_call | solution.py:29
  13.8 0.0 collective-permute-done.5.other_ref
  13.9 1.3 %shard_map.91 = (f32[4,384,128]{2,1,0:T(8,128)S(1)}, f32[4,384,128]{2,1,0:T(8,128)S(1)}, f32[4,192,128]{2,1,0:T(8,128)S(1)}) custom-call(bf16[192,512]{1,0:T(8,128)(2,1)S(1)} %collective-permute-done.1.mine_ref, bf16[192,512]{1,0:T(8,128)(2,1)S(1)} %collective-permute-done.5.other_ref, bf16[3,1024,512]{2,1,0:T(8,128)(2,1)S(1)} %copy-done, ...), custom_call_target="tpu_custom_call" | custom-call | flops 478150656 | bytes 7868416 | tf_op jit(solution)/shard_map/pallas_call | solution.py:29
  15.2 2.4 %collective-permute-done.4.block_ref.mine_ref = bf16[192,512]{1,0:T(8,128)(2,1)S(1)} collective-permute-done((bf16[192,512]{1,0:T(8,128)(2,1)S(1)}, bf16[192,512]{1,0:T(8,128)(2,1)S(1)}, u32[]{:S(2)}, u32[]{:S(2)}) %collective-permute-start.4) | collective-permute-done | bytes 196640 | tf_op jit(solution)/shard_map/ppermute | solution.py:447
  17.6 0.0 collective-permute-start.10
  17.6 1.3 %collective-permute-done.3.mine_ref = bf16[192,512]{1,0:T(8,128)(2,1)S(1)} collective-permute-done((bf16[192,512]{1,0:T(8,128)(2,1)S(1)}, bf16[192,512]{1,0:T(8,128)(2,1)S(1)}, u32[]{:S(2)}, u32[]{:S(2)}) %collective-permute-start.3) | collective-permute-done | bytes 196640 | tf_op jit(solution)/shard_map/ppermute | solution.py:448
  18.9 0.0 collective-permute-start.9
  18.9 1.6 %collective-permute-start.8 = (bf16[192,512]{1,0:T(8,128)(2,1)S(1)}, bf16[192,512]{1,0:T(8,128)(2,1)S(1)}, u32[]{:S(2)}, u32[]{:S(2)}) collective-permute-start(bf16[192,512]{1,0:T(8,128)(2,1)S(1)} %collective-permute-done.4.block_ref.mine_ref), channel_id=1, source_target_pairs={{2,0},{0,4},{4,8},{8,12},{12,14},{14,10},{10,6},{6,2},{3,1},{1,5},... | collective-permute-start | bytes 589832 | tf_op jit(solution)/shard_map/ppermute | solution.py:447
  20.4 0.4 collective-permute-start.7
  20.9 0.0 collective-permute-done.10.other_ref
  20.9 1.3 %shard_map.93 = (f32[4,384,128]{2,1,0:T(8,128)S(1)}, f32[4,384,128]{2,1,0:T(8,128)S(1)}, f32[4,192,128]{2,1,0:T(8,128)S(1)}) custom-call(bf16[192,512]{1,0:T(8,128)(2,1)S(1)} %collective-permute-done.4.block_ref.mine_ref, bf16[192,512]{1,0:T(8,128)(2,1)S(1)} %collective-permute-done.10.other_ref, bf16[3,1024,512]{2,1,0:T(8,128)(2,1)S(1)} %copy-done, ...), custom_call_target="tpu_custom_call" | custom-call | flops 478150656 | bytes 7868416 | tf_op jit(solution)/shard_map/pallas_call | solution.py:29
  22.2 0.0 collective-permute-done.9.other_ref
  22.2 1.3 %shard_map.94 = (f32[4,384,128]{2,1,0:T(8,128)S(1)}, f32[4,384,128]{2,1,0:T(8,128)S(1)}, f32[4,192,128]{2,1,0:T(8,128)S(1)}) custom-call(bf16[192,512]{1,0:T(8,128)(2,1)S(1)} %collective-permute-done.3.mine_ref, bf16[192,512]{1,0:T(8,128)(2,1)S(1)} %collective-permute-done.9.other_ref, bf16[3,1024,512]{2,1,0:T(8,128)(2,1)S(1)} %copy-done, ...), custom_call_target="tpu_custom_call" | custom-call | flops 478150656 | bytes 7868416 | tf_op jit(solution)/shard_map/pallas_call | solution.py:29
  23.5 2.6 %collective-permute-done.8.block_ref.mine_ref = bf16[192,512]{1,0:T(8,128)(2,1)S(1)} collective-permute-done((bf16[192,512]{1,0:T(8,128)(2,1)S(1)}, bf16[192,512]{1,0:T(8,128)(2,1)S(1)}, u32[]{:S(2)}, u32[]{:S(2)}) %collective-permute-start.8) | collective-permute-done | bytes 196640 | tf_op jit(solution)/shard_map/ppermute | solution.py:447
  26.2 0.0 collective-permute-start.14
  26.2 1.3 %collective-permute-done.7.mine_ref = bf16[192,512]{1,0:T(8,128)(2,1)S(1)} collective-permute-done((bf16[192,512]{1,0:T(8,128)(2,1)S(1)}, bf16[192,512]{1,0:T(8,128)(2,1)S(1)}, u32[]{:S(2)}, u32[]{:S(2)}) %collective-permute-start.7) | collective-permute-done | bytes 196640 | tf_op jit(solution)/shard_map/ppermute | solution.py:448
  27.5 0.0 collective-permute-start.13
  27.5 1.6 %collective-permute-start.12 = (bf16[96,512]{1,0:T(8,128)(2,1)S(1)}, bf16[96,512]{1,0:T(8,128)(2,1)S(1)}, u32[]{:S(2)}, u32[]{:S(2)}) collective-permute-start(bf16[96,512]{1,0:T(8,128)(2,1)S(1)} %slice.7), channel_id=1, source_target_pairs={{2,0},{0,4},{4,8},{8,12},{12,14},{14,10},{10,6},{6,2},{3,1},{1,5},... | collective-permute-start | bytes 294920 | tf_op jit(solution)/shard_map/ppermute | solution.py:447
  29.1 0.7 %collective-permute-start.11 = (bf16[96,512]{1,0:T(8,128)(2,1)S(1)}, bf16[96,512]{1,0:T(8,128)(2,1)S(1)}, u32[]{:S(2)}, u32[]{:S(2)}) collective-permute-start(bf16[96,512]{1,0:T(8,128)(2,1)S(1)} %slice.6), channel_id=1, source_target_pairs={{0,2},{4,0},{8,4},{12,8},{14,12},{10,14},{6,10},{2,6},{1,3},{5,1},... | collective-permute-start | bytes 294920 | tf_op jit(solution)/shard_map/ppermute | solution.py:448
  29.8 0.0 collective-permute-done.14.other_ref
  29.8 1.3 %shard_map.96 = (f32[4,384,128]{2,1,0:T(8,128)S(1)}, f32[4,384,128]{2,1,0:T(8,128)S(1)}, f32[4,192,128]{2,1,0:T(8,128)S(1)}) custom-call(bf16[192,512]{1,0:T(8,128)(2,1)S(1)} %collective-permute-done.8.block_ref.mine_ref, bf16[192,512]{1,0:T(8,128)(2,1)S(1)} %collective-permute-done.14.other_ref, bf16[3,1024,512]{2,1,0:T(8,128)(2,1)S(1)} %copy-done, ...), custom_call_target="tpu_custom_call" | custom-call | flops 478150656 | bytes 7868416 | tf_op jit(solution)/shard_map/pallas_call | solution.py:29
  31.1 0.0 collective-permute-done.13.other_ref
  31.1 1.3 %shard_map.97 = (f32[4,384,128]{2,1,0:T(8,128)S(1)}, f32[4,384,128]{2,1,0:T(8,128)S(1)}, f32[4,192,128]{2,1,0:T(8,128)S(1)}) custom-call(bf16[192,512]{1,0:T(8,128)(2,1)S(1)} %collective-permute-done.7.mine_ref, bf16[192,512]{1,0:T(8,128)(2,1)S(1)} %collective-permute-done.13.other_ref, bf16[3,1024,512]{2,1,0:T(8,128)(2,1)S(1)} %copy-done, ...), custom_call_target="tpu_custom_call" | custom-call | flops 478150656 | bytes 7868416 | tf_op jit(solution)/shard_map/pallas_call | solution.py:29
  32.5 0.0 copy-start.2
  32.5 0.3 collective-permute-done.12.block_ref.mine_ref
  32.7 0.0 collective-permute-start.16
  32.7 1.5 %collective-permute-done.11.mine_ref = bf16[96,512]{1,0:T(8,128)(2,1)S(1)} collective-permute-done((bf16[96,512]{1,0:T(8,128)(2,1)S(1)}, bf16[96,512]{1,0:T(8,128)(2,1)S(1)}, u32[]{:S(2)}, u32[]{:S(2)}) %collective-permute-start.11) | collective-permute-done | bytes 98336 | tf_op jit(solution)/shard_map/ppermute | solution.py:448
  34.3 0.0 collective-permute-start.15
  34.3 0.0 collective-permute-done.16.other_ref
  34.3 1.1 %shard_map.99 = (f32[4,384,128]{2,1,0:T(8,128)S(1)}, f32[4,384,128]{2,1,0:T(8,128)S(1)}, f32[4,192,128]{2,1,0:T(8,128)S(1)}) custom-call(bf16[96,512]{1,0:T(8,128)(2,1)S(1)} %collective-permute-done.12.block_ref.mine_ref, bf16[96,512]{1,0:T(8,128)(2,1)S(1)} %collective-permute-done.16.other_ref, bf16[3,1024,512]{2,1,0:T(8,128)(2,1)S(1)} %copy-done, ...), custom_call_target="tpu_custom_call" | custom-call | flops 239075328 | bytes 7671808 | tf_op jit(solution)/shard_map/pallas_call | solution.py:29
  35.4 0.2 collective-permute-done.15.other_ref
  35.6 0.0 copy-done.2
  35.6 1.3 %shard_map.100 = (bf16[2,64,1024]{2,1,0:T(8,128)(2,1)S(1)}, bf16[192,512]{1,0:T(8,128)(2,1)S(1)}) custom-call(bf16[96,512]{1,0:T(8,128)(2,1)S(1)} %collective-permute-done.11.mine_ref, bf16[96,512]{1,0:T(8,128)(2,1)S(1)} %collective-permute-done.15.other_ref, bf16[3,1024,512]{2,1,0:T(8,128)(2,1)S(1)} %copy-done, ...), custom_call_target="tpu_custom_call" | custom-call | flops 373293056 | bytes 7208960 | tf_op jit(solution)/shard_map/pallas_call | solution.py:29
  36.9 0.0 copy-start.1
  37.0 0.4 collective-permute-start.17
  37.4 0.4 shard_map.101.keep_ref
  37.8 0.8 %collective-permute-done.17.got_ref = bf16[2,64,1024]{2,1,0:T(8,128)(2,1)S(1)} collective-permute-done((bf16[2,64,1024]{2,1,0:T(8,128)(2,1)S(1)}, bf16[2,64,1024]{2,1,0:T(8,128)(2,1)S(1)}, u32[]{:S(2)}, u32[]{:S(2)}) %collective-permute-start.17) | collective-permute-done | bytes 262176 | tf_op jit(solution)/shard_map/ppermute | solution.py:480
  38.6 0.0 copy-done.3
  38.6 0.5 %shard_map.102 = (bf16[96,256]{1,0:T(8,128)(2,1)S(1)}, bf16[96,256]{1,0:T(8,128)(2,1)S(1)}) custom-call(f32[2,64,1024]{2,1,0:T(8,128)S(1)} %shard_map.101.keep_ref, bf16[2,64,1024]{2,1,0:T(8,128)(2,1)S(1)} %collective-permute-done.17.got_ref, bf16[2,1024,256]{2,1,0:T(8,128)(2,1)S(1)} %copy-done.3, f32[2,2,256]{2,1,0:T(2,128)S(1)} %copy-done.4), custom_call_target="tpu_custom_call" | custom-call | flops 83886080 | bytes 1937408 | tf_op jit(solution)/shard_map/pallas_call | solution.py:29
  39.1 1.6 %collective-permute-start.18 = (bf16[96,256]{1,0:T(8,128)(2,1)S(1)}, bf16[96,256]{1,0:T(8,128)(2,1)S(1)}, u32[]{:S(2)}, u32[]{:S(2)}) collective-permute-start(bf16[96,256]{1,0:T(8,128)(2,1)S(1)} %get-tuple-element.100.near_ref), channel_id=1, source_target_pairs={{0,2},{2,0},{4,6},{6,4},{8,10},{10,8},{12,14},{14,12},{1,3},{3,1},... | collective-permute-start | bytes 147464 | tf_op jit(solution)/shard_map/ppermute | solution.py:503
  40.6 2.5 %collective-permute-start.19 = (bf16[96,256]{1,0:T(8,128)(2,1)S(1)}, bf16[96,256]{1,0:T(8,128)(2,1)S(1)}, u32[]{:S(2)}, u32[]{:S(2)}) collective-permute-start(bf16[96,256]{1,0:T(8,128)(2,1)S(1)} %get-tuple-element.101.far_ref), channel_id=1, source_target_pairs={{2,4},{6,8},{10,12},{4,2},{8,6},{12,10},{3,5},{7,9},{11,13},{5,3},... | collective-permute-start | bytes 147464 | tf_op jit(solution)/shard_map/ppermute | solution.py:502
  43.1 0.4 shard_map.103
  43.5 0.0 collective-permute-done.18.got_near_ref
  43.5 3.9 %collective-permute-done.19.got_far_ref = bf16[96,256]{1,0:T(8,128)(2,1)S(1)} collective-permute-done((bf16[96,256]{1,0:T(8,128)(2,1)S(1)}, bf16[96,256]{1,0:T(8,128)(2,1)S(1)}, u32[]{:S(2)}, u32[]{:S(2)}) %collective-permute-start.19) | collective-permute-done | bytes 49184 | tf_op jit(solution)/shard_map/ppermute | solution.py:502
  47.5 1.2 %shard_map.104 = (bf16[2,48,256]{2,1,0:T(8,128)(2,1)}, bf16[1,24,256]{2,1,0:T(8,128)(2,1)}) custom-call(bf16[96,256]{1,0:T(8,128)(2,1)S(1)} %collective-permute-done.18.got_near_ref, bf16[96,256]{1,0:T(8,128)(2,1)S(1)} %collective-permute-done.19.got_far_ref, f32[128,256]{1,0:T(8,128)S(1)} %get-tuple-element.102.own_fine_ref, ...), custom_call_target="tpu_custom_call" | custom-call | flops 75497472 | bytes 2686976 | tf_op jit(solution)/shard_map/pallas_call | solution.py:29
  (11 shorter events, 0.1 us)
Async XLA Ops:
  0.6 2.0 %copy-start.5 = (f32[1024]{0:T(1024)S(1)}, f32[1024]{0:T(1024)}, u32[]{:S(2)}) copy-start(f32[1024]{0:T(1024)} %gain_ref.3) | copy-start | bytes 12292
  0.6 4.4 %copy-start = (bf16[3,1024,512]{2,1,0:T(8,128)(2,1)S(1)}, bf16[3,1024,512]{2,1,0:T(8,128)(2,1)}, u32[]{:S(2)}) copy-start(bf16[3,1024,512]{2,1,0:T(8,128)(2,1)} %weight_ref.20) | copy-start | bytes 9437188
  0.6 2.0 %collective-permute-start = (f32[192,512]{1,0:T(8,128)}, f32[192,512]{1,0:T(8,128)S(1)}, u32[]{:S(2)}, u32[]{:S(2)}) collective-permute-start(f32[192,512]{1,0:T(8,128)} %tokens_ref.1), channel_id=1, source_target_pairs={{0,1},{1,0},{2,3},{3,2},{4,5},{5,4},{6,7},{7,6},{8,9},{9,8},{10,11... | collective-permute-start | bytes 1179656 | tf_op jit(solution)/shard_map/ppermute | solution.py:412
  0.7 1.1 %copy-start.6 = (f32[192,512]{1,0:T(8,128)S(1)}, f32[192,512]{1,0:T(8,128)}, u32[]{:S(2)}) copy-start(f32[192,512]{1,0:T(8,128)} %tokens_ref.1) | copy-start | bytes 1179652
  3.0 7.0 %collective-permute-start.2 = (bf16[192,512]{1,0:T(8,128)(2,1)S(1)}, bf16[192,512]{1,0:T(8,128)(2,1)S(1)}, u32[]{:S(2)}, u32[]{:S(2)}) collective-permute-start(bf16[192,512]{1,0:T(8,128)(2,1)S(1)} %get-tuple-element.55.mine_ref), channel_id=1, source_target_pairs={{2,0},{0,4},{4,8},{8,12},{12,14},{14,10},{10,6},{6,2},{3,1},{1,5},... | collective-permute-start | bytes 589832 | tf_op jit(solution)/shard_map/ppermute | solution.py:430
  3.6 6.7 %collective-permute-start.1 = (bf16[192,512]{1,0:T(8,128)(2,1)S(1)}, bf16[192,512]{1,0:T(8,128)(2,1)S(1)}, u32[]{:S(2)}, u32[]{:S(2)}) collective-permute-start(bf16[192,512]{1,0:T(8,128)(2,1)S(1)} %get-tuple-element.55.mine_ref), channel_id=1, source_target_pairs={{0,2},{4,0},{8,4},{12,8},{14,12},{10,14},{6,10},{2,6},{1,3},{5,1},... | collective-permute-start | bytes 589832 | tf_op jit(solution)/shard_map/ppermute | solution.py:431
  10.0 2.5 %collective-permute-start.6 = (bf16[192,512]{1,0:T(8,128)(2,1)S(1)}, bf16[192,512]{1,0:T(8,128)(2,1)S(1)}, u32[]{:S(2)}, u32[]{:S(2)}) collective-permute-start(bf16[192,512]{1,0:T(8,128)(2,1)S(1)} %collective-permute-done.2.block_ref.mine_ref), channel_id=1, source_target_pairs={{0,1},{1,0},{2,3},{3,2},{4,5},{5,4},{6,7},{7,6},{8,9},{9,8},{10,11... | collective-permute-start | bytes 589832 | tf_op jit(solution)/shard_map/ppermute | solution.py:449
  10.2 3.6 %collective-permute-start.5 = (bf16[192,512]{1,0:T(8,128)(2,1)S(1)}, bf16[192,512]{1,0:T(8,128)(2,1)S(1)}, u32[]{:S(2)}, u32[]{:S(2)}) collective-permute-start(bf16[192,512]{1,0:T(8,128)(2,1)S(1)} %collective-permute-done.1.mine_ref), channel_id=1, source_target_pairs={{0,1},{1,0},{2,3},{3,2},{4,5},{5,4},{6,7},{7,6},{8,9},{9,8},{10,11... | collective-permute-start | bytes 589832 | tf_op jit(solution)/shard_map/ppermute | solution.py:449
  10.5 7.1 %collective-permute-start.4 = (bf16[192,512]{1,0:T(8,128)(2,1)S(1)}, bf16[192,512]{1,0:T(8,128)(2,1)S(1)}, u32[]{:S(2)}, u32[]{:S(2)}) collective-permute-start(bf16[192,512]{1,0:T(8,128)(2,1)S(1)} %collective-permute-done.2.block_ref.mine_ref), channel_id=1, source_target_pairs={{2,0},{0,4},{4,8},{8,12},{12,14},{14,10},{10,6},{6,2},{3,1},{1,5},... | collective-permute-start | bytes 589832 | tf_op jit(solution)/shard_map/ppermute | solution.py:447
  11.8 7.0 %collective-permute-start.3 = (bf16[192,512]{1,0:T(8,128)(2,1)S(1)}, bf16[192,512]{1,0:T(8,128)(2,1)S(1)}, u32[]{:S(2)}, u32[]{:S(2)}) collective-permute-start(bf16[192,512]{1,0:T(8,128)(2,1)S(1)} %collective-permute-done.1.mine_ref), channel_id=1, source_target_pairs={{0,2},{4,0},{8,4},{12,8},{14,12},{10,14},{6,10},{2,6},{1,3},{5,1},... | collective-permute-start | bytes 589832 | tf_op jit(solution)/shard_map/ppermute | solution.py:448
  17.6 3.3 %collective-permute-start.10 = (bf16[192,512]{1,0:T(8,128)(2,1)S(1)}, bf16[192,512]{1,0:T(8,128)(2,1)S(1)}, u32[]{:S(2)}, u32[]{:S(2)}) collective-permute-start(bf16[192,512]{1,0:T(8,128)(2,1)S(1)} %collective-permute-done.4.block_ref.mine_ref), channel_id=1, source_target_pairs={{0,1},{1,0},{2,3},{3,2},{4,5},{5,4},{6,7},{7,6},{8,9},{9,8},{10,11... | collective-permute-start | bytes 589832 | tf_op jit(solution)/shard_map/ppermute | solution.py:449
  18.9 3.4 %collective-permute-start.9 = (bf16[192,512]{1,0:T(8,128)(2,1)S(1)}, bf16[192,512]{1,0:T(8,128)(2,1)S(1)}, u32[]{:S(2)}, u32[]{:S(2)}) collective-permute-start(bf16[192,512]{1,0:T(8,128)(2,1)S(1)} %collective-permute-done.3.mine_ref), channel_id=1, source_target_pairs={{0,1},{1,0},{2,3},{3,2},{4,5},{5,4},{6,7},{7,6},{8,9},{9,8},{10,11... | collective-permute-start | bytes 589832 | tf_op jit(solution)/shard_map/ppermute | solution.py:449
  18.9 7.3 %collective-permute-start.8 = (bf16[192,512]{1,0:T(8,128)(2,1)S(1)}, bf16[192,512]{1,0:T(8,128)(2,1)S(1)}, u32[]{:S(2)}, u32[]{:S(2)}) collective-permute-start(bf16[192,512]{1,0:T(8,128)(2,1)S(1)} %collective-permute-done.4.block_ref.mine_ref), channel_id=1, source_target_pairs={{2,0},{0,4},{4,8},{8,12},{12,14},{14,10},{10,6},{6,2},{3,1},{1,5},... | collective-permute-start | bytes 589832 | tf_op jit(solution)/shard_map/ppermute | solution.py:447
  20.4 7.0 %collective-permute-start.7 = (bf16[192,512]{1,0:T(8,128)(2,1)S(1)}, bf16[192,512]{1,0:T(8,128)(2,1)S(1)}, u32[]{:S(2)}, u32[]{:S(2)}) collective-permute-start(bf16[192,512]{1,0:T(8,128)(2,1)S(1)} %collective-permute-done.3.mine_ref), channel_id=1, source_target_pairs={{0,2},{4,0},{8,4},{12,8},{14,12},{10,14},{6,10},{2,6},{1,3},{5,1},... | collective-permute-start | bytes 589832 | tf_op jit(solution)/shard_map/ppermute | solution.py:448
  26.2 3.6 %collective-permute-start.14 = (bf16[192,512]{1,0:T(8,128)(2,1)S(1)}, bf16[192,512]{1,0:T(8,128)(2,1)S(1)}, u32[]{:S(2)}, u32[]{:S(2)}) collective-permute-start(bf16[192,512]{1,0:T(8,128)(2,1)S(1)} %collective-permute-done.8.block_ref.mine_ref), channel_id=1, source_target_pairs={{0,1},{1,0},{2,3},{3,2},{4,5},{5,4},{6,7},{7,6},{8,9},{9,8},{10,11... | collective-permute-start | bytes 589832 | tf_op jit(solution)/shard_map/ppermute | solution.py:449
  27.5 3.7 %collective-permute-start.13 = (bf16[192,512]{1,0:T(8,128)(2,1)S(1)}, bf16[192,512]{1,0:T(8,128)(2,1)S(1)}, u32[]{:S(2)}, u32[]{:S(2)}) collective-permute-start(bf16[192,512]{1,0:T(8,128)(2,1)S(1)} %collective-permute-done.7.mine_ref), channel_id=1, source_target_pairs={{0,1},{1,0},{2,3},{3,2},{4,5},{5,4},{6,7},{7,6},{8,9},{9,8},{10,11... | collective-permute-start | bytes 589832 | tf_op jit(solution)/shard_map/ppermute | solution.py:449
  27.5 5.3 %collective-permute-start.12 = (bf16[96,512]{1,0:T(8,128)(2,1)S(1)}, bf16[96,512]{1,0:T(8,128)(2,1)S(1)}, u32[]{:S(2)}, u32[]{:S(2)}) collective-permute-start(bf16[96,512]{1,0:T(8,128)(2,1)S(1)} %slice.7), channel_id=1, source_target_pairs={{2,0},{0,4},{4,8},{8,12},{12,14},{14,10},{10,6},{6,2},{3,1},{1,5},... | collective-permute-start | bytes 294920 | tf_op jit(solution)/shard_map/ppermute | solution.py:447
  29.1 5.2 %collective-permute-start.11 = (bf16[96,512]{1,0:T(8,128)(2,1)S(1)}, bf16[96,512]{1,0:T(8,128)(2,1)S(1)}, u32[]{:S(2)}, u32[]{:S(2)}) collective-permute-start(bf16[96,512]{1,0:T(8,128)(2,1)S(1)} %slice.6), channel_id=1, source_target_pairs={{0,2},{4,0},{8,4},{12,8},{14,12},{10,14},{6,10},{2,6},{1,3},{5,1},... | collective-permute-start | bytes 294920 | tf_op jit(solution)/shard_map/ppermute | solution.py:448
  32.5 3.1 %copy-start.2 = (bf16[512,1024]{1,0:T(8,128)(2,1)S(1)}, bf16[512,1024]{1,0:T(8,128)(2,1)}, u32[]{:S(2)}) copy-start(bf16[512,1024]{1,0:T(8,128)(2,1)} %weight_ref.21) | copy-start | bytes 3145732
  32.7 1.6 %collective-permute-start.16 = (bf16[96,512]{1,0:T(8,128)(2,1)S(1)}, bf16[96,512]{1,0:T(8,128)(2,1)S(1)}, u32[]{:S(2)}, u32[]{:S(2)}) collective-permute-start(bf16[96,512]{1,0:T(8,128)(2,1)S(1)} %collective-permute-done.12.block_ref.mine_ref), channel_id=1, source_target_pairs={{0,1},{1,0},{2,3},{3,2},{4,5},{5,4},{6,7},{7,6},{8,9},{9,8},{10,11... | collective-permute-start | bytes 294920 | tf_op jit(solution)/shard_map/ppermute | solution.py:462
  34.3 1.3 %collective-permute-start.15 = (bf16[96,512]{1,0:T(8,128)(2,1)S(1)}, bf16[96,512]{1,0:T(8,128)(2,1)S(1)}, u32[]{:S(2)}, u32[]{:S(2)}) collective-permute-start(bf16[96,512]{1,0:T(8,128)(2,1)S(1)} %collective-permute-done.11.mine_ref), channel_id=1, source_target_pairs={{0,1},{1,0},{2,3},{3,2},{4,5},{5,4},{6,7},{7,6},{8,9},{9,8},{10,11... | collective-permute-start | bytes 294920 | tf_op jit(solution)/shard_map/ppermute | solution.py:462
  35.6 3.0 %copy-start.3 = (bf16[2,1024,256]{2,1,0:T(8,128)(2,1)S(1)}, bf16[2,1024,256]{2,1,0:T(8,128)(2,1)}, u32[]{:S(2)}) copy-start(bf16[2,1024,256]{2,1,0:T(8,128)(2,1)} %lateral_ref.1) | copy-start | bytes 3145732
  35.6 3.0 %copy-start.4 = (f32[2,2,256]{2,1,0:T(2,128)S(1)}, f32[2,2,256]{2,1,0:T(2,128)}, u32[]{:S(2)}) copy-start(f32[2,2,256]{2,1,0:T(2,128)} %gain_ref.5) | copy-start | bytes 12292
  36.9 6.2 %copy-start.1 = (bf16[2,3,3,256,256]{4,3,2,1,0:T(8,128)(2,1)S(1)}, bf16[2,3,3,256,256]{4,3,2,1,0:T(8,128)(2,1)}, u32[]{:S(2)}) copy-start(bf16[2,3,3,256,256]{4,3,2,1,0:T(8,128)(2,1)} %weight_ref.23) | copy-start | bytes 7077892
  37.0 1.6 %collective-permute-start.17 = (bf16[2,64,1024]{2,1,0:T(8,128)(2,1)S(1)}, bf16[2,64,1024]{2,1,0:T(8,128)(2,1)S(1)}, u32[]{:S(2)}, u32[]{:S(2)}) collective-permute-start(bf16[2,64,1024]{2,1,0:T(8,128)(2,1)S(1)} %get-tuple-element.99), channel_id=1, source_target_pairs={{0,1},{1,0},{2,3},{3,2},{4,5},{5,4},{6,7},{7,6},{8,9},{9,8},{10,11... | collective-permute-start | bytes 786440 | tf_op jit(solution)/shard_map/ppermute | solution.py:480
  39.1 4.5 %collective-permute-start.18 = (bf16[96,256]{1,0:T(8,128)(2,1)S(1)}, bf16[96,256]{1,0:T(8,128)(2,1)S(1)}, u32[]{:S(2)}, u32[]{:S(2)}) collective-permute-start(bf16[96,256]{1,0:T(8,128)(2,1)S(1)} %get-tuple-element.100.near_ref), channel_id=1, source_target_pairs={{0,2},{2,0},{4,6},{6,4},{8,10},{10,8},{12,14},{14,12},{1,3},{3,1},... | collective-permute-start | bytes 147464 | tf_op jit(solution)/shard_map/ppermute | solution.py:503
  40.6 6.9 %collective-permute-start.19 = (bf16[96,256]{1,0:T(8,128)(2,1)S(1)}, bf16[96,256]{1,0:T(8,128)(2,1)S(1)}, u32[]{:S(2)}, u32[]{:S(2)}) collective-permute-start(bf16[96,256]{1,0:T(8,128)(2,1)S(1)} %get-tuple-element.101.far_ref), channel_id=1, source_target_pairs={{2,4},{6,8},{10,12},{4,2},{8,6},{12,10},{3,5},{7,9},{11,13},{5,3},... | collective-permute-start | bytes 147464 | tf_op jit(solution)/shard_map/ppermute | solution.py:502

commit v7 on v6

--- a/solution.py
+++ b/solution.py
@@ -1,3 +1,4 @@
+import functools
 import math
 
 import jax
@@ -148,11 +149,11 @@
         )
 
 
-def absorb_blocks(mine_refs, other_refs, weight_ref, query_ref, top_ref, total_ref, mixed_ref):
-    mine = jnp.concatenate([ref[...] for ref in mine_refs], axis=0)
-    other = jnp.concatenate([ref[...] for ref in other_refs], axis=0)
-    keys = project(mine, other, weight_ref, 1)
-    values = project(mine, other, weight_ref, 2)
+def stacked(refs):
+    return jnp.concatenate([ref[...] for ref in refs], axis=0) if len(refs) > 1 else refs[0][...]
+
+
+def absorb_keys(keys, values, query_ref, top_ref, total_ref, mixed_ref):
     for pair in range(query_ref.shape[0]):
         old = top_ref[pair], total_ref[pair], mixed_ref[pair]
         yield pair, absorb(pair, query_ref[pair], keys, values, old)
@@ -162,23 +163,24 @@
     mark_ref[...] = block_ref[: mark_ref.shape[0], : mark_ref.shape[1]]
 
 
-def step_kernel(
-    mine_ref,
-    other_ref,
-    weight_ref,
-    query_ref,
-    top_ref,
-    total_ref,
-    mixed_ref,
-    mark_ref,
-    top_out,
-    total_out,
-    mixed_out,
-):
-    for pair, state in absorb_blocks(
-        (mine_ref,), (other_ref,), weight_ref, query_ref, top_ref, total_ref, mixed_ref
-    ):
-        top_out[pair], total_out[pair], mixed_out[pair] = state
+def step_kernel(pieces, *refs):
+    mine_refs, other_refs = refs[:pieces], refs[pieces : 2 * pieces]
+    weight_ref, *state_refs = refs[2 * pieces : 2 * pieces + 5]
+    out_refs = refs[-3:]
+    mine, other = stacked(mine_refs), stacked(other_refs)
+    keys = project(mine, other, weight_ref, 1)
+    values = project(mine, other, weight_ref, 2)
+    for pair, state in absorb_keys(keys, values, *state_refs):
+        for ref, value in zip(out_refs, state):
+            ref[pair] = value
+
+
+def half_kernel(mine_a, mine_b, weight_ref, mark_ref, keys_ref, values_ref):
+    mine = stacked((mine_a, mine_b))
+    half = mine.shape[1]
+    here = pl.ds(pl.multiple_of(lax.axis_index("head") * half, half), half)
+    keys_ref[...] = dot(mine, weight_ref[1, here, :])
+    values_ref[...] = dot(mine, weight_ref[2, here, :])
 
 
 def send_terms(att_ref, weight_ref, send_ref):
@@ -212,8 +214,10 @@
 
 
 def last_kernel(
-    mine_ref,
-    other_ref,
+    other_a,
+    other_b,
+    keys_ref,
+    values_ref,
     weight_ref,
     query_ref,
     top_ref,
@@ -225,8 +229,13 @@
 ):
     rows = mixed_ref.shape[1]
     low = low_lanes((rows, LANES))
-    for pair, (_, total, mixed) in absorb_blocks(
-        (mine_ref,), (other_ref,), weight_ref, query_ref, top_ref, total_ref, mixed_ref
+    other = stacked((other_a, other_b))
+    half = other.shape[1]
+    there = pl.ds(pl.multiple_of((1 - lax.axis_index("head")) * half, half), half)
+    keys = (keys_ref[...] + dot(other, weight_ref[1, there, :])).astype(BF16)
+    values = (values_ref[...] + dot(other, weight_ref[2, there, :])).astype(BF16)
+    for pair, (_, total, mixed) in absorb_keys(
+        keys, values, query_ref, top_ref, total_ref, mixed_ref
     ):
         cols = slice(pair * LANES, (pair + 1) * LANES)
         att_ref[:, cols] = (mixed / jnp.where(low, total[:rows], total[rows:])).astype(BF16)
@@ -414,7 +423,7 @@
     other, tokens = lax.optimization_barrier((other, tokens))
     term_out = ((grid_rows, window, features), BF16)
     out_flops = 2 * grid_rows * window * width * features
-    if blocks <= heads:
+    if 6 <= blocks <= heads:
         order = list(range(0, blocks, 2)) + list(range(blocks - 1, 0, -2))
         forth = [(order[i - 1], order[i]) for i in range(blocks)]
         back = [(target, source) for source, target in forth]
@@ -437,42 +446,55 @@
             flops=unit + 2 * rows * width * features,
             exps=heads * rows * rows,
         )
-        for step in range(1, blocks // 2):
-            ahead, state[0] = lax.optimization_barrier((ahead, state[0]))
-            behind, state[0] = lax.optimization_barrier((behind, state[0]))
-            parts = (ahead, behind)
-            (mark,) = call(mark_kernel, [((16, LANES), BF16)], (ahead,))
-            if step == blocks // 2 - 1:
-                ahead, behind = ahead[: rows // 2], behind[rows // 2 :]
-            ahead = lax.ppermute(ahead, "blk", forth)
-            behind = lax.ppermute(behind, "blk", back)
-            others = (lax.ppermute(parts[0], "head", swap), lax.ppermute(parts[1], "head", swap))
-            for block in zip(parts, others):
+        last = blocks // 2
+        ahead, behind = (ahead,), (behind,)
+        for step in range(1, last + 1):
+            first, state[0] = lax.optimization_barrier((ahead[0], state[0]))
+            ahead = (first,) + ahead[1:]
+            first, state[0] = lax.optimization_barrier((behind[0], state[0]))
+            behind = (first,) + behind[1:]
+            arrived = ahead, behind
+            (mark,) = call(mark_kernel, [((16, LANES), BF16)], (ahead[0],))
+            if step == last - 1:
+                ahead, behind = ahead[:1], behind[:1]
+            elif step == last - 2:
+                (whole_a,), (whole_b,) = ahead, behind
+                ahead = whole_a[: rows // 2], whole_a[rows // 2 :]
+                behind = whole_b[rows // 2 :], whole_b[: rows // 2]
+            if step < last:
+                ahead, behind = (
+                    tuple(lax.ppermute(piece, "blk", pairs_of) for piece in pieces)
+                    for pieces, pairs_of in ((ahead, forth), (behind, back))
+                )
+            traded = tuple(
+                tuple(lax.ppermute(piece, "head", swap) for piece in pieces)
+                for pieces in arrived
+            )
+            if step == last:
+                break
+            for mine, across_core in zip(arrived, traded):
                 state = call(
-                    step_kernel,
+                    functools.partial(step_kernel, len(mine)),
                     state_outs,
-                    block + (qkv_weight, queries) + tuple(state) + (mark,),
+                    mine + across_core + (qkv_weight, queries) + tuple(state) + (mark,),
                     flops=unit,
                     exps=heads * rows * rows,
                 )
             state = list(state)
-        ahead, state[0] = lax.optimization_barrier((ahead, state[0]))
-        behind, state[0] = lax.optimization_barrier((behind, state[0]))
-        (mark,) = call(mark_kernel, [((16, LANES), BF16)], (ahead,))
-        others = (lax.ppermute(ahead, "head", swap), lax.ppermute(behind, "head", swap))
-        state = call(
-            step_kernel,
-            state_outs,
-            (ahead, others[0], qkv_weight, queries) + tuple(state) + (mark,),
-            flops=unit // 2,
-            exps=heads * rows * rows // 2,
+        keys, values = call(
+            half_kernel,
+            [((rows, width), F32)] * 2,
+            (*arrived[0], *arrived[1], qkv_weight, mark),
+            flops=2 * rows * width * features,
         )
         peer_term, attended = call(
             last_kernel,
             [term_out, ((rows, width), BF16)],
-            (behind, others[1], qkv_weight, queries) + tuple(state) + (out_weight,),
-            flops=unit // 2 + out_flops,
-            exps=heads * rows * rows // 2,
+            (*traded[0], *traded[1], keys, values, qkv_weight, queries)
+            + tuple(state)
+            + (out_weight,),
+            flops=unit + out_flops,
+            exps=heads * rows * rows,
         )
     else:
         attended = attention_shared(tokens, other, norm_gain, qkv_weight, blocks // heads)

time: 48.8 us -> 52.3 us (1.072)
  starting transfers between devices: 13.3 us -> 17.1 us
  Pallas kernels: 14.5 us -> 13.8 us
    ppermute x14 -> x18, starting transfers between devices: 6.64 us -> 10 us  [the longest x8 8.16 us: body(): lax.ppermute(piece, 'blk', pairs_of)]
    ppermute x14 -> x18, waiting for transfers between devices: 9.6 us -> 10.3 us  [the longest x8 9.69 us: body(): lax.ppermute(piece, 'blk', pairs_of)]
    pallas_call x19, Pallas kernels: 14.5 us -> 13.8 us  [call(): pl.pallas_call(kernel, out_shape=outs, in_specs=specs(len(args)), out_spe...]
  transfers between devices with their start and end apart: 20 -> 24, of which waited for: 12 -> 12; matrix products, arithmetic and copies ran while one was open for 0% -> 0% of each run, Pallas kernels for 23% -> 20%
where the time goes in v7:
time: 52.3 us; the launch traced here: 52.1 us
  waiting for transfers between devices  19.2 us (37%)
  starting transfers between devices  17.1 us (33%)
  Pallas kernels  13.8 us (26%)
  local copies, waits for them, and re-layouts  1.19 us (2%)
  between operations  0.87 us (2%)
    pallas_call x19, Pallas kernels, call(): pl.pallas_call(kernel, out_shape=outs, in_specs=specs(len(args)), out_spe...  13.8 us
    ppermute x8, waiting for transfers between devices, body(): lax.ppermute(piece, 'blk', pairs_of)  9.69 us
    ppermute x8, starting transfers between devices, body(): lax.ppermute(piece, 'blk', pairs_of)  8.16 us
    ppermute x1, waiting for transfers between devices, body(): got_far = lax.ppermute(far, 'blk', far_pairs)  3.61 us
    ppermute x1, waiting for transfers between devices, body(): ahead = lax.ppermute(mine, 'blk', forth)  3.5 us
    ppermute x1, starting transfers between devices, body(): got_far = lax.ppermute(far, 'blk', far_pairs)  2.85 us
    ppermute x10, starting transfers between devices, body(): lax.ppermute(piece, 'head', swap)  1.85 us
    ppermute x1, starting transfers between devices, body(): got_near = lax.ppermute(near, 'blk', [(i, i ^ 1) for i in range(blocks)])  1.64 us
  transfers between devices with their start and end apart: 24, of which 12 were waited for; matrix products, arithmetic and copies ran while one was open for 0% of the time, Pallas kernels for 20%

profile of v7, /device:TPU:6, one launch (start us, length us, event | category | flops | bytes accessed | tf_op | source)
XLA Modules:
  0.0 52.1 jit_solution(5322409827365025255)
XLA Ops:
  0.6 0.1 collective-permute-start
  0.7 1.1 %copy-done.6 = f32[192,512]{1,0:T(8,128)S(1)} copy-done((f32[192,512]{1,0:T(8,128)S(1)}, f32[192,512]{1,0:T(8,128)}, u32[]{:S(2)}) %copy-start.6) | copy-done | bytes 393240
  1.9 0.7 %collective-permute-done.other_ref = f32[192,512]{1,0:T(8,128)S(1)} collective-permute-done((f32[192,512]{1,0:T(8,128)}, f32[192,512]{1,0:T(8,128)S(1)}, u32[]{:S(2)}, u32[]{:S(2)}) %collective-permute-start) | collective-permute-done | bytes 393248 | tf_op jit(solution)/shard_map/ppermute | solution.py:421
  2.7 0.3 shard_map.87
  3.0 0.6 %collective-permute-start.1 = (bf16[192,512]{1,0:T(8,128)(2,1)S(1)}, bf16[192,512]{1,0:T(8,128)(2,1)S(1)}, u32[]{:S(2)}, u32[]{:S(2)}) collective-permute-start(bf16[192,512]{1,0:T(8,128)(2,1)S(1)} %get-tuple-element.54.mine_ref), channel_id=1, source_target_pairs={{2,0},{0,4},{4,8},{8,12},{12,14},{14,10},{10,6},{6,2},{3,1},{1,5},... | collective-permute-start | bytes 589832 | tf_op jit(solution)/shard_map/ppermute | solution.py:439
  3.6 1.5 %collective-permute-start.3 = (bf16[192,512]{1,0:T(8,128)(2,1)S(1)}, bf16[192,512]{1,0:T(8,128)(2,1)S(1)}, u32[]{:S(2)}, u32[]{:S(2)}) collective-permute-start(bf16[192,512]{1,0:T(8,128)(2,1)S(1)} %get-tuple-element.54.mine_ref), channel_id=1, source_target_pairs={{0,2},{4,0},{8,4},{12,8},{14,12},{10,14},{6,10},{2,6},{1,3},{5,1},... | collective-permute-start | bytes 589832 | tf_op jit(solution)/shard_map/ppermute | solution.py:440
  5.1 1.4 %shard_map.88 = (bf16[4,384,128]{2,1,0:T(8,128)(2,1)S(1)}, f32[4,384,128]{2,1,0:T(8,128)S(1)}, f32[4,384,128]{2,1,0:T(8,128)S(1)}, f32[4,192,128]{2,1,0:T(8,128)S(1)}) custom-call(bf16[192,512]{1,0:T(8,128)(2,1)S(1)} %get-tuple-element.54.mine_ref, bf16[192,512]{1,0:T(8,128)(2,1)S(1)} %get-tuple-element.55.other_ref, bf16[3,1024,512]{2,1,0:T(8,128)(2,1)S(1)} %copy-done), custom_call_target="tpu_custom_call" | custom-call | flops 679477248 | bytes 5898240 | tf_op jit(solution)/shard_map/pallas_call | solution.py:30
  6.5 3.5 %collective-permute-done.1.block_ref.refs_0_ = bf16[192,512]{1,0:T(8,128)(2,1)S(1)} collective-permute-done((bf16[192,512]{1,0:T(8,128)(2,1)S(1)}, bf16[192,512]{1,0:T(8,128)(2,1)S(1)}, u32[]{:S(2)}, u32[]{:S(2)}) %collective-permute-start.1) | collective-permute-done | bytes 196640 | tf_op jit(solution)/shard_map/ppermute | solution.py:439
  10.0 0.0 collective-permute-start.5
  10.0 0.3 collective-permute-done.3.refs_0_
  10.2 0.3 collective-permute-start.4
  10.5 1.3 %collective-permute-start.2 = (bf16[192,512]{1,0:T(8,128)(2,1)S(1)}, bf16[192,512]{1,0:T(8,128)(2,1)S(1)}, u32[]{:S(2)}, u32[]{:S(2)}) collective-permute-start(bf16[192,512]{1,0:T(8,128)(2,1)S(1)} %collective-permute-done.1.block_ref.refs_0_), channel_id=1, source_target_pairs={{2,0},{0,4},{4,8},{8,12},{12,14},{14,10},{10,6},{6,2},{3,1},{1,5},... | collective-permute-start | bytes 589832 | tf_op jit(solution)/shard_map/ppermute | solution.py:466
  11.8 0.7 %collective-permute-start.7 = (bf16[192,512]{1,0:T(8,128)(2,1)S(1)}, bf16[192,512]{1,0:T(8,128)(2,1)S(1)}, u32[]{:S(2)}, u32[]{:S(2)}) collective-permute-start(bf16[192,512]{1,0:T(8,128)(2,1)S(1)} %collective-permute-done.3.refs_0_), channel_id=1, source_target_pairs={{0,2},{4,0},{8,4},{12,8},{14,12},{10,14},{6,10},{2,6},{1,3},{5,1},... | collective-permute-start | bytes 589832 | tf_op jit(solution)/shard_map/ppermute | solution.py:466
  12.5 0.0 collective-permute-done.5.refs_1_
  12.5 1.3 %shard_map.90 = (f32[4,384,128]{2,1,0:T(8,128)S(1)}, f32[4,384,128]{2,1,0:T(8,128)S(1)}, f32[4,192,128]{2,1,0:T(8,128)S(1)}) custom-call(bf16[192,512]{1,0:T(8,128)(2,1)S(1)} %collective-permute-done.1.block_ref.refs_0_, bf16[192,512]{1,0:T(8,128)(2,1)S(1)} %collective-permute-done.5.refs_1_, bf16[3,1024,512]{2,1,0:T(8,128)(2,1)S(1)} %copy-done, ...), custom_call_target="tpu_custom_call" | custom-call | flops 478150656 | bytes 7868416 | tf_op jit(solution)/shard_map/pallas_call | solution.py:30
  13.9 0.0 collective-permute-done.4.refs_1_
  13.9 1.3 %shard_map.91 = (f32[4,384,128]{2,1,0:T(8,128)S(1)}, f32[4,384,128]{2,1,0:T(8,128)S(1)}, f32[4,192,128]{2,1,0:T(8,128)S(1)}) custom-call(bf16[192,512]{1,0:T(8,128)(2,1)S(1)} %collective-permute-done.3.refs_0_, bf16[192,512]{1,0:T(8,128)(2,1)S(1)} %collective-permute-done.4.refs_1_, bf16[3,1024,512]{2,1,0:T(8,128)(2,1)S(1)} %copy-done, ...), custom_call_target="tpu_custom_call" | custom-call | flops 478150656 | bytes 7868416 | tf_op jit(solution)/shard_map/pallas_call | solution.py:30
  15.2 2.4 %collective-permute-done.2.block_ref.refs_0_ = bf16[192,512]{1,0:T(8,128)(2,1)S(1)} collective-permute-done((bf16[192,512]{1,0:T(8,128)(2,1)S(1)}, bf16[192,512]{1,0:T(8,128)(2,1)S(1)}, u32[]{:S(2)}, u32[]{:S(2)}) %collective-permute-start.2) | collective-permute-done | bytes 196640 | tf_op jit(solution)/shard_map/ppermute | solution.py:466
  17.6 0.0 collective-permute-start.9
  17.6 1.3 %collective-permute-done.7.refs_0_ = bf16[192,512]{1,0:T(8,128)(2,1)S(1)} collective-permute-done((bf16[192,512]{1,0:T(8,128)(2,1)S(1)}, bf16[192,512]{1,0:T(8,128)(2,1)S(1)}, u32[]{:S(2)}, u32[]{:S(2)}) %collective-permute-start.7) | collective-permute-done | bytes 196640 | tf_op jit(solution)/shard_map/ppermute | solution.py:466
  18.9 0.0 collective-permute-start.8
  18.9 1.6 %collective-permute-start.6 = (bf16[96,512]{1,0:T(8,128)(2,1)S(1)}, bf16[96,512]{1,0:T(8,128)(2,1)S(1)}, u32[]{:S(2)}, u32[]{:S(2)}) collective-permute-start(bf16[96,512]{1,0:T(8,128)(2,1)S(1)} %get-tuple-element.103), channel_id=1, source_target_pairs={{2,0},{0,4},{4,8},{8,12},{12,14},{14,10},{10,6},{6,2},{3,1},{1,5},... | collective-permute-start | bytes 294920 | tf_op jit(solution)/shard_map/ppermute | solution.py:466
  20.4 1.6 %collective-permute-start.15 = (bf16[96,512]{1,0:T(8,128)(2,1)S(1)}, bf16[96,512]{1,0:T(8,128)(2,1)S(1)}, u32[]{:S(2)}, u32[]{:S(2)}) collective-permute-start(bf16[96,512]{1,0:T(8,128)(2,1)S(1)} %get-tuple-element.102), channel_id=1, source_target_pairs={{2,0},{0,4},{4,8},{8,12},{12,14},{14,10},{10,6},{6,2},{3,1},{1,5},... | collective-permute-start | bytes 294920 | tf_op jit(solution)/shard_map/ppermute | solution.py:466
  22.0 0.5 collective-permute-start.11
  22.5 3.6 %collective-permute-done.15.refs_1_ = bf16[96,512]{1,0:T(8,128)(2,1)S(1)} collective-permute-done((bf16[96,512]{1,0:T(8,128)(2,1)S(1)}, bf16[96,512]{1,0:T(8,128)(2,1)S(1)}, u32[]{:S(2)}, u32[]{:S(2)}) %collective-permute-start.15) | collective-permute-done | bytes 98336 | tf_op jit(solution)/shard_map/ppermute | solution.py:466
  26.2 0.4 collective-permute-start.12
  26.6 0.0 collective-permute-done.9.refs_1_
  26.6 0.0 collective-permute-start.17
  26.6 1.3 %shard_map.93 = (f32[4,384,128]{2,1,0:T(8,128)S(1)}, f32[4,384,128]{2,1,0:T(8,128)S(1)}, f32[4,192,128]{2,1,0:T(8,128)S(1)}) custom-call(bf16[192,512]{1,0:T(8,128)(2,1)S(1)} %collective-permute-done.2.block_ref.refs_0_, bf16[192,512]{1,0:T(8,128)(2,1)S(1)} %collective-permute-done.9.refs_1_, bf16[3,1024,512]{2,1,0:T(8,128)(2,1)S(1)} %copy-done, ...), custom_call_target="tpu_custom_call" | custom-call | flops 478150656 | bytes 7868416 | tf_op jit(solution)/shard_map/pallas_call | solution.py:30
  28.0 0.0 collective-permute-done.8.refs_1_
  28.0 1.3 %shard_map.94 = (f32[4,384,128]{2,1,0:T(8,128)S(1)}, f32[4,384,128]{2,1,0:T(8,128)S(1)}, f32[4,192,128]{2,1,0:T(8,128)S(1)}) custom-call(bf16[192,512]{1,0:T(8,128)(2,1)S(1)} %collective-permute-done.7.refs_0_, bf16[192,512]{1,0:T(8,128)(2,1)S(1)} %collective-permute-done.8.refs_1_, bf16[3,1024,512]{2,1,0:T(8,128)(2,1)S(1)} %copy-done, ...), custom_call_target="tpu_custom_call" | custom-call | flops 478150656 | bytes 7868416 | tf_op jit(solution)/shard_map/pallas_call | solution.py:30
  29.3 0.0 collective-permute-done.6.block_ref.refs_0_
  29.3 0.6 %collective-permute-start.16 = (bf16[96,512]{1,0:T(8,128)(2,1)S(1)}, bf16[96,512]{1,0:T(8,128)(2,1)S(1)}, u32[]{:S(2)}, u32[]{:S(2)}) collective-permute-start(bf16[96,512]{1,0:T(8,128)(2,1)S(1)} %collective-permute-done.6.block_ref.refs_0_), channel_id=1, source_target_pairs={{0,1},{1,0},{2,3},{3,2},{4,5},{5,4},{6,7},{7,6},{8,9},{9,8},{10,11... | collective-permute-start | bytes 294920 | tf_op jit(solution)/shard_map/ppermute | solution.py:470
  29.9 0.9 %collective-permute-done.12.refs_1_ = bf16[96,512]{1,0:T(8,128)(2,1)S(1)} collective-permute-done((bf16[96,512]{1,0:T(8,128)(2,1)S(1)}, bf16[96,512]{1,0:T(8,128)(2,1)S(1)}, u32[]{:S(2)}, u32[]{:S(2)}) %collective-permute-start.12) | collective-permute-done | bytes 98336 | tf_op jit(solution)/shard_map/ppermute | solution.py:466
  30.8 0.0 collective-permute-start.14
  30.8 0.0 collective-permute-done.11.refs_0_
  30.8 0.5 collective-permute-start.13
  31.3 1.6 %collective-permute-start.10 = (bf16[96,512]{1,0:T(8,128)(2,1)S(1)}, bf16[96,512]{1,0:T(8,128)(2,1)S(1)}, u32[]{:S(2)}, u32[]{:S(2)}) collective-permute-start(bf16[96,512]{1,0:T(8,128)(2,1)S(1)} %collective-permute-done.6.block_ref.refs_0_), channel_id=1, source_target_pairs={{2,0},{0,4},{4,8},{8,12},{12,14},{14,10},{10,6},{6,2},{3,1},{1,5},... | collective-permute-start | bytes 294920 | tf_op jit(solution)/shard_map/ppermute | solution.py:466
  32.9 0.0 collective-permute-done.17.refs_3_
  32.9 0.5 collective-permute-start.19
  33.3 0.0 collective-permute-done.16.refs_2_
  33.3 1.3 %shard_map.96 = (f32[4,384,128]{2,1,0:T(8,128)S(1)}, f32[4,384,128]{2,1,0:T(8,128)S(1)}, f32[4,192,128]{2,1,0:T(8,128)S(1)}) custom-call(bf16[96,512]{1,0:T(8,128)(2,1)S(1)} %collective-permute-done.6.block_ref.refs_0_, bf16[96,512]{1,0:T(8,128)(2,1)S(1)} %collective-permute-done.15.refs_1_, bf16[96,512]{1,0:T(8,128)(2,1)S(1)} %collective-permute-done.16.refs_2_, ...), custom_call_target="tpu_custom_call" | custom-call | flops 478150656 | bytes 7868416 | tf_op jit(solution)/shard_map/pallas_call | solution.py:30
  34.7 0.0 collective-permute-done.14.refs_3_
  34.7 0.0 collective-permute-done.13.refs_2_
  34.7 1.3 %shard_map.97 = (f32[4,384,128]{2,1,0:T(8,128)S(1)}, f32[4,384,128]{2,1,0:T(8,128)S(1)}, f32[4,192,128]{2,1,0:T(8,128)S(1)}) custom-call(bf16[96,512]{1,0:T(8,128)(2,1)S(1)} %collective-permute-done.11.refs_0_, bf16[96,512]{1,0:T(8,128)(2,1)S(1)} %collective-permute-done.12.refs_1_, bf16[96,512]{1,0:T(8,128)(2,1)S(1)} %collective-permute-done.13.refs_2_, ...), custom_call_target="tpu_custom_call" | custom-call | flops 478150656 | bytes 7868416 | tf_op jit(solution)/shard_map/pallas_call | solution.py:30
  36.0 0.0 copy-start.2
  36.0 0.0 collective-permute-done.10.block_ref.mine_a
  36.0 1.5 %collective-permute-done.19.mine_b = bf16[96,512]{1,0:T(8,128)(2,1)S(1)} collective-permute-done((bf16[96,512]{1,0:T(8,128)(2,1)S(1)}, bf16[96,512]{1,0:T(8,128)(2,1)S(1)}, u32[]{:S(2)}, u32[]{:S(2)}) %collective-permute-start.19) | collective-permute-done | bytes 98336 | tf_op jit(solution)/shard_map/ppermute | solution.py:466
  37.5 0.5 collective-permute-start.18
  38.0 0.4 shard_map.99
  38.4 0.4 collective-permute-done.20.other_b
  38.8 0.2 collective-permute-done.18.other_a
  39.0 1.4 %shard_map.100 = (bf16[2,64,1024]{2,1,0:T(8,128)(2,1)S(1)}, bf16[192,512]{1,0:T(8,128)(2,1)S(1)}) custom-call(bf16[96,512]{1,0:T(8,128)(2,1)S(1)} %collective-permute-done.18.other_a, bf16[96,512]{1,0:T(8,128)(2,1)S(1)} %collective-permute-done.20.other_b, f32[192,512]{1,0:T(8,128)S(1)} %get-tuple-element.91.keys_ref, ...), custom_call_target="tpu_custom_call" | custom-call | flops 612368384 | bytes 7995392 | tf_op jit(solution)/shard_map/pallas_call | solution.py:30
  40.3 0.0 copy-start.1
  40.4 0.4 collective-permute-start.21
  40.8 0.4 shard_map.101.keep_ref
  41.2 0.8 %collective-permute-done.21.got_ref = bf16[2,64,1024]{2,1,0:T(8,128)(2,1)S(1)} collective-permute-done((bf16[2,64,1024]{2,1,0:T(8,128)(2,1)S(1)}, bf16[2,64,1024]{2,1,0:T(8,128)(2,1)S(1)}, u32[]{:S(2)}, u32[]{:S(2)}) %collective-permute-start.21) | collective-permute-done | bytes 262176 | tf_op jit(solution)/shard_map/ppermute | solution.py:502
  42.0 0.5 shard_map.102
  42.5 1.6 %collective-permute-start.22 = (bf16[96,256]{1,0:T(8,128)(2,1)S(1)}, bf16[96,256]{1,0:T(8,128)(2,1)S(1)}, u32[]{:S(2)}, u32[]{:S(2)}) collective-permute-start(bf16[96,256]{1,0:T(8,128)(2,1)S(1)} %get-tuple-element.98.near_ref), channel_id=1, source_target_pairs={{0,2},{2,0},{4,6},{6,4},{8,10},{10,8},{12,14},{14,12},{1,3},{3,1},... | collective-permute-start | bytes 147464 | tf_op jit(solution)/shard_map/ppermute | solution.py:525
  44.1 2.9 %collective-permute-start.23 = (bf16[96,256]{1,0:T(8,128)(2,1)S(1)}, bf16[96,256]{1,0:T(8,128)(2,1)S(1)}, u32[]{:S(2)}, u32[]{:S(2)}) collective-permute-start(bf16[96,256]{1,0:T(8,128)(2,1)S(1)} %get-tuple-element.99.far_ref), channel_id=1, source_target_pairs={{2,4},{6,8},{10,12},{4,2},{8,6},{12,10},{3,5},{7,9},{11,13},{5,3},... | collective-permute-start | bytes 147464 | tf_op jit(solution)/shard_map/ppermute | solution.py:524
  47.0 0.4 shard_map.103
  47.4 0.0 collective-permute-done.22.got_near_ref
  47.4 3.6 %collective-permute-done.23.got_far_ref = bf16[96,256]{1,0:T(8,128)(2,1)S(1)} collective-permute-done((bf16[96,256]{1,0:T(8,128)(2,1)S(1)}, bf16[96,256]{1,0:T(8,128)(2,1)S(1)}, u32[]{:S(2)}, u32[]{:S(2)}) %collective-permute-start.23) | collective-permute-done | bytes 49184 | tf_op jit(solution)/shard_map/ppermute | solution.py:524
  51.0 1.2 %shard_map.104 = (bf16[2,48,256]{2,1,0:T(8,128)(2,1)}, bf16[1,24,256]{2,1,0:T(8,128)(2,1)}) custom-call(bf16[96,256]{1,0:T(8,128)(2,1)S(1)} %collective-permute-done.22.got_near_ref, bf16[96,256]{1,0:T(8,128)(2,1)S(1)} %collective-permute-done.23.got_far_ref, f32[128,256]{1,0:T(8,128)S(1)} %get-tuple-element.100.own_fine_ref, ...), custom_call_target="tpu_custom_call" | custom-call | flops 75497472 | bytes 2686976 | tf_op jit(solution)/shard_map/pallas_call | solution.py:30
  (19 shorter events, 0.1 us)
Async XLA Ops:
  0.6 2.0 %copy-start.5 = (f32[1024]{0:T(1024)S(1)}, f32[1024]{0:T(1024)}, u32[]{:S(2)}) copy-start(f32[1024]{0:T(1024)} %gain_ref.3) | copy-start | bytes 12292
  0.6 4.4 %copy-start = (bf16[3,1024,512]{2,1,0:T(8,128)(2,1)S(1)}, bf16[3,1024,512]{2,1,0:T(8,128)(2,1)}, u32[]{:S(2)}) copy-start(bf16[3,1024,512]{2,1,0:T(8,128)(2,1)} %weight_ref.8) | copy-start | bytes 9437188
  0.6 2.0 %collective-permute-start = (f32[192,512]{1,0:T(8,128)}, f32[192,512]{1,0:T(8,128)S(1)}, u32[]{:S(2)}, u32[]{:S(2)}) collective-permute-start(f32[192,512]{1,0:T(8,128)} %tokens_ref.1), channel_id=1, source_target_pairs={{0,1},{1,0},{2,3},{3,2},{4,5},{5,4},{6,7},{7,6},{8,9},{9,8},{10,11... | collective-permute-start | bytes 1179656 | tf_op jit(solution)/shard_map/ppermute | solution.py:421
  0.7 1.1 %copy-start.6 = (f32[192,512]{1,0:T(8,128)S(1)}, f32[192,512]{1,0:T(8,128)}, u32[]{:S(2)}) copy-start(f32[192,512]{1,0:T(8,128)} %tokens_ref.1) | copy-start | bytes 1179652
  3.0 7.0 %collective-permute-start.1 = (bf16[192,512]{1,0:T(8,128)(2,1)S(1)}, bf16[192,512]{1,0:T(8,128)(2,1)S(1)}, u32[]{:S(2)}, u32[]{:S(2)}) collective-permute-start(bf16[192,512]{1,0:T(8,128)(2,1)S(1)} %get-tuple-element.54.mine_ref), channel_id=1, source_target_pairs={{2,0},{0,4},{4,8},{8,12},{12,14},{14,10},{10,6},{6,2},{3,1},{1,5},... | collective-permute-start | bytes 589832 | tf_op jit(solution)/shard_map/ppermute | solution.py:439
  3.6 6.7 %collective-permute-start.3 = (bf16[192,512]{1,0:T(8,128)(2,1)S(1)}, bf16[192,512]{1,0:T(8,128)(2,1)S(1)}, u32[]{:S(2)}, u32[]{:S(2)}) collective-permute-start(bf16[192,512]{1,0:T(8,128)(2,1)S(1)} %get-tuple-element.54.mine_ref), channel_id=1, source_target_pairs={{0,2},{4,0},{8,4},{12,8},{14,12},{10,14},{6,10},{2,6},{1,3},{5,1},... | collective-permute-start | bytes 589832 | tf_op jit(solution)/shard_map/ppermute | solution.py:440
  10.0 2.5 %collective-permute-start.5 = (bf16[192,512]{1,0:T(8,128)(2,1)S(1)}, bf16[192,512]{1,0:T(8,128)(2,1)S(1)}, u32[]{:S(2)}, u32[]{:S(2)}) collective-permute-start(bf16[192,512]{1,0:T(8,128)(2,1)S(1)} %collective-permute-done.1.block_ref.refs_0_), channel_id=1, source_target_pairs={{0,1},{1,0},{2,3},{3,2},{4,5},{5,4},{6,7},{7,6},{8,9},{9,8},{10,11... | collective-permute-start | bytes 589832 | tf_op jit(solution)/shard_map/ppermute | solution.py:470
  10.2 3.6 %collective-permute-start.4 = (bf16[192,512]{1,0:T(8,128)(2,1)S(1)}, bf16[192,512]{1,0:T(8,128)(2,1)S(1)}, u32[]{:S(2)}, u32[]{:S(2)}) collective-permute-start(bf16[192,512]{1,0:T(8,128)(2,1)S(1)} %collective-permute-done.3.refs_0_), channel_id=1, source_target_pairs={{0,1},{1,0},{2,3},{3,2},{4,5},{5,4},{6,7},{7,6},{8,9},{9,8},{10,11... | collective-permute-start | bytes 589832 | tf_op jit(solution)/shard_map/ppermute | solution.py:470
  10.5 7.1 %collective-permute-start.2 = (bf16[192,512]{1,0:T(8,128)(2,1)S(1)}, bf16[192,512]{1,0:T(8,128)(2,1)S(1)}, u32[]{:S(2)}, u32[]{:S(2)}) collective-permute-start(bf16[192,512]{1,0:T(8,128)(2,1)S(1)} %collective-permute-done.1.block_ref.refs_0_), channel_id=1, source_target_pairs={{2,0},{0,4},{4,8},{8,12},{12,14},{14,10},{10,6},{6,2},{3,1},{1,5},... | collective-permute-start | bytes 589832 | tf_op jit(solution)/shard_map/ppermute | solution.py:466
  11.8 7.0 %collective-permute-start.7 = (bf16[192,512]{1,0:T(8,128)(2,1)S(1)}, bf16[192,512]{1,0:T(8,128)(2,1)S(1)}, u32[]{:S(2)}, u32[]{:S(2)}) collective-permute-start(bf16[192,512]{1,0:T(8,128)(2,1)S(1)} %collective-permute-done.3.refs_0_), channel_id=1, source_target_pairs={{0,2},{4,0},{8,4},{12,8},{14,12},{10,14},{6,10},{2,6},{1,3},{5,1},... | collective-permute-start | bytes 589832 | tf_op jit(solution)/shard_map/ppermute | solution.py:466
  17.6 9.1 %collective-permute-start.9 = (bf16[192,512]{1,0:T(8,128)(2,1)S(1)}, bf16[192,512]{1,0:T(8,128)(2,1)S(1)}, u32[]{:S(2)}, u32[]{:S(2)}) collective-permute-start(bf16[192,512]{1,0:T(8,128)(2,1)S(1)} %collective-permute-done.2.block_ref.refs_0_), channel_id=1, source_target_pairs={{0,1},{1,0},{2,3},{3,2},{4,5},{5,4},{6,7},{7,6},{8,9},{9,8},{10,11... | collective-permute-start | bytes 589832 | tf_op jit(solution)/shard_map/ppermute | solution.py:470
  18.9 9.1 %collective-permute-start.8 = (bf16[192,512]{1,0:T(8,128)(2,1)S(1)}, bf16[192,512]{1,0:T(8,128)(2,1)S(1)}, u32[]{:S(2)}, u32[]{:S(2)}) collective-permute-start(bf16[192,512]{1,0:T(8,128)(2,1)S(1)} %collective-permute-done.7.refs_0_), channel_id=1, source_target_pairs={{0,1},{1,0},{2,3},{3,2},{4,5},{5,4},{6,7},{7,6},{8,9},{9,8},{10,11... | collective-permute-start | bytes 589832 | tf_op jit(solution)/shard_map/ppermute | solution.py:470
  18.9 10.4 %collective-permute-start.6 = (bf16[96,512]{1,0:T(8,128)(2,1)S(1)}, bf16[96,512]{1,0:T(8,128)(2,1)S(1)}, u32[]{:S(2)}, u32[]{:S(2)}) collective-permute-start(bf16[96,512]{1,0:T(8,128)(2,1)S(1)} %get-tuple-element.103), channel_id=1, source_target_pairs={{2,0},{0,4},{4,8},{8,12},{12,14},{14,10},{10,6},{6,2},{3,1},{1,5},... | collective-permute-start | bytes 294920 | tf_op jit(solution)/shard_map/ppermute | solution.py:466
  20.4 5.7 %collective-permute-start.15 = (bf16[96,512]{1,0:T(8,128)(2,1)S(1)}, bf16[96,512]{1,0:T(8,128)(2,1)S(1)}, u32[]{:S(2)}, u32[]{:S(2)}) collective-permute-start(bf16[96,512]{1,0:T(8,128)(2,1)S(1)} %get-tuple-element.102), channel_id=1, source_target_pairs={{2,0},{0,4},{4,8},{8,12},{12,14},{14,10},{10,6},{6,2},{3,1},{1,5},... | collective-permute-start | bytes 294920 | tf_op jit(solution)/shard_map/ppermute | solution.py:466
  22.0 8.8 %collective-permute-start.11 = (bf16[96,512]{1,0:T(8,128)(2,1)S(1)}, bf16[96,512]{1,0:T(8,128)(2,1)S(1)}, u32[]{:S(2)}, u32[]{:S(2)}) collective-permute-start(bf16[96,512]{1,0:T(8,128)(2,1)S(1)} %get-tuple-element.105), channel_id=1, source_target_pairs={{0,2},{4,0},{8,4},{12,8},{14,12},{10,14},{6,10},{2,6},{1,3},{5,1},... | collective-permute-start | bytes 294920 | tf_op jit(solution)/shard_map/ppermute | solution.py:466
  26.2 4.6 %collective-permute-start.12 = (bf16[96,512]{1,0:T(8,128)(2,1)S(1)}, bf16[96,512]{1,0:T(8,128)(2,1)S(1)}, u32[]{:S(2)}, u32[]{:S(2)}) collective-permute-start(bf16[96,512]{1,0:T(8,128)(2,1)S(1)} %get-tuple-element.104), channel_id=1, source_target_pairs={{0,2},{4,0},{8,4},{12,8},{14,12},{10,14},{6,10},{2,6},{1,3},{5,1},... | collective-permute-start | bytes 294920 | tf_op jit(solution)/shard_map/ppermute | solution.py:466
  26.6 6.3 %collective-permute-start.17 = (bf16[96,512]{1,0:T(8,128)(2,1)S(1)}, bf16[96,512]{1,0:T(8,128)(2,1)S(1)}, u32[]{:S(2)}, u32[]{:S(2)}) collective-permute-start(bf16[96,512]{1,0:T(8,128)(2,1)S(1)} %collective-permute-done.15.refs_1_), channel_id=1, source_target_pairs={{0,1},{1,0},{2,3},{3,2},{4,5},{5,4},{6,7},{7,6},{8,9},{9,8},{10,11... | collective-permute-start | bytes 294920 | tf_op jit(solution)/shard_map/ppermute | solution.py:470
  29.3 4.0 %collective-permute-start.16 = (bf16[96,512]{1,0:T(8,128)(2,1)S(1)}, bf16[96,512]{1,0:T(8,128)(2,1)S(1)}, u32[]{:S(2)}, u32[]{:S(2)}) collective-permute-start(bf16[96,512]{1,0:T(8,128)(2,1)S(1)} %collective-permute-done.6.block_ref.refs_0_), channel_id=1, source_target_pairs={{0,1},{1,0},{2,3},{3,2},{4,5},{5,4},{6,7},{7,6},{8,9},{9,8},{10,11... | collective-permute-start | bytes 294920 | tf_op jit(solution)/shard_map/ppermute | solution.py:470
  30.8 3.9 %collective-permute-start.14 = (bf16[96,512]{1,0:T(8,128)(2,1)S(1)}, bf16[96,512]{1,0:T(8,128)(2,1)S(1)}, u32[]{:S(2)}, u32[]{:S(2)}) collective-permute-start(bf16[96,512]{1,0:T(8,128)(2,1)S(1)} %collective-permute-done.12.refs_1_), channel_id=1, source_target_pairs={{0,1},{1,0},{2,3},{3,2},{4,5},{5,4},{6,7},{7,6},{8,9},{9,8},{10,11... | collective-permute-start | bytes 294920 | tf_op jit(solution)/shard_map/ppermute | solution.py:470
  30.8 3.9 %collective-permute-start.13 = (bf16[96,512]{1,0:T(8,128)(2,1)S(1)}, bf16[96,512]{1,0:T(8,128)(2,1)S(1)}, u32[]{:S(2)}, u32[]{:S(2)}) collective-permute-start(bf16[96,512]{1,0:T(8,128)(2,1)S(1)} %collective-permute-done.11.refs_0_), channel_id=1, source_target_pairs={{0,1},{1,0},{2,3},{3,2},{4,5},{5,4},{6,7},{7,6},{8,9},{9,8},{10,11... | collective-permute-start | bytes 294920 | tf_op jit(solution)/shard_map/ppermute | solution.py:470
  31.3 4.7 %collective-permute-start.10 = (bf16[96,512]{1,0:T(8,128)(2,1)S(1)}, bf16[96,512]{1,0:T(8,128)(2,1)S(1)}, u32[]{:S(2)}, u32[]{:S(2)}) collective-permute-start(bf16[96,512]{1,0:T(8,128)(2,1)S(1)} %collective-permute-done.6.block_ref.refs_0_), channel_id=1, source_target_pairs={{2,0},{0,4},{4,8},{8,12},{12,14},{14,10},{10,6},{6,2},{3,1},{1,5},... | collective-permute-start | bytes 294920 | tf_op jit(solution)/shard_map/ppermute | solution.py:466
  32.9 4.6 %collective-permute-start.19 = (bf16[96,512]{1,0:T(8,128)(2,1)S(1)}, bf16[96,512]{1,0:T(8,128)(2,1)S(1)}, u32[]{:S(2)}, u32[]{:S(2)}) collective-permute-start(bf16[96,512]{1,0:T(8,128)(2,1)S(1)} %collective-permute-done.11.refs_0_), channel_id=1, source_target_pairs={{0,2},{4,0},{8,4},{12,8},{14,12},{10,14},{6,10},{2,6},{1,3},{5,1},... | collective-permute-start | bytes 294920 | tf_op jit(solution)/shard_map/ppermute | solution.py:466
  36.0 3.0 %copy-start.2 = (bf16[512,1024]{1,0:T(8,128)(2,1)S(1)}, bf16[512,1024]{1,0:T(8,128)(2,1)}, u32[]{:S(2)}) copy-start(bf16[512,1024]{1,0:T(8,128)(2,1)} %weight_ref.9) | copy-start | bytes 3145732
  37.5 1.3 %collective-permute-start.20 = (bf16[96,512]{1,0:T(8,128)(2,1)S(1)}, bf16[96,512]{1,0:T(8,128)(2,1)S(1)}, u32[]{:S(2)}, u32[]{:S(2)}) collective-permute-start(bf16[96,512]{1,0:T(8,128)(2,1)S(1)} %collective-permute-done.19.mine_b), channel_id=1, source_target_pairs={{0,1},{1,0},{2,3},{3,2},{4,5},{5,4},{6,7},{7,6},{8,9},{9,8},{10,11... | collective-permute-start | bytes 294920 | tf_op jit(solution)/shard_map/ppermute | solution.py:470
  37.5 1.5 %collective-permute-start.18 = (bf16[96,512]{1,0:T(8,128)(2,1)S(1)}, bf16[96,512]{1,0:T(8,128)(2,1)S(1)}, u32[]{:S(2)}, u32[]{:S(2)}) collective-permute-start(bf16[96,512]{1,0:T(8,128)(2,1)S(1)} %collective-permute-done.10.block_ref.mine_a), channel_id=1, source_target_pairs={{0,1},{1,0},{2,3},{3,2},{4,5},{5,4},{6,7},{7,6},{8,9},{9,8},{10,11... | collective-permute-start | bytes 294920 | tf_op jit(solution)/shard_map/ppermute | solution.py:470
  39.0 3.0 %copy-start.3 = (bf16[2,1024,256]{2,1,0:T(8,128)(2,1)S(1)}, bf16[2,1024,256]{2,1,0:T(8,128)(2,1)}, u32[]{:S(2)}) copy-start(bf16[2,1024,256]{2,1,0:T(8,128)(2,1)} %lateral_ref.1) | copy-start | bytes 3145732
  39.0 3.0 %copy-start.4 = (f32[2,2,256]{2,1,0:T(2,128)S(1)}, f32[2,2,256]{2,1,0:T(2,128)}, u32[]{:S(2)}) copy-start(f32[2,2,256]{2,1,0:T(2,128)} %gain_ref.5) | copy-start | bytes 12292
  40.3 6.6 %copy-start.1 = (bf16[2,3,3,256,256]{4,3,2,1,0:T(8,128)(2,1)S(1)}, bf16[2,3,3,256,256]{4,3,2,1,0:T(8,128)(2,1)}, u32[]{:S(2)}) copy-start(bf16[2,3,3,256,256]{4,3,2,1,0:T(8,128)(2,1)} %weight_ref.11) | copy-start | bytes 7077892
  40.4 1.6 %collective-permute-start.21 = (bf16[2,64,1024]{2,1,0:T(8,128)(2,1)S(1)}, bf16[2,64,1024]{2,1,0:T(8,128)(2,1)S(1)}, u32[]{:S(2)}, u32[]{:S(2)}) collective-permute-start(bf16[2,64,1024]{2,1,0:T(8,128)(2,1)S(1)} %get-tuple-element.97), channel_id=1, source_target_pairs={{0,1},{1,0},{2,3},{3,2},{4,5},{5,4},{6,7},{7,6},{8,9},{9,8},{10,11... | collective-permute-start | bytes 786440 | tf_op jit(solution)/shard_map/ppermute | solution.py:502
  42.5 4.9 %collective-permute-start.22 = (bf16[96,256]{1,0:T(8,128)(2,1)S(1)}, bf16[96,256]{1,0:T(8,128)(2,1)S(1)}, u32[]{:S(2)}, u32[]{:S(2)}) collective-permute-start(bf16[96,256]{1,0:T(8,128)(2,1)S(1)} %get-tuple-element.98.near_ref), channel_id=1, source_target_pairs={{0,2},{2,0},{4,6},{6,4},{8,10},{10,8},{12,14},{14,12},{1,3},{3,1},... | collective-permute-start | bytes 147464 | tf_op jit(solution)/shard_map/ppermute | solution.py:525
  44.1 6.9 %collective-permute-start.23 = (bf16[96,256]{1,0:T(8,128)(2,1)S(1)}, bf16[96,256]{1,0:T(8,128)(2,1)S(1)}, u32[]{:S(2)}, u32[]{:S(2)}) collective-permute-start(bf16[96,256]{1,0:T(8,128)(2,1)S(1)} %get-tuple-element.99.far_ref), channel_id=1, source_target_pairs={{2,4},{6,8},{10,12},{4,2},{8,6},{12,10},{3,5},{7,9},{11,13},{5,3},... | collective-permute-start | bytes 147464 | tf_op jit(solution)/shard_map/ppermute | solution.py:524

commit v8 on v7

--- a/solution.py
+++ b/solution.py
@@ -1,4 +1,3 @@
-import functools
 import math
 
 import jax
@@ -149,10 +148,6 @@
         )
 
 
-def stacked(refs):
-    return jnp.concatenate([ref[...] for ref in refs], axis=0) if len(refs) > 1 else refs[0][...]
-
-
 def absorb_keys(keys, values, query_ref, top_ref, total_ref, mixed_ref):
     for pair in range(query_ref.shape[0]):
         old = top_ref[pair], total_ref[pair], mixed_ref[pair]
@@ -163,20 +158,28 @@
     mark_ref[...] = block_ref[: mark_ref.shape[0], : mark_ref.shape[1]]
 
 
-def step_kernel(pieces, *refs):
-    mine_refs, other_refs = refs[:pieces], refs[pieces : 2 * pieces]
-    weight_ref, *state_refs = refs[2 * pieces : 2 * pieces + 5]
-    out_refs = refs[-3:]
-    mine, other = stacked(mine_refs), stacked(other_refs)
+def step_kernel(
+    mine_ref,
+    other_ref,
+    weight_ref,
+    query_ref,
+    top_ref,
+    total_ref,
+    mixed_ref,
+    mark_ref,
+    top_out,
+    total_out,
+    mixed_out,
+):
+    mine, other = mine_ref[...], other_ref[...]
     keys = project(mine, other, weight_ref, 1)
     values = project(mine, other, weight_ref, 2)
-    for pair, state in absorb_keys(keys, values, *state_refs):
-        for ref, value in zip(out_refs, state):
-            ref[pair] = value
+    for pair, state in absorb_keys(keys, values, query_ref, top_ref, total_ref, mixed_ref):
+        top_out[pair], total_out[pair], mixed_out[pair] = state
 
 
 def half_kernel(mine_a, mine_b, weight_ref, mark_ref, keys_ref, values_ref):
-    mine = stacked((mine_a, mine_b))
+    mine = jnp.concatenate([mine_a[...], mine_b[...]], axis=0)
     half = mine.shape[1]
     here = pl.ds(pl.multiple_of(lax.axis_index("head") * half, half), half)
     keys_ref[...] = dot(mine, weight_ref[1, here, :])
@@ -229,7 +232,7 @@
 ):
     rows = mixed_ref.shape[1]
     low = low_lanes((rows, LANES))
-    other = stacked((other_a, other_b))
+    other = jnp.concatenate([other_a[...], other_b[...]], axis=0)
     half = other.shape[1]
     there = pl.ds(pl.multiple_of((1 - lax.axis_index("head")) * half, half), half)
     keys = (keys_ref[...] + dot(other, weight_ref[1, there, :])).astype(BF16)
@@ -247,16 +250,16 @@
 
 
 def lateral_kernel(
-    keep_ref, got_ref, lateral_ref, gain_ref, near_ref, far_ref, pool_ref, fine_ref
+    keep_ref, got_ref, lateral_ref, gain_ref, first_ref, second_ref, pool_ref, fine_ref
 ):
-    odd = lax.axis_index("blk") % 2
+    core = lax.axis_index("head")
     window, features = keep_ref.shape[1], keep_ref.shape[2]
     cells = (keep_ref[...] + got_ref[...].astype(F32)).astype(BF16)
     fine_ref[...] = layer_norm(
         dot(cells.reshape(2 * window, features), lateral_ref[0]), gain_ref[0, 0][None, :]
     ).astype(BF16)
-    near_ref[:window] = fine_ref[pl.ds(pl.multiple_of((1 - odd) * window, window), window), :]
-    far_ref[:window] = fine_ref[pl.ds(pl.multiple_of(odd * window, window), window), :]
+    first_ref[:window] = fine_ref[pl.ds(pl.multiple_of((1 - core) * window, window), window), :]
+    second_ref[:window] = fine_ref[pl.ds(pl.multiple_of(core * window, window), window), :]
     tall = jnp.maximum(cells[0].astype(F32), cells[1].astype(F32))
     pooled = []
     for part in range(features // LANES):
@@ -266,8 +269,8 @@
         pooled.append(jnp.maximum(even, odd).astype(BF16))
     pooled = jnp.concatenate(pooled, axis=1)
     coarse = layer_norm(dot(pooled, lateral_ref[1]), gain_ref[1, 0][None, :]).astype(BF16)
-    near_ref[window:] = coarse
-    far_ref[window:] = coarse
+    first_ref[window:] = coarse
+    second_ref[window:] = coarse
 
 
 def joined(terms, window):
@@ -279,12 +282,12 @@
     return left + middle + right
 
 
-def own_conv_kernel(near_ref, far_ref, weight_ref, fine_ref, coarse_ref, fine_in):
-    odd = lax.axis_index("blk") % 2
+def own_conv_kernel(first_ref, second_ref, weight_ref, fine_ref, coarse_ref, fine_in):
+    core = lax.axis_index("head")
     window = fine_ref.shape[0] // 2
-    for ref, place in ((near_ref, 1 - odd), (far_ref, odd)):
+    for ref, place in ((first_ref, 1 - core), (second_ref, core)):
         fine_in[pl.ds(pl.multiple_of(place * window, window), window), :] = ref[:window]
-    coarse = near_ref[window:]
+    coarse = first_ref[window:]
 
     def fine_terms(tap_col):
         to_lower = dot(fine_in[:window], weight_ref[0, 0, tap_col])
@@ -298,8 +301,8 @@
 
 
 def conv_kernel(
-    got_near_ref,
-    got_far_ref,
+    got_first_ref,
+    got_second_ref,
     own_fine_ref,
     own_coarse_ref,
     weight_ref,
@@ -311,11 +314,15 @@
     coarse_sum,
 ):
     core = lax.axis_index("head")
-    odd = lax.axis_index("blk") % 2
+    block = lax.axis_index("blk")
+    edge = (0, lax.axis_size("blk") - 1)
     window = fine_sum.shape[0] // 2
-    rows = got_near_ref.shape[0]
-    for ref, place in ((got_near_ref, 1 - odd), (got_far_ref, odd)):
-        edge_in[pl.ds(pl.multiple_of(place * rows, 32), rows), :] = ref[...]
+    rows = got_first_ref.shape[0]
+    for ref, place in ((got_first_ref, core), (got_second_ref, 1 - core)):
+        inside = block != jnp.where(place == 0, *edge)
+        edge_in[pl.ds(pl.multiple_of(place * rows, 32), rows), :] = jnp.where(
+            inside, ref[...].astype(F32), 0.0
+        ).astype(BF16)
 
     def fine_terms(tap_col):
         return jnp.concatenate(
@@ -423,7 +430,7 @@
     other, tokens = lax.optimization_barrier((other, tokens))
     term_out = ((grid_rows, window, features), BF16)
     out_flops = 2 * grid_rows * window * width * features
-    if 6 <= blocks <= heads:
+    if 4 <= blocks <= heads:
         order = list(range(0, blocks, 2)) + list(range(blocks - 1, 0, -2))
         forth = [(order[i - 1], order[i]) for i in range(blocks)]
         back = [(target, source) for source, target in forth]
@@ -447,36 +454,26 @@
             exps=heads * rows * rows,
         )
         last = blocks // 2
-        ahead, behind = (ahead,), (behind,)
         for step in range(1, last + 1):
-            first, state[0] = lax.optimization_barrier((ahead[0], state[0]))
-            ahead = (first,) + ahead[1:]
-            first, state[0] = lax.optimization_barrier((behind[0], state[0]))
-            behind = (first,) + behind[1:]
+            ahead, state[0] = lax.optimization_barrier((ahead, state[0]))
+            behind, state[0] = lax.optimization_barrier((behind, state[0]))
             arrived = ahead, behind
-            (mark,) = call(mark_kernel, [((16, LANES), BF16)], (ahead[0],))
+            (mark,) = call(mark_kernel, [((16, LANES), BF16)], (ahead,))
             if step == last - 1:
-                ahead, behind = ahead[:1], behind[:1]
-            elif step == last - 2:
-                (whole_a,), (whole_b,) = ahead, behind
-                ahead = whole_a[: rows // 2], whole_a[rows // 2 :]
-                behind = whole_b[rows // 2 :], whole_b[: rows // 2]
+                ahead, behind = ahead[: rows // 2], behind[rows // 2 :]
             if step < last:
-                ahead, behind = (
-                    tuple(lax.ppermute(piece, "blk", pairs_of) for piece in pieces)
-                    for pieces, pairs_of in ((ahead, forth), (behind, back))
-                )
-            traded = tuple(
-                tuple(lax.ppermute(piece, "head", swap) for piece in pieces)
-                for pieces in arrived
+                ahead = lax.ppermute(ahead, "blk", forth)
+                behind = lax.ppermute(behind, "blk", back)
+            traded = (
+                lax.ppermute(arrived[0], "head", swap), lax.ppermute(arrived[1], "head", swap)
             )
             if step == last:
                 break
-            for mine, across_core in zip(arrived, traded):
+            for block in zip(arrived, traded):
                 state = call(
-                    functools.partial(step_kernel, len(mine)),
+                    step_kernel,
                     state_outs,
-                    mine + across_core + (qkv_weight, queries) + tuple(state) + (mark,),
+                    block + (qkv_weight, queries) + tuple(state) + (mark,),
                     flops=unit,
                     exps=heads * rows * rows,
                 )
@@ -484,13 +481,13 @@
         keys, values = call(
             half_kernel,
             [((rows, width), F32)] * 2,
-            (*arrived[0], *arrived[1], qkv_weight, mark),
+            arrived + (qkv_weight, mark),
             flops=2 * rows * width * features,
         )
         peer_term, attended = call(
             last_kernel,
             [term_out, ((rows, width), BF16)],
-            (*traded[0], *traded[1], keys, values, qkv_weight, queries)
+            traded + (keys, values, qkv_weight, queries)
             + tuple(state)
             + (out_weight,),
             flops=unit + out_flops,
@@ -509,7 +506,7 @@
     )
 
     message = (window + window // 2, channels)
-    near, far = call(
+    first, second = call(
         lateral_kernel,
         [(message, BF16), (message, BF16)],
         (keep, peer_term, lateral_weight, level_gains),
@@ -519,22 +516,29 @@
         ],
         flops=5 * window * features * channels,
     )
-    far_pairs = [(i, i + 1) for i in range(1, blocks - 1, 2)]
-    far_pairs += [(j, i) for i, j in far_pairs]
-    got_far = lax.ppermute(far, "blk", far_pairs)
-    got_near = lax.ppermute(near, "blk", [(i, i ^ 1) for i in range(blocks)])
+    down_then_up = [
+        loop
+        for low in range(2)
+        for loop in [
+            [(cores * i + low, cores * (i + 1) + low) for i in range(blocks - 1)]
+            + [(cores * (i + 1) + 1 - low, cores * i + 1 - low) for i in range(blocks - 1)]
+            + [(cores * (blocks - 1) + low, cores * blocks - 1 - low), (1 - low, low)]
+        ]
+    ]
+    got_second = lax.ppermute(second, ("blk", "head"), down_then_up[1])
+    got_first = lax.ppermute(first, ("blk", "head"), down_then_up[0])
     sums = [((2 * window, channels), F32), ((window // 2, channels), F32)]
     own_sums = call(
         own_conv_kernel,
         sums,
-        (near, far, conv_weight),
+        (first, second, conv_weight),
         [pltpu.VMEM((2 * window, channels), BF16)],
         flops=27 * window * channels * channels,
     )
     return call(
         conv_kernel,
         [((grid_rows, cols, channels), BF16), ((grid_rows // 2, cols // 2, channels), BF16)],
-        (got_near, got_far, *own_sums, conv_weight, level_gains),
+        (got_first, got_second, *own_sums, conv_weight, level_gains),
         [pltpu.VMEM((2 * message[0], channels), BF16)]
         + [pltpu.VMEM(shape, dtype) for shape, dtype in sums],
         flops=18 * window * channels * channels,

time: 52.3 us -> 47.7 us (0.912); the launches traced: 52.1 us -> 46.8 us
  starting transfers between devices: 17.1 us -> 11.8 us
    ppermute x20 -> x16, starting transfers between devices: 14.5 us -> 9.22 us  [the longest x3 4.53 us: body(): ahead = lax.ppermute(ahead, 'blk', forth)]
    ppermute x20 -> x16, waiting for transfers between devices: 13.9 us -> 14 us  [the longest x3 5.26 us: body(): ahead = lax.ppermute(ahead, 'blk', forth)]
  transfers between devices with their start and end apart: 24 -> 20, of which waited for: 12 -> 14; matrix products, arithmetic and copies ran while one was open for 0% -> 0% of each run, Pallas kernels for 20% -> 22%
where the time goes in v8:
time: 47.7 us; the launch traced here: 46.8 us
  waiting for transfers between devices  19.2 us (40%)
  Pallas kernels  13.8 us (29%)
  starting transfers between devices  11.8 us (25%)
  local copies, waits for them, and re-layouts  1.18 us (2%)
  between operations  0.82 us (2%)
    pallas_call x19, Pallas kernels, call(): pl.pallas_call(kernel, out_shape=outs, in_specs=specs(len(args)), out_spe...  13.8 us
    ppermute x3, waiting for transfers between devices, body(): ahead = lax.ppermute(ahead, 'blk', forth)  5.26 us
    ppermute x3, starting transfers between devices, body(): ahead = lax.ppermute(ahead, 'blk', forth)  4.53 us
    ppermute x3, waiting for transfers between devices, body(): behind = lax.ppermute(behind, 'blk', back)  4.12 us
    ppermute x1, waiting for transfers between devices, body(): ahead = lax.ppermute(mine, 'blk', forth)  3.5 us
    ppermute x1, waiting for transfers between devices, body(): got_first = lax.ppermute(first, ('blk', 'head'), down_then_up[0])  2.35 us
    ppermute x3, starting transfers between devices, body(): behind = lax.ppermute(behind, 'blk', back)  1.83 us
    ppermute x1, waiting for transfers between devices, body(): got_second = lax.ppermute(second, ('blk', 'head'), down_then_up[1])  1.64 us
  transfers between devices with their start and end apart: 20, of which 14 were waited for; matrix products, arithmetic and copies ran while one was open for 0% of the time, Pallas kernels for 22%

profile of v8, /device:TPU:6, one launch (start us, length us, event | category | flops | bytes accessed | tf_op | source)
XLA Modules:
  0.0 46.8 jit_solution(12015035553273634778)
XLA Ops:
  0.6 0.0 copy-start.5
  0.6 0.0 copy-start
  0.6 0.1 collective-permute-start
  0.7 0.0 copy-start.6
  0.7 1.1 %copy-done.6 = f32[192,512]{1,0:T(8,128)S(1)} copy-done((f32[192,512]{1,0:T(8,128)S(1)}, f32[192,512]{1,0:T(8,128)}, u32[]{:S(2)}) %copy-start.6) | copy-done | bytes 393240
  1.9 0.7 %collective-permute-done.other_ref = f32[192,512]{1,0:T(8,128)S(1)} collective-permute-done((f32[192,512]{1,0:T(8,128)}, f32[192,512]{1,0:T(8,128)S(1)}, u32[]{:S(2)}, u32[]{:S(2)}) %collective-permute-start) | collective-permute-done | bytes 393248 | tf_op jit(solution)/shard_map/ppermute | solution.py:428
  2.6 0.0 copy-done.5
  2.7 0.3 shard_map.87
  3.0 0.6 %collective-permute-start.1 = (bf16[192,512]{1,0:T(8,128)(2,1)S(1)}, bf16[192,512]{1,0:T(8,128)(2,1)S(1)}, u32[]{:S(2)}, u32[]{:S(2)}) collective-permute-start(bf16[192,512]{1,0:T(8,128)(2,1)S(1)} %get-tuple-element.54.mine_ref), channel_id=1, source_target_pairs={{2,0},{0,4},{4,8},{8,12},{12,14},{14,10},{10,6},{6,2},{3,1},{1,5},... | collective-permute-start | bytes 589832 | tf_op jit(solution)/shard_map/ppermute | solution.py:446
  3.6 1.5 %collective-permute-start.3 = (bf16[192,512]{1,0:T(8,128)(2,1)S(1)}, bf16[192,512]{1,0:T(8,128)(2,1)S(1)}, u32[]{:S(2)}, u32[]{:S(2)}) collective-permute-start(bf16[192,512]{1,0:T(8,128)(2,1)S(1)} %get-tuple-element.54.mine_ref), channel_id=1, source_target_pairs={{0,2},{4,0},{8,4},{12,8},{14,12},{10,14},{6,10},{2,6},{1,3},{5,1},... | collective-permute-start | bytes 589832 | tf_op jit(solution)/shard_map/ppermute | solution.py:447
  5.1 0.0 copy-done
  5.1 1.4 %shard_map.88 = (bf16[4,384,128]{2,1,0:T(8,128)(2,1)S(1)}, f32[4,384,128]{2,1,0:T(8,128)S(1)}, f32[4,384,128]{2,1,0:T(8,128)S(1)}, f32[4,192,128]{2,1,0:T(8,128)S(1)}) custom-call(bf16[192,512]{1,0:T(8,128)(2,1)S(1)} %get-tuple-element.54.mine_ref, bf16[192,512]{1,0:T(8,128)(2,1)S(1)} %get-tuple-element.55.other_ref, bf16[3,1024,512]{2,1,0:T(8,128)(2,1)S(1)} %copy-done), custom_call_target="tpu_custom_call" | custom-call | flops 679477248 | bytes 5898240 | tf_op jit(solution)/shard_map/pallas_call | solution.py:29
  6.5 3.5 %collective-permute-done.1.block_ref.mine_ref = bf16[192,512]{1,0:T(8,128)(2,1)S(1)} collective-permute-done((bf16[192,512]{1,0:T(8,128)(2,1)S(1)}, bf16[192,512]{1,0:T(8,128)(2,1)S(1)}, u32[]{:S(2)}, u32[]{:S(2)}) %collective-permute-start.1) | collective-permute-done | bytes 196640 | tf_op jit(solution)/shard_map/ppermute | solution.py:446
  10.0 0.0 collective-permute-start.5
  10.0 0.3 collective-permute-done.3.mine_ref
  10.2 0.3 collective-permute-start.4
  10.5 1.3 %collective-permute-start.2 = (bf16[192,512]{1,0:T(8,128)(2,1)S(1)}, bf16[192,512]{1,0:T(8,128)(2,1)S(1)}, u32[]{:S(2)}, u32[]{:S(2)}) collective-permute-start(bf16[192,512]{1,0:T(8,128)(2,1)S(1)} %collective-permute-done.1.block_ref.mine_ref), channel_id=1, source_target_pairs={{2,0},{0,4},{4,8},{8,12},{12,14},{14,10},{10,6},{6,2},{3,1},{1,5},... | collective-permute-start | bytes 589832 | tf_op jit(solution)/shard_map/ppermute | solution.py:465
  11.8 0.7 %collective-permute-start.7 = (bf16[192,512]{1,0:T(8,128)(2,1)S(1)}, bf16[192,512]{1,0:T(8,128)(2,1)S(1)}, u32[]{:S(2)}, u32[]{:S(2)}) collective-permute-start(bf16[192,512]{1,0:T(8,128)(2,1)S(1)} %collective-permute-done.3.mine_ref), channel_id=1, source_target_pairs={{0,2},{4,0},{8,4},{12,8},{14,12},{10,14},{6,10},{2,6},{1,3},{5,1},... | collective-permute-start | bytes 589832 | tf_op jit(solution)/shard_map/ppermute | solution.py:466
  12.5 0.0 collective-permute-done.5.other_ref
  12.5 1.3 %shard_map.90 = (f32[4,384,128]{2,1,0:T(8,128)S(1)}, f32[4,384,128]{2,1,0:T(8,128)S(1)}, f32[4,192,128]{2,1,0:T(8,128)S(1)}) custom-call(bf16[192,512]{1,0:T(8,128)(2,1)S(1)} %collective-permute-done.1.block_ref.mine_ref, bf16[192,512]{1,0:T(8,128)(2,1)S(1)} %collective-permute-done.5.other_ref, bf16[3,1024,512]{2,1,0:T(8,128)(2,1)S(1)} %copy-done, ...), custom_call_target="tpu_custom_call" | custom-call | flops 478150656 | bytes 7868416 | tf_op jit(solution)/shard_map/pallas_call | solution.py:29
  13.9 0.0 collective-permute-done.4.other_ref
  13.9 1.3 %shard_map.91 = (f32[4,384,128]{2,1,0:T(8,128)S(1)}, f32[4,384,128]{2,1,0:T(8,128)S(1)}, f32[4,192,128]{2,1,0:T(8,128)S(1)}) custom-call(bf16[192,512]{1,0:T(8,128)(2,1)S(1)} %collective-permute-done.3.mine_ref, bf16[192,512]{1,0:T(8,128)(2,1)S(1)} %collective-permute-done.4.other_ref, bf16[3,1024,512]{2,1,0:T(8,128)(2,1)S(1)} %copy-done, ...), custom_call_target="tpu_custom_call" | custom-call | flops 478150656 | bytes 7868416 | tf_op jit(solution)/shard_map/pallas_call | solution.py:29
  15.2 2.4 %collective-permute-done.2.block_ref.mine_ref = bf16[192,512]{1,0:T(8,128)(2,1)S(1)} collective-permute-done((bf16[192,512]{1,0:T(8,128)(2,1)S(1)}, bf16[192,512]{1,0:T(8,128)(2,1)S(1)}, u32[]{:S(2)}, u32[]{:S(2)}) %collective-permute-start.2) | collective-permute-done | bytes 196640 | tf_op jit(solution)/shard_map/ppermute | solution.py:465
  17.6 0.0 collective-permute-start.9
  17.6 1.3 %collective-permute-done.7.mine_ref = bf16[192,512]{1,0:T(8,128)(2,1)S(1)} collective-permute-done((bf16[192,512]{1,0:T(8,128)(2,1)S(1)}, bf16[192,512]{1,0:T(8,128)(2,1)S(1)}, u32[]{:S(2)}, u32[]{:S(2)}) %collective-permute-start.7) | collective-permute-done | bytes 196640 | tf_op jit(solution)/shard_map/ppermute | solution.py:466
  18.9 0.0 collective-permute-start.8
  18.9 1.6 %collective-permute-start.6 = (bf16[192,512]{1,0:T(8,128)(2,1)S(1)}, bf16[192,512]{1,0:T(8,128)(2,1)S(1)}, u32[]{:S(2)}, u32[]{:S(2)}) collective-permute-start(bf16[192,512]{1,0:T(8,128)(2,1)S(1)} %collective-permute-done.2.block_ref.mine_ref), channel_id=1, source_target_pairs={{2,0},{0,4},{4,8},{8,12},{12,14},{14,10},{10,6},{6,2},{3,1},{1,5},... | collective-permute-start | bytes 589832 | tf_op jit(solution)/shard_map/ppermute | solution.py:465
  20.4 0.4 collective-permute-start.11
  20.9 0.0 collective-permute-done.9.other_ref
  20.9 1.3 %shard_map.93 = (f32[4,384,128]{2,1,0:T(8,128)S(1)}, f32[4,384,128]{2,1,0:T(8,128)S(1)}, f32[4,192,128]{2,1,0:T(8,128)S(1)}) custom-call(bf16[192,512]{1,0:T(8,128)(2,1)S(1)} %collective-permute-done.2.block_ref.mine_ref, bf16[192,512]{1,0:T(8,128)(2,1)S(1)} %collective-permute-done.9.other_ref, bf16[3,1024,512]{2,1,0:T(8,128)(2,1)S(1)} %copy-done, ...), custom_call_target="tpu_custom_call" | custom-call | flops 478150656 | bytes 7868416 | tf_op jit(solution)/shard_map/pallas_call | solution.py:29
  22.2 0.0 collective-permute-done.8.other_ref
  22.2 1.3 %shard_map.94 = (f32[4,384,128]{2,1,0:T(8,128)S(1)}, f32[4,384,128]{2,1,0:T(8,128)S(1)}, f32[4,192,128]{2,1,0:T(8,128)S(1)}) custom-call(bf16[192,512]{1,0:T(8,128)(2,1)S(1)} %collective-permute-done.7.mine_ref, bf16[192,512]{1,0:T(8,128)(2,1)S(1)} %collective-permute-done.8.other_ref, bf16[3,1024,512]{2,1,0:T(8,128)(2,1)S(1)} %copy-done, ...), custom_call_target="tpu_custom_call" | custom-call | flops 478150656 | bytes 7868416 | tf_op jit(solution)/shard_map/pallas_call | solution.py:29
  23.6 2.6 %collective-permute-done.6.block_ref.mine_ref = bf16[192,512]{1,0:T(8,128)(2,1)S(1)} collective-permute-done((bf16[192,512]{1,0:T(8,128)(2,1)S(1)}, bf16[192,512]{1,0:T(8,128)(2,1)S(1)}, u32[]{:S(2)}, u32[]{:S(2)}) %collective-permute-start.6) | collective-permute-done | bytes 196640 | tf_op jit(solution)/shard_map/ppermute | solution.py:465
  26.2 0.0 collective-permute-start.13
  26.2 1.3 %collective-permute-done.11.mine_ref = bf16[192,512]{1,0:T(8,128)(2,1)S(1)} collective-permute-done((bf16[192,512]{1,0:T(8,128)(2,1)S(1)}, bf16[192,512]{1,0:T(8,128)(2,1)S(1)}, u32[]{:S(2)}, u32[]{:S(2)}) %collective-permute-start.11) | collective-permute-done | bytes 196640 | tf_op jit(solution)/shard_map/ppermute | solution.py:466
  27.5 0.0 collective-permute-start.12
  27.5 1.6 %collective-permute-start.10 = (bf16[96,512]{1,0:T(8,128)(2,1)S(1)}, bf16[96,512]{1,0:T(8,128)(2,1)S(1)}, u32[]{:S(2)}, u32[]{:S(2)}) collective-permute-start(bf16[96,512]{1,0:T(8,128)(2,1)S(1)} %slice.6), channel_id=1, source_target_pairs={{2,0},{0,4},{4,8},{8,12},{12,14},{14,10},{10,6},{6,2},{3,1},{1,5},... | collective-permute-start | bytes 294920 | tf_op jit(solution)/shard_map/ppermute | solution.py:465
  29.1 0.7 %collective-permute-start.15 = (bf16[96,512]{1,0:T(8,128)(2,1)S(1)}, bf16[96,512]{1,0:T(8,128)(2,1)S(1)}, u32[]{:S(2)}, u32[]{:S(2)}) collective-permute-start(bf16[96,512]{1,0:T(8,128)(2,1)S(1)} %slice.7), channel_id=1, source_target_pairs={{0,2},{4,0},{8,4},{12,8},{14,12},{10,14},{6,10},{2,6},{1,3},{5,1},... | collective-permute-start | bytes 294920 | tf_op jit(solution)/shard_map/ppermute | solution.py:466
  29.8 0.0 collective-permute-done.13.other_ref
  29.8 1.3 %shard_map.96 = (f32[4,384,128]{2,1,0:T(8,128)S(1)}, f32[4,384,128]{2,1,0:T(8,128)S(1)}, f32[4,192,128]{2,1,0:T(8,128)S(1)}) custom-call(bf16[192,512]{1,0:T(8,128)(2,1)S(1)} %collective-permute-done.6.block_ref.mine_ref, bf16[192,512]{1,0:T(8,128)(2,1)S(1)} %collective-permute-done.13.other_ref, bf16[3,1024,512]{2,1,0:T(8,128)(2,1)S(1)} %copy-done, ...), custom_call_target="tpu_custom_call" | custom-call | flops 478150656 | bytes 7868416 | tf_op jit(solution)/shard_map/pallas_call | solution.py:29
  31.1 0.0 collective-permute-done.12.other_ref
  31.1 1.3 %shard_map.97 = (f32[4,384,128]{2,1,0:T(8,128)S(1)}, f32[4,384,128]{2,1,0:T(8,128)S(1)}, f32[4,192,128]{2,1,0:T(8,128)S(1)}) custom-call(bf16[192,512]{1,0:T(8,128)(2,1)S(1)} %collective-permute-done.11.mine_ref, bf16[192,512]{1,0:T(8,128)(2,1)S(1)} %collective-permute-done.12.other_ref, bf16[3,1024,512]{2,1,0:T(8,128)(2,1)S(1)} %copy-done, ...), custom_call_target="tpu_custom_call" | custom-call | flops 478150656 | bytes 7868416 | tf_op jit(solution)/shard_map/pallas_call | solution.py:29
  32.4 0.0 copy-start.2
  32.5 0.3 collective-permute-done.10.block_ref.mine_a
  32.7 1.5 %collective-permute-done.15.mine_b = bf16[96,512]{1,0:T(8,128)(2,1)S(1)} collective-permute-done((bf16[96,512]{1,0:T(8,128)(2,1)S(1)}, bf16[96,512]{1,0:T(8,128)(2,1)S(1)}, u32[]{:S(2)}, u32[]{:S(2)}) %collective-permute-start.15) | collective-permute-done | bytes 98336 | tf_op jit(solution)/shard_map/ppermute | solution.py:466
  34.3 0.0 collective-permute-start.16
  34.3 0.5 %collective-permute-start.14 = (bf16[96,512]{1,0:T(8,128)(2,1)S(1)}, bf16[96,512]{1,0:T(8,128)(2,1)S(1)}, u32[]{:S(2)}, u32[]{:S(2)}) collective-permute-start(bf16[96,512]{1,0:T(8,128)(2,1)S(1)} %collective-permute-done.10.block_ref.mine_a), channel_id=1, source_target_pairs={{0,1},{1,0},{2,3},{3,2},{4,5},{5,4},{6,7},{7,6},{8,9},{9,8},{10,11... | collective-permute-start | bytes 294920 | tf_op jit(solution)/shard_map/ppermute | solution.py:468
  34.8 0.4 shard_map.99
  35.2 0.4 collective-permute-done.16.other_b
  35.6 0.2 collective-permute-done.14.other_a
  35.7 1.4 %shard_map.100 = (bf16[2,64,1024]{2,1,0:T(8,128)(2,1)S(1)}, bf16[192,512]{1,0:T(8,128)(2,1)S(1)}) custom-call(bf16[96,512]{1,0:T(8,128)(2,1)S(1)} %collective-permute-done.14.other_a, bf16[96,512]{1,0:T(8,128)(2,1)S(1)} %collective-permute-done.16.other_b, f32[192,512]{1,0:T(8,128)S(1)} %get-tuple-element.91.keys_ref, ...), custom_call_target="tpu_custom_call" | custom-call | flops 612368384 | bytes 7995392 | tf_op jit(solution)/shard_map/pallas_call | solution.py:29
  37.1 0.0 copy-start.1
  37.1 0.4 collective-permute-start.17
  37.5 0.4 shard_map.101.keep_ref
  37.9 0.8 %collective-permute-done.17.got_ref = bf16[2,64,1024]{2,1,0:T(8,128)(2,1)S(1)} collective-permute-done((bf16[2,64,1024]{2,1,0:T(8,128)(2,1)S(1)}, bf16[2,64,1024]{2,1,0:T(8,128)(2,1)S(1)}, u32[]{:S(2)}, u32[]{:S(2)}) %collective-permute-start.17) | collective-permute-done | bytes 262176 | tf_op jit(solution)/shard_map/ppermute | solution.py:499
  38.7 0.0 copy-done.4
  38.7 0.5 %shard_map.102 = (bf16[96,256]{1,0:T(8,128)(2,1)S(1)}, bf16[96,256]{1,0:T(8,128)(2,1)S(1)}) custom-call(f32[2,64,1024]{2,1,0:T(8,128)S(1)} %shard_map.101.keep_ref, bf16[2,64,1024]{2,1,0:T(8,128)(2,1)S(1)} %collective-permute-done.17.got_ref, bf16[2,1024,256]{2,1,0:T(8,128)(2,1)S(1)} %copy-done.3, f32[2,2,256]{2,1,0:T(2,128)S(1)} %copy-done.4), custom_call_target="tpu_custom_call" | custom-call | flops 83886080 | bytes 1937408 | tf_op jit(solution)/shard_map/pallas_call | solution.py:29
  39.2 1.5 %collective-permute-start.18 = (bf16[96,256]{1,0:T(8,128)(2,1)S(1)}, bf16[96,256]{1,0:T(8,128)(2,1)S(1)}, u32[]{:S(2)}, u32[]{:S(2)}) collective-permute-start(bf16[96,256]{1,0:T(8,128)(2,1)S(1)} %get-tuple-element.98.first_ref), channel_id=1, source_target_pairs={{0,2},{2,4},{4,6},{6,8},{8,10},{10,12},{12,14},{3,1},{5,3},{7,5},{... | collective-permute-start | bytes 147464 | tf_op jit(solution)/shard_map/ppermute | solution.py:529
  40.7 0.6 %collective-permute-start.19 = (bf16[96,256]{1,0:T(8,128)(2,1)S(1)}, bf16[96,256]{1,0:T(8,128)(2,1)S(1)}, u32[]{:S(2)}, u32[]{:S(2)}) collective-permute-start(bf16[96,256]{1,0:T(8,128)(2,1)S(1)} %get-tuple-element.99.second_ref), channel_id=1, source_target_pairs={{1,3},{3,5},{5,7},{7,9},{9,11},{11,13},{13,15},{2,0},{4,2},{6,4},{... | collective-permute-start | bytes 147464 | tf_op jit(solution)/shard_map/ppermute | solution.py:528
  41.3 0.0 copy-done.1
  41.3 0.4 shard_map.103
  41.7 2.3 %collective-permute-done.18.got_first_ref = bf16[96,256]{1,0:T(8,128)(2,1)S(1)} collective-permute-done((bf16[96,256]{1,0:T(8,128)(2,1)S(1)}, bf16[96,256]{1,0:T(8,128)(2,1)S(1)}, u32[]{:S(2)}, u32[]{:S(2)}) %collective-permute-start.18) | collective-permute-done | bytes 49184 | tf_op jit(solution)/shard_map/ppermute | solution.py:529
  44.0 1.6 %collective-permute-done.19.got_second_ref = bf16[96,256]{1,0:T(8,128)(2,1)S(1)} collective-permute-done((bf16[96,256]{1,0:T(8,128)(2,1)S(1)}, bf16[96,256]{1,0:T(8,128)(2,1)S(1)}, u32[]{:S(2)}, u32[]{:S(2)}) %collective-permute-start.19) | collective-permute-done | bytes 49184 | tf_op jit(solution)/shard_map/ppermute | solution.py:528
  45.7 1.2 %shard_map.104 = (bf16[2,48,256]{2,1,0:T(8,128)(2,1)}, bf16[1,24,256]{2,1,0:T(8,128)(2,1)}) custom-call(bf16[96,256]{1,0:T(8,128)(2,1)S(1)} %collective-permute-done.18.got_first_ref, bf16[96,256]{1,0:T(8,128)(2,1)S(1)} %collective-permute-done.19.got_second_ref, f32[128,256]{1,0:T(8,128)S(1)} %get-tuple-element.100.own_fine_ref, ...), custom_call_target="tpu_custom_call" | custom-call | flops 75497472 | bytes 2686976 | tf_op jit(solution)/shard_map/pallas_call | solution.py:29
  (11 shorter events, 0.1 us)
Async XLA Ops:
  0.6 2.0 %copy-start.5 = (f32[1024]{0:T(1024)S(1)}, f32[1024]{0:T(1024)}, u32[]{:S(2)}) copy-start(f32[1024]{0:T(1024)} %gain_ref.3) | copy-start | bytes 12292
  0.6 4.4 %copy-start = (bf16[3,1024,512]{2,1,0:T(8,128)(2,1)S(1)}, bf16[3,1024,512]{2,1,0:T(8,128)(2,1)}, u32[]{:S(2)}) copy-start(bf16[3,1024,512]{2,1,0:T(8,128)(2,1)} %weight_ref.20) | copy-start | bytes 9437188
  0.6 2.0 %collective-permute-start = (f32[192,512]{1,0:T(8,128)}, f32[192,512]{1,0:T(8,128)S(1)}, u32[]{:S(2)}, u32[]{:S(2)}) collective-permute-start(f32[192,512]{1,0:T(8,128)} %tokens_ref.1), channel_id=1, source_target_pairs={{0,1},{1,0},{2,3},{3,2},{4,5},{5,4},{6,7},{7,6},{8,9},{9,8},{10,11... | collective-permute-start | bytes 1179656 | tf_op jit(solution)/shard_map/ppermute | solution.py:428
  0.7 1.1 %copy-start.6 = (f32[192,512]{1,0:T(8,128)S(1)}, f32[192,512]{1,0:T(8,128)}, u32[]{:S(2)}) copy-start(f32[192,512]{1,0:T(8,128)} %tokens_ref.1) | copy-start | bytes 1179652
  3.0 7.0 %collective-permute-start.1 = (bf16[192,512]{1,0:T(8,128)(2,1)S(1)}, bf16[192,512]{1,0:T(8,128)(2,1)S(1)}, u32[]{:S(2)}, u32[]{:S(2)}) collective-permute-start(bf16[192,512]{1,0:T(8,128)(2,1)S(1)} %get-tuple-element.54.mine_ref), channel_id=1, source_target_pairs={{2,0},{0,4},{4,8},{8,12},{12,14},{14,10},{10,6},{6,2},{3,1},{1,5},... | collective-permute-start | bytes 589832 | tf_op jit(solution)/shard_map/ppermute | solution.py:446
  3.6 6.7 %collective-permute-start.3 = (bf16[192,512]{1,0:T(8,128)(2,1)S(1)}, bf16[192,512]{1,0:T(8,128)(2,1)S(1)}, u32[]{:S(2)}, u32[]{:S(2)}) collective-permute-start(bf16[192,512]{1,0:T(8,128)(2,1)S(1)} %get-tuple-element.54.mine_ref), channel_id=1, source_target_pairs={{0,2},{4,0},{8,4},{12,8},{14,12},{10,14},{6,10},{2,6},{1,3},{5,1},... | collective-permute-start | bytes 589832 | tf_op jit(solution)/shard_map/ppermute | solution.py:447
  10.0 2.5 %collective-permute-start.5 = (bf16[192,512]{1,0:T(8,128)(2,1)S(1)}, bf16[192,512]{1,0:T(8,128)(2,1)S(1)}, u32[]{:S(2)}, u32[]{:S(2)}) collective-permute-start(bf16[192,512]{1,0:T(8,128)(2,1)S(1)} %collective-permute-done.1.block_ref.mine_ref), channel_id=1, source_target_pairs={{0,1},{1,0},{2,3},{3,2},{4,5},{5,4},{6,7},{7,6},{8,9},{9,8},{10,11... | collective-permute-start | bytes 589832 | tf_op jit(solution)/shard_map/ppermute | solution.py:468
  10.2 3.6 %collective-permute-start.4 = (bf16[192,512]{1,0:T(8,128)(2,1)S(1)}, bf16[192,512]{1,0:T(8,128)(2,1)S(1)}, u32[]{:S(2)}, u32[]{:S(2)}) collective-permute-start(bf16[192,512]{1,0:T(8,128)(2,1)S(1)} %collective-permute-done.3.mine_ref), channel_id=1, source_target_pairs={{0,1},{1,0},{2,3},{3,2},{4,5},{5,4},{6,7},{7,6},{8,9},{9,8},{10,11... | collective-permute-start | bytes 589832 | tf_op jit(solution)/shard_map/ppermute | solution.py:468
  10.5 7.1 %collective-permute-start.2 = (bf16[192,512]{1,0:T(8,128)(2,1)S(1)}, bf16[192,512]{1,0:T(8,128)(2,1)S(1)}, u32[]{:S(2)}, u32[]{:S(2)}) collective-permute-start(bf16[192,512]{1,0:T(8,128)(2,1)S(1)} %collective-permute-done.1.block_ref.mine_ref), channel_id=1, source_target_pairs={{2,0},{0,4},{4,8},{8,12},{12,14},{14,10},{10,6},{6,2},{3,1},{1,5},... | collective-permute-start | bytes 589832 | tf_op jit(solution)/shard_map/ppermute | solution.py:465
  11.8 7.0 %collective-permute-start.7 = (bf16[192,512]{1,0:T(8,128)(2,1)S(1)}, bf16[192,512]{1,0:T(8,128)(2,1)S(1)}, u32[]{:S(2)}, u32[]{:S(2)}) collective-permute-start(bf16[192,512]{1,0:T(8,128)(2,1)S(1)} %collective-permute-done.3.mine_ref), channel_id=1, source_target_pairs={{0,2},{4,0},{8,4},{12,8},{14,12},{10,14},{6,10},{2,6},{1,3},{5,1},... | collective-permute-start | bytes 589832 | tf_op jit(solution)/shard_map/ppermute | solution.py:466
  17.6 3.3 %collective-permute-start.9 = (bf16[192,512]{1,0:T(8,128)(2,1)S(1)}, bf16[192,512]{1,0:T(8,128)(2,1)S(1)}, u32[]{:S(2)}, u32[]{:S(2)}) collective-permute-start(bf16[192,512]{1,0:T(8,128)(2,1)S(1)} %collective-permute-done.2.block_ref.mine_ref), channel_id=1, source_target_pairs={{0,1},{1,0},{2,3},{3,2},{4,5},{5,4},{6,7},{7,6},{8,9},{9,8},{10,11... | collective-permute-start | bytes 589832 | tf_op jit(solution)/shard_map/ppermute | solution.py:468
  18.9 3.4 %collective-permute-start.8 = (bf16[192,512]{1,0:T(8,128)(2,1)S(1)}, bf16[192,512]{1,0:T(8,128)(2,1)S(1)}, u32[]{:S(2)}, u32[]{:S(2)}) collective-permute-start(bf16[192,512]{1,0:T(8,128)(2,1)S(1)} %collective-permute-done.7.mine_ref), channel_id=1, source_target_pairs={{0,1},{1,0},{2,3},{3,2},{4,5},{5,4},{6,7},{7,6},{8,9},{9,8},{10,11... | collective-permute-start | bytes 589832 | tf_op jit(solution)/shard_map/ppermute | solution.py:468
  18.9 7.3 %collective-permute-start.6 = (bf16[192,512]{1,0:T(8,128)(2,1)S(1)}, bf16[192,512]{1,0:T(8,128)(2,1)S(1)}, u32[]{:S(2)}, u32[]{:S(2)}) collective-permute-start(bf16[192,512]{1,0:T(8,128)(2,1)S(1)} %collective-permute-done.2.block_ref.mine_ref), channel_id=1, source_target_pairs={{2,0},{0,4},{4,8},{8,12},{12,14},{14,10},{10,6},{6,2},{3,1},{1,5},... | collective-permute-start | bytes 589832 | tf_op jit(solution)/shard_map/ppermute | solution.py:465
  20.4 7.0 %collective-permute-start.11 = (bf16[192,512]{1,0:T(8,128)(2,1)S(1)}, bf16[192,512]{1,0:T(8,128)(2,1)S(1)}, u32[]{:S(2)}, u32[]{:S(2)}) collective-permute-start(bf16[192,512]{1,0:T(8,128)(2,1)S(1)} %collective-permute-done.7.mine_ref), channel_id=1, source_target_pairs={{0,2},{4,0},{8,4},{12,8},{14,12},{10,14},{6,10},{2,6},{1,3},{5,1},... | collective-permute-start | bytes 589832 | tf_op jit(solution)/shard_map/ppermute | solution.py:466
  26.2 3.6 %collective-permute-start.13 = (bf16[192,512]{1,0:T(8,128)(2,1)S(1)}, bf16[192,512]{1,0:T(8,128)(2,1)S(1)}, u32[]{:S(2)}, u32[]{:S(2)}) collective-permute-start(bf16[192,512]{1,0:T(8,128)(2,1)S(1)} %collective-permute-done.6.block_ref.mine_ref), channel_id=1, source_target_pairs={{0,1},{1,0},{2,3},{3,2},{4,5},{5,4},{6,7},{7,6},{8,9},{9,8},{10,11... | collective-permute-start | bytes 589832 | tf_op jit(solution)/shard_map/ppermute | solution.py:468
  27.5 3.7 %collective-permute-start.12 = (bf16[192,512]{1,0:T(8,128)(2,1)S(1)}, bf16[192,512]{1,0:T(8,128)(2,1)S(1)}, u32[]{:S(2)}, u32[]{:S(2)}) collective-permute-start(bf16[192,512]{1,0:T(8,128)(2,1)S(1)} %collective-permute-done.11.mine_ref), channel_id=1, source_target_pairs={{0,1},{1,0},{2,3},{3,2},{4,5},{5,4},{6,7},{7,6},{8,9},{9,8},{10,11... | collective-permute-start | bytes 589832 | tf_op jit(solution)/shard_map/ppermute | solution.py:468
  27.5 5.3 %collective-permute-start.10 = (bf16[96,512]{1,0:T(8,128)(2,1)S(1)}, bf16[96,512]{1,0:T(8,128)(2,1)S(1)}, u32[]{:S(2)}, u32[]{:S(2)}) collective-permute-start(bf16[96,512]{1,0:T(8,128)(2,1)S(1)} %slice.6), channel_id=1, source_target_pairs={{2,0},{0,4},{4,8},{8,12},{12,14},{14,10},{10,6},{6,2},{3,1},{1,5},... | collective-permute-start | bytes 294920 | tf_op jit(solution)/shard_map/ppermute | solution.py:465
  29.1 5.1 %collective-permute-start.15 = (bf16[96,512]{1,0:T(8,128)(2,1)S(1)}, bf16[96,512]{1,0:T(8,128)(2,1)S(1)}, u32[]{:S(2)}, u32[]{:S(2)}) collective-permute-start(bf16[96,512]{1,0:T(8,128)(2,1)S(1)} %slice.7), channel_id=1, source_target_pairs={{0,2},{4,0},{8,4},{12,8},{14,12},{10,14},{6,10},{2,6},{1,3},{5,1},... | collective-permute-start | bytes 294920 | tf_op jit(solution)/shard_map/ppermute | solution.py:466
  32.4 3.3 %copy-start.2 = (bf16[512,1024]{1,0:T(8,128)(2,1)S(1)}, bf16[512,1024]{1,0:T(8,128)(2,1)}, u32[]{:S(2)}) copy-start(bf16[512,1024]{1,0:T(8,128)(2,1)} %weight_ref.21) | copy-start | bytes 3145732
  34.3 1.3 %collective-permute-start.16 = (bf16[96,512]{1,0:T(8,128)(2,1)S(1)}, bf16[96,512]{1,0:T(8,128)(2,1)S(1)}, u32[]{:S(2)}, u32[]{:S(2)}) collective-permute-start(bf16[96,512]{1,0:T(8,128)(2,1)S(1)} %collective-permute-done.15.mine_b), channel_id=1, source_target_pairs={{0,1},{1,0},{2,3},{3,2},{4,5},{5,4},{6,7},{7,6},{8,9},{9,8},{10,11... | collective-permute-start | bytes 294920 | tf_op jit(solution)/shard_map/ppermute | solution.py:468
  34.3 1.5 %collective-permute-start.14 = (bf16[96,512]{1,0:T(8,128)(2,1)S(1)}, bf16[96,512]{1,0:T(8,128)(2,1)S(1)}, u32[]{:S(2)}, u32[]{:S(2)}) collective-permute-start(bf16[96,512]{1,0:T(8,128)(2,1)S(1)} %collective-permute-done.10.block_ref.mine_a), channel_id=1, source_target_pairs={{0,1},{1,0},{2,3},{3,2},{4,5},{5,4},{6,7},{7,6},{8,9},{9,8},{10,11... | collective-permute-start | bytes 294920 | tf_op jit(solution)/shard_map/ppermute | solution.py:468
  35.7 3.0 %copy-start.3 = (bf16[2,1024,256]{2,1,0:T(8,128)(2,1)S(1)}, bf16[2,1024,256]{2,1,0:T(8,128)(2,1)}, u32[]{:S(2)}) copy-start(bf16[2,1024,256]{2,1,0:T(8,128)(2,1)} %lateral_ref.1) | copy-start | bytes 3145732
  35.7 3.0 %copy-start.4 = (f32[2,2,256]{2,1,0:T(2,128)S(1)}, f32[2,2,256]{2,1,0:T(2,128)}, u32[]{:S(2)}) copy-start(f32[2,2,256]{2,1,0:T(2,128)} %gain_ref.5) | copy-start | bytes 12292
  37.1 4.2 %copy-start.1 = (bf16[2,3,3,256,256]{4,3,2,1,0:T(8,128)(2,1)S(1)}, bf16[2,3,3,256,256]{4,3,2,1,0:T(8,128)(2,1)}, u32[]{:S(2)}) copy-start(bf16[2,3,3,256,256]{4,3,2,1,0:T(8,128)(2,1)} %weight_ref.23) | copy-start | bytes 7077892
  37.1 1.6 %collective-permute-start.17 = (bf16[2,64,1024]{2,1,0:T(8,128)(2,1)S(1)}, bf16[2,64,1024]{2,1,0:T(8,128)(2,1)S(1)}, u32[]{:S(2)}, u32[]{:S(2)}) collective-permute-start(bf16[2,64,1024]{2,1,0:T(8,128)(2,1)S(1)} %get-tuple-element.97), channel_id=1, source_target_pairs={{0,1},{1,0},{2,3},{3,2},{4,5},{5,4},{6,7},{7,6},{8,9},{9,8},{10,11... | collective-permute-start | bytes 786440 | tf_op jit(solution)/shard_map/ppermute | solution.py:499
  39.2 4.8 %collective-permute-start.18 = (bf16[96,256]{1,0:T(8,128)(2,1)S(1)}, bf16[96,256]{1,0:T(8,128)(2,1)S(1)}, u32[]{:S(2)}, u32[]{:S(2)}) collective-permute-start(bf16[96,256]{1,0:T(8,128)(2,1)S(1)} %get-tuple-element.98.first_ref), channel_id=1, source_target_pairs={{0,2},{2,4},{4,6},{6,8},{8,10},{10,12},{12,14},{3,1},{5,3},{7,5},{... | collective-permute-start | bytes 147464 | tf_op jit(solution)/shard_map/ppermute | solution.py:529
  40.7 5.0 %collective-permute-start.19 = (bf16[96,256]{1,0:T(8,128)(2,1)S(1)}, bf16[96,256]{1,0:T(8,128)(2,1)S(1)}, u32[]{:S(2)}, u32[]{:S(2)}) collective-permute-start(bf16[96,256]{1,0:T(8,128)(2,1)S(1)} %get-tuple-element.99.second_ref), channel_id=1, source_target_pairs={{1,3},{3,5},{5,7},{7,9},{9,11},{11,13},{13,15},{2,0},{4,2},{6,4},{... | collective-permute-start | bytes 147464 | tf_op jit(solution)/shard_map/ppermute | solution.py:528

commit v9 on v8

--- a/solution.py
+++ b/solution.py
@@ -16,23 +16,23 @@
 MIB = 1024 * 1024
 
 
-def specs(count):
-    return [pl.BlockSpec(memory_space=pltpu.VMEM)] * count
+def specs(count, space):
+    return [pl.BlockSpec(memory_space=space)] * count
 
 
 def nbytes(*arrays):
     return sum(math.prod(a.shape) * jnp.dtype(a.dtype).itemsize for a in arrays)
 
 
-def call(kernel, outs, args, scratch=(), flops=0, exps=0, limit=24):
+def call(kernel, outs, args, scratch=(), flops=0, exps=0, out_space=pltpu.VMEM):
     outs = tuple(jax.ShapeDtypeStruct(shape, dtype) for shape, dtype in outs)
     return pl.pallas_call(
         kernel,
         out_shape=outs,
-        in_specs=specs(len(args)),
-        out_specs=tuple(specs(len(outs))),
+        in_specs=specs(len(args), pltpu.VMEM),
+        out_specs=tuple(specs(len(outs), out_space)),
         scratch_shapes=list(scratch),
-        compiler_params=pltpu.CompilerParams(vmem_limit_bytes=limit * MIB),
+        compiler_params=pltpu.CompilerParams(vmem_limit_bytes=24 * MIB),
         cost_estimate=pl.CostEstimate(
             flops=flops, transcendentals=exps, bytes_accessed=nbytes(*args, *outs)
         ),
@@ -312,6 +312,9 @@
     edge_in,
     fine_sum,
     coarse_sum,
+    fine_out,
+    coarse_out,
+    sems,
 ):
     core = lax.axis_index("head")
     block = lax.axis_index("blk")
@@ -338,16 +341,26 @@
             edge_in[rows + window :], weight_ref[1, 2, tap_col]
         )
 
-    fine_sum[...] = own_fine_ref[...] + joined(fine_terms, window)
-    coarse_sum[...] = own_coarse_ref[...] + joined(coarse_terms, window // 2)
     cols = fine_ref.shape[1]
     shift = GRID_COLS - window
     inset = cols - shift
+    copies = [
+        pltpu.make_async_copy(source.at[row], target.at[row], sems.at[place])
+        for place, (source, target, row) in enumerate(
+            [(fine_out, fine_ref, 0), (fine_out, fine_ref, 1), (coarse_out, coarse_ref, 0)]
+        )
+    ]
+    fine_sum[...] = own_fine_ref[...] + joined(fine_terms, window)
     for row in range(2):
         here = pl.ds(pl.multiple_of(row * window + core * inset, 8), cols)
-        fine_ref[row] = layer_norm(fine_sum[here, :], gain_ref[0, 1][None, :]).astype(BF16)
+        fine_out[row] = layer_norm(fine_sum[here, :], gain_ref[0, 1][None, :]).astype(BF16)
+        copies[row].start()
+    coarse_sum[...] = own_coarse_ref[...] + joined(coarse_terms, window // 2)
     here = pl.ds(pl.multiple_of(core * (inset // 2), 8), cols // 2)
-    coarse_ref[0] = layer_norm(coarse_sum[here, :], gain_ref[1, 1][None, :]).astype(BF16)
+    coarse_out[0] = layer_norm(coarse_sum[here, :], gain_ref[1, 1][None, :]).astype(BF16)
+    copies[2].start()
+    for copy in copies:
+        copy.wait()
 
 
 def attend_shared(queries, keys, values):
@@ -454,13 +467,14 @@
             exps=heads * rows * rows,
         )
         last = blocks // 2
+        cut = 2 * rows // 3
         for step in range(1, last + 1):
             ahead, state[0] = lax.optimization_barrier((ahead, state[0]))
             behind, state[0] = lax.optimization_barrier((behind, state[0]))
             arrived = ahead, behind
             (mark,) = call(mark_kernel, [((16, LANES), BF16)], (ahead,))
             if step == last - 1:
-                ahead, behind = ahead[: rows // 2], behind[rows // 2 :]
+                ahead, behind = ahead[:cut], behind[cut:]
             if step < last:
                 ahead = lax.ppermute(ahead, "blk", forth)
                 behind = lax.ppermute(behind, "blk", back)
@@ -535,13 +549,20 @@
         [pltpu.VMEM((2 * window, channels), BF16)],
         flops=27 * window * channels * channels,
     )
+    outs = [
+        ((grid_rows, cols, channels), BF16),
+        ((grid_rows // 2, cols // 2, channels), BF16),
+    ]
+    scratch = [pltpu.VMEM(shape, dtype) for shape, dtype in sums + outs]
     return call(
         conv_kernel,
-        [((grid_rows, cols, channels), BF16), ((grid_rows // 2, cols // 2, channels), BF16)],
+        outs,
         (got_first, got_second, *own_sums, conv_weight, level_gains),
         [pltpu.VMEM((2 * message[0], channels), BF16)]
-        + [pltpu.VMEM(shape, dtype) for shape, dtype in sums],
+        + scratch
+        + [pltpu.SemaphoreType.DMA((3,))],
         flops=18 * window * channels * channels,
+        out_space=pl.ANY,
     )
 
 

time: 47.7 us -> 47.5 us (level); the launches traced: 46.8 us -> 47.3 us
    ppermute x3, waiting for transfers between devices: 4.12 us -> 2.75 us  [body(): behind = lax.ppermute(behind, 'blk', back)]
    ppermute x1, starting transfers between devices: 1.46 us -> 2.56 us  [body(): got_first = lax.ppermute(first, ('blk', 'head'), down_then_up[0])]
    ppermute x1, waiting for transfers between devices: 1.64 us -> 2.71 us  [body(): got_second = lax.ppermute(second, ('blk', 'head'), down_then_up[1])]
    ppermute x3, waiting for transfers between devices: 5.26 us -> 5.98 us  [body(): ahead = lax.ppermute(ahead, 'blk', forth)]
    ppermute x1, starting transfers between devices: 0.62 us -> 0.01 us  [body(): got_second = lax.ppermute(second, ('blk', 'head'), down_then_up[1])]
    ppermute x4, starting transfers between devices: 0.52 us -> 0.01 us  [body(): lax.ppermute(arrived[0], 'head', swap)]
  transfers between devices with their start and end apart: 20 -> 20, of which waited for: 14 -> 13; matrix products, arithmetic and copies ran while one was open for 0% -> 0% of each run, Pallas kernels for 22% -> 22%
where the time goes in v9:
time: 47.5 us; the launch traced here: 47.3 us
  waiting for transfers between devices  19.2 us (40%)
  Pallas kernels  13.9 us (29%)
  starting transfers between devices  12.1 us (25%)
  local copies, waits for them, and re-layouts  1.18 us (2%)
  between operations  0.99 us (2%)
    pallas_call x19, Pallas kernels, call(): pl.pallas_call(kernel, out_shape=outs, in_specs=specs(len(args), pltpu.VM...  13.9 us
    ppermute x3, waiting for transfers between devices, body(): ahead = lax.ppermute(ahead, 'blk', forth)  5.98 us
    ppermute x3, starting transfers between devices, body(): ahead = lax.ppermute(ahead, 'blk', forth)  4.53 us
    ppermute x1, waiting for transfers between devices, body(): ahead = lax.ppermute(mine, 'blk', forth)  3.5 us
    ppermute x3, waiting for transfers between devices, body(): behind = lax.ppermute(behind, 'blk', back)  2.75 us
    ppermute x1, waiting for transfers between devices, body(): got_second = lax.ppermute(second, ('blk', 'head'), down_then_up[1])  2.71 us
    ppermute x1, starting transfers between devices, body(): got_first = lax.ppermute(first, ('blk', 'head'), down_then_up[0])  2.56 us
    ppermute x1, waiting for transfers between devices, body(): got_first = lax.ppermute(first, ('blk', 'head'), down_then_up[0])  1.9 us
  transfers between devices with their start and end apart: 20, of which 13 were waited for; matrix products, arithmetic and copies ran while one was open for 0% of the time, Pallas kernels for 22%

profile of v9, /device:TPU:6, one launch (start us, length us, event | category | flops | bytes accessed | tf_op | source)
XLA Modules:
  0.0 47.3 jit_solution(8899220983377684125)
XLA Ops:
  0.6 0.0 copy-start.5
  0.6 0.0 copy-start
  0.6 0.1 collective-permute-start
  0.7 0.0 copy-start.6
  0.7 1.1 %copy-done.6 = f32[192,512]{1,0:T(8,128)S(1)} copy-done((f32[192,512]{1,0:T(8,128)S(1)}, f32[192,512]{1,0:T(8,128)}, u32[]{:S(2)}) %copy-start.6) | copy-done | bytes 393240
  1.9 0.7 %collective-permute-done.other_ref = f32[192,512]{1,0:T(8,128)S(1)} collective-permute-done((f32[192,512]{1,0:T(8,128)}, f32[192,512]{1,0:T(8,128)S(1)}, u32[]{:S(2)}, u32[]{:S(2)}) %collective-permute-start) | collective-permute-done | bytes 393248 | tf_op jit(solution)/shard_map/ppermute | solution.py:441
  2.6 0.0 copy-done.5
  2.7 0.3 shard_map.87
  3.0 0.6 %collective-permute-start.1 = (bf16[192,512]{1,0:T(8,128)(2,1)S(1)}, bf16[192,512]{1,0:T(8,128)(2,1)S(1)}, u32[]{:S(2)}, u32[]{:S(2)}) collective-permute-start(bf16[192,512]{1,0:T(8,128)(2,1)S(1)} %get-tuple-element.54.mine_ref), channel_id=1, source_target_pairs={{2,0},{0,4},{4,8},{8,12},{12,14},{14,10},{10,6},{6,2},{3,1},{1,5},... | collective-permute-start | bytes 589832 | tf_op jit(solution)/shard_map/ppermute | solution.py:459
  3.6 1.5 %collective-permute-start.3 = (bf16[192,512]{1,0:T(8,128)(2,1)S(1)}, bf16[192,512]{1,0:T(8,128)(2,1)S(1)}, u32[]{:S(2)}, u32[]{:S(2)}) collective-permute-start(bf16[192,512]{1,0:T(8,128)(2,1)S(1)} %get-tuple-element.54.mine_ref), channel_id=1, source_target_pairs={{0,2},{4,0},{8,4},{12,8},{14,12},{10,14},{6,10},{2,6},{1,3},{5,1},... | collective-permute-start | bytes 589832 | tf_op jit(solution)/shard_map/ppermute | solution.py:460
  5.1 0.0 copy-done
  5.1 1.4 %shard_map.88 = (bf16[4,384,128]{2,1,0:T(8,128)(2,1)S(1)}, f32[4,384,128]{2,1,0:T(8,128)S(1)}, f32[4,384,128]{2,1,0:T(8,128)S(1)}, f32[4,192,128]{2,1,0:T(8,128)S(1)}) custom-call(bf16[192,512]{1,0:T(8,128)(2,1)S(1)} %get-tuple-element.54.mine_ref, bf16[192,512]{1,0:T(8,128)(2,1)S(1)} %get-tuple-element.55.other_ref, bf16[3,1024,512]{2,1,0:T(8,128)(2,1)S(1)} %copy-done), custom_call_target="tpu_custom_call" | custom-call | flops 679477248 | bytes 5898240 | tf_op jit(solution)/shard_map/pallas_call | solution.py:29
  6.5 3.5 %collective-permute-done.1.block_ref.mine_ref = bf16[192,512]{1,0:T(8,128)(2,1)S(1)} collective-permute-done((bf16[192,512]{1,0:T(8,128)(2,1)S(1)}, bf16[192,512]{1,0:T(8,128)(2,1)S(1)}, u32[]{:S(2)}, u32[]{:S(2)}) %collective-permute-start.1) | collective-permute-done | bytes 196640 | tf_op jit(solution)/shard_map/ppermute | solution.py:459
  10.0 0.0 collective-permute-start.5
  10.0 0.3 collective-permute-done.3.mine_ref
  10.2 0.3 collective-permute-start.4
  10.5 1.3 %collective-permute-start.2 = (bf16[192,512]{1,0:T(8,128)(2,1)S(1)}, bf16[192,512]{1,0:T(8,128)(2,1)S(1)}, u32[]{:S(2)}, u32[]{:S(2)}) collective-permute-start(bf16[192,512]{1,0:T(8,128)(2,1)S(1)} %collective-permute-done.1.block_ref.mine_ref), channel_id=1, source_target_pairs={{2,0},{0,4},{4,8},{8,12},{12,14},{14,10},{10,6},{6,2},{3,1},{1,5},... | collective-permute-start | bytes 589832 | tf_op jit(solution)/shard_map/ppermute | solution.py:479
  11.8 0.7 %collective-permute-start.7 = (bf16[192,512]{1,0:T(8,128)(2,1)S(1)}, bf16[192,512]{1,0:T(8,128)(2,1)S(1)}, u32[]{:S(2)}, u32[]{:S(2)}) collective-permute-start(bf16[192,512]{1,0:T(8,128)(2,1)S(1)} %collective-permute-done.3.mine_ref), channel_id=1, source_target_pairs={{0,2},{4,0},{8,4},{12,8},{14,12},{10,14},{6,10},{2,6},{1,3},{5,1},... | collective-permute-start | bytes 589832 | tf_op jit(solution)/shard_map/ppermute | solution.py:480
  12.5 0.0 collective-permute-done.5.other_ref
  12.5 1.3 %shard_map.90 = (f32[4,384,128]{2,1,0:T(8,128)S(1)}, f32[4,384,128]{2,1,0:T(8,128)S(1)}, f32[4,192,128]{2,1,0:T(8,128)S(1)}) custom-call(bf16[192,512]{1,0:T(8,128)(2,1)S(1)} %collective-permute-done.1.block_ref.mine_ref, bf16[192,512]{1,0:T(8,128)(2,1)S(1)} %collective-permute-done.5.other_ref, bf16[3,1024,512]{2,1,0:T(8,128)(2,1)S(1)} %copy-done, ...), custom_call_target="tpu_custom_call" | custom-call | flops 478150656 | bytes 7868416 | tf_op jit(solution)/shard_map/pallas_call | solution.py:29
  13.9 0.0 collective-permute-done.4.other_ref
  13.9 1.3 %shard_map.91 = (f32[4,384,128]{2,1,0:T(8,128)S(1)}, f32[4,384,128]{2,1,0:T(8,128)S(1)}, f32[4,192,128]{2,1,0:T(8,128)S(1)}) custom-call(bf16[192,512]{1,0:T(8,128)(2,1)S(1)} %collective-permute-done.3.mine_ref, bf16[192,512]{1,0:T(8,128)(2,1)S(1)} %collective-permute-done.4.other_ref, bf16[3,1024,512]{2,1,0:T(8,128)(2,1)S(1)} %copy-done, ...), custom_call_target="tpu_custom_call" | custom-call | flops 478150656 | bytes 7868416 | tf_op jit(solution)/shard_map/pallas_call | solution.py:29
  15.2 2.4 %collective-permute-done.2.block_ref.mine_ref = bf16[192,512]{1,0:T(8,128)(2,1)S(1)} collective-permute-done((bf16[192,512]{1,0:T(8,128)(2,1)S(1)}, bf16[192,512]{1,0:T(8,128)(2,1)S(1)}, u32[]{:S(2)}, u32[]{:S(2)}) %collective-permute-start.2) | collective-permute-done | bytes 196640 | tf_op jit(solution)/shard_map/ppermute | solution.py:479
  17.6 0.0 collective-permute-start.9
  17.6 1.3 %collective-permute-done.7.mine_ref = bf16[192,512]{1,0:T(8,128)(2,1)S(1)} collective-permute-done((bf16[192,512]{1,0:T(8,128)(2,1)S(1)}, bf16[192,512]{1,0:T(8,128)(2,1)S(1)}, u32[]{:S(2)}, u32[]{:S(2)}) %collective-permute-start.7) | collective-permute-done | bytes 196640 | tf_op jit(solution)/shard_map/ppermute | solution.py:480
  18.9 0.0 collective-permute-start.8
  18.9 1.6 %collective-permute-start.6 = (bf16[192,512]{1,0:T(8,128)(2,1)S(1)}, bf16[192,512]{1,0:T(8,128)(2,1)S(1)}, u32[]{:S(2)}, u32[]{:S(2)}) collective-permute-start(bf16[192,512]{1,0:T(8,128)(2,1)S(1)} %collective-permute-done.2.block_ref.mine_ref), channel_id=1, source_target_pairs={{2,0},{0,4},{4,8},{8,12},{12,14},{14,10},{10,6},{6,2},{3,1},{1,5},... | collective-permute-start | bytes 589832 | tf_op jit(solution)/shard_map/ppermute | solution.py:479
  20.4 0.4 collective-permute-start.11
  20.9 0.0 collective-permute-done.9.other_ref
  20.9 1.3 %shard_map.93 = (f32[4,384,128]{2,1,0:T(8,128)S(1)}, f32[4,384,128]{2,1,0:T(8,128)S(1)}, f32[4,192,128]{2,1,0:T(8,128)S(1)}) custom-call(bf16[192,512]{1,0:T(8,128)(2,1)S(1)} %collective-permute-done.2.block_ref.mine_ref, bf16[192,512]{1,0:T(8,128)(2,1)S(1)} %collective-permute-done.9.other_ref, bf16[3,1024,512]{2,1,0:T(8,128)(2,1)S(1)} %copy-done, ...), custom_call_target="tpu_custom_call" | custom-call | flops 478150656 | bytes 7868416 | tf_op jit(solution)/shard_map/pallas_call | solution.py:29
  22.2 0.0 collective-permute-done.8.other_ref
  22.2 1.3 %shard_map.94 = (f32[4,384,128]{2,1,0:T(8,128)S(1)}, f32[4,384,128]{2,1,0:T(8,128)S(1)}, f32[4,192,128]{2,1,0:T(8,128)S(1)}) custom-call(bf16[192,512]{1,0:T(8,128)(2,1)S(1)} %collective-permute-done.7.mine_ref, bf16[192,512]{1,0:T(8,128)(2,1)S(1)} %collective-permute-done.8.other_ref, bf16[3,1024,512]{2,1,0:T(8,128)(2,1)S(1)} %copy-done, ...), custom_call_target="tpu_custom_call" | custom-call | flops 478150656 | bytes 7868416 | tf_op jit(solution)/shard_map/pallas_call | solution.py:29
  23.5 2.6 %collective-permute-done.6.block_ref.mine_ref = bf16[192,512]{1,0:T(8,128)(2,1)S(1)} collective-permute-done((bf16[192,512]{1,0:T(8,128)(2,1)S(1)}, bf16[192,512]{1,0:T(8,128)(2,1)S(1)}, u32[]{:S(2)}, u32[]{:S(2)}) %collective-permute-start.6) | collective-permute-done | bytes 196640 | tf_op jit(solution)/shard_map/ppermute | solution.py:479
  26.2 0.0 collective-permute-start.13
  26.2 1.3 %collective-permute-done.11.mine_ref = bf16[192,512]{1,0:T(8,128)(2,1)S(1)} collective-permute-done((bf16[192,512]{1,0:T(8,128)(2,1)S(1)}, bf16[192,512]{1,0:T(8,128)(2,1)S(1)}, u32[]{:S(2)}, u32[]{:S(2)}) %collective-permute-start.11) | collective-permute-done | bytes 196640 | tf_op jit(solution)/shard_map/ppermute | solution.py:480
  27.5 0.0 collective-permute-start.12
  27.5 1.6 %collective-permute-start.10 = (bf16[128,512]{1,0:T(8,128)(2,1)S(1)}, bf16[128,512]{1,0:T(8,128)(2,1)S(1)}, u32[]{:S(2)}, u32[]{:S(2)}) collective-permute-start(bf16[128,512]{1,0:T(8,128)(2,1)S(1)} %slice.6), channel_id=1, source_target_pairs={{2,0},{0,4},{4,8},{8,12},{12,14},{14,10},{10,6},{6,2},{3,1},{1,5},... | collective-permute-start | bytes 393224 | tf_op jit(solution)/shard_map/ppermute | solution.py:479
  29.1 0.7 %collective-permute-start.15 = (bf16[64,512]{1,0:T(8,128)(2,1)S(1)}, bf16[64,512]{1,0:T(8,128)(2,1)S(1)}, u32[]{:S(2)}, u32[]{:S(2)}) collective-permute-start(bf16[64,512]{1,0:T(8,128)(2,1)S(1)} %slice.7), channel_id=1, source_target_pairs={{0,2},{4,0},{8,4},{12,8},{14,12},{10,14},{6,10},{2,6},{1,3},{5,1},... | collective-permute-start | bytes 196616 | tf_op jit(solution)/shard_map/ppermute | solution.py:480
  29.8 0.0 collective-permute-done.13.other_ref
  29.8 1.3 %shard_map.96 = (f32[4,384,128]{2,1,0:T(8,128)S(1)}, f32[4,384,128]{2,1,0:T(8,128)S(1)}, f32[4,192,128]{2,1,0:T(8,128)S(1)}) custom-call(bf16[192,512]{1,0:T(8,128)(2,1)S(1)} %collective-permute-done.6.block_ref.mine_ref, bf16[192,512]{1,0:T(8,128)(2,1)S(1)} %collective-permute-done.13.other_ref, bf16[3,1024,512]{2,1,0:T(8,128)(2,1)S(1)} %copy-done, ...), custom_call_target="tpu_custom_call" | custom-call | flops 478150656 | bytes 7868416 | tf_op jit(solution)/shard_map/pallas_call | solution.py:29
  31.1 0.0 collective-permute-done.12.other_ref
  31.1 1.3 %shard_map.97 = (f32[4,384,128]{2,1,0:T(8,128)S(1)}, f32[4,384,128]{2,1,0:T(8,128)S(1)}, f32[4,192,128]{2,1,0:T(8,128)S(1)}) custom-call(bf16[192,512]{1,0:T(8,128)(2,1)S(1)} %collective-permute-done.11.mine_ref, bf16[192,512]{1,0:T(8,128)(2,1)S(1)} %collective-permute-done.12.other_ref, bf16[3,1024,512]{2,1,0:T(8,128)(2,1)S(1)} %copy-done, ...), custom_call_target="tpu_custom_call" | custom-call | flops 478150656 | bytes 7868416 | tf_op jit(solution)/shard_map/pallas_call | solution.py:29
  32.4 0.0 copy-start.2
  32.5 1.0 %collective-permute-done.10.block_ref.mine_a = bf16[128,512]{1,0:T(8,128)(2,1)S(1)} collective-permute-done((bf16[128,512]{1,0:T(8,128)(2,1)S(1)}, bf16[128,512]{1,0:T(8,128)(2,1)S(1)}, u32[]{:S(2)}, u32[]{:S(2)}) %collective-permute-start.10) | collective-permute-done | bytes 131104 | tf_op jit(solution)/shard_map/ppermute | solution.py:479
  33.4 0.0 collective-permute-start.14
  33.5 0.2 collective-permute-done.15.mine_b
  33.6 0.3 collective-permute-start.16
  34.0 0.4 shard_map.99
  34.3 0.5 %collective-permute-done.16.other_b = bf16[64,512]{1,0:T(8,128)(2,1)S(1)} collective-permute-done((bf16[64,512]{1,0:T(8,128)(2,1)S(1)}, bf16[64,512]{1,0:T(8,128)(2,1)S(1)}, u32[]{:S(2)}, u32[]{:S(2)}) %collective-permute-start.16) | collective-permute-done | bytes 65568 | tf_op jit(solution)/shard_map/ppermute | solution.py:482
  34.9 0.0 collective-permute-done.14.other_a
  34.9 0.0 copy-done.2
  34.9 0.0 copy-start.4
  34.9 1.4 %shard_map.100 = (bf16[2,64,1024]{2,1,0:T(8,128)(2,1)S(1)}, bf16[192,512]{1,0:T(8,128)(2,1)S(1)}) custom-call(bf16[128,512]{1,0:T(8,128)(2,1)S(1)} %collective-permute-done.14.other_a, bf16[64,512]{1,0:T(8,128)(2,1)S(1)} %collective-permute-done.16.other_b, f32[192,512]{1,0:T(8,128)S(1)} %get-tuple-element.91.keys_ref, ...), custom_call_target="tpu_custom_call" | custom-call | flops 612368384 | bytes 7995392 | tf_op jit(solution)/shard_map/pallas_call | solution.py:29
  36.3 0.0 copy-start.1
  36.3 0.4 collective-permute-start.17
  36.7 0.4 shard_map.101.keep_ref
  37.1 0.8 %collective-permute-done.17.got_ref = bf16[2,64,1024]{2,1,0:T(8,128)(2,1)S(1)} collective-permute-done((bf16[2,64,1024]{2,1,0:T(8,128)(2,1)S(1)}, bf16[2,64,1024]{2,1,0:T(8,128)(2,1)S(1)}, u32[]{:S(2)}, u32[]{:S(2)}) %collective-permute-start.17) | collective-permute-done | bytes 262176 | tf_op jit(solution)/shard_map/ppermute | solution.py:513
  37.9 0.5 %shard_map.102 = (bf16[96,256]{1,0:T(8,128)(2,1)S(1)}, bf16[96,256]{1,0:T(8,128)(2,1)S(1)}) custom-call(f32[2,64,1024]{2,1,0:T(8,128)S(1)} %shard_map.101.keep_ref, bf16[2,64,1024]{2,1,0:T(8,128)(2,1)S(1)} %collective-permute-done.17.got_ref, bf16[2,1024,256]{2,1,0:T(8,128)(2,1)S(1)} %copy-done.3, f32[2,2,256]{2,1,0:T(2,128)S(1)} %copy-done.4), custom_call_target="tpu_custom_call" | custom-call | flops 83886080 | bytes 1937408 | tf_op jit(solution)/shard_map/pallas_call | solution.py:29
  38.4 2.6 %collective-permute-start.18 = (bf16[96,256]{1,0:T(8,128)(2,1)S(1)}, bf16[96,256]{1,0:T(8,128)(2,1)S(1)}, u32[]{:S(2)}, u32[]{:S(2)}) collective-permute-start(bf16[96,256]{1,0:T(8,128)(2,1)S(1)} %get-tuple-element.98.first_ref), channel_id=1, source_target_pairs={{0,2},{2,4},{4,6},{6,8},{8,10},{10,12},{12,14},{3,1},{5,3},{7,5},{... | collective-permute-start | bytes 147464 | tf_op jit(solution)/shard_map/ppermute | solution.py:543
  41.0 0.0 collective-permute-start.19
  41.0 0.4 shard_map.103
  41.4 1.9 %collective-permute-done.18.got_first_ref = bf16[96,256]{1,0:T(8,128)(2,1)S(1)} collective-permute-done((bf16[96,256]{1,0:T(8,128)(2,1)S(1)}, bf16[96,256]{1,0:T(8,128)(2,1)S(1)}, u32[]{:S(2)}, u32[]{:S(2)}) %collective-permute-start.18) | collective-permute-done | bytes 49184 | tf_op jit(solution)/shard_map/ppermute | solution.py:543
  43.3 2.7 %collective-permute-done.19.got_second_ref = bf16[96,256]{1,0:T(8,128)(2,1)S(1)} collective-permute-done((bf16[96,256]{1,0:T(8,128)(2,1)S(1)}, bf16[96,256]{1,0:T(8,128)(2,1)S(1)}, u32[]{:S(2)}, u32[]{:S(2)}) %collective-permute-start.19) | collective-permute-done | bytes 49184 | tf_op jit(solution)/shard_map/ppermute | solution.py:542
  46.0 1.2 %shard_map.104 = (bf16[2,48,256]{2,1,0:T(8,128)(2,1)}, bf16[1,24,256]{2,1,0:T(8,128)(2,1)}) custom-call(bf16[96,256]{1,0:T(8,128)(2,1)S(1)} %collective-permute-done.18.got_first_ref, bf16[96,256]{1,0:T(8,128)(2,1)S(1)} %collective-permute-done.19.got_second_ref, f32[128,256]{1,0:T(8,128)S(1)} %get-tuple-element.100.own_fine_ref, ...), custom_call_target="tpu_custom_call" | custom-call | flops 75497472 | bytes 2686976 | tf_op jit(solution)/shard_map/pallas_call | solution.py:29
  (11 shorter events, 0.1 us)
Async XLA Ops:
  0.6 2.0 %copy-start.5 = (f32[1024]{0:T(1024)S(1)}, f32[1024]{0:T(1024)}, u32[]{:S(2)}) copy-start(f32[1024]{0:T(1024)} %gain_ref.3) | copy-start | bytes 12292
  0.6 4.4 %copy-start = (bf16[3,1024,512]{2,1,0:T(8,128)(2,1)S(1)}, bf16[3,1024,512]{2,1,0:T(8,128)(2,1)}, u32[]{:S(2)}) copy-start(bf16[3,1024,512]{2,1,0:T(8,128)(2,1)} %weight_ref.20) | copy-start | bytes 9437188
  0.6 2.0 %collective-permute-start = (f32[192,512]{1,0:T(8,128)}, f32[192,512]{1,0:T(8,128)S(1)}, u32[]{:S(2)}, u32[]{:S(2)}) collective-permute-start(f32[192,512]{1,0:T(8,128)} %tokens_ref.1), channel_id=1, source_target_pairs={{0,1},{1,0},{2,3},{3,2},{4,5},{5,4},{6,7},{7,6},{8,9},{9,8},{10,11... | collective-permute-start | bytes 1179656 | tf_op jit(solution)/shard_map/ppermute | solution.py:441
  0.7 1.1 %copy-start.6 = (f32[192,512]{1,0:T(8,128)S(1)}, f32[192,512]{1,0:T(8,128)}, u32[]{:S(2)}) copy-start(f32[192,512]{1,0:T(8,128)} %tokens_ref.1) | copy-start | bytes 1179652
  3.0 7.0 %collective-permute-start.1 = (bf16[192,512]{1,0:T(8,128)(2,1)S(1)}, bf16[192,512]{1,0:T(8,128)(2,1)S(1)}, u32[]{:S(2)}, u32[]{:S(2)}) collective-permute-start(bf16[192,512]{1,0:T(8,128)(2,1)S(1)} %get-tuple-element.54.mine_ref), channel_id=1, source_target_pairs={{2,0},{0,4},{4,8},{8,12},{12,14},{14,10},{10,6},{6,2},{3,1},{1,5},... | collective-permute-start | bytes 589832 | tf_op jit(solution)/shard_map/ppermute | solution.py:459
  3.6 6.7 %collective-permute-start.3 = (bf16[192,512]{1,0:T(8,128)(2,1)S(1)}, bf16[192,512]{1,0:T(8,128)(2,1)S(1)}, u32[]{:S(2)}, u32[]{:S(2)}) collective-permute-start(bf16[192,512]{1,0:T(8,128)(2,1)S(1)} %get-tuple-element.54.mine_ref), channel_id=1, source_target_pairs={{0,2},{4,0},{8,4},{12,8},{14,12},{10,14},{6,10},{2,6},{1,3},{5,1},... | collective-permute-start | bytes 589832 | tf_op jit(solution)/shard_map/ppermute | solution.py:460
  10.0 2.5 %collective-permute-start.5 = (bf16[192,512]{1,0:T(8,128)(2,1)S(1)}, bf16[192,512]{1,0:T(8,128)(2,1)S(1)}, u32[]{:S(2)}, u32[]{:S(2)}) collective-permute-start(bf16[192,512]{1,0:T(8,128)(2,1)S(1)} %collective-permute-done.1.block_ref.mine_ref), channel_id=1, source_target_pairs={{0,1},{1,0},{2,3},{3,2},{4,5},{5,4},{6,7},{7,6},{8,9},{9,8},{10,11... | collective-permute-start | bytes 589832 | tf_op jit(solution)/shard_map/ppermute | solution.py:482
  10.2 3.6 %collective-permute-start.4 = (bf16[192,512]{1,0:T(8,128)(2,1)S(1)}, bf16[192,512]{1,0:T(8,128)(2,1)S(1)}, u32[]{:S(2)}, u32[]{:S(2)}) collective-permute-start(bf16[192,512]{1,0:T(8,128)(2,1)S(1)} %collective-permute-done.3.mine_ref), channel_id=1, source_target_pairs={{0,1},{1,0},{2,3},{3,2},{4,5},{5,4},{6,7},{7,6},{8,9},{9,8},{10,11... | collective-permute-start | bytes 589832 | tf_op jit(solution)/shard_map/ppermute | solution.py:482
  10.5 7.1 %collective-permute-start.2 = (bf16[192,512]{1,0:T(8,128)(2,1)S(1)}, bf16[192,512]{1,0:T(8,128)(2,1)S(1)}, u32[]{:S(2)}, u32[]{:S(2)}) collective-permute-start(bf16[192,512]{1,0:T(8,128)(2,1)S(1)} %collective-permute-done.1.block_ref.mine_ref), channel_id=1, source_target_pairs={{2,0},{0,4},{4,8},{8,12},{12,14},{14,10},{10,6},{6,2},{3,1},{1,5},... | collective-permute-start | bytes 589832 | tf_op jit(solution)/shard_map/ppermute | solution.py:479
  11.8 7.0 %collective-permute-start.7 = (bf16[192,512]{1,0:T(8,128)(2,1)S(1)}, bf16[192,512]{1,0:T(8,128)(2,1)S(1)}, u32[]{:S(2)}, u32[]{:S(2)}) collective-permute-start(bf16[192,512]{1,0:T(8,128)(2,1)S(1)} %collective-permute-done.3.mine_ref), channel_id=1, source_target_pairs={{0,2},{4,0},{8,4},{12,8},{14,12},{10,14},{6,10},{2,6},{1,3},{5,1},... | collective-permute-start | bytes 589832 | tf_op jit(solution)/shard_map/ppermute | solution.py:480
  17.6 3.3 %collective-permute-start.9 = (bf16[192,512]{1,0:T(8,128)(2,1)S(1)}, bf16[192,512]{1,0:T(8,128)(2,1)S(1)}, u32[]{:S(2)}, u32[]{:S(2)}) collective-permute-start(bf16[192,512]{1,0:T(8,128)(2,1)S(1)} %collective-permute-done.2.block_ref.mine_ref), channel_id=1, source_target_pairs={{0,1},{1,0},{2,3},{3,2},{4,5},{5,4},{6,7},{7,6},{8,9},{9,8},{10,11... | collective-permute-start | bytes 589832 | tf_op jit(solution)/shard_map/ppermute | solution.py:482
  18.9 3.4 %collective-permute-start.8 = (bf16[192,512]{1,0:T(8,128)(2,1)S(1)}, bf16[192,512]{1,0:T(8,128)(2,1)S(1)}, u32[]{:S(2)}, u32[]{:S(2)}) collective-permute-start(bf16[192,512]{1,0:T(8,128)(2,1)S(1)} %collective-permute-done.7.mine_ref), channel_id=1, source_target_pairs={{0,1},{1,0},{2,3},{3,2},{4,5},{5,4},{6,7},{7,6},{8,9},{9,8},{10,11... | collective-permute-start | bytes 589832 | tf_op jit(solution)/shard_map/ppermute | solution.py:482
  18.9 7.3 %collective-permute-start.6 = (bf16[192,512]{1,0:T(8,128)(2,1)S(1)}, bf16[192,512]{1,0:T(8,128)(2,1)S(1)}, u32[]{:S(2)}, u32[]{:S(2)}) collective-permute-start(bf16[192,512]{1,0:T(8,128)(2,1)S(1)} %collective-permute-done.2.block_ref.mine_ref), channel_id=1, source_target_pairs={{2,0},{0,4},{4,8},{8,12},{12,14},{14,10},{10,6},{6,2},{3,1},{1,5},... | collective-permute-start | bytes 589832 | tf_op jit(solution)/shard_map/ppermute | solution.py:479
  20.4 7.0 %collective-permute-start.11 = (bf16[192,512]{1,0:T(8,128)(2,1)S(1)}, bf16[192,512]{1,0:T(8,128)(2,1)S(1)}, u32[]{:S(2)}, u32[]{:S(2)}) collective-permute-start(bf16[192,512]{1,0:T(8,128)(2,1)S(1)} %collective-permute-done.7.mine_ref), channel_id=1, source_target_pairs={{0,2},{4,0},{8,4},{12,8},{14,12},{10,14},{6,10},{2,6},{1,3},{5,1},... | collective-permute-start | bytes 589832 | tf_op jit(solution)/shard_map/ppermute | solution.py:480
  26.2 3.6 %collective-permute-start.13 = (bf16[192,512]{1,0:T(8,128)(2,1)S(1)}, bf16[192,512]{1,0:T(8,128)(2,1)S(1)}, u32[]{:S(2)}, u32[]{:S(2)}) collective-permute-start(bf16[192,512]{1,0:T(8,128)(2,1)S(1)} %collective-permute-done.6.block_ref.mine_ref), channel_id=1, source_target_pairs={{0,1},{1,0},{2,3},{3,2},{4,5},{5,4},{6,7},{7,6},{8,9},{9,8},{10,11... | collective-permute-start | bytes 589832 | tf_op jit(solution)/shard_map/ppermute | solution.py:482
  27.5 3.7 %collective-permute-start.12 = (bf16[192,512]{1,0:T(8,128)(2,1)S(1)}, bf16[192,512]{1,0:T(8,128)(2,1)S(1)}, u32[]{:S(2)}, u32[]{:S(2)}) collective-permute-start(bf16[192,512]{1,0:T(8,128)(2,1)S(1)} %collective-permute-done.11.mine_ref), channel_id=1, source_target_pairs={{0,1},{1,0},{2,3},{3,2},{4,5},{5,4},{6,7},{7,6},{8,9},{9,8},{10,11... | collective-permute-start | bytes 589832 | tf_op jit(solution)/shard_map/ppermute | solution.py:482
  27.5 6.0 %collective-permute-start.10 = (bf16[128,512]{1,0:T(8,128)(2,1)S(1)}, bf16[128,512]{1,0:T(8,128)(2,1)S(1)}, u32[]{:S(2)}, u32[]{:S(2)}) collective-permute-start(bf16[128,512]{1,0:T(8,128)(2,1)S(1)} %slice.6), channel_id=1, source_target_pairs={{2,0},{0,4},{4,8},{8,12},{12,14},{14,10},{10,6},{6,2},{3,1},{1,5},... | collective-permute-start | bytes 393224 | tf_op jit(solution)/shard_map/ppermute | solution.py:479
  29.1 4.5 %collective-permute-start.15 = (bf16[64,512]{1,0:T(8,128)(2,1)S(1)}, bf16[64,512]{1,0:T(8,128)(2,1)S(1)}, u32[]{:S(2)}, u32[]{:S(2)}) collective-permute-start(bf16[64,512]{1,0:T(8,128)(2,1)S(1)} %slice.7), channel_id=1, source_target_pairs={{0,2},{4,0},{8,4},{12,8},{14,12},{10,14},{6,10},{2,6},{1,3},{5,1},... | collective-permute-start | bytes 196616 | tf_op jit(solution)/shard_map/ppermute | solution.py:480
  32.4 2.4 %copy-start.2 = (bf16[512,1024]{1,0:T(8,128)(2,1)S(1)}, bf16[512,1024]{1,0:T(8,128)(2,1)}, u32[]{:S(2)}) copy-start(bf16[512,1024]{1,0:T(8,128)(2,1)} %weight_ref.21) | copy-start | bytes 3145732
  33.4 1.4 %collective-permute-start.14 = (bf16[128,512]{1,0:T(8,128)(2,1)S(1)}, bf16[128,512]{1,0:T(8,128)(2,1)S(1)}, u32[]{:S(2)}, u32[]{:S(2)}) collective-permute-start(bf16[128,512]{1,0:T(8,128)(2,1)S(1)} %collective-permute-done.10.block_ref.mine_a), channel_id=1, source_target_pairs={{0,1},{1,0},{2,3},{3,2},{4,5},{5,4},{6,7},{7,6},{8,9},{9,8},{10,11... | collective-permute-start | bytes 393224 | tf_op jit(solution)/shard_map/ppermute | solution.py:482
  33.6 1.3 %collective-permute-start.16 = (bf16[64,512]{1,0:T(8,128)(2,1)S(1)}, bf16[64,512]{1,0:T(8,128)(2,1)S(1)}, u32[]{:S(2)}, u32[]{:S(2)}) collective-permute-start(bf16[64,512]{1,0:T(8,128)(2,1)S(1)} %collective-permute-done.15.mine_b), channel_id=1, source_target_pairs={{0,1},{1,0},{2,3},{3,2},{4,5},{5,4},{6,7},{7,6},{8,9},{9,8},{10,11... | collective-permute-start | bytes 196616 | tf_op jit(solution)/shard_map/ppermute | solution.py:482
  34.9 3.0 %copy-start.3 = (bf16[2,1024,256]{2,1,0:T(8,128)(2,1)S(1)}, bf16[2,1024,256]{2,1,0:T(8,128)(2,1)}, u32[]{:S(2)}) copy-start(bf16[2,1024,256]{2,1,0:T(8,128)(2,1)} %lateral_ref.1) | copy-start | bytes 3145732
  34.9 3.0 %copy-start.4 = (f32[2,2,256]{2,1,0:T(2,128)S(1)}, f32[2,2,256]{2,1,0:T(2,128)}, u32[]{:S(2)}) copy-start(f32[2,2,256]{2,1,0:T(2,128)} %gain_ref.5) | copy-start | bytes 12292
  36.3 4.7 %copy-start.1 = (bf16[2,3,3,256,256]{4,3,2,1,0:T(8,128)(2,1)S(1)}, bf16[2,3,3,256,256]{4,3,2,1,0:T(8,128)(2,1)}, u32[]{:S(2)}) copy-start(bf16[2,3,3,256,256]{4,3,2,1,0:T(8,128)(2,1)} %weight_ref.23) | copy-start | bytes 7077892
  36.3 1.6 %collective-permute-start.17 = (bf16[2,64,1024]{2,1,0:T(8,128)(2,1)S(1)}, bf16[2,64,1024]{2,1,0:T(8,128)(2,1)S(1)}, u32[]{:S(2)}, u32[]{:S(2)}) collective-permute-start(bf16[2,64,1024]{2,1,0:T(8,128)(2,1)S(1)} %get-tuple-element.97), channel_id=1, source_target_pairs={{0,1},{1,0},{2,3},{3,2},{4,5},{5,4},{6,7},{7,6},{8,9},{9,8},{10,11... | collective-permute-start | bytes 786440 | tf_op jit(solution)/shard_map/ppermute | solution.py:513
  38.4 4.8 %collective-permute-start.18 = (bf16[96,256]{1,0:T(8,128)(2,1)S(1)}, bf16[96,256]{1,0:T(8,128)(2,1)S(1)}, u32[]{:S(2)}, u32[]{:S(2)}) collective-permute-start(bf16[96,256]{1,0:T(8,128)(2,1)S(1)} %get-tuple-element.98.first_ref), channel_id=1, source_target_pairs={{0,2},{2,4},{4,6},{6,8},{8,10},{10,12},{12,14},{3,1},{5,3},{7,5},{... | collective-permute-start | bytes 147464 | tf_op jit(solution)/shard_map/ppermute | solution.py:543
  41.0 5.0 %collective-permute-start.19 = (bf16[96,256]{1,0:T(8,128)(2,1)S(1)}, bf16[96,256]{1,0:T(8,128)(2,1)S(1)}, u32[]{:S(2)}, u32[]{:S(2)}) collective-permute-start(bf16[96,256]{1,0:T(8,128)(2,1)S(1)} %get-tuple-element.99.second_ref), channel_id=1, source_target_pairs={{1,3},{3,5},{5,7},{7,9},{9,11},{11,13},{13,15},{2,0},{4,2},{6,4},{... | collective-permute-start | bytes 147464 | tf_op jit(solution)/shard_map/ppermute | solution.py:542

commit v10 on v8

--- a/solution.py
+++ b/solution.py
@@ -24,7 +24,7 @@
     return sum(math.prod(a.shape) * jnp.dtype(a.dtype).itemsize for a in arrays)
 
 
-def call(kernel, outs, args, scratch=(), flops=0, exps=0, limit=24):
+def call(kernel, outs, args, scratch=(), flops=0, exps=0):
     outs = tuple(jax.ShapeDtypeStruct(shape, dtype) for shape, dtype in outs)
     return pl.pallas_call(
         kernel,
@@ -32,7 +32,7 @@
         in_specs=specs(len(args)),
         out_specs=tuple(specs(len(outs))),
         scratch_shapes=list(scratch),
-        compiler_params=pltpu.CompilerParams(vmem_limit_bytes=limit * MIB),
+        compiler_params=pltpu.CompilerParams(vmem_limit_bytes=24 * MIB),
         cost_estimate=pl.CostEstimate(
             flops=flops, transcendentals=exps, bytes_accessed=nbytes(*args, *outs)
         ),
@@ -338,11 +338,11 @@
             edge_in[rows + window :], weight_ref[1, 2, tap_col]
         )
 
-    fine_sum[...] = own_fine_ref[...] + joined(fine_terms, window)
-    coarse_sum[...] = own_coarse_ref[...] + joined(coarse_terms, window // 2)
     cols = fine_ref.shape[1]
     shift = GRID_COLS - window
     inset = cols - shift
+    fine_sum[...] = own_fine_ref[...] + joined(fine_terms, window)
+    coarse_sum[...] = own_coarse_ref[...] + joined(coarse_terms, window // 2)
     for row in range(2):
         here = pl.ds(pl.multiple_of(row * window + core * inset, 8), cols)
         fine_ref[row] = layer_norm(fine_sum[here, :], gain_ref[0, 1][None, :]).astype(BF16)
@@ -454,13 +454,14 @@
             exps=heads * rows * rows,
         )
         last = blocks // 2
+        cut = 5 * rows // 6
         for step in range(1, last + 1):
             ahead, state[0] = lax.optimization_barrier((ahead, state[0]))
             behind, state[0] = lax.optimization_barrier((behind, state[0]))
             arrived = ahead, behind
             (mark,) = call(mark_kernel, [((16, LANES), BF16)], (ahead,))
             if step == last - 1:
-                ahead, behind = ahead[: rows // 2], behind[rows // 2 :]
+                ahead, behind = ahead[:cut], behind[cut:]
             if step < last:
                 ahead = lax.ppermute(ahead, "blk", forth)
                 behind = lax.ppermute(behind, "blk", back)

time: 47.7 us -> 51.7 us (1.084); the launches traced: 46.8 us -> 51.5 us
  waiting for transfers between devices: 19.2 us -> 24.3 us
    ppermute x3, waiting for transfers between devices: 5.26 us -> 7.37 us  [body(): ahead = lax.ppermute(ahead, 'blk', forth)]
    ppermute x3, waiting for transfers between devices: 4.12 us -> 6.05 us  [body(): behind = lax.ppermute(behind, 'blk', back)]
    ppermute x1, starting transfers between devices: 1.46 us -> 2.56 us  [body(): got_first = lax.ppermute(first, ('blk', 'head'), down_then_up[0])]
    ppermute x1, waiting for transfers between devices: 1.64 us -> 2.53 us  [body(): got_second = lax.ppermute(second, ('blk', 'head'), down_then_up[1])]
    ppermute x1, starting transfers between devices: 0.62 us -> 0.01 us  [body(): got_second = lax.ppermute(second, ('blk', 'head'), down_then_up[1])]
  transfers between devices with their start and end apart: 20 -> 20, of which waited for: 14 -> 13; matrix products, arithmetic and copies ran while one was open for 0% -> 0% of each run, Pallas kernels for 22% -> 20%
where the time goes in v10:
time: 51.7 us; the launch traced here: 51.5 us
  waiting for transfers between devices  24.3 us (47%)
  Pallas kernels  13.8 us (27%)
  starting transfers between devices  11.3 us (22%)
  local copies, waits for them, and re-layouts  1.18 us (2%)
  between operations  0.83 us (2%)
    pallas_call x19, Pallas kernels, call(): pl.pallas_call(kernel, out_shape=outs, in_specs=specs(len(args)), out_spe...  13.8 us
    ppermute x3, waiting for transfers between devices, body(): ahead = lax.ppermute(ahead, 'blk', forth)  7.37 us
    ppermute x3, waiting for transfers between devices, body(): behind = lax.ppermute(behind, 'blk', back)  6.05 us
    ppermute x3, starting transfers between devices, body(): ahead = lax.ppermute(ahead, 'blk', forth)  4.53 us
    ppermute x1, waiting for transfers between devices, body(): ahead = lax.ppermute(mine, 'blk', forth)  3.5 us
    ppermute x1, starting transfers between devices, body(): got_first = lax.ppermute(first, ('blk', 'head'), down_then_up[0])  2.56 us
    ppermute x1, waiting for transfers between devices, body(): got_second = lax.ppermute(second, ('blk', 'head'), down_then_up[1])  2.53 us
    ppermute x1, waiting for transfers between devices, body(): got_first = lax.ppermute(first, ('blk', 'head'), down_then_up[0])  2.07 us
  transfers between devices with their start and end apart: 20, of which 13 were waited for; matrix products, arithmetic and copies ran while one was open for 0% of the time, Pallas kernels for 20%

profile of v10, /device:TPU:6, one launch (start us, length us, event | category | flops | bytes accessed | tf_op | source)
XLA Modules:
  0.0 51.5 jit_solution(1375142177100723129)
XLA Ops:
  0.6 0.0 copy-start.5
  0.6 0.0 copy-start
  0.6 0.1 collective-permute-start
  0.7 0.0 copy-start.6
  0.7 1.1 %copy-done.6 = f32[192,512]{1,0:T(8,128)S(1)} copy-done((f32[192,512]{1,0:T(8,128)S(1)}, f32[192,512]{1,0:T(8,128)}, u32[]{:S(2)}) %copy-start.6) | copy-done | bytes 393240
  1.9 0.7 %collective-permute-done.other_ref = f32[192,512]{1,0:T(8,128)S(1)} collective-permute-done((f32[192,512]{1,0:T(8,128)}, f32[192,512]{1,0:T(8,128)S(1)}, u32[]{:S(2)}, u32[]{:S(2)}) %collective-permute-start) | collective-permute-done | bytes 393248 | tf_op jit(solution)/shard_map/ppermute | solution.py:428
  2.6 0.0 copy-done.5
  2.7 0.3 shard_map.87
  3.0 0.6 %collective-permute-start.1 = (bf16[192,512]{1,0:T(8,128)(2,1)S(1)}, bf16[192,512]{1,0:T(8,128)(2,1)S(1)}, u32[]{:S(2)}, u32[]{:S(2)}) collective-permute-start(bf16[192,512]{1,0:T(8,128)(2,1)S(1)} %get-tuple-element.54.mine_ref), channel_id=1, source_target_pairs={{2,0},{0,4},{4,8},{8,12},{12,14},{14,10},{10,6},{6,2},{3,1},{1,5},... | collective-permute-start | bytes 589832 | tf_op jit(solution)/shard_map/ppermute | solution.py:446
  3.6 1.5 %collective-permute-start.3 = (bf16[192,512]{1,0:T(8,128)(2,1)S(1)}, bf16[192,512]{1,0:T(8,128)(2,1)S(1)}, u32[]{:S(2)}, u32[]{:S(2)}) collective-permute-start(bf16[192,512]{1,0:T(8,128)(2,1)S(1)} %get-tuple-element.54.mine_ref), channel_id=1, source_target_pairs={{0,2},{4,0},{8,4},{12,8},{14,12},{10,14},{6,10},{2,6},{1,3},{5,1},... | collective-permute-start | bytes 589832 | tf_op jit(solution)/shard_map/ppermute | solution.py:447
  5.1 0.0 copy-done
  5.1 1.4 %shard_map.88 = (bf16[4,384,128]{2,1,0:T(8,128)(2,1)S(1)}, f32[4,384,128]{2,1,0:T(8,128)S(1)}, f32[4,384,128]{2,1,0:T(8,128)S(1)}, f32[4,192,128]{2,1,0:T(8,128)S(1)}) custom-call(bf16[192,512]{1,0:T(8,128)(2,1)S(1)} %get-tuple-element.54.mine_ref, bf16[192,512]{1,0:T(8,128)(2,1)S(1)} %get-tuple-element.55.other_ref, bf16[3,1024,512]{2,1,0:T(8,128)(2,1)S(1)} %copy-done), custom_call_target="tpu_custom_call" | custom-call | flops 679477248 | bytes 5898240 | tf_op jit(solution)/shard_map/pallas_call | solution.py:29
  6.5 3.5 %collective-permute-done.1.block_ref.mine_ref = bf16[192,512]{1,0:T(8,128)(2,1)S(1)} collective-permute-done((bf16[192,512]{1,0:T(8,128)(2,1)S(1)}, bf16[192,512]{1,0:T(8,128)(2,1)S(1)}, u32[]{:S(2)}, u32[]{:S(2)}) %collective-permute-start.1) | collective-permute-done | bytes 196640 | tf_op jit(solution)/shard_map/ppermute | solution.py:446
  10.0 0.0 collective-permute-start.5
  10.0 0.3 collective-permute-done.3.mine_ref
  10.2 0.3 collective-permute-start.4
  10.5 1.3 %collective-permute-start.2 = (bf16[192,512]{1,0:T(8,128)(2,1)S(1)}, bf16[192,512]{1,0:T(8,128)(2,1)S(1)}, u32[]{:S(2)}, u32[]{:S(2)}) collective-permute-start(bf16[192,512]{1,0:T(8,128)(2,1)S(1)} %collective-permute-done.1.block_ref.mine_ref), channel_id=1, source_target_pairs={{2,0},{0,4},{4,8},{8,12},{12,14},{14,10},{10,6},{6,2},{3,1},{1,5},... | collective-permute-start | bytes 589832 | tf_op jit(solution)/shard_map/ppermute | solution.py:466
  11.8 0.7 %collective-permute-start.7 = (bf16[192,512]{1,0:T(8,128)(2,1)S(1)}, bf16[192,512]{1,0:T(8,128)(2,1)S(1)}, u32[]{:S(2)}, u32[]{:S(2)}) collective-permute-start(bf16[192,512]{1,0:T(8,128)(2,1)S(1)} %collective-permute-done.3.mine_ref), channel_id=1, source_target_pairs={{0,2},{4,0},{8,4},{12,8},{14,12},{10,14},{6,10},{2,6},{1,3},{5,1},... | collective-permute-start | bytes 589832 | tf_op jit(solution)/shard_map/ppermute | solution.py:467
  12.5 0.0 collective-permute-done.5.other_ref
  12.5 1.3 %shard_map.90 = (f32[4,384,128]{2,1,0:T(8,128)S(1)}, f32[4,384,128]{2,1,0:T(8,128)S(1)}, f32[4,192,128]{2,1,0:T(8,128)S(1)}) custom-call(bf16[192,512]{1,0:T(8,128)(2,1)S(1)} %collective-permute-done.1.block_ref.mine_ref, bf16[192,512]{1,0:T(8,128)(2,1)S(1)} %collective-permute-done.5.other_ref, bf16[3,1024,512]{2,1,0:T(8,128)(2,1)S(1)} %copy-done, ...), custom_call_target="tpu_custom_call" | custom-call | flops 478150656 | bytes 7868416 | tf_op jit(solution)/shard_map/pallas_call | solution.py:29
  13.9 0.0 collective-permute-done.4.other_ref
  13.9 1.3 %shard_map.91 = (f32[4,384,128]{2,1,0:T(8,128)S(1)}, f32[4,384,128]{2,1,0:T(8,128)S(1)}, f32[4,192,128]{2,1,0:T(8,128)S(1)}) custom-call(bf16[192,512]{1,0:T(8,128)(2,1)S(1)} %collective-permute-done.3.mine_ref, bf16[192,512]{1,0:T(8,128)(2,1)S(1)} %collective-permute-done.4.other_ref, bf16[3,1024,512]{2,1,0:T(8,128)(2,1)S(1)} %copy-done, ...), custom_call_target="tpu_custom_call" | custom-call | flops 478150656 | bytes 7868416 | tf_op jit(solution)/shard_map/pallas_call | solution.py:29
  15.2 2.4 %collective-permute-done.2.block_ref.mine_ref = bf16[192,512]{1,0:T(8,128)(2,1)S(1)} collective-permute-done((bf16[192,512]{1,0:T(8,128)(2,1)S(1)}, bf16[192,512]{1,0:T(8,128)(2,1)S(1)}, u32[]{:S(2)}, u32[]{:S(2)}) %collective-permute-start.2) | collective-permute-done | bytes 196640 | tf_op jit(solution)/shard_map/ppermute | solution.py:466
  17.6 0.0 collective-permute-start.9
  17.6 1.3 %collective-permute-done.7.mine_ref = bf16[192,512]{1,0:T(8,128)(2,1)S(1)} collective-permute-done((bf16[192,512]{1,0:T(8,128)(2,1)S(1)}, bf16[192,512]{1,0:T(8,128)(2,1)S(1)}, u32[]{:S(2)}, u32[]{:S(2)}) %collective-permute-start.7) | collective-permute-done | bytes 196640 | tf_op jit(solution)/shard_map/ppermute | solution.py:467
  18.9 0.0 collective-permute-start.8
  18.9 1.6 %collective-permute-start.6 = (bf16[192,512]{1,0:T(8,128)(2,1)S(1)}, bf16[192,512]{1,0:T(8,128)(2,1)S(1)}, u32[]{:S(2)}, u32[]{:S(2)}) collective-permute-start(bf16[192,512]{1,0:T(8,128)(2,1)S(1)} %collective-permute-done.2.block_ref.mine_ref), channel_id=1, source_target_pairs={{2,0},{0,4},{4,8},{8,12},{12,14},{14,10},{10,6},{6,2},{3,1},{1,5},... | collective-permute-start | bytes 589832 | tf_op jit(solution)/shard_map/ppermute | solution.py:466
  20.4 0.4 collective-permute-start.11
  20.9 0.0 collective-permute-done.9.other_ref
  20.9 1.3 %shard_map.93 = (f32[4,384,128]{2,1,0:T(8,128)S(1)}, f32[4,384,128]{2,1,0:T(8,128)S(1)}, f32[4,192,128]{2,1,0:T(8,128)S(1)}) custom-call(bf16[192,512]{1,0:T(8,128)(2,1)S(1)} %collective-permute-done.2.block_ref.mine_ref, bf16[192,512]{1,0:T(8,128)(2,1)S(1)} %collective-permute-done.9.other_ref, bf16[3,1024,512]{2,1,0:T(8,128)(2,1)S(1)} %copy-done, ...), custom_call_target="tpu_custom_call" | custom-call | flops 478150656 | bytes 7868416 | tf_op jit(solution)/shard_map/pallas_call | solution.py:29
  22.2 0.0 collective-permute-done.8.other_ref
  22.2 1.3 %shard_map.94 = (f32[4,384,128]{2,1,0:T(8,128)S(1)}, f32[4,384,128]{2,1,0:T(8,128)S(1)}, f32[4,192,128]{2,1,0:T(8,128)S(1)}) custom-call(bf16[192,512]{1,0:T(8,128)(2,1)S(1)} %collective-permute-done.7.mine_ref, bf16[192,512]{1,0:T(8,128)(2,1)S(1)} %collective-permute-done.8.other_ref, bf16[3,1024,512]{2,1,0:T(8,128)(2,1)S(1)} %copy-done, ...), custom_call_target="tpu_custom_call" | custom-call | flops 478150656 | bytes 7868416 | tf_op jit(solution)/shard_map/pallas_call | solution.py:29
  23.5 2.6 %collective-permute-done.6.block_ref.mine_ref = bf16[192,512]{1,0:T(8,128)(2,1)S(1)} collective-permute-done((bf16[192,512]{1,0:T(8,128)(2,1)S(1)}, bf16[192,512]{1,0:T(8,128)(2,1)S(1)}, u32[]{:S(2)}, u32[]{:S(2)}) %collective-permute-start.6) | collective-permute-done | bytes 196640 | tf_op jit(solution)/shard_map/ppermute | solution.py:466
  26.2 0.0 collective-permute-start.13
  26.2 1.3 %collective-permute-done.11.mine_ref = bf16[192,512]{1,0:T(8,128)(2,1)S(1)} collective-permute-done((bf16[192,512]{1,0:T(8,128)(2,1)S(1)}, bf16[192,512]{1,0:T(8,128)(2,1)S(1)}, u32[]{:S(2)}, u32[]{:S(2)}) %collective-permute-start.11) | collective-permute-done | bytes 196640 | tf_op jit(solution)/shard_map/ppermute | solution.py:467
  27.5 0.0 collective-permute-start.12
  27.5 1.6 %collective-permute-start.10 = (bf16[160,512]{1,0:T(8,128)(2,1)S(1)}, bf16[160,512]{1,0:T(8,128)(2,1)S(1)}, u32[]{:S(2)}, u32[]{:S(2)}) collective-permute-start(bf16[160,512]{1,0:T(8,128)(2,1)S(1)} %slice.6), channel_id=1, source_target_pairs={{2,0},{0,4},{4,8},{8,12},{12,14},{14,10},{10,6},{6,2},{3,1},{1,5},... | collective-permute-start | bytes 491528 | tf_op jit(solution)/shard_map/ppermute | solution.py:466
  29.1 0.0 collective-permute-done.13.other_ref
  29.1 1.3 %shard_map.96 = (f32[4,384,128]{2,1,0:T(8,128)S(1)}, f32[4,384,128]{2,1,0:T(8,128)S(1)}, f32[4,192,128]{2,1,0:T(8,128)S(1)}) custom-call(bf16[192,512]{1,0:T(8,128)(2,1)S(1)} %collective-permute-done.6.block_ref.mine_ref, bf16[192,512]{1,0:T(8,128)(2,1)S(1)} %collective-permute-done.13.other_ref, bf16[3,1024,512]{2,1,0:T(8,128)(2,1)S(1)} %copy-done, ...), custom_call_target="tpu_custom_call" | custom-call | flops 478150656 | bytes 7868416 | tf_op jit(solution)/shard_map/pallas_call | solution.py:29
  30.4 0.0 collective-permute-done.12.other_ref
  30.5 1.3 %shard_map.97 = (f32[4,384,128]{2,1,0:T(8,128)S(1)}, f32[4,384,128]{2,1,0:T(8,128)S(1)}, f32[4,192,128]{2,1,0:T(8,128)S(1)}) custom-call(bf16[192,512]{1,0:T(8,128)(2,1)S(1)} %collective-permute-done.11.mine_ref, bf16[192,512]{1,0:T(8,128)(2,1)S(1)} %collective-permute-done.12.other_ref, bf16[3,1024,512]{2,1,0:T(8,128)(2,1)S(1)} %copy-done, ...), custom_call_target="tpu_custom_call" | custom-call | flops 478150656 | bytes 7868416 | tf_op jit(solution)/shard_map/pallas_call | solution.py:29
  31.8 0.0 copy-start.2
  31.8 2.4 %collective-permute-done.10.block_ref.mine_a = bf16[160,512]{1,0:T(8,128)(2,1)S(1)} collective-permute-done((bf16[160,512]{1,0:T(8,128)(2,1)S(1)}, bf16[160,512]{1,0:T(8,128)(2,1)S(1)}, u32[]{:S(2)}, u32[]{:S(2)}) %collective-permute-start.10) | collective-permute-done | bytes 163872 | tf_op jit(solution)/shard_map/ppermute | solution.py:466
  34.2 0.0 collective-permute-start.14
  34.2 0.5 collective-permute-start.15
  34.6 3.5 %collective-permute-done.15.mine_b = bf16[32,512]{1,0:T(8,128)(2,1)S(1)} collective-permute-done((bf16[32,512]{1,0:T(8,128)(2,1)S(1)}, bf16[32,512]{1,0:T(8,128)(2,1)S(1)}, u32[]{:S(2)}, u32[]{:S(2)}) %collective-permute-start.15) | collective-permute-done | bytes 32800 | tf_op jit(solution)/shard_map/ppermute | solution.py:467
  38.1 0.0 collective-permute-start.16
  38.1 0.4 shard_map.99
  38.5 0.8 %collective-permute-done.16.other_b = bf16[32,512]{1,0:T(8,128)(2,1)S(1)} collective-permute-done((bf16[32,512]{1,0:T(8,128)(2,1)S(1)}, bf16[32,512]{1,0:T(8,128)(2,1)S(1)}, u32[]{:S(2)}, u32[]{:S(2)}) %collective-permute-start.16) | collective-permute-done | bytes 32800 | tf_op jit(solution)/shard_map/ppermute | solution.py:469
  39.3 0.0 collective-permute-done.14.other_a
  39.3 0.0 copy-done.2
  39.3 0.0 copy-start.4
  39.3 1.4 %shard_map.100 = (bf16[2,64,1024]{2,1,0:T(8,128)(2,1)S(1)}, bf16[192,512]{1,0:T(8,128)(2,1)S(1)}) custom-call(bf16[160,512]{1,0:T(8,128)(2,1)S(1)} %collective-permute-done.14.other_a, bf16[32,512]{1,0:T(8,128)(2,1)S(1)} %collective-permute-done.16.other_b, f32[192,512]{1,0:T(8,128)S(1)} %get-tuple-element.91.keys_ref, ...), custom_call_target="tpu_custom_call" | custom-call | flops 612368384 | bytes 7995392 | tf_op jit(solution)/shard_map/pallas_call | solution.py:29
  40.7 0.0 copy-start.1
  40.7 0.2 collective-permute-start.17
  40.9 0.4 shard_map.101.keep_ref
  41.3 1.0 %collective-permute-done.17.got_ref = bf16[2,64,1024]{2,1,0:T(8,128)(2,1)S(1)} collective-permute-done((bf16[2,64,1024]{2,1,0:T(8,128)(2,1)S(1)}, bf16[2,64,1024]{2,1,0:T(8,128)(2,1)S(1)}, u32[]{:S(2)}, u32[]{:S(2)}) %collective-permute-start.17) | collective-permute-done | bytes 262176 | tf_op jit(solution)/shard_map/ppermute | solution.py:500
  42.3 0.5 shard_map.102
  42.8 2.6 %collective-permute-start.18 = (bf16[96,256]{1,0:T(8,128)(2,1)S(1)}, bf16[96,256]{1,0:T(8,128)(2,1)S(1)}, u32[]{:S(2)}, u32[]{:S(2)}) collective-permute-start(bf16[96,256]{1,0:T(8,128)(2,1)S(1)} %get-tuple-element.98.first_ref), channel_id=1, source_target_pairs={{0,2},{2,4},{4,6},{6,8},{8,10},{10,12},{12,14},{3,1},{5,3},{7,5},{... | collective-permute-start | bytes 147464 | tf_op jit(solution)/shard_map/ppermute | solution.py:530
  45.4 0.0 collective-permute-start.19
  45.4 0.4 shard_map.103
  45.8 2.1 %collective-permute-done.18.got_first_ref = bf16[96,256]{1,0:T(8,128)(2,1)S(1)} collective-permute-done((bf16[96,256]{1,0:T(8,128)(2,1)S(1)}, bf16[96,256]{1,0:T(8,128)(2,1)S(1)}, u32[]{:S(2)}, u32[]{:S(2)}) %collective-permute-start.18) | collective-permute-done | bytes 49184 | tf_op jit(solution)/shard_map/ppermute | solution.py:530
  47.8 2.5 %collective-permute-done.19.got_second_ref = bf16[96,256]{1,0:T(8,128)(2,1)S(1)} collective-permute-done((bf16[96,256]{1,0:T(8,128)(2,1)S(1)}, bf16[96,256]{1,0:T(8,128)(2,1)S(1)}, u32[]{:S(2)}, u32[]{:S(2)}) %collective-permute-start.19) | collective-permute-done | bytes 49184 | tf_op jit(solution)/shard_map/ppermute | solution.py:529
  50.4 1.2 %shard_map.104 = (bf16[2,48,256]{2,1,0:T(8,128)(2,1)}, bf16[1,24,256]{2,1,0:T(8,128)(2,1)}) custom-call(bf16[96,256]{1,0:T(8,128)(2,1)S(1)} %collective-permute-done.18.got_first_ref, bf16[96,256]{1,0:T(8,128)(2,1)S(1)} %collective-permute-done.19.got_second_ref, f32[128,256]{1,0:T(8,128)S(1)} %get-tuple-element.100.own_fine_ref, ...), custom_call_target="tpu_custom_call" | custom-call | flops 75497472 | bytes 2686976 | tf_op jit(solution)/shard_map/pallas_call | solution.py:29
  (11 shorter events, 0.1 us)
Async XLA Ops:
  0.6 2.0 %copy-start.5 = (f32[1024]{0:T(1024)S(1)}, f32[1024]{0:T(1024)}, u32[]{:S(2)}) copy-start(f32[1024]{0:T(1024)} %gain_ref.3) | copy-start | bytes 12292
  0.6 4.4 %copy-start = (bf16[3,1024,512]{2,1,0:T(8,128)(2,1)S(1)}, bf16[3,1024,512]{2,1,0:T(8,128)(2,1)}, u32[]{:S(2)}) copy-start(bf16[3,1024,512]{2,1,0:T(8,128)(2,1)} %weight_ref.20) | copy-start | bytes 9437188
  0.6 2.0 %collective-permute-start = (f32[192,512]{1,0:T(8,128)}, f32[192,512]{1,0:T(8,128)S(1)}, u32[]{:S(2)}, u32[]{:S(2)}) collective-permute-start(f32[192,512]{1,0:T(8,128)} %tokens_ref.1), channel_id=1, source_target_pairs={{0,1},{1,0},{2,3},{3,2},{4,5},{5,4},{6,7},{7,6},{8,9},{9,8},{10,11... | collective-permute-start | bytes 1179656 | tf_op jit(solution)/shard_map/ppermute | solution.py:428
  0.7 1.1 %copy-start.6 = (f32[192,512]{1,0:T(8,128)S(1)}, f32[192,512]{1,0:T(8,128)}, u32[]{:S(2)}) copy-start(f32[192,512]{1,0:T(8,128)} %tokens_ref.1) | copy-start | bytes 1179652
  3.0 7.0 %collective-permute-start.1 = (bf16[192,512]{1,0:T(8,128)(2,1)S(1)}, bf16[192,512]{1,0:T(8,128)(2,1)S(1)}, u32[]{:S(2)}, u32[]{:S(2)}) collective-permute-start(bf16[192,512]{1,0:T(8,128)(2,1)S(1)} %get-tuple-element.54.mine_ref), channel_id=1, source_target_pairs={{2,0},{0,4},{4,8},{8,12},{12,14},{14,10},{10,6},{6,2},{3,1},{1,5},... | collective-permute-start | bytes 589832 | tf_op jit(solution)/shard_map/ppermute | solution.py:446
  3.6 6.7 %collective-permute-start.3 = (bf16[192,512]{1,0:T(8,128)(2,1)S(1)}, bf16[192,512]{1,0:T(8,128)(2,1)S(1)}, u32[]{:S(2)}, u32[]{:S(2)}) collective-permute-start(bf16[192,512]{1,0:T(8,128)(2,1)S(1)} %get-tuple-element.54.mine_ref), channel_id=1, source_target_pairs={{0,2},{4,0},{8,4},{12,8},{14,12},{10,14},{6,10},{2,6},{1,3},{5,1},... | collective-permute-start | bytes 589832 | tf_op jit(solution)/shard_map/ppermute | solution.py:447
  10.0 2.5 %collective-permute-start.5 = (bf16[192,512]{1,0:T(8,128)(2,1)S(1)}, bf16[192,512]{1,0:T(8,128)(2,1)S(1)}, u32[]{:S(2)}, u32[]{:S(2)}) collective-permute-start(bf16[192,512]{1,0:T(8,128)(2,1)S(1)} %collective-permute-done.1.block_ref.mine_ref), channel_id=1, source_target_pairs={{0,1},{1,0},{2,3},{3,2},{4,5},{5,4},{6,7},{7,6},{8,9},{9,8},{10,11... | collective-permute-start | bytes 589832 | tf_op jit(solution)/shard_map/ppermute | solution.py:469
  10.2 3.6 %collective-permute-start.4 = (bf16[192,512]{1,0:T(8,128)(2,1)S(1)}, bf16[192,512]{1,0:T(8,128)(2,1)S(1)}, u32[]{:S(2)}, u32[]{:S(2)}) collective-permute-start(bf16[192,512]{1,0:T(8,128)(2,1)S(1)} %collective-permute-done.3.mine_ref), channel_id=1, source_target_pairs={{0,1},{1,0},{2,3},{3,2},{4,5},{5,4},{6,7},{7,6},{8,9},{9,8},{10,11... | collective-permute-start | bytes 589832 | tf_op jit(solution)/shard_map/ppermute | solution.py:469
  10.5 7.1 %collective-permute-start.2 = (bf16[192,512]{1,0:T(8,128)(2,1)S(1)}, bf16[192,512]{1,0:T(8,128)(2,1)S(1)}, u32[]{:S(2)}, u32[]{:S(2)}) collective-permute-start(bf16[192,512]{1,0:T(8,128)(2,1)S(1)} %collective-permute-done.1.block_ref.mine_ref), channel_id=1, source_target_pairs={{2,0},{0,4},{4,8},{8,12},{12,14},{14,10},{10,6},{6,2},{3,1},{1,5},... | collective-permute-start | bytes 589832 | tf_op jit(solution)/shard_map/ppermute | solution.py:466
  11.8 7.0 %collective-permute-start.7 = (bf16[192,512]{1,0:T(8,128)(2,1)S(1)}, bf16[192,512]{1,0:T(8,128)(2,1)S(1)}, u32[]{:S(2)}, u32[]{:S(2)}) collective-permute-start(bf16[192,512]{1,0:T(8,128)(2,1)S(1)} %collective-permute-done.3.mine_ref), channel_id=1, source_target_pairs={{0,2},{4,0},{8,4},{12,8},{14,12},{10,14},{6,10},{2,6},{1,3},{5,1},... | collective-permute-start | bytes 589832 | tf_op jit(solution)/shard_map/ppermute | solution.py:467
  17.6 3.3 %collective-permute-start.9 = (bf16[192,512]{1,0:T(8,128)(2,1)S(1)}, bf16[192,512]{1,0:T(8,128)(2,1)S(1)}, u32[]{:S(2)}, u32[]{:S(2)}) collective-permute-start(bf16[192,512]{1,0:T(8,128)(2,1)S(1)} %collective-permute-done.2.block_ref.mine_ref), channel_id=1, source_target_pairs={{0,1},{1,0},{2,3},{3,2},{4,5},{5,4},{6,7},{7,6},{8,9},{9,8},{10,11... | collective-permute-start | bytes 589832 | tf_op jit(solution)/shard_map/ppermute | solution.py:469
  18.9 3.4 %collective-permute-start.8 = (bf16[192,512]{1,0:T(8,128)(2,1)S(1)}, bf16[192,512]{1,0:T(8,128)(2,1)S(1)}, u32[]{:S(2)}, u32[]{:S(2)}) collective-permute-start(bf16[192,512]{1,0:T(8,128)(2,1)S(1)} %collective-permute-done.7.mine_ref), channel_id=1, source_target_pairs={{0,1},{1,0},{2,3},{3,2},{4,5},{5,4},{6,7},{7,6},{8,9},{9,8},{10,11... | collective-permute-start | bytes 589832 | tf_op jit(solution)/shard_map/ppermute | solution.py:469
  18.9 7.3 %collective-permute-start.6 = (bf16[192,512]{1,0:T(8,128)(2,1)S(1)}, bf16[192,512]{1,0:T(8,128)(2,1)S(1)}, u32[]{:S(2)}, u32[]{:S(2)}) collective-permute-start(bf16[192,512]{1,0:T(8,128)(2,1)S(1)} %collective-permute-done.2.block_ref.mine_ref), channel_id=1, source_target_pairs={{2,0},{0,4},{4,8},{8,12},{12,14},{14,10},{10,6},{6,2},{3,1},{1,5},... | collective-permute-start | bytes 589832 | tf_op jit(solution)/shard_map/ppermute | solution.py:466
  20.4 7.0 %collective-permute-start.11 = (bf16[192,512]{1,0:T(8,128)(2,1)S(1)}, bf16[192,512]{1,0:T(8,128)(2,1)S(1)}, u32[]{:S(2)}, u32[]{:S(2)}) collective-permute-start(bf16[192,512]{1,0:T(8,128)(2,1)S(1)} %collective-permute-done.7.mine_ref), channel_id=1, source_target_pairs={{0,2},{4,0},{8,4},{12,8},{14,12},{10,14},{6,10},{2,6},{1,3},{5,1},... | collective-permute-start | bytes 589832 | tf_op jit(solution)/shard_map/ppermute | solution.py:467
  26.2 3.0 %collective-permute-start.13 = (bf16[192,512]{1,0:T(8,128)(2,1)S(1)}, bf16[192,512]{1,0:T(8,128)(2,1)S(1)}, u32[]{:S(2)}, u32[]{:S(2)}) collective-permute-start(bf16[192,512]{1,0:T(8,128)(2,1)S(1)} %collective-permute-done.6.block_ref.mine_ref), channel_id=1, source_target_pairs={{0,1},{1,0},{2,3},{3,2},{4,5},{5,4},{6,7},{7,6},{8,9},{9,8},{10,11... | collective-permute-start | bytes 589832 | tf_op jit(solution)/shard_map/ppermute | solution.py:469
  27.5 3.0 %collective-permute-start.12 = (bf16[192,512]{1,0:T(8,128)(2,1)S(1)}, bf16[192,512]{1,0:T(8,128)(2,1)S(1)}, u32[]{:S(2)}, u32[]{:S(2)}) collective-permute-start(bf16[192,512]{1,0:T(8,128)(2,1)S(1)} %collective-permute-done.11.mine_ref), channel_id=1, source_target_pairs={{0,1},{1,0},{2,3},{3,2},{4,5},{5,4},{6,7},{7,6},{8,9},{9,8},{10,11... | collective-permute-start | bytes 589832 | tf_op jit(solution)/shard_map/ppermute | solution.py:469
  27.5 6.7 %collective-permute-start.10 = (bf16[160,512]{1,0:T(8,128)(2,1)S(1)}, bf16[160,512]{1,0:T(8,128)(2,1)S(1)}, u32[]{:S(2)}, u32[]{:S(2)}) collective-permute-start(bf16[160,512]{1,0:T(8,128)(2,1)S(1)} %slice.6), channel_id=1, source_target_pairs={{2,0},{0,4},{4,8},{8,12},{12,14},{14,10},{10,6},{6,2},{3,1},{1,5},... | collective-permute-start | bytes 491528 | tf_op jit(solution)/shard_map/ppermute | solution.py:466
  31.8 7.5 %copy-start.2 = (bf16[512,1024]{1,0:T(8,128)(2,1)S(1)}, bf16[512,1024]{1,0:T(8,128)(2,1)}, u32[]{:S(2)}) copy-start(bf16[512,1024]{1,0:T(8,128)(2,1)} %weight_ref.21) | copy-start | bytes 3145732
  34.2 5.1 %collective-permute-start.14 = (bf16[160,512]{1,0:T(8,128)(2,1)S(1)}, bf16[160,512]{1,0:T(8,128)(2,1)S(1)}, u32[]{:S(2)}, u32[]{:S(2)}) collective-permute-start(bf16[160,512]{1,0:T(8,128)(2,1)S(1)} %collective-permute-done.10.block_ref.mine_a), channel_id=1, source_target_pairs={{0,1},{1,0},{2,3},{3,2},{4,5},{5,4},{6,7},{7,6},{8,9},{9,8},{10,11... | collective-permute-start | bytes 491528 | tf_op jit(solution)/shard_map/ppermute | solution.py:469
  34.2 3.9 %collective-permute-start.15 = (bf16[32,512]{1,0:T(8,128)(2,1)S(1)}, bf16[32,512]{1,0:T(8,128)(2,1)S(1)}, u32[]{:S(2)}, u32[]{:S(2)}) collective-permute-start(bf16[32,512]{1,0:T(8,128)(2,1)S(1)} %slice.7), channel_id=1, source_target_pairs={{0,2},{4,0},{8,4},{12,8},{14,12},{10,14},{6,10},{2,6},{1,3},{5,1},... | collective-permute-start | bytes 98312 | tf_op jit(solution)/shard_map/ppermute | solution.py:467
  38.1 1.2 %collective-permute-start.16 = (bf16[32,512]{1,0:T(8,128)(2,1)S(1)}, bf16[32,512]{1,0:T(8,128)(2,1)S(1)}, u32[]{:S(2)}, u32[]{:S(2)}) collective-permute-start(bf16[32,512]{1,0:T(8,128)(2,1)S(1)} %collective-permute-done.15.mine_b), channel_id=1, source_target_pairs={{0,1},{1,0},{2,3},{3,2},{4,5},{5,4},{6,7},{7,6},{8,9},{9,8},{10,11... | collective-permute-start | bytes 98312 | tf_op jit(solution)/shard_map/ppermute | solution.py:469
  39.3 3.0 %copy-start.3 = (bf16[2,1024,256]{2,1,0:T(8,128)(2,1)S(1)}, bf16[2,1024,256]{2,1,0:T(8,128)(2,1)}, u32[]{:S(2)}) copy-start(bf16[2,1024,256]{2,1,0:T(8,128)(2,1)} %lateral_ref.1) | copy-start | bytes 3145732
  39.3 3.0 %copy-start.4 = (f32[2,2,256]{2,1,0:T(2,128)S(1)}, f32[2,2,256]{2,1,0:T(2,128)}, u32[]{:S(2)}) copy-start(f32[2,2,256]{2,1,0:T(2,128)} %gain_ref.5) | copy-start | bytes 12292
  40.7 4.7 %copy-start.1 = (bf16[2,3,3,256,256]{4,3,2,1,0:T(8,128)(2,1)S(1)}, bf16[2,3,3,256,256]{4,3,2,1,0:T(8,128)(2,1)}, u32[]{:S(2)}) copy-start(bf16[2,3,3,256,256]{4,3,2,1,0:T(8,128)(2,1)} %weight_ref.23) | copy-start | bytes 7077892
  40.7 1.6 %collective-permute-start.17 = (bf16[2,64,1024]{2,1,0:T(8,128)(2,1)S(1)}, bf16[2,64,1024]{2,1,0:T(8,128)(2,1)S(1)}, u32[]{:S(2)}, u32[]{:S(2)}) collective-permute-start(bf16[2,64,1024]{2,1,0:T(8,128)(2,1)S(1)} %get-tuple-element.97), channel_id=1, source_target_pairs={{0,1},{1,0},{2,3},{3,2},{4,5},{5,4},{6,7},{7,6},{8,9},{9,8},{10,11... | collective-permute-start | bytes 786440 | tf_op jit(solution)/shard_map/ppermute | solution.py:500
  42.8 5.0 %collective-permute-start.18 = (bf16[96,256]{1,0:T(8,128)(2,1)S(1)}, bf16[96,256]{1,0:T(8,128)(2,1)S(1)}, u32[]{:S(2)}, u32[]{:S(2)}) collective-permute-start(bf16[96,256]{1,0:T(8,128)(2,1)S(1)} %get-tuple-element.98.first_ref), channel_id=1, source_target_pairs={{0,2},{2,4},{4,6},{6,8},{8,10},{10,12},{12,14},{3,1},{5,3},{7,5},{... | collective-permute-start | bytes 147464 | tf_op jit(solution)/shard_map/ppermute | solution.py:530
  45.4 5.0 %collective-permute-start.19 = (bf16[96,256]{1,0:T(8,128)(2,1)S(1)}, bf16[96,256]{1,0:T(8,128)(2,1)S(1)}, u32[]{:S(2)}, u32[]{:S(2)}) collective-permute-start(bf16[96,256]{1,0:T(8,128)(2,1)S(1)} %get-tuple-element.99.second_ref), channel_id=1, source_target_pairs={{1,3},{3,5},{5,7},{7,9},{9,11},{11,13},{13,15},{2,0},{4,2},{6,4},{... | collective-permute-start | bytes 147464 | tf_op jit(solution)/shard_map/ppermute | solution.py:529

commit v11 on v10

--- a/solution.py
+++ b/solution.py
@@ -300,49 +300,45 @@
     coarse_ref[...] = joined(lambda tap_col: dot(coarse, weight_ref[1, 1, tap_col]), window // 2)
 
 
+def add_edge(got_ref, side, weight_ref, fine_ref, coarse_ref):
+    window = fine_ref.shape[0] // 2
+    inside = lax.axis_index("blk") != side * (lax.axis_size("blk") - 1)
+    edge = jnp.where(inside, got_ref[...].astype(F32), 0.0).astype(BF16)
+    here = pl.ds(pl.multiple_of(side * window, window), window)
+    fine_ref[here, :] += joined(
+        lambda tap_col: dot(edge[:window], weight_ref[0, 2 * side, tap_col]), window
+    )
+    coarse_ref[...] += joined(
+        lambda tap_col: dot(edge[window:], weight_ref[1, 2 * side, tap_col]), window // 2
+    )
+
+
+def first_edge_kernel(
+    got_ref, own_fine_ref, own_coarse_ref, weight_ref, fine_ref, coarse_ref
+):
+    fine_ref[...] = own_fine_ref[...]
+    coarse_ref[...] = own_coarse_ref[...]
+    add_edge(got_ref, lax.axis_index("head"), weight_ref, fine_ref, coarse_ref)
+
+
 def conv_kernel(
-    got_first_ref,
-    got_second_ref,
+    got_ref,
     own_fine_ref,
     own_coarse_ref,
     weight_ref,
     gain_ref,
     fine_ref,
     coarse_ref,
-    edge_in,
     fine_sum,
     coarse_sum,
 ):
     core = lax.axis_index("head")
-    block = lax.axis_index("blk")
-    edge = (0, lax.axis_size("blk") - 1)
     window = fine_sum.shape[0] // 2
-    rows = got_first_ref.shape[0]
-    for ref, place in ((got_first_ref, core), (got_second_ref, 1 - core)):
-        inside = block != jnp.where(place == 0, *edge)
-        edge_in[pl.ds(pl.multiple_of(place * rows, 32), rows), :] = jnp.where(
-            inside, ref[...].astype(F32), 0.0
-        ).astype(BF16)
-
-    def fine_terms(tap_col):
-        return jnp.concatenate(
-            [
-                dot(edge_in[:window], weight_ref[0, 0, tap_col]),
-                dot(edge_in[rows : rows + window], weight_ref[0, 2, tap_col]),
-            ],
-            axis=0,
-        )
-
-    def coarse_terms(tap_col):
-        return dot(edge_in[window:rows], weight_ref[1, 0, tap_col]) + dot(
-            edge_in[rows + window :], weight_ref[1, 2, tap_col]
-        )
-
+    fine_sum[...] = own_fine_ref[...]
+    coarse_sum[...] = own_coarse_ref[...]
+    add_edge(got_ref, 1 - core, weight_ref, fine_sum, coarse_sum)
     cols = fine_ref.shape[1]
-    shift = GRID_COLS - window
-    inset = cols - shift
-    fine_sum[...] = own_fine_ref[...] + joined(fine_terms, window)
-    coarse_sum[...] = own_coarse_ref[...] + joined(coarse_terms, window // 2)
+    inset = cols - (GRID_COLS - window)
     for row in range(2):
         here = pl.ds(pl.multiple_of(row * window + core * inset, 8), cols)
         fine_ref[row] = layer_norm(fine_sum[here, :], gain_ref[0, 1][None, :]).astype(BF16)
@@ -536,13 +532,18 @@
         [pltpu.VMEM((2 * window, channels), BF16)],
         flops=27 * window * channels * channels,
     )
+    own_sums = call(
+        first_edge_kernel,
+        sums,
+        (got_first, *own_sums, conv_weight),
+        flops=9 * window * channels * channels,
+    )
     return call(
         conv_kernel,
         [((grid_rows, cols, channels), BF16), ((grid_rows // 2, cols // 2, channels), BF16)],
-        (got_first, got_second, *own_sums, conv_weight, level_gains),
-        [pltpu.VMEM((2 * message[0], channels), BF16)]
-        + [pltpu.VMEM(shape, dtype) for shape, dtype in sums],
-        flops=18 * window * channels * channels,
+        (got_second, *own_sums, conv_weight, level_gains),
+        [pltpu.VMEM(shape, dtype) for shape, dtype in sums],
+        flops=9 * window * channels * channels,
     )
 
 

time: 51.7 us -> 51.6 us (level)
    pallas_call x19 -> x20, Pallas kernels: 13.8 us -> 14 us  [call(): pl.pallas_call(kernel, out_shape=outs, in_specs=specs(len(args)), out_spe...]
  transfers between devices with their start and end apart: 20 -> 20, of which waited for: 13 -> 13; matrix products, arithmetic and copies ran while one was open for 0% -> 0% of each run, Pallas kernels for 20% -> 21%
where the time goes in v11:
time: 51.6 us; the launch traced here: 51.4 us
  waiting for transfers between devices  24.1 us (47%)
  Pallas kernels  14 us (27%)
  starting transfers between devices  11.3 us (22%)
  local copies, waits for them, and re-layouts  1.18 us (2%)
  between operations  0.84 us (2%)
    pallas_call x20, Pallas kernels, call(): pl.pallas_call(kernel, out_shape=outs, in_specs=specs(len(args)), out_spe...  14 us
    ppermute x3, waiting for transfers between devices, body(): ahead = lax.ppermute(ahead, 'blk', forth)  7.37 us
    ppermute x3, waiting for transfers between devices, body(): behind = lax.ppermute(behind, 'blk', back)  6.05 us
    ppermute x3, starting transfers between devices, body(): ahead = lax.ppermute(ahead, 'blk', forth)  4.53 us
    ppermute x1, waiting for transfers between devices, body(): ahead = lax.ppermute(mine, 'blk', forth)  3.5 us
    ppermute x1, starting transfers between devices, body(): got_first = lax.ppermute(first, ('blk', 'head'), down_then_up[0])  2.56 us
    ppermute x1, waiting for transfers between devices, body(): got_second = lax.ppermute(second, ('blk', 'head'), down_then_up[1])  2.28 us
    ppermute x1, waiting for transfers between devices, body(): got_first = lax.ppermute(first, ('blk', 'head'), down_then_up[0])  2.07 us
  transfers between devices with their start and end apart: 20, of which 13 were waited for; matrix products, arithmetic and copies ran while one was open for 0% of the time, Pallas kernels for 21%

profile of v11, /device:TPU:6, one launch (start us, length us, event | category | flops | bytes accessed | tf_op | source)
XLA Modules:
  0.0 51.4 jit_solution(8716072511201451430)
XLA Ops:
  0.6 0.0 copy-start.5
  0.6 0.0 copy-start
  0.6 0.1 collective-permute-start
  0.7 0.0 copy-start.6
  0.7 1.1 %copy-done.6 = f32[192,512]{1,0:T(8,128)S(1)} copy-done((f32[192,512]{1,0:T(8,128)S(1)}, f32[192,512]{1,0:T(8,128)}, u32[]{:S(2)}) %copy-start.6) | copy-done | bytes 393240
  1.9 0.7 %collective-permute-done.other_ref = f32[192,512]{1,0:T(8,128)S(1)} collective-permute-done((f32[192,512]{1,0:T(8,128)}, f32[192,512]{1,0:T(8,128)S(1)}, u32[]{:S(2)}, u32[]{:S(2)}) %collective-permute-start) | collective-permute-done | bytes 393248 | tf_op jit(solution)/shard_map/ppermute | solution.py:424
  2.6 0.0 copy-done.5
  2.7 0.3 shard_map.87
  3.0 0.6 %collective-permute-start.1 = (bf16[192,512]{1,0:T(8,128)(2,1)S(1)}, bf16[192,512]{1,0:T(8,128)(2,1)S(1)}, u32[]{:S(2)}, u32[]{:S(2)}) collective-permute-start(bf16[192,512]{1,0:T(8,128)(2,1)S(1)} %get-tuple-element.56.mine_ref), channel_id=1, source_target_pairs={{2,0},{0,4},{4,8},{8,12},{12,14},{14,10},{10,6},{6,2},{3,1},{1,5},... | collective-permute-start | bytes 589832 | tf_op jit(solution)/shard_map/ppermute | solution.py:442
  3.6 1.5 %collective-permute-start.3 = (bf16[192,512]{1,0:T(8,128)(2,1)S(1)}, bf16[192,512]{1,0:T(8,128)(2,1)S(1)}, u32[]{:S(2)}, u32[]{:S(2)}) collective-permute-start(bf16[192,512]{1,0:T(8,128)(2,1)S(1)} %get-tuple-element.56.mine_ref), channel_id=1, source_target_pairs={{0,2},{4,0},{8,4},{12,8},{14,12},{10,14},{6,10},{2,6},{1,3},{5,1},... | collective-permute-start | bytes 589832 | tf_op jit(solution)/shard_map/ppermute | solution.py:443
  5.1 1.4 %shard_map.88 = (bf16[4,384,128]{2,1,0:T(8,128)(2,1)S(1)}, f32[4,384,128]{2,1,0:T(8,128)S(1)}, f32[4,384,128]{2,1,0:T(8,128)S(1)}, f32[4,192,128]{2,1,0:T(8,128)S(1)}) custom-call(bf16[192,512]{1,0:T(8,128)(2,1)S(1)} %get-tuple-element.56.mine_ref, bf16[192,512]{1,0:T(8,128)(2,1)S(1)} %get-tuple-element.57.other_ref, bf16[3,1024,512]{2,1,0:T(8,128)(2,1)S(1)} %copy-done), custom_call_target="tpu_custom_call" | custom-call | flops 679477248 | bytes 5898240 | tf_op jit(solution)/shard_map/pallas_call | solution.py:29
  6.5 3.5 %collective-permute-done.1.block_ref.mine_ref = bf16[192,512]{1,0:T(8,128)(2,1)S(1)} collective-permute-done((bf16[192,512]{1,0:T(8,128)(2,1)S(1)}, bf16[192,512]{1,0:T(8,128)(2,1)S(1)}, u32[]{:S(2)}, u32[]{:S(2)}) %collective-permute-start.1) | collective-permute-done | bytes 196640 | tf_op jit(solution)/shard_map/ppermute | solution.py:442
  10.0 0.0 collective-permute-start.5
  10.0 0.3 collective-permute-done.3.mine_ref
  10.2 0.3 collective-permute-start.4
  10.5 1.3 %collective-permute-start.2 = (bf16[192,512]{1,0:T(8,128)(2,1)S(1)}, bf16[192,512]{1,0:T(8,128)(2,1)S(1)}, u32[]{:S(2)}, u32[]{:S(2)}) collective-permute-start(bf16[192,512]{1,0:T(8,128)(2,1)S(1)} %collective-permute-done.1.block_ref.mine_ref), channel_id=1, source_target_pairs={{2,0},{0,4},{4,8},{8,12},{12,14},{14,10},{10,6},{6,2},{3,1},{1,5},... | collective-permute-start | bytes 589832 | tf_op jit(solution)/shard_map/ppermute | solution.py:462
  11.8 0.7 %collective-permute-start.7 = (bf16[192,512]{1,0:T(8,128)(2,1)S(1)}, bf16[192,512]{1,0:T(8,128)(2,1)S(1)}, u32[]{:S(2)}, u32[]{:S(2)}) collective-permute-start(bf16[192,512]{1,0:T(8,128)(2,1)S(1)} %collective-permute-done.3.mine_ref), channel_id=1, source_target_pairs={{0,2},{4,0},{8,4},{12,8},{14,12},{10,14},{6,10},{2,6},{1,3},{5,1},... | collective-permute-start | bytes 589832 | tf_op jit(solution)/shard_map/ppermute | solution.py:463
  12.5 0.0 collective-permute-done.5.other_ref
  12.5 1.3 %shard_map.90 = (f32[4,384,128]{2,1,0:T(8,128)S(1)}, f32[4,384,128]{2,1,0:T(8,128)S(1)}, f32[4,192,128]{2,1,0:T(8,128)S(1)}) custom-call(bf16[192,512]{1,0:T(8,128)(2,1)S(1)} %collective-permute-done.1.block_ref.mine_ref, bf16[192,512]{1,0:T(8,128)(2,1)S(1)} %collective-permute-done.5.other_ref, bf16[3,1024,512]{2,1,0:T(8,128)(2,1)S(1)} %copy-done, ...), custom_call_target="tpu_custom_call" | custom-call | flops 478150656 | bytes 7868416 | tf_op jit(solution)/shard_map/pallas_call | solution.py:29
  13.9 0.0 collective-permute-done.4.other_ref
  13.9 1.3 %shard_map.91 = (f32[4,384,128]{2,1,0:T(8,128)S(1)}, f32[4,384,128]{2,1,0:T(8,128)S(1)}, f32[4,192,128]{2,1,0:T(8,128)S(1)}) custom-call(bf16[192,512]{1,0:T(8,128)(2,1)S(1)} %collective-permute-done.3.mine_ref, bf16[192,512]{1,0:T(8,128)(2,1)S(1)} %collective-permute-done.4.other_ref, bf16[3,1024,512]{2,1,0:T(8,128)(2,1)S(1)} %copy-done, ...), custom_call_target="tpu_custom_call" | custom-call | flops 478150656 | bytes 7868416 | tf_op jit(solution)/shard_map/pallas_call | solution.py:29
  15.2 2.4 %collective-permute-done.2.block_ref.mine_ref = bf16[192,512]{1,0:T(8,128)(2,1)S(1)} collective-permute-done((bf16[192,512]{1,0:T(8,128)(2,1)S(1)}, bf16[192,512]{1,0:T(8,128)(2,1)S(1)}, u32[]{:S(2)}, u32[]{:S(2)}) %collective-permute-start.2) | collective-permute-done | bytes 196640 | tf_op jit(solution)/shard_map/ppermute | solution.py:462
  17.6 0.0 collective-permute-start.9
  17.6 1.3 %collective-permute-done.7.mine_ref = bf16[192,512]{1,0:T(8,128)(2,1)S(1)} collective-permute-done((bf16[192,512]{1,0:T(8,128)(2,1)S(1)}, bf16[192,512]{1,0:T(8,128)(2,1)S(1)}, u32[]{:S(2)}, u32[]{:S(2)}) %collective-permute-start.7) | collective-permute-done | bytes 196640 | tf_op jit(solution)/shard_map/ppermute | solution.py:463
  18.9 0.0 collective-permute-start.8
  18.9 1.6 %collective-permute-start.6 = (bf16[192,512]{1,0:T(8,128)(2,1)S(1)}, bf16[192,512]{1,0:T(8,128)(2,1)S(1)}, u32[]{:S(2)}, u32[]{:S(2)}) collective-permute-start(bf16[192,512]{1,0:T(8,128)(2,1)S(1)} %collective-permute-done.2.block_ref.mine_ref), channel_id=1, source_target_pairs={{2,0},{0,4},{4,8},{8,12},{12,14},{14,10},{10,6},{6,2},{3,1},{1,5},... | collective-permute-start | bytes 589832 | tf_op jit(solution)/shard_map/ppermute | solution.py:462
  20.4 0.4 collective-permute-start.11
  20.9 0.0 collective-permute-done.9.other_ref
  20.9 1.3 %shard_map.93 = (f32[4,384,128]{2,1,0:T(8,128)S(1)}, f32[4,384,128]{2,1,0:T(8,128)S(1)}, f32[4,192,128]{2,1,0:T(8,128)S(1)}) custom-call(bf16[192,512]{1,0:T(8,128)(2,1)S(1)} %collective-permute-done.2.block_ref.mine_ref, bf16[192,512]{1,0:T(8,128)(2,1)S(1)} %collective-permute-done.9.other_ref, bf16[3,1024,512]{2,1,0:T(8,128)(2,1)S(1)} %copy-done, ...), custom_call_target="tpu_custom_call" | custom-call | flops 478150656 | bytes 7868416 | tf_op jit(solution)/shard_map/pallas_call | solution.py:29
  22.2 0.0 collective-permute-done.8.other_ref
  22.2 1.3 %shard_map.94 = (f32[4,384,128]{2,1,0:T(8,128)S(1)}, f32[4,384,128]{2,1,0:T(8,128)S(1)}, f32[4,192,128]{2,1,0:T(8,128)S(1)}) custom-call(bf16[192,512]{1,0:T(8,128)(2,1)S(1)} %collective-permute-done.7.mine_ref, bf16[192,512]{1,0:T(8,128)(2,1)S(1)} %collective-permute-done.8.other_ref, bf16[3,1024,512]{2,1,0:T(8,128)(2,1)S(1)} %copy-done, ...), custom_call_target="tpu_custom_call" | custom-call | flops 478150656 | bytes 7868416 | tf_op jit(solution)/shard_map/pallas_call | solution.py:29
  23.5 2.6 %collective-permute-done.6.block_ref.mine_ref = bf16[192,512]{1,0:T(8,128)(2,1)S(1)} collective-permute-done((bf16[192,512]{1,0:T(8,128)(2,1)S(1)}, bf16[192,512]{1,0:T(8,128)(2,1)S(1)}, u32[]{:S(2)}, u32[]{:S(2)}) %collective-permute-start.6) | collective-permute-done | bytes 196640 | tf_op jit(solution)/shard_map/ppermute | solution.py:462
  26.2 0.0 collective-permute-start.13
  26.2 1.3 %collective-permute-done.11.mine_ref = bf16[192,512]{1,0:T(8,128)(2,1)S(1)} collective-permute-done((bf16[192,512]{1,0:T(8,128)(2,1)S(1)}, bf16[192,512]{1,0:T(8,128)(2,1)S(1)}, u32[]{:S(2)}, u32[]{:S(2)}) %collective-permute-start.11) | collective-permute-done | bytes 196640 | tf_op jit(solution)/shard_map/ppermute | solution.py:463
  27.5 0.0 collective-permute-start.12
  27.5 1.6 %collective-permute-start.10 = (bf16[160,512]{1,0:T(8,128)(2,1)S(1)}, bf16[160,512]{1,0:T(8,128)(2,1)S(1)}, u32[]{:S(2)}, u32[]{:S(2)}) collective-permute-start(bf16[160,512]{1,0:T(8,128)(2,1)S(1)} %slice.6), channel_id=1, source_target_pairs={{2,0},{0,4},{4,8},{8,12},{12,14},{14,10},{10,6},{6,2},{3,1},{1,5},... | collective-permute-start | bytes 491528 | tf_op jit(solution)/shard_map/ppermute | solution.py:462
  29.1 0.0 collective-permute-done.13.other_ref
  29.1 1.3 %shard_map.96 = (f32[4,384,128]{2,1,0:T(8,128)S(1)}, f32[4,384,128]{2,1,0:T(8,128)S(1)}, f32[4,192,128]{2,1,0:T(8,128)S(1)}) custom-call(bf16[192,512]{1,0:T(8,128)(2,1)S(1)} %collective-permute-done.6.block_ref.mine_ref, bf16[192,512]{1,0:T(8,128)(2,1)S(1)} %collective-permute-done.13.other_ref, bf16[3,1024,512]{2,1,0:T(8,128)(2,1)S(1)} %copy-done, ...), custom_call_target="tpu_custom_call" | custom-call | flops 478150656 | bytes 7868416 | tf_op jit(solution)/shard_map/pallas_call | solution.py:29
  30.4 0.0 collective-permute-done.12.other_ref
  30.5 1.3 %shard_map.97 = (f32[4,384,128]{2,1,0:T(8,128)S(1)}, f32[4,384,128]{2,1,0:T(8,128)S(1)}, f32[4,192,128]{2,1,0:T(8,128)S(1)}) custom-call(bf16[192,512]{1,0:T(8,128)(2,1)S(1)} %collective-permute-done.11.mine_ref, bf16[192,512]{1,0:T(8,128)(2,1)S(1)} %collective-permute-done.12.other_ref, bf16[3,1024,512]{2,1,0:T(8,128)(2,1)S(1)} %copy-done, ...), custom_call_target="tpu_custom_call" | custom-call | flops 478150656 | bytes 7868416 | tf_op jit(solution)/shard_map/pallas_call | solution.py:29
  31.8 0.0 copy-start.2
  31.8 2.4 %collective-permute-done.10.block_ref.mine_a = bf16[160,512]{1,0:T(8,128)(2,1)S(1)} collective-permute-done((bf16[160,512]{1,0:T(8,128)(2,1)S(1)}, bf16[160,512]{1,0:T(8,128)(2,1)S(1)}, u32[]{:S(2)}, u32[]{:S(2)}) %collective-permute-start.10) | collective-permute-done | bytes 163872 | tf_op jit(solution)/shard_map/ppermute | solution.py:462
  34.2 0.0 collective-permute-start.14
  34.2 0.5 collective-permute-start.15
  34.6 3.5 %collective-permute-done.15.mine_b = bf16[32,512]{1,0:T(8,128)(2,1)S(1)} collective-permute-done((bf16[32,512]{1,0:T(8,128)(2,1)S(1)}, bf16[32,512]{1,0:T(8,128)(2,1)S(1)}, u32[]{:S(2)}, u32[]{:S(2)}) %collective-permute-start.15) | collective-permute-done | bytes 32800 | tf_op jit(solution)/shard_map/ppermute | solution.py:463
  38.1 0.0 collective-permute-start.16
  38.1 0.4 shard_map.99
  38.5 0.8 %collective-permute-done.16.other_b = bf16[32,512]{1,0:T(8,128)(2,1)S(1)} collective-permute-done((bf16[32,512]{1,0:T(8,128)(2,1)S(1)}, bf16[32,512]{1,0:T(8,128)(2,1)S(1)}, u32[]{:S(2)}, u32[]{:S(2)}) %collective-permute-start.16) | collective-permute-done | bytes 32800 | tf_op jit(solution)/shard_map/ppermute | solution.py:465
  39.3 0.0 collective-permute-done.14.other_a
  39.3 0.0 copy-done.2
  39.3 0.0 copy-start.4
  39.3 1.4 %shard_map.100 = (bf16[2,64,1024]{2,1,0:T(8,128)(2,1)S(1)}, bf16[192,512]{1,0:T(8,128)(2,1)S(1)}) custom-call(bf16[160,512]{1,0:T(8,128)(2,1)S(1)} %collective-permute-done.14.other_a, bf16[32,512]{1,0:T(8,128)(2,1)S(1)} %collective-permute-done.16.other_b, f32[192,512]{1,0:T(8,128)S(1)} %get-tuple-element.93.keys_ref, ...), custom_call_target="tpu_custom_call" | custom-call | flops 612368384 | bytes 7995392 | tf_op jit(solution)/shard_map/pallas_call | solution.py:29
  40.7 0.0 copy-start.1
  40.7 0.2 collective-permute-start.17
  40.9 0.4 shard_map.101.keep_ref
  41.3 1.0 %collective-permute-done.17.got_ref = bf16[2,64,1024]{2,1,0:T(8,128)(2,1)S(1)} collective-permute-done((bf16[2,64,1024]{2,1,0:T(8,128)(2,1)S(1)}, bf16[2,64,1024]{2,1,0:T(8,128)(2,1)S(1)}, u32[]{:S(2)}, u32[]{:S(2)}) %collective-permute-start.17) | collective-permute-done | bytes 262176 | tf_op jit(solution)/shard_map/ppermute | solution.py:496
  42.3 0.5 shard_map.102
  42.8 2.6 %collective-permute-start.19 = (bf16[96,256]{1,0:T(8,128)(2,1)S(1)}, bf16[96,256]{1,0:T(8,128)(2,1)S(1)}, u32[]{:S(2)}, u32[]{:S(2)}) collective-permute-start(bf16[96,256]{1,0:T(8,128)(2,1)S(1)} %get-tuple-element.101.first_ref), channel_id=1, source_target_pairs={{0,2},{2,4},{4,6},{6,8},{8,10},{10,12},{12,14},{3,1},{5,3},{7,5},{... | collective-permute-start | bytes 147464 | tf_op jit(solution)/shard_map/ppermute | solution.py:526
  45.4 0.0 collective-permute-start.18
  45.4 0.4 shard_map.103
  45.7 2.1 %collective-permute-done.19.got_ref = bf16[96,256]{1,0:T(8,128)(2,1)S(1)} collective-permute-done((bf16[96,256]{1,0:T(8,128)(2,1)S(1)}, bf16[96,256]{1,0:T(8,128)(2,1)S(1)}, u32[]{:S(2)}, u32[]{:S(2)}) %collective-permute-start.19) | collective-permute-done | bytes 49184 | tf_op jit(solution)/shard_map/ppermute | solution.py:526
  47.8 0.2 shard_map.104
  48.1 2.3 %collective-permute-done.18.got_ref = bf16[96,256]{1,0:T(8,128)(2,1)S(1)} collective-permute-done((bf16[96,256]{1,0:T(8,128)(2,1)S(1)}, bf16[96,256]{1,0:T(8,128)(2,1)S(1)}, u32[]{:S(2)}, u32[]{:S(2)}) %collective-permute-start.18) | collective-permute-done | bytes 49184 | tf_op jit(solution)/shard_map/ppermute | solution.py:525
  50.4 1.0 %shard_map.105 = (bf16[2,48,256]{2,1,0:T(8,128)(2,1)}, bf16[1,24,256]{2,1,0:T(8,128)(2,1)}) custom-call(bf16[96,256]{1,0:T(8,128)(2,1)S(1)} %collective-permute-done.18.got_ref, f32[128,256]{1,0:T(8,128)S(1)} %get-tuple-element.104.own_fine_ref, f32[32,256]{1,0:T(8,128)S(1)} %get-tuple-element.105.own_coarse_ref, bf16[2,3,3,256,256]{4,3,2,1,0:T(8,128)(2,1)S(1)} %copy-done.1, ...), custom_call_target="tpu_custom_call" | custom-call | flops 37748736 | bytes 2637824 | tf_op jit(solution)/shard_map/pallas_call | solution.py:29
  (12 shorter events, 0.1 us)
Async XLA Ops:
  0.6 2.0 %copy-start.5 = (f32[1024]{0:T(1024)S(1)}, f32[1024]{0:T(1024)}, u32[]{:S(2)}) copy-start(f32[1024]{0:T(1024)} %gain_ref.3) | copy-start | bytes 12292
  0.6 4.4 %copy-start = (bf16[3,1024,512]{2,1,0:T(8,128)(2,1)S(1)}, bf16[3,1024,512]{2,1,0:T(8,128)(2,1)}, u32[]{:S(2)}) copy-start(bf16[3,1024,512]{2,1,0:T(8,128)(2,1)} %weight_ref.21) | copy-start | bytes 9437188
  0.6 2.0 %collective-permute-start = (f32[192,512]{1,0:T(8,128)}, f32[192,512]{1,0:T(8,128)S(1)}, u32[]{:S(2)}, u32[]{:S(2)}) collective-permute-start(f32[192,512]{1,0:T(8,128)} %tokens_ref.1), channel_id=1, source_target_pairs={{0,1},{1,0},{2,3},{3,2},{4,5},{5,4},{6,7},{7,6},{8,9},{9,8},{10,11... | collective-permute-start | bytes 1179656 | tf_op jit(solution)/shard_map/ppermute | solution.py:424
  0.7 1.1 %copy-start.6 = (f32[192,512]{1,0:T(8,128)S(1)}, f32[192,512]{1,0:T(8,128)}, u32[]{:S(2)}) copy-start(f32[192,512]{1,0:T(8,128)} %tokens_ref.1) | copy-start | bytes 1179652
  3.0 7.0 %collective-permute-start.1 = (bf16[192,512]{1,0:T(8,128)(2,1)S(1)}, bf16[192,512]{1,0:T(8,128)(2,1)S(1)}, u32[]{:S(2)}, u32[]{:S(2)}) collective-permute-start(bf16[192,512]{1,0:T(8,128)(2,1)S(1)} %get-tuple-element.56.mine_ref), channel_id=1, source_target_pairs={{2,0},{0,4},{4,8},{8,12},{12,14},{14,10},{10,6},{6,2},{3,1},{1,5},... | collective-permute-start | bytes 589832 | tf_op jit(solution)/shard_map/ppermute | solution.py:442
  3.6 6.7 %collective-permute-start.3 = (bf16[192,512]{1,0:T(8,128)(2,1)S(1)}, bf16[192,512]{1,0:T(8,128)(2,1)S(1)}, u32[]{:S(2)}, u32[]{:S(2)}) collective-permute-start(bf16[192,512]{1,0:T(8,128)(2,1)S(1)} %get-tuple-element.56.mine_ref), channel_id=1, source_target_pairs={{0,2},{4,0},{8,4},{12,8},{14,12},{10,14},{6,10},{2,6},{1,3},{5,1},... | collective-permute-start | bytes 589832 | tf_op jit(solution)/shard_map/ppermute | solution.py:443
  10.0 2.5 %collective-permute-start.5 = (bf16[192,512]{1,0:T(8,128)(2,1)S(1)}, bf16[192,512]{1,0:T(8,128)(2,1)S(1)}, u32[]{:S(2)}, u32[]{:S(2)}) collective-permute-start(bf16[192,512]{1,0:T(8,128)(2,1)S(1)} %collective-permute-done.1.block_ref.mine_ref), channel_id=1, source_target_pairs={{0,1},{1,0},{2,3},{3,2},{4,5},{5,4},{6,7},{7,6},{8,9},{9,8},{10,11... | collective-permute-start | bytes 589832 | tf_op jit(solution)/shard_map/ppermute | solution.py:465
  10.2 3.6 %collective-permute-start.4 = (bf16[192,512]{1,0:T(8,128)(2,1)S(1)}, bf16[192,512]{1,0:T(8,128)(2,1)S(1)}, u32[]{:S(2)}, u32[]{:S(2)}) collective-permute-start(bf16[192,512]{1,0:T(8,128)(2,1)S(1)} %collective-permute-done.3.mine_ref), channel_id=1, source_target_pairs={{0,1},{1,0},{2,3},{3,2},{4,5},{5,4},{6,7},{7,6},{8,9},{9,8},{10,11... | collective-permute-start | bytes 589832 | tf_op jit(solution)/shard_map/ppermute | solution.py:465
  10.5 7.1 %collective-permute-start.2 = (bf16[192,512]{1,0:T(8,128)(2,1)S(1)}, bf16[192,512]{1,0:T(8,128)(2,1)S(1)}, u32[]{:S(2)}, u32[]{:S(2)}) collective-permute-start(bf16[192,512]{1,0:T(8,128)(2,1)S(1)} %collective-permute-done.1.block_ref.mine_ref), channel_id=1, source_target_pairs={{2,0},{0,4},{4,8},{8,12},{12,14},{14,10},{10,6},{6,2},{3,1},{1,5},... | collective-permute-start | bytes 589832 | tf_op jit(solution)/shard_map/ppermute | solution.py:462
  11.8 7.0 %collective-permute-start.7 = (bf16[192,512]{1,0:T(8,128)(2,1)S(1)}, bf16[192,512]{1,0:T(8,128)(2,1)S(1)}, u32[]{:S(2)}, u32[]{:S(2)}) collective-permute-start(bf16[192,512]{1,0:T(8,128)(2,1)S(1)} %collective-permute-done.3.mine_ref), channel_id=1, source_target_pairs={{0,2},{4,0},{8,4},{12,8},{14,12},{10,14},{6,10},{2,6},{1,3},{5,1},... | collective-permute-start | bytes 589832 | tf_op jit(solution)/shard_map/ppermute | solution.py:463
  17.6 3.3 %collective-permute-start.9 = (bf16[192,512]{1,0:T(8,128)(2,1)S(1)}, bf16[192,512]{1,0:T(8,128)(2,1)S(1)}, u32[]{:S(2)}, u32[]{:S(2)}) collective-permute-start(bf16[192,512]{1,0:T(8,128)(2,1)S(1)} %collective-permute-done.2.block_ref.mine_ref), channel_id=1, source_target_pairs={{0,1},{1,0},{2,3},{3,2},{4,5},{5,4},{6,7},{7,6},{8,9},{9,8},{10,11... | collective-permute-start | bytes 589832 | tf_op jit(solution)/shard_map/ppermute | solution.py:465
  18.9 3.4 %collective-permute-start.8 = (bf16[192,512]{1,0:T(8,128)(2,1)S(1)}, bf16[192,512]{1,0:T(8,128)(2,1)S(1)}, u32[]{:S(2)}, u32[]{:S(2)}) collective-permute-start(bf16[192,512]{1,0:T(8,128)(2,1)S(1)} %collective-permute-done.7.mine_ref), channel_id=1, source_target_pairs={{0,1},{1,0},{2,3},{3,2},{4,5},{5,4},{6,7},{7,6},{8,9},{9,8},{10,11... | collective-permute-start | bytes 589832 | tf_op jit(solution)/shard_map/ppermute | solution.py:465
  18.9 7.3 %collective-permute-start.6 = (bf16[192,512]{1,0:T(8,128)(2,1)S(1)}, bf16[192,512]{1,0:T(8,128)(2,1)S(1)}, u32[]{:S(2)}, u32[]{:S(2)}) collective-permute-start(bf16[192,512]{1,0:T(8,128)(2,1)S(1)} %collective-permute-done.2.block_ref.mine_ref), channel_id=1, source_target_pairs={{2,0},{0,4},{4,8},{8,12},{12,14},{14,10},{10,6},{6,2},{3,1},{1,5},... | collective-permute-start | bytes 589832 | tf_op jit(solution)/shard_map/ppermute | solution.py:462
  20.4 7.0 %collective-permute-start.11 = (bf16[192,512]{1,0:T(8,128)(2,1)S(1)}, bf16[192,512]{1,0:T(8,128)(2,1)S(1)}, u32[]{:S(2)}, u32[]{:S(2)}) collective-permute-start(bf16[192,512]{1,0:T(8,128)(2,1)S(1)} %collective-permute-done.7.mine_ref), channel_id=1, source_target_pairs={{0,2},{4,0},{8,4},{12,8},{14,12},{10,14},{6,10},{2,6},{1,3},{5,1},... | collective-permute-start | bytes 589832 | tf_op jit(solution)/shard_map/ppermute | solution.py:463
  26.2 3.0 %collective-permute-start.13 = (bf16[192,512]{1,0:T(8,128)(2,1)S(1)}, bf16[192,512]{1,0:T(8,128)(2,1)S(1)}, u32[]{:S(2)}, u32[]{:S(2)}) collective-permute-start(bf16[192,512]{1,0:T(8,128)(2,1)S(1)} %collective-permute-done.6.block_ref.mine_ref), channel_id=1, source_target_pairs={{0,1},{1,0},{2,3},{3,2},{4,5},{5,4},{6,7},{7,6},{8,9},{9,8},{10,11... | collective-permute-start | bytes 589832 | tf_op jit(solution)/shard_map/ppermute | solution.py:465
  27.5 3.0 %collective-permute-start.12 = (bf16[192,512]{1,0:T(8,128)(2,1)S(1)}, bf16[192,512]{1,0:T(8,128)(2,1)S(1)}, u32[]{:S(2)}, u32[]{:S(2)}) collective-permute-start(bf16[192,512]{1,0:T(8,128)(2,1)S(1)} %collective-permute-done.11.mine_ref), channel_id=1, source_target_pairs={{0,1},{1,0},{2,3},{3,2},{4,5},{5,4},{6,7},{7,6},{8,9},{9,8},{10,11... | collective-permute-start | bytes 589832 | tf_op jit(solution)/shard_map/ppermute | solution.py:465
  27.5 6.7 %collective-permute-start.10 = (bf16[160,512]{1,0:T(8,128)(2,1)S(1)}, bf16[160,512]{1,0:T(8,128)(2,1)S(1)}, u32[]{:S(2)}, u32[]{:S(2)}) collective-permute-start(bf16[160,512]{1,0:T(8,128)(2,1)S(1)} %slice.6), channel_id=1, source_target_pairs={{2,0},{0,4},{4,8},{8,12},{12,14},{14,10},{10,6},{6,2},{3,1},{1,5},... | collective-permute-start | bytes 491528 | tf_op jit(solution)/shard_map/ppermute | solution.py:462
  31.8 7.5 %copy-start.2 = (bf16[512,1024]{1,0:T(8,128)(2,1)S(1)}, bf16[512,1024]{1,0:T(8,128)(2,1)}, u32[]{:S(2)}) copy-start(bf16[512,1024]{1,0:T(8,128)(2,1)} %weight_ref.22) | copy-start | bytes 3145732
  34.2 5.1 %collective-permute-start.14 = (bf16[160,512]{1,0:T(8,128)(2,1)S(1)}, bf16[160,512]{1,0:T(8,128)(2,1)S(1)}, u32[]{:S(2)}, u32[]{:S(2)}) collective-permute-start(bf16[160,512]{1,0:T(8,128)(2,1)S(1)} %collective-permute-done.10.block_ref.mine_a), channel_id=1, source_target_pairs={{0,1},{1,0},{2,3},{3,2},{4,5},{5,4},{6,7},{7,6},{8,9},{9,8},{10,11... | collective-permute-start | bytes 491528 | tf_op jit(solution)/shard_map/ppermute | solution.py:465
  34.2 3.9 %collective-permute-start.15 = (bf16[32,512]{1,0:T(8,128)(2,1)S(1)}, bf16[32,512]{1,0:T(8,128)(2,1)S(1)}, u32[]{:S(2)}, u32[]{:S(2)}) collective-permute-start(bf16[32,512]{1,0:T(8,128)(2,1)S(1)} %slice.7), channel_id=1, source_target_pairs={{0,2},{4,0},{8,4},{12,8},{14,12},{10,14},{6,10},{2,6},{1,3},{5,1},... | collective-permute-start | bytes 98312 | tf_op jit(solution)/shard_map/ppermute | solution.py:463
  38.1 1.2 %collective-permute-start.16 = (bf16[32,512]{1,0:T(8,128)(2,1)S(1)}, bf16[32,512]{1,0:T(8,128)(2,1)S(1)}, u32[]{:S(2)}, u32[]{:S(2)}) collective-permute-start(bf16[32,512]{1,0:T(8,128)(2,1)S(1)} %collective-permute-done.15.mine_b), channel_id=1, source_target_pairs={{0,1},{1,0},{2,3},{3,2},{4,5},{5,4},{6,7},{7,6},{8,9},{9,8},{10,11... | collective-permute-start | bytes 98312 | tf_op jit(solution)/shard_map/ppermute | solution.py:465
  39.3 3.0 %copy-start.3 = (bf16[2,1024,256]{2,1,0:T(8,128)(2,1)S(1)}, bf16[2,1024,256]{2,1,0:T(8,128)(2,1)}, u32[]{:S(2)}) copy-start(bf16[2,1024,256]{2,1,0:T(8,128)(2,1)} %lateral_ref.1) | copy-start | bytes 3145732
  39.3 3.0 %copy-start.4 = (f32[2,2,256]{2,1,0:T(2,128)S(1)}, f32[2,2,256]{2,1,0:T(2,128)}, u32[]{:S(2)}) copy-start(f32[2,2,256]{2,1,0:T(2,128)} %gain_ref.5) | copy-start | bytes 12292
  40.7 4.7 %copy-start.1 = (bf16[2,3,3,256,256]{4,3,2,1,0:T(8,128)(2,1)S(1)}, bf16[2,3,3,256,256]{4,3,2,1,0:T(8,128)(2,1)}, u32[]{:S(2)}) copy-start(bf16[2,3,3,256,256]{4,3,2,1,0:T(8,128)(2,1)} %weight_ref.25) | copy-start | bytes 7077892
  40.7 1.6 %collective-permute-start.17 = (bf16[2,64,1024]{2,1,0:T(8,128)(2,1)S(1)}, bf16[2,64,1024]{2,1,0:T(8,128)(2,1)S(1)}, u32[]{:S(2)}, u32[]{:S(2)}) collective-permute-start(bf16[2,64,1024]{2,1,0:T(8,128)(2,1)S(1)} %get-tuple-element.99), channel_id=1, source_target_pairs={{0,1},{1,0},{2,3},{3,2},{4,5},{5,4},{6,7},{7,6},{8,9},{9,8},{10,11... | collective-permute-start | bytes 786440 | tf_op jit(solution)/shard_map/ppermute | solution.py:496
  42.8 5.0 %collective-permute-start.19 = (bf16[96,256]{1,0:T(8,128)(2,1)S(1)}, bf16[96,256]{1,0:T(8,128)(2,1)S(1)}, u32[]{:S(2)}, u32[]{:S(2)}) collective-permute-start(bf16[96,256]{1,0:T(8,128)(2,1)S(1)} %get-tuple-element.101.first_ref), channel_id=1, source_target_pairs={{0,2},{2,4},{4,6},{6,8},{8,10},{10,12},{12,14},{3,1},{5,3},{7,5},{... | collective-permute-start | bytes 147464 | tf_op jit(solution)/shard_map/ppermute | solution.py:526
  45.4 5.0 %collective-permute-start.18 = (bf16[96,256]{1,0:T(8,128)(2,1)S(1)}, bf16[96,256]{1,0:T(8,128)(2,1)S(1)}, u32[]{:S(2)}, u32[]{:S(2)}) collective-permute-start(bf16[96,256]{1,0:T(8,128)(2,1)S(1)} %get-tuple-element.100.second_ref), channel_id=1, source_target_pairs={{1,3},{3,5},{5,7},{7,9},{9,11},{11,13},{13,15},{2,0},{4,2},{6,4},{... | collective-permute-start | bytes 147464 | tf_op jit(solution)/shard_map/ppermute | solution.py:525
